TPU v7x, 256 devices: a whole 4x4x8 slice. The times are simulated.
256 devices in a mesh: ctx: 32 (over z, x_hi, core), tp: 8 (over y, x_lo).
Axes of the slice: x: 4 (x_hi: 2, x_lo: 2; x = x_hi * 2 + x_lo), y: 4, z: 8, core: 2. Of those that a mesh axis runs over, the one named last changes fastest.
Arguments:
- compressed: bfloat16 [4096, 1536], P('ctx', 'tp'), may hold values from -6 to 6
- latent: bfloat16 [4096, 576], P('ctx'), may hold values from -276 to 276
- w_uq: bfloat16 [1536, 12288], P(None, 'tp'), may hold values from -0.15625 to 0.15625
- w_uk: bfloat16 [512, 8192], P('ctx', 'tp'), may hold values from -0.5 to 0.5
- w_uv: bfloat16 [512, 8192], P('ctx', 'tp'), may hold values from -0.8984375 to 0.8984375
- span_ids: int32 [64], replicated, may hold values from 0 to 63, as said below
Outputs:
- attended: bfloat16 [4096, 8192], P('ctx', 'tp')
Inputs may be any that keep to these rules, and one draw needn't show every extreme that they name: `span_ids`: entries 2 d and 2 d + 1 hold spans c and 63 - c for some c < 32, in that order; every span appears once.
All inputs are finite; a program needn't handle non-finite values.
Results may differ from a plain program's by a relative error of at most 0.0085.
The roundings to bfloat16 on the way count: a program that leaves them out, or rounds other values in their place, can miss the bound.
Values may be sent and summed in bfloat16 or wider, within the bound.
No kernel may reach another device: no remote copies, remote signals or barrier semaphores. Data moves between devices by JAX's collectives and lax.ppermute only.
A program may use at most 64 MiB of HBM per device.

v0:
```python
import jax
import jax.numpy as jnp
from jax import lax
from jax.sharding import PartitionSpec as P

NOPE = 128
ROPE = 64
VDIM = 128
KV = 512


def per_device(compressed, latent, w_uq, w_uk, w_uv, span_ids):
    row_count = compressed.shape[0]
    span_len = row_count // 2
    heads_dev = w_uk.shape[1] // NOPE
    span_count = span_ids.shape[0]
    total_slots = span_count * span_len
    softmax_scale = (NOPE + ROPE) ** (-0.5)
    query_proj = jnp.dot(
        lax.all_gather(compressed, "tp", axis=1, tiled=True),
        w_uq,
        preferred_element_type=jnp.float32,
    )
    query_proj = query_proj.astype(jnp.bfloat16).reshape(row_count, heads_dev, NOPE + ROPE)
    q_nope = query_proj[:, :, :NOPE]
    q_rope = query_proj[:, :, NOPE:]
    shard_rows = lax.all_gather(w_uk, "ctx", axis=0, tiled=True)
    key_block = shard_rows.reshape(shard_rows.shape[0], heads_dev, NOPE)
    q_latent = jnp.einsum(
        "rhk,chk->rhc", q_nope, key_block, preferred_element_type=jnp.float32
    ).astype(jnp.bfloat16)
    q_full = jnp.concatenate([q_latent, q_rope], axis=2)
    positions = jnp.repeat(
        span_ids, span_len, total_repeat_length=total_slots
    ) * span_len + jnp.tile(jnp.arange(span_len, dtype=jnp.int32), span_count)
    q_positions = lax.dynamic_slice_in_dim(positions, lax.axis_index("ctx") * row_count, row_count)
    queries = [
        q_full[slot_j * span_len : (slot_j + 1) * span_len].reshape(span_len * heads_dev, KV + ROPE)
        for slot_j in range(2)
    ]
    query_pos = [q_positions[slot_j * span_len : (slot_j + 1) * span_len] for slot_j in range(2)]

    def update(state, q_matrix, q_pos, key_rows, key_pos):
        highest, totals, running = state
        scores = (
            lax.dot_general(
                q_matrix, key_rows, (((1,), (1,)), ((), ())), preferred_element_type=jnp.float32
            )
            * softmax_scale
        )
        visible = key_pos[None, :] <= q_pos[:, None]
        visible = jnp.broadcast_to(
            visible[:, None, :], (q_pos.shape[0], heads_dev, key_pos.shape[0])
        ).reshape(q_matrix.shape[0], key_pos.shape[0])
        scores = jnp.where(visible, scores, -1e30)
        new_high = jnp.maximum(highest, jnp.max(scores, axis=1))
        weights = jnp.where(visible, jnp.exp(scores - new_high[:, None]), 0.0)
        totals = jnp.sum(weights, axis=1)
        running = jnp.dot(
            weights.astype(jnp.bfloat16), key_rows[:, :KV], preferred_element_type=jnp.float32
        )
        return (new_high, totals, running)

    def visit_span(state, slot_j, key_rows, key_pos):
        return lax.cond(
            jnp.min(key_pos) <= jnp.max(query_pos[slot_j]),
            lambda inner: update(inner, queries[slot_j], query_pos[slot_j], key_rows, key_pos),
            lambda inner: inner,
            state,
        )

    score_rows = span_len * heads_dev
    initial = tuple(
        (
            (
                jnp.full((score_rows,), -1e30, jnp.float32),
                jnp.zeros((score_rows,), jnp.float32),
                jnp.zeros((score_rows, KV), jnp.float32),
            )
            for slot_j in range(2)
        )
    )

    def fold_keys(states, shard_rows):
        key_pos = lax.slice_in_dim(positions, 0, shard_rows.shape[0], axis=0)
        return tuple(
            (visit_span(states[slot_j], slot_j, shard_rows, key_pos) for slot_j in range(2))
        )

    states = fold_keys(initial, lax.all_gather(latent, "ctx", axis=0, tiled=True))
    mixed = jnp.concatenate(
        [
            (states[slot_j][2] / states[slot_j][1][:, None])
            .astype(jnp.bfloat16)
            .reshape(span_len, heads_dev, KV)
            for slot_j in range(2)
        ],
        axis=0,
    )
    shard_rows = lax.all_gather(w_uv, "ctx", axis=0, tiled=True)
    value_block = shard_rows.reshape(shard_rows.shape[0], heads_dev, VDIM)
    result = jnp.einsum("rhc,chv->rhv", mixed, value_block, preferred_element_type=jnp.float32)
    return result.reshape(row_count, heads_dev * VDIM).astype(jnp.bfloat16)


def solution(mesh):
    placed = (P("ctx", "tp"), P("ctx", None), P(None, "tp"), P("ctx", "tp"), P("ctx", "tp"), P())
    return jax.shard_map(
        per_device, mesh=mesh, in_specs=placed, out_specs=P("ctx", "tp"), check_vma=False
    )
```

profile of v0, /device:TPU:1, one launch (start us, length us, event | category | flops | bytes accessed | tf_op | source)
XLA Modules:
  0.0 294.5 jit_solution(12755800408900300186)
XLA Ops:
  6.5 0.0 all-gather.4.cloned.1.call-start
  6.5 0.7 all-gather.4.cloned.1.call-update
  7.3 0.0 all-gather.8.cloned.1.call-start
  7.3 0.7 all-gather.8.cloned.1.call-update
  8.0 0.0 all-gather.6.cloned.1.call-start
  8.1 1.7 copy.31
  9.8 0.0 all-gather.6.cloned.1.call-update
  9.8 0.1 tile.14
  9.9 25.2 %all_gather.12 = bf16[128,1536]{0,1:T(8,128)(2,1)S(1)} all-gather(bf16[128,192]{0,1:T(8,128)(2,1)} %param.12), channel_id=1, replica_groups=mesh['ctx'=32,'tp'=8] {'tp'}, dimensions={1}, use_global_device_ids=true | all-gather | bytes 442368 | tf_op jit(solution)/shard_map/all_gather | solution.py:20
  35.1 3.2 %convolution_convert_fusion = bf16[128,1536]{1,0:T(8,128)(2,1)S(1)} fusion(bf16[128,1536]{0,1:T(8,128)(2,1)S(1)} %all_gather.12, bf16[1536,1536]{1,0:T(8,128)(2,1)} %param.14), kind=kOutput, calls=%fused_computation.38 | convolution fusion | flops 604176384 | bytes 5505024 | tf_op jit(solution)/shard_map/dot_general | solution.py:19
  38.3 0.2 copy.26
  38.5 0.2 copy.40
  38.7 0.1 broadcast.180
  38.8 0.1 reshape.182
  38.9 0.8 add_add_fusion.1
  39.7 0.1 add.86
  39.8 0.1 sub.31
  39.9 1.6 fusion.41
  41.5 2.1 fusion.38
  43.5 2.1 fusion.39
  45.6 2.1 fusion.40
  47.7 0.8 add_add_fusion.3
  48.5 4.5 %compare_select_fusion.1 = (s32[4096,1]{0,1:T(1,128)S(1)}, s32[4096,1]{0,1:T(1,128)S(1)}) fusion(s32[]{:T(128)} %bitcast.63, s32[]{:T(128)} %bitcast.64, s32[]{:T(128)} %bitcast.65, s32[]{:T(128)} %bitcast.66, s32[]{:T(128)} %bitcast.67, s32[]{:T(128)} %bitcast.69, s32[]{:T(128)} %bitcast.68, s32[4096,1]{0,1:T(1,128)S(1)} %bitcast.133, ...), kind=kLoop, calls=%fused_computation.109 | loop fusion | flops 57344 | bytes 65564 | tf_op jit(solution)/shard_map/jit(_take)/gather | solution.py:33
  53.0 2.9 compare_reduce_fusion.56
  55.9 0.0 copy-done.1
  55.9 35.8 %multiply_add_fusion = (s32[4096]{0:T(1024)S(1)}, s32[4096]{0:T(1024)S(1)}) fusion(s32[4096]{0:T(1024)S(1)} %tile.14, s32[32,128]{1,0:T(8,128)S(1)} %copy-done.1, s32[32]{0:T(128)S(1)} %iota_multiply_fusion, pred[4096]{0:T(1024)(128)(4,1)S(1)} %get-tuple-element.133, pred[4096]{0:T(1024)(128)(4,1)S(1)} %get-tuple-element.132, ...), kind=kLoop, calls=%fused_computation.122 | loop fusion | flops 278528 | bytes 315748 | tf_op jit(solution)/shard_map/add | solution.py:33
  91.7 0.1 dynamic_slice.3
  91.8 0.6 add_reduce_fusion
  92.4 0.7 slice_reduce_fusion.1
  95.6 0.0 all-gather.4.cloned.1.call-done
  95.7 1.5 copy.28
  97.2 72.0 %all-gather.8.cloned.1.call-done = bf16[512,1024]{1,0:T(8,128)(2,1)} async-done(((bf16[16,1024]{1,0:T(8,128)(2,1)}), bf16[512,1024]{1,0:T(8,128)(2,1)}) %all-gather.8.cloned.1.call-update) | async-done | bytes 1048592 | tf_op jit(solution)/shard_map/all_gather | solution.py:100
  169.2 2.3 copy.36
  171.5 0.5 fusion.30
  172.0 0.1 pad_maximum_fusion
  172.1 87.4 %all-gather.6.cloned.1.call-done = bf16[4096,576]{1,0:T(8,128)(2,1)} async-done(((bf16[128,576]{1,0:T(8,128)(2,1)}), bf16[4096,576]{1,0:T(8,128)(2,1)}) %all-gather.6.cloned.1.call-update) | async-done | bytes 4718608 | tf_op jit(solution)/shard_map/all_gather | solution.py:90
  259.5 13.2 %conditional.2 = (f32[512]{0:T(512)S(1)}, f32[512,512]{1,0:T(8,128)S(1)}) conditional(s32[]{:T(128)} %convert_element_type.36, () %tuple.25, (s32[4096]{0:T(1024)S(1)}, s32[64]{0:T(128)S(1)}, bf16[128,8,576]{2,0,1:T(8,128)(2,1)S(1)}, bf16[4096,576]{1,0:T(8,128)(2,1)}) %tuple.26), branch_computations={%region_2.3_spmd, %region_3.6_spmd} | conditional | flops 4590927360 | bytes 54948160 | solution.py:65
  259.5 0.2 broadcast_compare_fusion
  259.7 0.0 slice-start
  259.7 0.7 copy.32
  260.5 0.0 slice-start.1
  260.5 6.5 %fusion = (f32[512]{0:T(512)S(1)}, f32[512,4096]{1,0:T(8,128)S(1)}) fusion(pred[64,4096]{1,0:T(8,128)(4,1)S(1)} %broadcast_compare_fusion, bf16[4096,576]{1,0:T(8,128)(2,1)} %get-tuple-element.40, bf16[128,8,576]{2,1,0:T(8,128)(2,1)S(1)} %copy.32), kind=kOutput, calls=%fused_computation.2 | convolution fusion | flops 2422210048 | bytes 14026752 | tf_op jit(solution)/shard_map/cond/branch_1_fun/dot_general | solution.py:46
  267.0 0.0 slice-done
  267.1 0.0 slice-done.1
  267.1 2.6 fusion.3
  269.6 3.1 %fusion.2 = f32[512]{0:T(512)S(1)} fusion(f32[512,4096]{1,0:T(8,128)S(1)} %get-tuple-element.141, f32[512]{0:T(512)S(1)} %broadcast_maximum_fusion, pred[64,4096]{1,0:T(8,128)(4,1)S(1)} %broadcast_compare_fusion), kind=kLoop, calls=%fused_computation.4 | loop fusion | flops 10485248 | bytes 8654848 | tf_op jit(solution)/shard_map/cond/branch_1_fun/reduce_sum | solution.py:58
  272.7 0.1 fusion.34
  272.8 0.2 copy.34
  273.0 0.0 copy-start
  273.0 13.3 %conditional.3 = (f32[512]{0:T(512)S(1)}, f32[512,512]{1,0:T(8,128)S(1)}) conditional(s32[]{:T(128)} %convert_element_type.41, () %tuple.27, (s32[4096]{0:T(1024)S(1)}, s32[64]{0:T(128)S(1)}, bf16[128,8,576]{2,0,1:T(8,128)(2,1)S(1)}, bf16[4096,576]{1,0:T(8,128)(2,1)}) %tuple.28), branch_computations={%region_7.8_spmd, %region_8.11_spmd} | conditional | flops 4590927360 | bytes 54948160 | solution.py:65
  273.3 0.2 broadcast_compare_fusion.1
  273.5 0.0 slice-start.2
  273.5 0.7 copy.33
  274.2 0.0 slice-start.3
  274.2 6.5 %fusion.15 = (f32[512]{0:T(512)S(1)}, f32[512,4096]{1,0:T(8,128)S(1)}) fusion(pred[64,4096]{1,0:T(8,128)(4,1)S(1)} %broadcast_compare_fusion.1, bf16[4096,576]{1,0:T(8,128)(2,1)} %get-tuple-element.44, bf16[128,8,576]{2,1,0:T(8,128)(2,1)S(1)} %copy.33), kind=kOutput, calls=%fused_computation.21 | convolution fusion | flops 2422210048 | bytes 14026752 | tf_op jit(solution)/shard_map/cond/branch_1_fun/dot_general | solution.py:46
  280.8 0.0 slice-done.2
  280.8 0.0 slice-done.3
  280.8 2.5 fusion.18
  283.3 2.9 %fusion.17 = f32[512]{0:T(512)S(1)} fusion(f32[512,4096]{1,0:T(8,128)S(1)} %get-tuple-element.143, f32[512]{0:T(512)S(1)} %broadcast_maximum_fusion.1, pred[64,4096]{1,0:T(8,128)(4,1)S(1)} %broadcast_compare_fusion.1), kind=kLoop, calls=%fused_computation.23 | loop fusion | flops 10485248 | bytes 8654848 | tf_op jit(solution)/shard_map/cond/branch_1_fun/reduce_sum | solution.py:58
  286.3 0.1 fusion.35
  286.4 0.2 copy.35
  286.6 0.0 copy-done
  286.6 0.5 convolution_convert_fusion.2
  287.1 0.9 copy.37
  (8 shorter events, 0.0 us)
Async XLA Ops:
  6.5 49.4 %copy-start.1 = (s32[32,128]{1,0:T(8,128)S(1)}, s32[32,128]{1,0:T(8,128)}, u32[]{:S(2)}) copy-start(s32[32,128]{1,0:T(8,128)} %constant.125.clone.1) | copy-start | bytes 49156
  6.5 89.1 %all-gather.4.cloned.1.call-start = ((), (), s32[]{:S(2)}) async-start(), calls=%async_computation | async-start | bytes 1081344 | tf_op jit(solution)/shard_map/all_gather | solution.py:27
  7.3 161.9 %all-gather.8.cloned.1.call-start = ((), (), s32[]{:S(2)}) async-start(), calls=%async_computation.2 | async-start | bytes 1081344 | tf_op jit(solution)/shard_map/all_gather | solution.py:100
  8.0 251.5 %all-gather.6.cloned.1.call-start = ((), (), s32[]{:S(2)}) async-start(), calls=%async_computation.1 | async-start | bytes 5406720 | tf_op jit(solution)/shard_map/all_gather | solution.py:90
  259.7 7.3 %slice-start = ((s8[5242880]{0:T(1024)(128)(4,1)}), s8[4194304]{0:T(1024)(128)(4,1)S(1)}, s32[]{:S(2)}) async-start(s8[5242880]{0:T(1024)(128)(4,1)} %bitcast.135), calls=%async_computation.3 | async-start | bytes 8388608 | tf_op jit(solution)/shard_map/cond
  260.5 6.6 %slice-start.1 = ((s8[5242880]{0:T(1024)(128)(4,1)}), s8[1048576]{0:T(1024)(128)(4,1)S(1)}, s32[]{:S(2)}) async-start(s8[5242880]{0:T(1024)(128)(4,1)} %bitcast.135), calls=%async_computation.4 | async-start | bytes 2097152 | tf_op jit(solution)/shard_map/cond
  273.0 13.6 %copy-start = (bf16[512,1024]{0,1:T(8,128)(2,1)S(1)}, bf16[512,1024]{0,1:T(8,128)(2,1)}, u32[]{:S(2)}) copy-start(bf16[512,1024]{0,1:T(8,128)(2,1)} %copy.36) | copy-start | bytes 3145732
  273.5 7.3 %slice-start.2 = ((s8[5242880]{0:T(1024)(128)(4,1)}), s8[4194304]{0:T(1024)(128)(4,1)S(1)}, s32[]{:S(2)}) async-start(s8[5242880]{0:T(1024)(128)(4,1)} %bitcast.137), calls=%async_computation.5 | async-start | bytes 8388608 | tf_op jit(solution)/shard_map/cond
  274.2 6.6 %slice-start.3 = ((s8[5242880]{0:T(1024)(128)(4,1)}), s8[1048576]{0:T(1024)(128)(4,1)S(1)}, s32[]{:S(2)}) async-start(s8[5242880]{0:T(1024)(128)(4,1)} %bitcast.137), calls=%async_computation.6 | async-start | bytes 2097152 | tf_op jit(solution)/shard_map/cond
Sparse Core Ops, SparseCore 0:
  10.1 81.7 all-gather.3
  94.7 74.4 all-gather.7
  172.0 87.5 all-gather.5
where the time goes:
time: 295 us; the launch traced here: 294 us
  waiting for transfers between devices  161 us (55%)
  other arithmetic  53 us (18%)
  blocking collectives  25.2 us (9%)
  matrix products  22.2 us (8%)
  local copies, waits for them, and re-layouts  16.9 us (6%)
  between operations  15.7 us (5%)
    all_gather x1, waiting for transfers between devices, per_device(): lax.all_gather(latent, 'ctx', axis=0, tiled=True)  87.4 us
    all_gather x1, waiting for transfers between devices, per_device(): shard_rows = lax.all_gather(w_uv, 'ctx', axis=0, tiled=True)  72 us
    add x1, other arithmetic, per_device(): jnp.repeat(span_ids, span_len, total_repeat_length=total_slots) * span_len  35.8 us
    all_gather x1, blocking collectives, per_device(): lax.all_gather(compressed, 'tp', axis=1, tiled=True)  25.2 us
    dot_general x2, matrix products, update(): lax.dot_general(q_matrix, key_rows, (((1,), (1,)), ((), ())), preferred_e...  13.1 us
    gather x4, local copies, waits for them, and re-layouts, per_device(): jnp.repeat(span_ids, span_len, total_repeat_length=total_slots) * span_len  7.81 us
    gather x2, other arithmetic, per_device(): jnp.repeat(span_ids, span_len, total_repeat_length=total_slots) * span_len  7.4 us
    reduce_sum x2, other arithmetic, update(): totals = jnp.sum(weights, axis=1)  6.01 us
  transfers between devices with their start and end apart: 3, of which 2 were waited for; matrix products, arithmetic and copies ran while one was open for 22% of the time, Pallas kernels for 0%

commit v1 on v0

v1 whole, which is shorter than its diff:
```python
import functools
import math

import jax
import jax.numpy as jnp
from jax import lax
from jax.experimental import pallas as pl
from jax.experimental.pallas import tpu as pltpu
from jax.sharding import Mesh, PartitionSpec as P

NOPE = 128
ROPE = 64
VDIM = 128
KV = 512
KW = 640
SPAN = 64
MASKED = -1e30
EXP2_SCALE = (NOPE + ROPE) ** (-0.5) * math.log2(math.e)


def gather_blocks(x, axes, count):
    copies = jnp.broadcast_to(x[None], (count,) + x.shape)
    return lax.all_to_all(copies, axes, 0, 0, tiled=True)


def other_core(x):
    return lax.ppermute(x, "core", [(0, 1), (1, 0)])


def dot_t(a, b):
    return lax.dot_general(a, b, (((1,), (1,)), ((), ())), preferred_element_type=jnp.float32)


def attend(q, keys, key_pos, q_pos, open_keys):
    s = dot_t(q, keys)
    masked = jnp.where(key_pos[:, open_keys:] <= q_pos, s[:, open_keys:], MASKED)
    if open_keys:
        s = jnp.concatenate([s[:, :open_keys], masked], axis=1)
    else:
        s = masked
    high = jnp.max(s, axis=1, keepdims=True)
    w = jnp.exp2((s - high) * EXP2_SCALE)
    total = jnp.sum(w, axis=1, keepdims=True)
    acc = jnp.dot(w.astype(jnp.bfloat16), keys[:, :KV], preferred_element_type=jnp.float32)
    return high, total, acc


def tiles(heads, tile):
    for slot in range(2):
        for row in range(0, heads * SPAN, tile):
            yield slot, row


def query_positions(scal_ref, slot, tile):
    within = lax.broadcasted_iota(jnp.int32, (tile, 1), 0) % SPAN
    return scal_ref[1 + slot] * SPAN + within


def weave(scal_ref, own_ref, oth_ref, dst_ref):
    core = scal_ref[0]
    rows = 16
    for i in range(own_ref.shape[0] // rows):
        at = pl.multiple_of((2 * i + core) * rows, rows)
        ot = pl.multiple_of((2 * i + 1 - core) * rows, rows)
        dst_ref[pl.ds(at, rows), :] = own_ref[i * rows : (i + 1) * rows, :]
        dst_ref[pl.ds(ot, rows), :] = oth_ref[i * rows : (i + 1) * rows, :]


def first_kernel(
    heads, tile, scal_ref, qn_ref, qr_ref, wko_ref, wkx_ref, key_ref, kpos_ref,
    qf_ref, m_ref, l_ref, acc_ref, wk_ref,
):
    weave(scal_ref, wko_ref, wkx_ref, wk_ref)
    for h in range(heads):
        cols = slice(h * NOPE, (h + 1) * NOPE)
        q_latent = dot_t(qn_ref[:, cols], wk_ref[:, cols]).astype(jnp.bfloat16)
        for slot in range(2):
            rows = slice(h * SPAN, (h + 1) * SPAN)
            toks = slice(slot * SPAN, (slot + 1) * SPAN)
            qf_ref[slot, rows, :KV] = q_latent[toks, :]
            qf_ref[slot, rows, KV:] = qr_ref[toks, cols]
    half = key_ref.shape[0] // 2
    for slot, row in tiles(heads, tile):
        rows = slice(row, row + tile)
        n = half if slot == 0 else 2 * half
        high, total, acc = attend(
            qf_ref[slot, rows, :], key_ref[:n, :], kpos_ref[:, :n],
            query_positions(scal_ref, slot, tile), 0 if slot == 0 else half,
        )
        m_ref[slot, rows, :] = jnp.broadcast_to(high, (tile, 128))
        l_ref[slot, rows, :] = jnp.broadcast_to(total, (tile, 128))
        acc_ref[slot, rows, :] = acc


def second_kernel(
    heads, tile, scal_ref, qf_ref, m_ref, l_ref, acc_ref, key_ref, kpos_ref, wvo_ref, wvx_ref,
    out_ref, wv_ref, mix_ref,
):
    weave(scal_ref, wvo_ref, wvx_ref, wv_ref)
    half = key_ref.shape[0] // 2
    for slot, row in tiles(heads, tile):
        rows = slice(row, row + tile)
        n = half if slot == 0 else 2 * half
        high, total, acc = attend(
            qf_ref[slot, rows, :], key_ref[:n, :], kpos_ref[:, :n],
            query_positions(scal_ref, slot, tile), 0 if slot == 0 else half,
        )
        high0 = m_ref[slot, rows, :1]
        top = jnp.maximum(high, high0)
        a0 = jnp.exp2((high0 - top) * EXP2_SCALE)
        a1 = jnp.exp2((high - top) * EXP2_SCALE)
        total = a0 * l_ref[slot, rows, :1] + a1 * total
        mixed = (a0 * acc_ref[slot, rows, :] + a1 * acc) / total
        mix_ref[slot, rows, :] = mixed.astype(jnp.bfloat16)
    for h in range(heads):
        cols = slice(h * VDIM, (h + 1) * VDIM)
        rows = slice(h * SPAN, (h + 1) * SPAN)
        both = jnp.concatenate([mix_ref[0, rows, :], mix_ref[1, rows, :]], axis=0)
        out_ref[:, cols] = jnp.dot(
            both, wv_ref[:, cols], preferred_element_type=jnp.float32
        ).astype(jnp.bfloat16)


def call(kernel, outs, scratch, flops, *args):
    specs = [pl.BlockSpec(memory_space=pltpu.SMEM)] + [
        pl.BlockSpec(memory_space=pltpu.VMEM) for _ in args[1:]
    ]
    size = sum(math.prod(a.shape) * a.dtype.itemsize for a in args)
    return pl.pallas_call(
        kernel,
        out_shape=outs,
        in_specs=specs,
        out_specs=jax.tree.map(lambda _: pl.BlockSpec(memory_space=pltpu.VMEM), outs),
        scratch_shapes=scratch,
        compiler_params=pltpu.CompilerParams(vmem_limit_bytes=48 << 20),
        cost_estimate=pl.CostEstimate(flops=flops, bytes_accessed=size, transcendentals=flops // 1000),
    )(*args)


def per_device(compressed, latent, w_uq, w_uk, w_uv, span_ids):
    toks = compressed.shape[0]
    heads = w_uk.shape[1] // NOPE
    zs, xhs, ys, xls = (lax.axis_size(a) for a in ("z", "xh", "y", "xl"))
    tps = ys * xls
    core = lax.axis_index("core")
    tp = lax.axis_index(("y", "xl"))
    ctx = lax.axis_index(("z", "xh", "core"))
    part = toks // tps

    mine = lax.dynamic_slice_in_dim(latent, tp * part, part, 0)
    mine = jnp.pad(mine, ((0, 0), (0, KW - latent.shape[1])))
    column = gather_blocks(mine, "z", zs).reshape(zs * part, KW)
    keys = gather_blocks(column, ("y", "xl", "xh"), tps * xhs).reshape(-1, KW)
    keys_x = other_core(keys)

    features = gather_blocks(compressed.T, ("y", "xl"), tps).reshape(-1, toks)
    query = lax.dot_general(
        features, w_uq, (((0,), (0,)), ((), ())), preferred_element_type=jnp.float32
    ).astype(jnp.bfloat16)
    query = query.reshape(toks, heads, NOPE + ROPE)
    q_nope = query[:, :, :NOPE].reshape(toks, heads * NOPE)
    q_rope = jnp.pad(query[:, :, NOPE:], ((0, 0), (0, 0), (0, KW - KV - ROPE)))
    q_rope = q_rope.reshape(toks, heads * (KW - KV))

    wk = gather_blocks(w_uk, ("z", "xh"), zs * xhs).reshape(-1, w_uk.shape[1])
    wk_x = other_core(wk)
    wv = gather_blocks(w_uv, ("z", "xh"), zs * xhs).reshape(-1, w_uv.shape[1])
    wv_x = other_core(wv)

    spans = span_ids.reshape(zs, xhs, 2, 2)
    quarter = SPAN // part
    base = jnp.transpose(spans, (2, 3, 1, 0)) * SPAN
    base = jnp.broadcast_to(base[:, :, None, :, :, None], (2, 2, quarter, xhs, zs, part))
    offset = (
        jnp.arange(quarter, dtype=jnp.int32)[:, None, None, None] * part
        + jnp.arange(part, dtype=jnp.int32)[None, None, None, :]
    )
    kpos = (base + offset[None, None]).reshape(2, 1, -1)
    kpos_own = lax.dynamic_index_in_dim(kpos, core, 0, keepdims=False)
    kpos_oth = lax.dynamic_index_in_dim(kpos, 1 - core, 0, keepdims=False)
    scal = jnp.concatenate([core[None], lax.dynamic_slice_in_dim(span_ids, 2 * ctx, 2)])

    rows, tile = heads * SPAN, 256
    f32, b16 = jnp.float32, jnp.bfloat16
    shape = jax.ShapeDtypeStruct
    flops = 2 * 3 * rows * (keys.shape[0] // 2) * (KW + KV)
    qf, m, l, acc = call(
        functools.partial(first_kernel, heads, tile),
        (
            shape((2, rows, KW), b16),
            shape((2, rows, 128), f32),
            shape((2, rows, 128), f32),
            shape((2, rows, KV), f32),
        ),
        [pltpu.VMEM((KV, w_uk.shape[1]), b16)],
        flops, scal, q_nope, q_rope, wk, wk_x, keys, kpos_own,
    )
    return call(
        functools.partial(second_kernel, heads, tile),
        shape((toks, heads * VDIM), b16),
        [pltpu.VMEM((KV, w_uv.shape[1]), b16), pltpu.VMEM((2, rows, KV), b16)],
        flops, scal, qf, m, l, acc, keys_x, kpos_oth, wv, wv_x,
    )


def solution(mesh):
    fine = Mesh(mesh.devices.reshape(8, 2, 2, 4, 2), ("z", "xh", "core", "y", "xl"))
    ctx, tp = ("z", "xh", "core"), ("y", "xl")
    placed = (P(ctx, tp), P(ctx, None), P(None, tp), P(ctx, tp), P(ctx, tp), P())
    return jax.shard_map(
        per_device, mesh=fine, in_specs=placed, out_specs=P(ctx, tp), check_vma=False
    )
```

time: 295 us -> 133 us (0.45)
  the two profiles are of different devices: /device:TPU:1 before, /device:TPU:2 now
where the time goes in v1:
time: 133 us; the launch traced here: 132 us
  blocking collectives  55.6 us (42%)
  waiting for transfers between devices  38.7 us (29%)
  Pallas kernels  16 us (12%)
  starting transfers between devices  13.2 us (10%)
  local copies, waits for them, and re-layouts  5.29 us (4%)
  matrix products  3.16 us (2%)
    all_to_all x2, blocking collectives, gather_blocks(): return lax.all_to_all(copies, axes, 0, 0, tiled=True)  55.6 us
    all_to_all x3, waiting for transfers between devices, gather_blocks(): return lax.all_to_all(copies, axes, 0, 0, tiled=True)  38.7 us
    pallas_call x2, Pallas kernels, call(): pl.pallas_call(kernel, out_shape=outs, in_specs=specs, out_specs=jax.tree...  16 us
    all_to_all x3, starting transfers between devices, gather_blocks(): return lax.all_to_all(copies, axes, 0, 0, tiled=True)  12.3 us
    dot_general x1, matrix products, per_device(): lax.dot_general(features, w_uq, (((0,), (0,)), ((), ())), preferred_eleme...  3.16 us
    broadcast_in_dim x5, local copies, waits for them, and re-layouts, gather_blocks(): copies = jnp.broadcast_to(x[None], (count,) + x.shape)  2.92 us
  transfers between devices with their start and end apart: 6, of which 3 were waited for; matrix products, arithmetic and copies ran while one was open for 5% of the time, Pallas kernels for 6%

profile of v1, /device:TPU:2, one launch (start us, length us, event | category | flops | bytes accessed | tf_op | source)
XLA Modules:
  0.0 132.4 jit_solution(13010647709307549829)
XLA Ops:
  0.0 0.0 copy-start
  0.0 0.9 copy-done
  0.9 0.1 constant_dynamic-slice_fusion
  1.0 0.1 copy.16
  1.2 18.0 %all_to_all.25 = bf16[8,16,640]{2,1,0:T(8,128)(2,1)S(1)} all-to-all(bf16[8,16,640]{2,1,0:T(8,128)(2,1)S(1)} %broadcast_in_dim.21), channel_id=1, replica_groups=mesh['z'=8,'xh'=2,'core'=2,'y'=4,'xl'=2] {'z'}, dimensions={0} | all-to-all | bytes 327680 | tf_op jit(solution)/shard_map/all_to_all | solution.py:23
  19.2 0.3 broadcast_in_dim.23
  19.5 0.0 copy-start.2
  19.5 0.0 copy-start.3
  19.5 37.5 %all_to_all.26 = bf16[16,128,640]{2,1,0:T(8,128)(2,1)} all-to-all(bf16[16,128,640]{2,1,0:T(8,128)(2,1)S(1)} %broadcast_in_dim.23), channel_id=1, replica_groups=mesh['z'=8,'xh'=2,'core'=2,'y'=4,'xl'=2] {'y','xl','xh'}, dimensions={0} | all-to-all | bytes 5242880 | tf_op jit(solution)/shard_map/all_to_all | solution.py:23
  57.1 0.0 copy-done.2
  57.1 0.0 copy-start.4
  57.1 0.0 copy-start.1
  57.1 0.9 broadcast_in_dim.20
  58.0 4.5 %all-to-all-start.1 = ((bf16[16,16,1024]{2,1,0:T(8,128)(2,1)}), bf16[16,16,1024]{2,1,0:T(8,128)(2,1)S(1)}, u32[]{:S(2)}, u32[]{:S(2)}) async-start(bf16[16,16,1024]{2,1,0:T(8,128)(2,1)} %broadcast_in_dim.20), calls=%async_computation.1 | async-start | bytes 1048576 | tf_op jit(solution)/shard_map/all_to_all | solution.py:23
  62.5 0.1 collective-permute-start.1
  62.6 17.1 %all-to-all-done.1 = bf16[16,16,1024]{2,1,0:T(8,128)(2,1)S(1)} async-done(((bf16[16,16,1024]{2,1,0:T(8,128)(2,1)}), bf16[16,16,1024]{2,1,0:T(8,128)(2,1)S(1)}, u32[]{:S(2)}, u32[]{:S(2)}) %all-to-all-start.1) | async-done | bytes 524320 | tf_op jit(solution)/shard_map/all_to_all | solution.py:23
  79.8 0.0 copy-done.3
  79.8 0.9 broadcast_in_dim.26
  80.7 3.6 %all-to-all-start.4 = ((bf16[16,16,1024]{2,1,0:T(8,128)(2,1)}), bf16[16,16,1024]{2,1,0:T(8,128)(2,1)S(1)}, u32[]{:S(2)}, u32[]{:S(2)}) async-start(bf16[16,16,1024]{2,1,0:T(8,128)(2,1)} %broadcast_in_dim.26), calls=%async_computation.4 | async-start | bytes 1048576 | tf_op jit(solution)/shard_map/all_to_all | solution.py:23
  84.2 0.0 copy-done.4
  84.3 0.1 mul.42
  84.4 0.1 copy.13
  84.5 0.1 broadcast_in_dim.24
  84.6 0.1 broadcast_in_dim.25
  84.7 0.1 iota_add_fusion
  84.8 0.1 add.74
  84.9 15.7 %all-to-all-done.4 = bf16[16,16,1024]{2,1,0:T(8,128)(2,1)S(1)} async-done(((bf16[16,16,1024]{2,1,0:T(8,128)(2,1)}), bf16[16,16,1024]{2,1,0:T(8,128)(2,1)S(1)}, u32[]{:S(2)}, u32[]{:S(2)}) %all-to-all-start.4) | async-done | bytes 524320 | tf_op jit(solution)/shard_map/all_to_all | solution.py:23
  100.6 0.0 copy-done.1
  100.6 0.8 broadcast_in_dim.19
  101.4 4.2 %all-to-all-start = ((bf16[8,192,128]{2,1,0:T(8,128)(2,1)}), bf16[8,192,128]{2,1,0:T(8,128)(2,1)S(1)}, u32[]{:S(2)}, u32[]{:S(2)}) async-start(bf16[8,192,128]{2,1,0:T(8,128)(2,1)} %broadcast_in_dim.19), calls=%async_computation | async-start | bytes 786432 | tf_op jit(solution)/shard_map/all_to_all | solution.py:23
  105.6 0.1 collective-permute-start
  105.8 0.1 dynamic_slice.13
  105.9 0.1 pad_add_fusion.scal_ref
  105.9 0.7 collective-permute-start.2
  106.6 5.9 %all-to-all-done = bf16[8,192,128]{2,1,0:T(8,128)(2,1)S(1)} async-done(((bf16[8,192,128]{2,1,0:T(8,128)(2,1)}), bf16[8,192,128]{2,1,0:T(8,128)(2,1)S(1)}, u32[]{:S(2)}, u32[]{:S(2)}) %all-to-all-start) | async-done | bytes 393248 | tf_op jit(solution)/shard_map/all_to_all | solution.py:23
  112.5 3.2 %convolution_convert_fusion = bf16[128,1536]{1,0:T(8,128)(2,1)S(1)} fusion(bf16[1536,128]{1,0:T(8,128)(2,1)S(1)} %bitcast.29, bf16[1536,1536]{1,0:T(8,128)(2,1)} %param.8), kind=kOutput, calls=%fused_computation | convolution fusion | flops 604176384 | bytes 5505024 | tf_op jit(solution)/shard_map/dot_general | solution.py:157
  115.6 0.2 copy.9
  116.0 0.1 copy.15.qr_ref
  116.1 0.1 copy.14.qn_ref
  116.3 0.0 collective-permute-done.wkx_ref
  116.3 7.5 %shard_map.64 = (bf16[2,512,640]{2,1,0:T(8,128)(2,1)S(1)}, f32[2,512,128]{2,1,0:T(8,128)S(1)}, f32[2,512,128]{2,1,0:T(8,128)S(1)}, f32[2,512,512]{2,1,0:T(8,128)S(1)}) custom-call(s32[3]{0:T(128)S(1)} %pad_add_fusion.scal_ref, bf16[128,1024]{1,0:T(8,128)(2,1)S(1)} %copy.14.qn_ref, bf16[128,1024]{1,0:T(8,128)(2,1)S(1)} %copy.15.qr_ref, ...), custom_call_target="tpu_custom_call" | custom-call | flops 3623878656 | bytes 4202508 | tf_op jit(solution)/shard_map/pallas_call | solution.py:129
  123.8 0.0 collective-permute-done.2.wvx_ref
  123.8 0.0 collective-permute-done.1.key_ref
  123.8 8.5 %shard_map.65 = bf16[128,1024]{1,0:T(8,128)(2,1)} custom-call(s32[3]{0:T(128)S(1)} %pad_add_fusion.scal_ref, bf16[2,512,640]{2,1,0:T(8,128)(2,1)S(1)} %get-tuple-element.9.qf_ref, f32[2,512,128]{2,1,0:T(8,128)S(1)} %get-tuple-element.10.m_ref, f32[2,512,128]{2,1,0:T(8,128)S(1)} %get-tuple-element.11.l_ref, f32[2,512,512]{2,1,0:T(8,128)S(1)} %get-tuple-element.12.acc_ref, ...), custom_call_target="tpu_custom_call" | custom-call | flops 3623878656 | bytes 8134668 | tf_op jit(solution)/shard_map/pallas_call | solution.py:129
  (10 shorter events, 0.1 us)
Async XLA Ops:
  0.0 0.9 copy-start
  19.5 37.6 %copy-start.2 = (bf16[16,1024]{1,0:T(8,128)(2,1)S(1)}, bf16[16,1024]{1,0:T(8,128)(2,1)}, u32[]{:S(2)}) copy-start(bf16[16,1024]{1,0:T(8,128)(2,1)} %param.9) | copy-start | bytes 98308
  19.5 60.2 %copy-start.3 = (bf16[16,1024]{1,0:T(8,128)(2,1)S(1)}, bf16[16,1024]{1,0:T(8,128)(2,1)}, u32[]{:S(2)}) copy-start(bf16[16,1024]{1,0:T(8,128)(2,1)} %param.10) | copy-start | bytes 98308
  57.1 27.2 %copy-start.4 = (s32[64]{0:T(128)S(1)}, s32[64]{0:T(128)}, u32[]{:S(2)}) copy-start(s32[64]{0:T(128)} %param.11) | copy-start | bytes 772
  57.1 43.5 %copy-start.1 = (bf16[128,192]{0,1:T(8,128)(2,1)S(1)}, bf16[128,192]{0,1:T(8,128)(2,1)}, u32[]{:S(2)}) copy-start(bf16[128,192]{0,1:T(8,128)(2,1)} %param.6) | copy-start | bytes 147460
  58.0 21.8 %all-to-all-start.1 = ((bf16[16,16,1024]{2,1,0:T(8,128)(2,1)}), bf16[16,16,1024]{2,1,0:T(8,128)(2,1)S(1)}, u32[]{:S(2)}, u32[]{:S(2)}) async-start(bf16[16,16,1024]{2,1,0:T(8,128)(2,1)} %broadcast_in_dim.20), calls=%async_computation.1 | async-start | bytes 1048576 | tf_op jit(solution)/shard_map/all_to_all | solution.py:23
  62.5 61.3 %collective-permute-start.1 = (bf16[2048,640]{1,0:T(8,128)(2,1)}, bf16[2048,640]{1,0:T(8,128)(2,1)}, u32[]{:S(2)}, u32[]{:S(2)}) collective-permute-start(bf16[2048,640]{1,0:T(8,128)(2,1)} %bitcast.25), channel_id=1, source_target_pairs={{0,8},{8,0},{1,9},{9,1},{2,10},{10,2},{3,11},{11,3},{4,12},{12,4},... | collective-permute-start | bytes 7864328 | tf_op jit(solution)/shard_map/ppermute | solution.py:27
  80.7 19.9 %all-to-all-start.4 = ((bf16[16,16,1024]{2,1,0:T(8,128)(2,1)}), bf16[16,16,1024]{2,1,0:T(8,128)(2,1)S(1)}, u32[]{:S(2)}, u32[]{:S(2)}) async-start(bf16[16,16,1024]{2,1,0:T(8,128)(2,1)} %broadcast_in_dim.26), calls=%async_computation.4 | async-start | bytes 1048576 | tf_op jit(solution)/shard_map/all_to_all | solution.py:23
  101.4 11.0 %all-to-all-start = ((bf16[8,192,128]{2,1,0:T(8,128)(2,1)}), bf16[8,192,128]{2,1,0:T(8,128)(2,1)S(1)}, u32[]{:S(2)}, u32[]{:S(2)}) async-start(bf16[8,192,128]{2,1,0:T(8,128)(2,1)} %broadcast_in_dim.19), calls=%async_computation | async-start | bytes 786432 | tf_op jit(solution)/shard_map/all_to_all | solution.py:23
  105.6 10.6 %collective-permute-start = (bf16[256,1024]{1,0:T(8,128)(2,1)S(1)}, bf16[256,1024]{1,0:T(8,128)(2,1)S(1)}, u32[]{:S(2)}, u32[]{:S(2)}) collective-permute-start(bf16[256,1024]{1,0:T(8,128)(2,1)S(1)} %bitcast.23), channel_id=1, source_target_pairs={{0,8},{8,0},{1,9},{9,1},{2,10},{10,2},{3,11},{11,3},{4,12},{12,4},... | collective-permute-start | bytes 1572872 | tf_op jit(solution)/shard_map/ppermute | solution.py:27
  105.9 17.9 %collective-permute-start.2 = (bf16[256,1024]{1,0:T(8,128)(2,1)S(1)}, bf16[256,1024]{1,0:T(8,128)(2,1)S(1)}, u32[]{:S(2)}, u32[]{:S(2)}) collective-permute-start(bf16[256,1024]{1,0:T(8,128)(2,1)S(1)} %bitcast.21), channel_id=1, source_target_pairs={{0,8},{8,0},{1,9},{9,1},{2,10},{10,2},{3,11},{11,3},{4,12},{12,4},... | collective-permute-start | bytes 1572872 | tf_op jit(solution)/shard_map/ppermute | solution.py:27

commit v2 on v0

v2 whole, which is shorter than its diff:
```python
import functools
import math

import jax
import jax.numpy as jnp
from jax import lax
from jax.experimental import pallas as pl
from jax.experimental.pallas import tpu as pltpu
from jax.sharding import Mesh, PartitionSpec as P

NOPE = 128
ROPE = 64
VDIM = 128
KV = 512
KW = 640
SPAN = 64
LANES = 128
MASKED = -1e30
EXP2_SCALE = (NOPE + ROPE) ** (-0.5) * math.log2(math.e)


def gather_blocks(x, axes, count):
    copies = jnp.broadcast_to(x[None], (count,) + x.shape)
    return lax.all_to_all(copies, axes, 0, 0, tiled=True)


def shift(x, axis, by):
    n = lax.axis_size(axis)
    return lax.ppermute(x, axis, [(i, (i + by) % n) for i in range(n)])


def dot_t(a, b):
    return lax.dot_general(a, b, (((1,), (1,)), ((), ())), preferred_element_type=jnp.float32)


def pack_shard(latent):
    toks = latent.shape[0]
    content = latent[:, :KV].reshape(toks, KV // LANES, LANES).transpose(1, 0, 2).reshape(-1, LANES)
    rope = jnp.concatenate([latent[: toks // 2, KV:], latent[toks // 2 :, KV:]], axis=1)
    return jnp.concatenate([content, rope], axis=0)


def weave(core, own_ref, oth_ref, dst_ref):
    rows = 16
    for i in range(own_ref.shape[0] // rows):
        at = pl.multiple_of((2 * i + core) * rows, rows)
        ot = pl.multiple_of((2 * i + 1 - core) * rows, rows)
        dst_ref[pl.ds(at, rows), :] = own_ref[i * rows : (i + 1) * rows, :]
        dst_ref[pl.ds(ot, rows), :] = oth_ref[i * rows : (i + 1) * rows, :]


def load_keys(piece_refs, klo_ref, khi_ref):
    i = 0
    for piece in piece_refs:
        for j in range(piece.shape[0]):
            rows = slice(i * SPAN, (i + 1) * SPAN)
            for b in range(KV // LANES):
                cols = slice(b * LANES, (b + 1) * LANES)
                klo_ref[rows, cols] = piece[j, b * LANES : b * LANES + SPAN, :]
                khi_ref[rows, cols] = piece[j, b * LANES + SPAN : (b + 1) * LANES, :]
            klo_ref[rows, KV:] = piece[j, KV:, :]
            khi_ref[rows, KV:] = piece[j, KV:, :]
            i += 1


def key_positions(shards, span_ref, slot):
    lane = lax.broadcasted_iota(jnp.int32, (1, LANES), 1)
    rows = []
    for i in range(0, len(shards), 2):
        a, b = span_ref[2 * shards[i] + slot], span_ref[2 * shards[i + 1] + slot]
        rows.append(jnp.where(lane < SPAN, a, b) * SPAN + lane % SPAN)
    return jnp.concatenate(rows, axis=1)


def attention_kernel(layout, heads, tile, first, last, *refs):
    refs = list(refs)
    take = lambda n: [refs.pop(0) for _ in range(n)]
    idx_ref, span_ref = take(2)
    z, xh, core, slot0 = (idx_ref[i] for i in range(4))
    if first:
        qn_ref, qlo_ref, qhi_ref, wko_ref, wkx_ref = take(5)
    else:
        q0_ref, q1_ref, q2_ref, m_ref, l_ref, acc_ref = take(6)
    piece_refs = take(len(layout))
    if last:
        wvo_ref, wvx_ref = take(2)
        (out_ref,) = take(1)
        wv_ref, mix_ref = take(2)
    else:
        if first:
            q0_ref, q1_ref, q2_ref = take(3)
        mo_ref, lo_ref, acco_ref = take(3)
        if first:
            (wk_ref,) = take(1)
    klo_ref, khi_ref = take(2)

    shards = []
    for dz, which in layout:
        for dx, dc in which:
            zz = lax.rem(z + dz + 8, 8)
            xx = 1 - xh if dx else xh
            cc = 1 - core if dc else core
            shards.append((zz * 2 + xx) * 2 + cc)
    n = len(shards) * SPAN
    load_keys(piece_refs, klo_ref, khi_ref)
    pos_lo = key_positions(shards, span_ref, 0)
    pos_hi = key_positions(shards, span_ref, 1)
    within = lax.broadcasted_iota(jnp.int32, (tile, 1), 0) % SPAN

    if first:
        weave(core, wko_ref, wkx_ref, wk_ref)
        for h in range(heads):
            cols = slice(h * NOPE, (h + 1) * NOPE)
            rows = slice(h * SPAN, (h + 1) * SPAN)
            q_latent = dot_t(qn_ref[:, cols], wk_ref[:, cols]).astype(jnp.bfloat16)
            q0_ref[rows, :KV] = q_latent[:SPAN, :]
            q0_ref[rows, KV:] = qlo_ref[:SPAN, cols]
            q1_ref[rows, :KV] = q_latent[SPAN:, :]
            q1_ref[rows, KV:] = qlo_ref[SPAN:, cols]
            q2_ref[rows, :KV] = q_latent[SPAN:, :]
            q2_ref[rows, KV:] = qhi_ref[SPAN:, cols]
    if last:
        weave(core, wvo_ref, wvx_ref, wv_ref)

    for slot in range(2):
        for row in range(0, heads * SPAN, tile):
            rows = slice(row, row + tile)
            q_pos = span_ref[slot0 + slot] * SPAN + within
            if slot == 0:
                s = jnp.where(pos_lo <= q_pos, dot_t(q0_ref[rows, :], klo_ref[...]), MASKED)
            else:
                s_lo = dot_t(q1_ref[rows, :], klo_ref[...])
                s_hi = jnp.where(pos_hi <= q_pos, dot_t(q2_ref[rows, :], khi_ref[...]), MASKED)
                s = jnp.concatenate([s_lo, s_hi], axis=1)
            high = jnp.max(s, axis=1, keepdims=True)
            if not first:
                old = m_ref[slot, rows, :1]
                high = jnp.maximum(high, old)
            w = jnp.exp2((s - high) * EXP2_SCALE)
            total = jnp.sum(w, axis=1, keepdims=True)
            w = w.astype(jnp.bfloat16)
            acc = jnp.dot(w[:, :n], klo_ref[:, :KV], preferred_element_type=jnp.float32)
            if slot == 1:
                acc += jnp.dot(w[:, n:], khi_ref[:, :KV], preferred_element_type=jnp.float32)
            if not first:
                fade = jnp.exp2((old - high) * EXP2_SCALE)
                total += fade * l_ref[slot, rows, :1]
                acc += fade * acc_ref[slot, rows, :]
            if last:
                mix_ref[slot, rows, :] = (acc / total).astype(jnp.bfloat16)
            else:
                mo_ref[slot, rows, :] = jnp.broadcast_to(high, (tile, LANES))
                lo_ref[slot, rows, :] = jnp.broadcast_to(total, (tile, LANES))
                acco_ref[slot, rows, :] = acc
    if last:
        for h in range(heads):
            cols = slice(h * VDIM, (h + 1) * VDIM)
            rows = slice(h * SPAN, (h + 1) * SPAN)
            both = jnp.concatenate([mix_ref[0, rows, :], mix_ref[1, rows, :]], axis=0)
            out_ref[:, cols] = jnp.dot(
                both, wv_ref[:, cols], preferred_element_type=jnp.float32
            ).astype(jnp.bfloat16)


def attention(layout, heads, first, last, scalars, inputs, pieces, tail, cols):
    rows = heads * SPAN
    f32, b16 = jnp.float32, jnp.bfloat16
    shape = jax.ShapeDtypeStruct
    keys = sum(p.shape[0] for p in pieces) * SPAN
    state = [shape((2, rows, LANES), f32), shape((2, rows, LANES), f32), shape((2, rows, KV), f32)]
    scratch = [pltpu.VMEM((keys, KW), b16), pltpu.VMEM((keys, KW), b16)]
    aliases = {}
    if last:
        outs = [shape((2 * SPAN, cols), b16)]
        scratch = [pltpu.VMEM((KV, cols), b16), pltpu.VMEM((2, rows, KV), b16)] + scratch
    else:
        outs = list(state)
        if first:
            outs = [shape((rows, KW), b16)] * 3 + outs
            scratch = [pltpu.VMEM((KV, cols), b16)] + scratch
        else:
            aliases = {5: 0, 6: 1, 7: 2}
    args = [*scalars, *inputs, *pieces, *tail]
    flops = 2 * 3 * rows * keys * (KW + KV)
    size = sum(math.prod(a.shape) * a.dtype.itemsize for a in args)
    vmem = pl.BlockSpec(memory_space=pltpu.VMEM)
    return pl.pallas_call(
        functools.partial(attention_kernel, layout, heads, min(rows, 256), first, last),
        out_shape=outs,
        in_specs=[pl.BlockSpec(memory_space=pltpu.SMEM)] * 2 + [vmem] * (len(args) - 2),
        out_specs=[vmem] * len(outs),
        scratch_shapes=scratch,
        input_output_aliases=aliases,
        compiler_params=pltpu.CompilerParams(vmem_limit_bytes=48 << 20),
        cost_estimate=pl.CostEstimate(
            flops=flops, bytes_accessed=size, transcendentals=3 * rows * keys
        ),
    )(*args)


def per_device(compressed, latent, w_uq, w_uk, w_uv, span_ids):
    toks = compressed.shape[0]
    cols = w_uk.shape[1]
    heads = cols // NOPE
    zs, xhs, ys, xls = (lax.axis_size(a) for a in ("z", "xh", "y", "xl"))
    ctx = lax.axis_index(("z", "xh", "core"))
    idx = jnp.stack([lax.axis_index("z"), lax.axis_index("xh"), lax.axis_index("core"), 2 * ctx])

    shard = pack_shard(latent)[None]
    here = jnp.concatenate([shard, shift(shard, "xh", 1)], axis=0)
    both, first_xh, second_xh = ((0, 0), (1, 0)), ((0, 0),), ((1, 0),)
    steps = [[(0, both, here)]]
    ahead = behind = here
    for k in range(1, zs // 2):
        ahead, behind = shift(ahead, "z", 1), shift(behind, "z", -1)
        steps.append([(-k, both, ahead), (k, both, behind)])
    steps.append(
        [
            (-(zs // 2), first_xh, shift(ahead[:1], "z", 1)),
            (zs // 2, second_xh, shift(behind[1:], "z", -1)),
        ]
    )
    flip = lambda which: tuple((dx, 1) for dx, _ in which)
    steps = [
        step + [(dz, flip(which), shift(piece, "core", 1)) for dz, which, piece in step]
        for step in steps
    ]

    wk = gather_blocks(w_uk, ("z", "xh"), zs * xhs).reshape(-1, cols)
    wk_x = shift(wk, "core", 1)
    wv = gather_blocks(w_uv, ("z", "xh"), zs * xhs).reshape(-1, cols)
    wv_x = shift(wv, "core", 1)

    features = gather_blocks(compressed.T, ("y", "xl"), ys * xls).reshape(-1, toks)
    query = lax.dot_general(
        features, w_uq, (((0,), (0,)), ((), ())), preferred_element_type=jnp.float32
    ).astype(jnp.bfloat16)
    query = query.reshape(toks, heads, NOPE + ROPE)
    q_nope = query[:, :, :NOPE].reshape(toks, cols)
    q_rope = query[:, :, NOPE:]
    q_lo = jnp.pad(q_rope, ((0, 0), (0, 0), (0, ROPE))).reshape(toks, heads * LANES)
    q_hi = jnp.pad(q_rope, ((0, 0), (0, 0), (ROPE, 0))).reshape(toks, heads * LANES)

    def run(group, first, last, inputs, tail):
        group = [piece for step in group for piece in step]
        layout = tuple((dz, which) for dz, which, _ in group)
        pieces = [piece for _, _, piece in group]
        return attention(layout, heads, first, last, [idx, span_ids], inputs, pieces, tail, cols)

    state = run(steps[:3], True, False, [q_nope, q_lo, q_hi, wk, wk_x], [])
    queries, state = state[:3], state[3:]
    state = run(steps[3:4], False, False, [*queries, *state], [])
    (out,) = run(steps[4:], False, True, [*queries, *state], [wv, wv_x])
    return out


def solution(mesh):
    fine = Mesh(mesh.devices.reshape(8, 2, 2, 4, 2), ("z", "xh", "core", "y", "xl"))
    ctx, tp = ("z", "xh", "core"), ("y", "xl")
    placed = (P(ctx, tp), P(ctx, None), P(None, tp), P(ctx, tp), P(ctx, tp), P())
    return jax.shard_map(
        per_device, mesh=fine, in_specs=placed, out_specs=P(ctx, tp), check_vma=False
    )
```

time: 295 us -> 129 us (0.44)
  waiting for transfers between devices: 161 us -> 18.3 us
  other arithmetic: 53 us -> 0.19 us
  starting transfers between devices: 0.08 us -> 46.2 us
  Pallas kernels: 0 us -> 22.2 us
  matrix products: 22.2 us -> 4.01 us
  between operations: 15.7 us -> 0.15 us
  blocking collectives: 25.2 us -> 13.6 us
  local copies, waits for them, and re-layouts: 16.9 us -> 23.1 us
    all_gather x3 -> x0, waiting for transfers between devices: 159 us -> none  [the longest x1 87.4 us: per_device(): lax.all_gather(latent, 'ctx', axis=0, tiled=True)]
    add x1 -> x0, other arithmetic: 35.8 us -> none  [per_device(): jnp.repeat(span_ids, span_len, total_repeat_length=total_slots) * span_len]
    ppermute x0 -> x20, starting transfers between devices: none -> 28.7 us  [shift(): return lax.ppermute(x, axis, [(i, (i + by) % n) for i in range(n)])]
    all_gather x1 -> x0, blocking collectives: 25.2 us -> none  [per_device(): lax.all_gather(compressed, 'tp', axis=1, tiled=True)]
    pallas_call x0 -> x3, Pallas kernels: none -> 22.2 us  [attention(): pl.pallas_call(functools.partial(attention_kernel, layout, heads, min(row...]
    ppermute x0 -> x20, waiting for transfers between devices: none -> 18.3 us  [shift(): return lax.ppermute(x, axis, [(i, (i + by) % n) for i in range(n)])]
    dot_general x7 -> x1, matrix products: 22.2 us -> 4.01 us  [per_device(): lax.dot_general(features, w_uq, (((0,), (0,)), ((), ())), preferred_eleme...]
    all_to_all x0 -> x2, starting transfers between devices: none -> 17.5 us  [gather_blocks(): return lax.all_to_all(copies, axes, 0, 0, tiled=True)]
  transfers between devices with their start and end apart: 3 -> 22, of which waited for: 2 -> 3; matrix products, arithmetic and copies ran while one was open for 22% -> 14% of each run, Pallas kernels for 0% -> 13%
where the time goes in v2:
time: 129 us; the launch traced here: 128 us
  starting transfers between devices  46.2 us (36%)
  local copies, waits for them, and re-layouts  23.1 us (18%)
  Pallas kernels  22.2 us (17%)
  waiting for transfers between devices  18.3 us (14%)
  blocking collectives  13.6 us (11%)
  matrix products  4.01 us (3%)
    ppermute x20, starting transfers between devices, shift(): return lax.ppermute(x, axis, [(i, (i + by) % n) for i in range(n)])  28.7 us
    pallas_call x3, Pallas kernels, attention(): pl.pallas_call(functools.partial(attention_kernel, layout, heads, min(row...  22.2 us
    ppermute x20, waiting for transfers between devices, shift(): return lax.ppermute(x, axis, [(i, (i + by) % n) for i in range(n)])  18.3 us
    all_to_all x2, starting transfers between devices, gather_blocks(): return lax.all_to_all(copies, axes, 0, 0, tiled=True)  17.5 us
    all_to_all x1, blocking collectives, gather_blocks(): return lax.all_to_all(copies, axes, 0, 0, tiled=True)  13.6 us
    unnamed x22, local copies, waits for them, and re-layouts  7.05 us
    broadcast_in_dim x3, local copies, waits for them, and re-layouts, gather_blocks(): copies = jnp.broadcast_to(x[None], (count,) + x.shape)  4.07 us
    dot_general x1, matrix products, per_device(): lax.dot_general(features, w_uq, (((0,), (0,)), ((), ())), preferred_eleme...  4.01 us
  transfers between devices with their start and end apart: 22, of which 3 were waited for; matrix products, arithmetic and copies ran while one was open for 14% of the time, Pallas kernels for 13%

profile of v2, /device:TPU:1, one launch (start us, length us, event | category | flops | bytes accessed | tf_op | source)
XLA Modules:
  0.0 127.8 jit_solution(4994679124267189596)
XLA Ops:
  0.0 0.8 broadcast_in_dim.8
  0.9 13.6 %all_to_all.15 = bf16[8,192,128]{2,1,0:T(8,128)(2,1)} all-to-all(bf16[8,192,128]{2,1,0:T(8,128)(2,1)S(1)} %broadcast_in_dim.8), channel_id=1, replica_groups=mesh['z'=8,'xh'=2,'core'=2,'y'=4,'xl'=2] {'y','xl'}, dimensions={0} | all-to-all | bytes 786432 | tf_op jit(solution)/shard_map/all_to_all | solution.py:24
  14.5 1.6 %broadcast_in_dim.9 = bf16[16,16,1024]{2,1,0:T(8,128)(2,1)} broadcast(bf16[16,1024]{1,0:T(8,128)(2,1)} %param.9), dimensions={1,2} | broadcast | bytes 557056 | tf_op jit(solution)/shard_map/broadcast_in_dim | solution.py:23
  16.1 10.5 %all-to-all-start.1 = ((bf16[16,16,1024]{2,1,0:T(8,128)(2,1)}), bf16[16,16,1024]{2,1,0:T(8,128)(2,1)S(1)}, u32[]{:S(2)}, u32[]{:S(2)}) async-start(bf16[16,16,1024]{2,1,0:T(8,128)(2,1)} %broadcast_in_dim.9), calls=%async_computation.1 | async-start | bytes 1048576 | tf_op jit(solution)/shard_map/all_to_all | solution.py:24
  26.5 0.9 fusion
  27.4 0.9 slice.23
  28.3 0.1 copy.23
  28.4 0.1 copy.24
  28.5 0.1 copy.17
  28.7 0.1 maximum_bitcast_fusion
  28.8 2.9 %collective-permute-start.1 = (bf16[1,576,128]{2,1,0:T(8,128)(2,1)S(1)}, bf16[1,576,128]{2,1,0:T(8,128)(2,1)S(1)}, u32[]{:S(2)}, u32[]{:S(2)}) collective-permute-start(bf16[1,576,128]{2,1,0:T(8,128)(2,1)S(1)} %maximum_bitcast_fusion), channel_id=1, source_target_pairs={{0,16},{16,0},{1,17},{17,1},{2,18},{18,2},{3,19},{19,3},{4,20},{20... | collective-permute-start | bytes 442376 | tf_op jit(solution)/shard_map/ppermute | solution.py:29
  31.7 3.6 %collective-permute-done.1 = bf16[1,576,128]{2,1,0:T(8,128)(2,1)S(1)} collective-permute-done((bf16[1,576,128]{2,1,0:T(8,128)(2,1)S(1)}, bf16[1,576,128]{2,1,0:T(8,128)(2,1)S(1)}, u32[]{:S(2)}, u32[]{:S(2)}) %collective-permute-start.1) | collective-permute-done | bytes 147488 | tf_op jit(solution)/shard_map/ppermute | solution.py:29
  35.3 1.5 %collective-permute-start.3 = (bf16[2,576,128]{2,1,0:T(8,128)(2,1)S(1)}, bf16[2,576,128]{2,1,0:T(8,128)(2,1)S(1)}, u32[]{:S(2)}, u32[]{:S(2)}) collective-permute-start(bf16[2,576,128]{2,1,0:T(8,128)(2,1)S(1)} %pad_maximum_fusion.refs_7_), channel_id=1, source_target_pairs={{0,32},{32,64},{64,96},{96,128},{128,160},{160,192},{192,224},{224... | collective-permute-start | bytes 884744 | tf_op jit(solution)/shard_map/ppermute | solution.py:29
  36.8 2.6 %collective-permute-start.4 = (bf16[2,576,128]{2,1,0:T(8,128)(2,1)S(1)}, bf16[2,576,128]{2,1,0:T(8,128)(2,1)S(1)}, u32[]{:S(2)}, u32[]{:S(2)}) collective-permute-start(bf16[2,576,128]{2,1,0:T(8,128)(2,1)S(1)} %pad_maximum_fusion.refs_7_), channel_id=1, source_target_pairs={{0,224},{32,0},{64,32},{96,64},{128,96},{160,128},{192,160},{224,1... | collective-permute-start | bytes 884744 | tf_op jit(solution)/shard_map/ppermute | solution.py:29
  39.4 6.9 %collective-permute-done.3.refs_9_ = bf16[2,576,128]{2,1,0:T(8,128)(2,1)S(1)} collective-permute-done((bf16[2,576,128]{2,1,0:T(8,128)(2,1)S(1)}, bf16[2,576,128]{2,1,0:T(8,128)(2,1)S(1)}, u32[]{:S(2)}, u32[]{:S(2)}) %collective-permute-start.3) | collective-permute-done | bytes 294944 | tf_op jit(solution)/shard_map/ppermute | solution.py:29
  46.3 2.7 %collective-permute-start.8 = (bf16[2,576,128]{2,1,0:T(8,128)(2,1)S(1)}, bf16[2,576,128]{2,1,0:T(8,128)(2,1)}, u32[]{:S(2)}, u32[]{:S(2)}) collective-permute-start(bf16[2,576,128]{2,1,0:T(8,128)(2,1)S(1)} %collective-permute-done.4.refs_10_), channel_id=1, source_target_pairs={{0,224},{32,0},{64,32},{96,64},{128,96},{160,128},{192,160},{224,1... | collective-permute-start | bytes 884744 | tf_op jit(solution)/shard_map/ppermute | solution.py:29
  48.9 1.6 %broadcast_in_dim.11 = bf16[16,16,1024]{2,1,0:T(8,128)(2,1)} broadcast(bf16[16,1024]{1,0:T(8,128)(2,1)} %param.10), dimensions={1,2} | broadcast | bytes 557056 | tf_op jit(solution)/shard_map/broadcast_in_dim | solution.py:23
  50.5 7.0 %all-to-all-start.2 = ((bf16[16,16,1024]{2,1,0:T(8,128)(2,1)}), bf16[16,16,1024]{2,1,0:T(8,128)(2,1)S(1)}, u32[]{:S(2)}, u32[]{:S(2)}) async-start(bf16[16,16,1024]{2,1,0:T(8,128)(2,1)} %broadcast_in_dim.11), calls=%async_computation.2 | async-start | bytes 1048576 | tf_op jit(solution)/shard_map/all_to_all | solution.py:24
  57.6 0.0 collective-permute-done.7.refs_13_
  57.6 1.4 %collective-permute-start.11 = (bf16[2,576,128]{2,1,0:T(8,128)(2,1)}, bf16[2,576,128]{2,1,0:T(8,128)(2,1)S(1)}, u32[]{:S(2)}, u32[]{:S(2)}) collective-permute-start(bf16[2,576,128]{2,1,0:T(8,128)(2,1)} %collective-permute-done.7.refs_13_), channel_id=1, source_target_pairs={{0,32},{32,64},{64,96},{96,128},{128,160},{160,192},{192,224},{224... | collective-permute-start | bytes 884744 | tf_op jit(solution)/shard_map/ppermute | solution.py:29
  59.1 1.3 %collective-permute-start.12 = (bf16[2,576,128]{2,1,0:T(8,128)(2,1)}, bf16[2,576,128]{2,1,0:T(8,128)(2,1)S(1)}, u32[]{:S(2)}, u32[]{:S(2)}) collective-permute-start(bf16[2,576,128]{2,1,0:T(8,128)(2,1)} %collective-permute-done.8.refs_14_), channel_id=1, source_target_pairs={{0,224},{32,0},{64,32},{96,64},{128,96},{160,128},{192,160},{224,1... | collective-permute-start | bytes 884744 | tf_op jit(solution)/shard_map/ppermute | solution.py:29
  60.4 6.4 %collective-permute-start.2 = (bf16[2,576,128]{2,1,0:T(8,128)(2,1)S(1)}, bf16[2,576,128]{2,1,0:T(8,128)(2,1)S(1)}, u32[]{:S(2)}, u32[]{:S(2)}) collective-permute-start(bf16[2,576,128]{2,1,0:T(8,128)(2,1)S(1)} %pad_maximum_fusion.refs_7_), channel_id=1, source_target_pairs={{0,8},{8,0},{1,9},{9,1},{2,10},{10,2},{3,11},{11,3},{4,12},{12,4},... | collective-permute-start | bytes 884744 | tf_op jit(solution)/shard_map/ppermute | solution.py:29
  66.8 0.5 collective-permute-start.6
  67.3 7.8 %collective-permute-done.11.refs_8_ = bf16[2,576,128]{2,1,0:T(8,128)(2,1)S(1)} collective-permute-done((bf16[2,576,128]{2,1,0:T(8,128)(2,1)}, bf16[2,576,128]{2,1,0:T(8,128)(2,1)S(1)}, u32[]{:S(2)}, u32[]{:S(2)}) %collective-permute-start.11) | collective-permute-done | bytes 294944 | tf_op jit(solution)/shard_map/ppermute | solution.py:29
  75.1 4.5 %collective-permute-start = (bf16[256,1024]{1,0:T(8,128)(2,1)S(1)}, bf16[256,1024]{1,0:T(8,128)(2,1)S(1)}, u32[]{:S(2)}, u32[]{:S(2)}) collective-permute-start(bf16[256,1024]{1,0:T(8,128)(2,1)S(1)} %bitcast.22), channel_id=1, source_target_pairs={{0,8},{8,0},{1,9},{9,1},{2,10},{10,2},{3,11},{11,3},{4,12},{12,4},... | collective-permute-start | bytes 1572872 | tf_op jit(solution)/shard_map/ppermute | solution.py:29
  79.6 0.1 pad_add_fusion.refs_0_
  79.7 0.7 slice.30
  80.3 0.0 collective-permute-start.10
  80.3 0.7 slice.31
  81.0 0.0 collective-permute-done.2.refs_8_
  81.0 0.7 copy-done.8
  81.7 0.5 collective-permute-start.9
  82.2 0.0 collective-permute-done.6.refs_12_
  82.2 2.7 %collective-permute-start.16 = (bf16[1,576,128]{2,1,0:T(8,128)(2,1)}, bf16[1,576,128]{2,1,0:T(8,128)(2,1)S(1)}, u32[]{:S(2)}, u32[]{:S(2)}) collective-permute-start(bf16[1,576,128]{2,1,0:T(8,128)(2,1)} %slice.31), channel_id=1, source_target_pairs={{0,224},{32,0},{64,32},{96,64},{128,96},{160,128},{192,160},{224,1... | collective-permute-start | bytes 442376 | tf_op jit(solution)/shard_map/ppermute | solution.py:29
  84.9 4.0 %convolution_convert_fusion = bf16[128,1536]{1,0:T(8,128)(2,1)} fusion(bf16[1536,128]{1,0:T(8,128)(2,1)} %bitcast.26, bf16[1536,1536]{1,0:T(8,128)(2,1)} %param.8), kind=kOutput, calls=%fused_computation | convolution fusion | flops 604176384 | bytes 5505024 | tf_op jit(solution)/shard_map/dot_general | solution.py:235
  88.9 1.9 %copy.13 = bf16[128,1536]{0,1:T(8,128)(2,1)} copy(bf16[128,1536]{1,0:T(8,128)(2,1)} %convolution_convert_fusion) | data formatting | bytes 786432 | tf_op jit(solution)/shard_map/convert_element_type | solution.py:237
  90.9 0.9 slice.29
  91.8 1.7 %slice.28 = bf16[128,8,128]{0,2,1:T(8,128)(2,1)} slice(bf16[128,8,192]{0,2,1:T(8,128)(2,1)} %bitcast.25), slice={[0:128], [0:8], [0:128]} | slice | bytes 524288 | tf_op jit(solution)/shard_map/slice | solution.py:239
  93.5 0.9 fusion.1
  94.4 1.1 copy.21.refs_3_
  95.5 1.1 copy.22.refs_4_
  96.5 1.1 copy.20.refs_2_
  97.6 0.0 all-to-all-done.2
  97.6 0.0 collective-permute-done.10.refs_16_
  97.7 0.7 collective-permute-start.19
  98.3 0.0 collective-permute-done.9.refs_15_
  98.3 0.1 collective-permute-start.13
  98.4 0.0 collective-permute-done.15.refs_8_
  98.4 0.4 collective-permute-start.14
  98.8 0.0 collective-permute-done.16.refs_9_
  98.8 0.1 collective-permute-start.17
  98.9 0.0 collective-permute-done.refs_6_
  98.9 0.4 collective-permute-start.18
  99.4 1.0 copy-done.5
  100.3 1.0 copy-done.7
  101.3 1.0 copy-done.9
  102.2 9.9 %shard_map.64 = (bf16[512,640]{1,0:T(8,128)(2,1)}, bf16[512,640]{1,0:T(8,128)(2,1)}, bf16[512,640]{1,0:T(8,128)(2,1)}, f32[2,512,128]{2,1,0:T(8,128)S(1)}, f32[2...) custom-call(s32[4]{0:T(128)S(1)} %pad_add_fusion.refs_0_, s32[64]{0:T(128)S(1)} %copy-done.3, ...), custom_call_target="tpu_custom_call" | custom-call | flops 4529848320 | bytes 4784400 | tf_op jit(solution)/shard_map/pallas_call | solution.py:187
  112.2 1.1 copy-done
  113.3 1.1 copy-done.1
  114.4 1.1 copy-done.2
  115.5 6.7 %shard_map.65 = (f32[2,512,128]{2,1,0:T(8,128)S(1)}, f32[2,512,128]{2,1,0:T(8,128)S(1)}, f32[2,512,512]{2,1,0:T(8,128)}) custom-call(s32[4]{0:T(128)S(1)} %pad_add_fusion.refs_0_, s32[64]{0:T(128)S(1)} %copy-done.3, bf16[512,640]{1,0:T(8,128)(2,1)S(1)} %copy-done, ...), custom_call_target="tpu_custom_call", output_to_operand_aliasing={{0}: (5, {}), {1}: (6, {}), {2}: (7, {})} | custom-call | flops 1811939328 | bytes 6291728 | tf_op jit(solution)/shard_map/pallas_call | solution.py:187
  122.2 0.0 collective-permute-done.17.refs_10_
  122.2 0.0 collective-permute-done.18.refs_11_
  122.2 5.6 %shard_map.66 = bf16[128,1024]{1,0:T(8,128)(2,1)} custom-call(s32[4]{0:T(128)S(1)} %pad_add_fusion.refs_0_, s32[64]{0:T(128)S(1)} %copy-done.3, bf16[512,640]{1,0:T(8,128)(2,1)S(1)} %copy-done, bf16[512,640]{1,0:T(8,128)(2,1)S(1)} %copy-done.1, bf16[512,640]{1,0:T(8,128)(2,1)S(1)} %copy-done.2, f32[2,512,128]{2,1,0:T(8,128)S(1)} %get-tuple-element.20.refs_5_, ...), custom_call_target="tpu_custom_call" | custom-call | flops 905969664 | bytes 6750480 | tf_op jit(solution)/shard_map/pallas_call | solution.py:187
  (25 shorter events, 0.1 us)
Async XLA Ops:
  16.1 32.9 %all-to-all-start.1 = ((bf16[16,16,1024]{2,1,0:T(8,128)(2,1)}), bf16[16,16,1024]{2,1,0:T(8,128)(2,1)S(1)}, u32[]{:S(2)}, u32[]{:S(2)}) async-start(bf16[16,16,1024]{2,1,0:T(8,128)(2,1)} %broadcast_in_dim.9), calls=%async_computation.1 | async-start | bytes 1048576 | tf_op jit(solution)/shard_map/all_to_all | solution.py:24
  28.8 6.5 %collective-permute-start.1 = (bf16[1,576,128]{2,1,0:T(8,128)(2,1)S(1)}, bf16[1,576,128]{2,1,0:T(8,128)(2,1)S(1)}, u32[]{:S(2)}, u32[]{:S(2)}) collective-permute-start(bf16[1,576,128]{2,1,0:T(8,128)(2,1)S(1)} %maximum_bitcast_fusion), channel_id=1, source_target_pairs={{0,16},{16,0},{1,17},{17,1},{2,18},{18,2},{3,19},{19,3},{4,20},{20... | collective-permute-start | bytes 442376 | tf_op jit(solution)/shard_map/ppermute | solution.py:29
  35.3 10.9 %collective-permute-start.3 = (bf16[2,576,128]{2,1,0:T(8,128)(2,1)S(1)}, bf16[2,576,128]{2,1,0:T(8,128)(2,1)S(1)}, u32[]{:S(2)}, u32[]{:S(2)}) collective-permute-start(bf16[2,576,128]{2,1,0:T(8,128)(2,1)S(1)} %pad_maximum_fusion.refs_7_), channel_id=1, source_target_pairs={{0,32},{32,64},{64,96},{96,128},{128,160},{160,192},{192,224},{224... | collective-permute-start | bytes 884744 | tf_op jit(solution)/shard_map/ppermute | solution.py:29
  36.8 9.4 %collective-permute-start.4 = (bf16[2,576,128]{2,1,0:T(8,128)(2,1)S(1)}, bf16[2,576,128]{2,1,0:T(8,128)(2,1)S(1)}, u32[]{:S(2)}, u32[]{:S(2)}) collective-permute-start(bf16[2,576,128]{2,1,0:T(8,128)(2,1)S(1)} %pad_maximum_fusion.refs_7_), channel_id=1, source_target_pairs={{0,224},{32,0},{64,32},{96,64},{128,96},{160,128},{192,160},{224,1... | collective-permute-start | bytes 884744 | tf_op jit(solution)/shard_map/ppermute | solution.py:29
  46.2 48.1 %copy-start.4 = (bf16[2,576,128]{2,1,0:T(8,128)(2,1)}, bf16[2,576,128]{2,1,0:T(8,128)(2,1)S(1)}, u32[]{:S(2)}) copy-start(bf16[2,576,128]{2,1,0:T(8,128)(2,1)S(1)} %collective-permute-done.3.refs_9_) | copy-start | bytes 884740
  46.3 11.4 %collective-permute-start.7 = (bf16[2,576,128]{2,1,0:T(8,128)(2,1)S(1)}, bf16[2,576,128]{2,1,0:T(8,128)(2,1)}, u32[]{:S(2)}, u32[]{:S(2)}) collective-permute-start(bf16[2,576,128]{2,1,0:T(8,128)(2,1)S(1)} %collective-permute-done.3.refs_9_), channel_id=1, source_target_pairs={{0,32},{32,64},{64,96},{96,128},{128,160},{160,192},{192,224},{224... | collective-permute-start | bytes 884744 | tf_op jit(solution)/shard_map/ppermute | solution.py:29
  46.3 48.1 %copy-start.6 = (bf16[2,576,128]{2,1,0:T(8,128)(2,1)}, bf16[2,576,128]{2,1,0:T(8,128)(2,1)S(1)}, u32[]{:S(2)}) copy-start(bf16[2,576,128]{2,1,0:T(8,128)(2,1)S(1)} %collective-permute-done.4.refs_10_) | copy-start | bytes 884740
  46.3 12.8 %collective-permute-start.8 = (bf16[2,576,128]{2,1,0:T(8,128)(2,1)S(1)}, bf16[2,576,128]{2,1,0:T(8,128)(2,1)}, u32[]{:S(2)}, u32[]{:S(2)}) collective-permute-start(bf16[2,576,128]{2,1,0:T(8,128)(2,1)S(1)} %collective-permute-done.4.refs_10_), channel_id=1, source_target_pairs={{0,224},{32,0},{64,32},{96,64},{128,96},{160,128},{192,160},{224,1... | collective-permute-start | bytes 884744 | tf_op jit(solution)/shard_map/ppermute | solution.py:29
  50.5 47.1 %all-to-all-start.2 = ((bf16[16,16,1024]{2,1,0:T(8,128)(2,1)}), bf16[16,16,1024]{2,1,0:T(8,128)(2,1)S(1)}, u32[]{:S(2)}, u32[]{:S(2)}) async-start(bf16[16,16,1024]{2,1,0:T(8,128)(2,1)} %broadcast_in_dim.11), calls=%async_computation.2 | async-start | bytes 1048576 | tf_op jit(solution)/shard_map/all_to_all | solution.py:24
  57.6 17.5 %collective-permute-start.11 = (bf16[2,576,128]{2,1,0:T(8,128)(2,1)}, bf16[2,576,128]{2,1,0:T(8,128)(2,1)S(1)}, u32[]{:S(2)}, u32[]{:S(2)}) collective-permute-start(bf16[2,576,128]{2,1,0:T(8,128)(2,1)} %collective-permute-done.7.refs_13_), channel_id=1, source_target_pairs={{0,32},{32,64},{64,96},{96,128},{128,160},{160,192},{192,224},{224... | collective-permute-start | bytes 884744 | tf_op jit(solution)/shard_map/ppermute | solution.py:29
  59.1 21.3 %collective-permute-start.12 = (bf16[2,576,128]{2,1,0:T(8,128)(2,1)}, bf16[2,576,128]{2,1,0:T(8,128)(2,1)S(1)}, u32[]{:S(2)}, u32[]{:S(2)}) collective-permute-start(bf16[2,576,128]{2,1,0:T(8,128)(2,1)} %collective-permute-done.8.refs_14_), channel_id=1, source_target_pairs={{0,224},{32,0},{64,32},{96,64},{128,96},{160,128},{192,160},{224,1... | collective-permute-start | bytes 884744 | tf_op jit(solution)/shard_map/ppermute | solution.py:29
  60.4 20.6 %collective-permute-start.2 = (bf16[2,576,128]{2,1,0:T(8,128)(2,1)S(1)}, bf16[2,576,128]{2,1,0:T(8,128)(2,1)S(1)}, u32[]{:S(2)}, u32[]{:S(2)}) collective-permute-start(bf16[2,576,128]{2,1,0:T(8,128)(2,1)S(1)} %pad_maximum_fusion.refs_7_), channel_id=1, source_target_pairs={{0,8},{8,0},{1,9},{9,1},{2,10},{10,2},{3,11},{11,3},{4,12},{12,4},... | collective-permute-start | bytes 884744 | tf_op jit(solution)/shard_map/ppermute | solution.py:29
  66.8 15.4 %collective-permute-start.5 = (bf16[2,576,128]{2,1,0:T(8,128)(2,1)S(1)}, bf16[2,576,128]{2,1,0:T(8,128)(2,1)}, u32[]{:S(2)}, u32[]{:S(2)}) collective-permute-start(bf16[2,576,128]{2,1,0:T(8,128)(2,1)S(1)} %collective-permute-done.3.refs_9_), channel_id=1, source_target_pairs={{0,8},{8,0},{1,9},{9,1},{2,10},{10,2},{3,11},{11,3},{4,12},{12,4},... | collective-permute-start | bytes 884744 | tf_op jit(solution)/shard_map/ppermute | solution.py:29
  66.8 15.4 %collective-permute-start.6 = (bf16[2,576,128]{2,1,0:T(8,128)(2,1)S(1)}, bf16[2,576,128]{2,1,0:T(8,128)(2,1)}, u32[]{:S(2)}, u32[]{:S(2)}) collective-permute-start(bf16[2,576,128]{2,1,0:T(8,128)(2,1)S(1)} %collective-permute-done.4.refs_10_), channel_id=1, source_target_pairs={{0,8},{8,0},{1,9},{9,1},{2,10},{10,2},{3,11},{11,3},{4,12},{12,4},... | collective-permute-start | bytes 884744 | tf_op jit(solution)/shard_map/ppermute | solution.py:29
  75.1 23.8 %collective-permute-start = (bf16[256,1024]{1,0:T(8,128)(2,1)S(1)}, bf16[256,1024]{1,0:T(8,128)(2,1)S(1)}, u32[]{:S(2)}, u32[]{:S(2)}) collective-permute-start(bf16[256,1024]{1,0:T(8,128)(2,1)S(1)} %bitcast.22), channel_id=1, source_target_pairs={{0,8},{8,0},{1,9},{9,1},{2,10},{10,2},{3,11},{11,3},{4,12},{12,4},... | collective-permute-start | bytes 1572872 | tf_op jit(solution)/shard_map/ppermute | solution.py:29
  80.3 17.3 %collective-permute-start.10 = (bf16[2,576,128]{2,1,0:T(8,128)(2,1)}, bf16[2,576,128]{2,1,0:T(8,128)(2,1)}, u32[]{:S(2)}, u32[]{:S(2)}) collective-permute-start(bf16[2,576,128]{2,1,0:T(8,128)(2,1)} %collective-permute-done.8.refs_14_), channel_id=1, source_target_pairs={{0,8},{8,0},{1,9},{9,1},{2,10},{10,2},{3,11},{11,3},{4,12},{12,4},... | collective-permute-start | bytes 884744 | tf_op jit(solution)/shard_map/ppermute | solution.py:29
  81.0 18.3 %copy-start.3 = (s32[64]{0:T(128)S(1)}, s32[64]{0:T(128)}, u32[]{:S(2)}) copy-start(s32[64]{0:T(128)} %refs_1_.5) | copy-start | bytes 772
  81.0 0.7 copy-start.8
  81.7 16.6 %collective-permute-start.9 = (bf16[2,576,128]{2,1,0:T(8,128)(2,1)}, bf16[2,576,128]{2,1,0:T(8,128)(2,1)}, u32[]{:S(2)}, u32[]{:S(2)}) collective-permute-start(bf16[2,576,128]{2,1,0:T(8,128)(2,1)} %collective-permute-done.7.refs_13_), channel_id=1, source_target_pairs={{0,8},{8,0},{1,9},{9,1},{2,10},{10,2},{3,11},{11,3},{4,12},{12,4},... | collective-permute-start | bytes 884744 | tf_op jit(solution)/shard_map/ppermute | solution.py:29
  82.2 16.2 %collective-permute-start.15 = (bf16[1,576,128]{2,1,0:T(8,128)(2,1)}, bf16[1,576,128]{2,1,0:T(8,128)(2,1)S(1)}, u32[]{:S(2)}, u32[]{:S(2)}) collective-permute-start(bf16[1,576,128]{2,1,0:T(8,128)(2,1)} %slice.30), channel_id=1, source_target_pairs={{0,32},{32,64},{64,96},{96,128},{128,160},{160,192},{192,224},{224... | collective-permute-start | bytes 442376 | tf_op jit(solution)/shard_map/ppermute | solution.py:29
  82.2 16.6 %collective-permute-start.16 = (bf16[1,576,128]{2,1,0:T(8,128)(2,1)}, bf16[1,576,128]{2,1,0:T(8,128)(2,1)S(1)}, u32[]{:S(2)}, u32[]{:S(2)}) collective-permute-start(bf16[1,576,128]{2,1,0:T(8,128)(2,1)} %slice.31), channel_id=1, source_target_pairs={{0,224},{32,0},{64,32},{96,64},{128,96},{160,128},{192,160},{224,1... | collective-permute-start | bytes 442376 | tf_op jit(solution)/shard_map/ppermute | solution.py:29
  97.7 24.5 %collective-permute-start.19 = (bf16[256,1024]{1,0:T(8,128)(2,1)S(1)}, bf16[256,1024]{1,0:T(8,128)(2,1)S(1)}, u32[]{:S(2)}, u32[]{:S(2)}) collective-permute-start(bf16[256,1024]{1,0:T(8,128)(2,1)S(1)} %bitcast.20), channel_id=1, source_target_pairs={{0,8},{8,0},{1,9},{9,1},{2,10},{10,2},{3,11},{11,3},{4,12},{12,4},... | collective-permute-start | bytes 1572872 | tf_op jit(solution)/shard_map/ppermute | solution.py:29
  98.3 13.9 %collective-permute-start.13 = (bf16[2,576,128]{2,1,0:T(8,128)(2,1)S(1)}, bf16[2,576,128]{2,1,0:T(8,128)(2,1)S(1)}, u32[]{:S(2)}, u32[]{:S(2)}) collective-permute-start(bf16[2,576,128]{2,1,0:T(8,128)(2,1)S(1)} %collective-permute-done.11.refs_8_), channel_id=1, source_target_pairs={{0,8},{8,0},{1,9},{9,1},{2,10},{10,2},{3,11},{11,3},{4,12},{12,4},... | collective-permute-start | bytes 884744 | tf_op jit(solution)/shard_map/ppermute | solution.py:29
  98.4 13.8 %collective-permute-start.14 = (bf16[2,576,128]{2,1,0:T(8,128)(2,1)S(1)}, bf16[2,576,128]{2,1,0:T(8,128)(2,1)S(1)}, u32[]{:S(2)}, u32[]{:S(2)}) collective-permute-start(bf16[2,576,128]{2,1,0:T(8,128)(2,1)S(1)} %collective-permute-done.12.refs_9_), channel_id=1, source_target_pairs={{0,8},{8,0},{1,9},{9,1},{2,10},{10,2},{3,11},{11,3},{4,12},{12,4},... | collective-permute-start | bytes 884744 | tf_op jit(solution)/shard_map/ppermute | solution.py:29
  98.8 23.3 %collective-permute-start.17 = (bf16[1,576,128]{2,1,0:T(8,128)(2,1)S(1)}, bf16[1,576,128]{2,1,0:T(8,128)(2,1)S(1)}, u32[]{:S(2)}, u32[]{:S(2)}) collective-permute-start(bf16[1,576,128]{2,1,0:T(8,128)(2,1)S(1)} %collective-permute-done.15.refs_8_), channel_id=1, source_target_pairs={{0,8},{8,0},{1,9},{9,1},{2,10},{10,2},{3,11},{11,3},{4,12},{12,4},... | collective-permute-start | bytes 442376 | tf_op jit(solution)/shard_map/ppermute | solution.py:29
  98.9 23.2 %collective-permute-start.18 = (bf16[1,576,128]{2,1,0:T(8,128)(2,1)S(1)}, bf16[1,576,128]{2,1,0:T(8,128)(2,1)S(1)}, u32[]{:S(2)}, u32[]{:S(2)}) collective-permute-start(bf16[1,576,128]{2,1,0:T(8,128)(2,1)S(1)} %collective-permute-done.16.refs_9_), channel_id=1, source_target_pairs={{0,8},{8,0},{1,9},{9,1},{2,10},{10,2},{3,11},{11,3},{4,12},{12,4},... | collective-permute-start | bytes 442376 | tf_op jit(solution)/shard_map/ppermute | solution.py:29
  99.4 1.0 copy-start.5
  100.3 1.0 copy-start.7
  101.3 1.0 copy-start.9
  112.2 1.1 copy-start
  113.3 1.1 copy-start.1
  114.4 1.1 copy-start.2

commit v3 on v2

v3 whole, which is shorter than its diff:
```python
import functools
import math

import jax
import jax.numpy as jnp
from jax import lax
from jax.experimental import pallas as pl
from jax.experimental.pallas import tpu as pltpu
from jax.sharding import Mesh, PartitionSpec as P

NOPE = 128
ROPE = 64
VDIM = 128
KV = 512
SPAN = 64
LANES = 128
MASKED = -1e30
EXP2_SCALE = (NOPE + ROPE) ** (-0.5) * math.log2(math.e)


def gather_blocks(x, axes, count):
    copies = jnp.broadcast_to(x[None], (count,) + x.shape)
    return lax.all_to_all(copies, axes, 0, 0, tiled=True)


def after(x, *done):
    for d in done:
        x = x + d[(0,) * d.ndim] * jnp.zeros((), x.dtype)
    return x


def shift(x, axis, by):
    n = lax.axis_size(axis)
    return lax.ppermute(x, axis, [(i, (i + by) % n) for i in range(n)])


def dot(a, b):
    return jnp.dot(a, b, preferred_element_type=jnp.float32)


def dot_t(a, b):
    return lax.dot_general(a, b, (((1,), (1,)), ((), ())), preferred_element_type=jnp.float32)


def weave(xh, core, own_ref, oth_ref, dst_ref):
    rows = 16
    for i in range(own_ref.shape[0] // rows):
        pair = (i // 2) * 2 + (xh if i % 2 == 0 else 1 - xh)
        at = pl.multiple_of((2 * pair + core) * rows, rows)
        ot = pl.multiple_of((2 * pair + 1 - core) * rows, rows)
        dst_ref[pl.ds(at, rows), :] = own_ref[i * rows : (i + 1) * rows, :]
        dst_ref[pl.ds(ot, rows), :] = oth_ref[i * rows : (i + 1) * rows, :]


def load_keys(piece_refs, klo_ref, khi_ref):
    shards = [(ref, j) for ref in piece_refs for j in range(ref.shape[0])]
    for i in range(0, len(shards), 2):
        (ref_a, a), (ref_b, b) = shards[i : i + 2]
        left, right = ref_a[a], ref_b[b]
        cols = slice(i * SPAN, (i + 2) * SPAN)
        klo_ref[:, cols] = jnp.concatenate([left[:, :SPAN], right[:, :SPAN]], axis=1)
        khi_ref[:, cols] = jnp.concatenate([left[:, SPAN:], right[:, SPAN:]], axis=1)


def key_positions(shards, span_ref, slot):
    lane = lax.broadcasted_iota(jnp.int32, (1, LANES), 1)
    rows = []
    for i in range(0, len(shards), 2):
        a, b = span_ref[2 * shards[i] + slot], span_ref[2 * shards[i + 1] + slot]
        rows.append(jnp.where(lane < SPAN, a, b) * SPAN + lane % SPAN)
    return jnp.concatenate(rows, axis=1)


def attention_kernel(layout, heads, tile, first, last, *refs):
    refs = list(refs)
    take = lambda n: [refs.pop(0) for _ in range(n)]
    idx_ref, span_ref = take(2)
    z, xh, core, slot0 = (idx_ref[i] for i in range(4))
    if first:
        query_ref, wko_ref, wkx_ref = take(3)
    else:
        q_ref, m_ref, l_ref, acc_ref = take(4)
    piece_refs = take(len(layout))
    if last:
        wvo_ref, wvx_ref = take(2)
        (out_ref,) = take(1)
        wv_ref, mix_ref = take(2)
    else:
        if first:
            (q_ref,) = take(1)
        mo_ref, lo_ref, acco_ref = take(3)
        if first:
            (wk_ref,) = take(1)
    klo_ref, khi_ref = take(2)

    shards = []
    for dz, which in layout:
        for dx, dc in which:
            zz = lax.rem(z + dz + 8, 8)
            xx = 1 - xh if dx else xh
            cc = 1 - core if dc else core
            shards.append((zz * 2 + xx) * 2 + cc)
    n = len(shards) * SPAN
    load_keys(piece_refs, klo_ref, khi_ref)
    pos_lo = key_positions(shards, span_ref, 0)
    pos_hi = key_positions(shards, span_ref, 1)
    within = lax.broadcasted_iota(jnp.int32, (tile, 1), 0) % SPAN

    if first:
        weave(xh, core, wko_ref, wkx_ref, wk_ref)
        for h in range(heads):
            cols = slice(h * NOPE, (h + 1) * NOPE)
            rows = slice(h * SPAN, (h + 1) * SPAN)
            at = h * (NOPE + ROPE)
            q_latent = dot_t(query_ref[:, at : at + NOPE], wk_ref[:, cols]).astype(jnp.bfloat16)
            q_rope = query_ref[:, at + NOPE : at + NOPE + ROPE]
            for slot in range(2):
                toks = slice(slot * SPAN, (slot + 1) * SPAN)
                q_ref[slot, rows, :KV] = q_latent[toks, :]
                q_ref[slot, rows, KV:] = q_rope[toks, :]
    if last:
        weave(xh, core, wvo_ref, wvx_ref, wv_ref)

    for slot in range(2):
        for row in range(0, heads * SPAN, tile):
            rows = slice(row, row + tile)
            q_pos = span_ref[slot0 + slot] * SPAN + within
            if slot == 0:
                s = jnp.where(pos_lo <= q_pos, dot(q_ref[slot, rows, :], klo_ref[...]), MASKED)
            else:
                s_lo = dot(q_ref[slot, rows, :], klo_ref[...])
                s_hi = jnp.where(pos_hi <= q_pos, dot(q_ref[slot, rows, :], khi_ref[...]), MASKED)
                s = jnp.concatenate([s_lo, s_hi], axis=1)
            high = jnp.max(s, axis=1, keepdims=True)
            if not first:
                old = m_ref[slot, rows, :1]
                high = jnp.maximum(high, old)
            w = jnp.exp2((s - high) * EXP2_SCALE)
            total = jnp.sum(w, axis=1, keepdims=True)
            w = w.astype(jnp.bfloat16)
            acc = dot_t(w[:, :n], klo_ref[:KV, :])
            if slot == 1:
                acc += dot_t(w[:, n:], khi_ref[:KV, :])
            if not first:
                fade = jnp.exp2((old - high) * EXP2_SCALE)
                total += fade * l_ref[slot, rows, :1]
                acc += fade * acc_ref[slot, rows, :]
            if last:
                mix_ref[slot, rows, :] = (acc / total).astype(jnp.bfloat16)
            else:
                mo_ref[slot, rows, :] = jnp.broadcast_to(high, (tile, LANES))
                lo_ref[slot, rows, :] = jnp.broadcast_to(total, (tile, LANES))
                acco_ref[slot, rows, :] = acc
    if last:
        for h in range(heads):
            cols = slice(h * VDIM, (h + 1) * VDIM)
            rows = slice(h * SPAN, (h + 1) * SPAN)
            both = jnp.concatenate([mix_ref[0, rows, :], mix_ref[1, rows, :]], axis=0)
            out_ref[:, cols] = dot(both, wv_ref[:, cols]).astype(jnp.bfloat16)


def attention(layout, heads, first, last, scalars, inputs, pieces, tail, cols):
    rows = heads * SPAN
    f32, b16 = jnp.float32, jnp.bfloat16
    shape = jax.ShapeDtypeStruct
    keys = sum(p.shape[0] for p in pieces) * SPAN
    state = [shape((2, rows, LANES), f32), shape((2, rows, LANES), f32), shape((2, rows, KV), f32)]
    scratch = [pltpu.VMEM((KV + ROPE, keys), b16), pltpu.VMEM((KV + ROPE, keys), b16)]
    aliases = {}
    if last:
        outs = [shape((2 * SPAN, cols), b16)]
        scratch = [pltpu.VMEM((KV, cols), b16), pltpu.VMEM((2, rows, KV), b16)] + scratch
    else:
        outs = list(state)
        if first:
            outs = [shape((2, rows, KV + ROPE), b16)] + outs
            scratch = [pltpu.VMEM((KV, cols), b16)] + scratch
        else:
            aliases = {3: 0, 4: 1, 5: 2}
    args = [*scalars, *inputs, *pieces, *tail]
    flops = 2 * 3 * rows * keys * (KV + ROPE + KV)
    size = sum(math.prod(a.shape) * a.dtype.itemsize for a in args)
    vmem = pl.BlockSpec(memory_space=pltpu.VMEM)
    return pl.pallas_call(
        functools.partial(attention_kernel, layout, heads, min(rows, 256), first, last),
        out_shape=outs,
        in_specs=[pl.BlockSpec(memory_space=pltpu.SMEM)] * 2 + [vmem] * (len(args) - 2),
        out_specs=[vmem] * len(outs),
        scratch_shapes=scratch,
        input_output_aliases=aliases,
        compiler_params=pltpu.CompilerParams(vmem_limit_bytes=28 << 20),
        cost_estimate=pl.CostEstimate(
            flops=flops, bytes_accessed=size, transcendentals=3 * rows * keys
        ),
    )(*args)


def per_device(compressed, latent, w_uq, w_uk, w_uv, span_ids):
    toks = compressed.shape[0]
    cols = w_uk.shape[1]
    heads = cols // NOPE
    zs, ys, xls = (lax.axis_size(a) for a in ("z", "y", "xl"))
    ctx = lax.axis_index(("z", "xh", "core"))
    idx = jnp.stack([lax.axis_index("z"), lax.axis_index("xh"), lax.axis_index("core"), 2 * ctx])

    shard = latent.T[None]
    here = jnp.concatenate([shard, shift(shard, "xh", 1)], axis=0)
    both, first_xh, second_xh = ((0, 0), (1, 0)), ((0, 0),), ((1, 0),)
    steps = [[(0, both, here)]]
    ahead = behind = here
    arrived = []
    for k in range(1, zs // 2):
        ahead, behind = shift(ahead, "z", 1), shift(behind, "z", -1)
        steps.append([(-k, both, ahead), (k, both, behind)])
        arrived += [ahead, behind]
    steps.append(
        [
            (-(zs // 2), first_xh, shift(ahead[:1], "z", 1)),
            (zs // 2, second_xh, shift(behind[1:], "z", -1)),
        ]
    )
    flip = lambda which: tuple((dx, 1) for dx, _ in which)
    steps = [
        step + [(dz, flip(which), shift(piece, "core", 1)) for dz, which, piece in step]
        for step in steps
    ]

    weights = jnp.concatenate([w_uk, w_uv], axis=0)
    weights_x = shift(weights, "xh", 1)
    shard_rows = w_uk.shape[0]
    features = after(compressed.T, weights_x, here)
    features = gather_blocks(features, ("y", "xl"), ys * xls).reshape(-1, toks)
    query = lax.dot_general(
        features, w_uq, (((0,), (0,)), ((), ())), preferred_element_type=jnp.float32
    ).astype(jnp.bfloat16)
    wk = jnp.concatenate([w_uk, weights_x[:shard_rows]], axis=0)
    wk = after(wk, features, arrived[0], arrived[1])
    wk = gather_blocks(wk, "z", zs).reshape(-1, cols)
    wk_x = shift(wk, "core", 1)
    wv = jnp.concatenate([w_uv, weights_x[shard_rows:]], axis=0)
    wv = after(wv, wk, query, arrived[2], arrived[3])
    wv = gather_blocks(wv, "z", zs).reshape(-1, cols)
    wv_x = shift(wv, "core", 1)

    def run(group, first, last, inputs, tail):
        group = [piece for step in group for piece in step]
        layout = tuple((dz, which) for dz, which, _ in group)
        pieces = [piece for _, _, piece in group]
        return attention(layout, heads, first, last, [idx, span_ids], inputs, pieces, tail, cols)

    state = run(steps[:3], True, False, [query, wk, wk_x], [])
    queries, state = state[:1], state[1:]
    (out,) = run(steps[3:], False, True, [*queries, *state], [wv, wv_x])
    return out


def solution(mesh):
    fine = Mesh(mesh.devices.reshape(8, 2, 2, 4, 2), ("z", "xh", "core", "y", "xl"))
    ctx, tp = ("z", "xh", "core"), ("y", "xl")
    placed = (P(ctx, tp), P(ctx, None), P(None, tp), P(ctx, tp), P(ctx, tp), P())
    return jax.shard_map(
        per_device, mesh=fine, in_specs=placed, out_specs=P(ctx, tp), check_vma=False
    )
```

time: 129 us -> 121 us (0.938)
  waiting for transfers between devices: 18.3 us -> 32.8 us
  blocking collectives: 13.6 us -> 0 us
  starting transfers between devices: 46.2 us -> 39.9 us
  Pallas kernels: 22.2 us -> 15.9 us
  between operations: 0.15 us -> 5.99 us
  local copies, waits for them, and re-layouts: 23.1 us -> 19.2 us
  other arithmetic: 0.19 us -> 3.42 us
    ppermute x20 -> x21, waiting for transfers between devices: 18.3 us -> 32.6 us  [shift(): return lax.ppermute(x, axis, [(i, (i + by) % n) for i in range(n)])]
    all_to_all x1 -> x0, blocking collectives: 13.6 us -> none  [gather_blocks(): return lax.all_to_all(copies, axes, 0, 0, tiled=True)]
    pallas_call x3 -> x2, Pallas kernels: 22.2 us -> 15.9 us  [attention(): pl.pallas_call(functools.partial(attention_kernel, layout, heads, min(row...]
    ppermute x20 -> x21, starting transfers between devices: 28.7 us -> 24.9 us  [shift(): return lax.ppermute(x, axis, [(i, (i + by) % n) for i in range(n)])]
    reshape x4 -> x0, local copies, waits for them, and re-layouts: 3.4 us -> none  [the longest x1 1.09 us: per_device(): q_nope = query[:, :, :NOPE].reshape(toks, cols)]
    all_to_all x2 -> x3, starting transfers between devices: 17.5 us -> 15 us  [gather_blocks(): return lax.all_to_all(copies, axes, 0, 0, tiled=True)]
    slice x4 -> x10, local copies, waits for them, and re-layouts: 4.38 us -> 6.75 us  [the longest x9 6.74 us: after(): x = x + d[(0,) * d.ndim] * jnp.zeros((), x.dtype)]
    convert_element_type x1 -> x0, local copies, waits for them, and re-layouts: 1.93 us -> none  [per_device(): query = lax.dot_general(features, w_uq, (((0,), (0,)), ((), ())), preferr...]
  transfers between devices with their start and end apart: 22 -> 24, of which waited for: 3 -> 5; matrix products, arithmetic and copies ran while one was open for 14% -> 11% of each run, Pallas kernels for 13% -> 7%
where the time goes in v3:
time: 121 us; the launch traced here: 120 us
  starting transfers between devices  39.9 us (33%)
  waiting for transfers between devices  32.8 us (27%)
  local copies, waits for them, and re-layouts  19.2 us (16%)
  Pallas kernels  15.9 us (13%)
  between operations  5.99 us (5%)
  other arithmetic  3.42 us (3%)
  matrix products  3.14 us (3%)
    ppermute x21, waiting for transfers between devices, shift(): return lax.ppermute(x, axis, [(i, (i + by) % n) for i in range(n)])  32.6 us
    ppermute x21, starting transfers between devices, shift(): return lax.ppermute(x, axis, [(i, (i + by) % n) for i in range(n)])  24.9 us
    pallas_call x2, Pallas kernels, attention(): pl.pallas_call(functools.partial(attention_kernel, layout, heads, min(row...  15.9 us
    all_to_all x3, starting transfers between devices, gather_blocks(): return lax.all_to_all(copies, axes, 0, 0, tiled=True)  15 us
    unnamed x28, local copies, waits for them, and re-layouts  8.64 us
    slice x9, local copies, waits for them, and re-layouts, after(): x = x + d[(0,) * d.ndim] * jnp.zeros((), x.dtype)  6.74 us
    dot_general x1, matrix products, per_device(): lax.dot_general(features, w_uq, (((0,), (0,)), ((), ())), preferred_eleme...  3.14 us
    broadcast_in_dim x3, local copies, waits for them, and re-layouts, gather_blocks(): copies = jnp.broadcast_to(x[None], (count,) + x.shape)  2.48 us
  transfers between devices with their start and end apart: 24, of which 5 were waited for; matrix products, arithmetic and copies ran while one was open for 11% of the time, Pallas kernels for 7%

profile of v3, /device:TPU:1, one launch (start us, length us, event | category | flops | bytes accessed | tf_op | source)
XLA Modules:
  0.0 120.4 jit_solution(6941363078296246519)
XLA Ops:
  0.0 0.8 pad_maximum_fusion.2
  0.8 3.6 %collective-permute-start = (bf16[32,1024]{1,0:T(8,128)(2,1)S(1)}, bf16[32,1024]{1,0:T(8,128)(2,1)S(1)}, u32[]{:S(2)}, u32[]{:S(2)}) collective-permute-start(bf16[32,1024]{1,0:T(8,128)(2,1)S(1)} %pad_maximum_fusion.2), channel_id=1, source_target_pairs={{0,16},{16,0},{1,17},{17,1},{2,18},{18,2},{3,19},{19,3},{4,20},{20... | collective-permute-start | bytes 196616 | tf_op jit(solution)/shard_map/ppermute | solution.py:34
  4.4 0.1 collective-permute-start.1
  4.5 1.2 %slice.53 = bf16[1,1,1]{2,1,0:T(2,128)(2,1)} slice(bf16[1,576,128]{2,1,0:T(8,128)(2,1)} %bitcast.31), slice={[0:1], [0:1], [0:1]} | slice | bytes 4 | tf_op jit(solution)/shard_map/slice | solution.py:28
  6.4 0.5 slice.52
  7.5 0.8 add_bitcast_fusion
  8.3 0.8 broadcast_in_dim.9
  9.1 5.2 %all-to-all-start = ((bf16[8,192,128]{2,1,0:T(8,128)(2,1)}), bf16[8,192,128]{2,1,0:T(8,128)(2,1)S(1)}, u32[]{:S(2)}, u32[]{:S(2)}) async-start(bf16[8,192,128]{2,1,0:T(8,128)(2,1)} %broadcast_in_dim.9), calls=%async_computation | async-start | bytes 786432 | tf_op jit(solution)/shard_map/all_to_all | solution.py:23
  14.4 0.9 pad_maximum_fusion.refs_5_
  15.3 1.7 %collective-permute-start.2 = (bf16[2,576,128]{2,1,0:T(8,128)(2,1)S(1)}, bf16[2,576,128]{2,1,0:T(8,128)(2,1)S(1)}, u32[]{:S(2)}, u32[]{:S(2)}) collective-permute-start(bf16[2,576,128]{2,1,0:T(8,128)(2,1)S(1)} %pad_maximum_fusion.refs_5_), channel_id=1, source_target_pairs={{0,32},{32,64},{64,96},{96,128},{128,160},{160,192},{192,224},{224... | collective-permute-start | bytes 884744 | tf_op jit(solution)/shard_map/ppermute | solution.py:34
  17.0 4.0 %collective-permute-start.3 = (bf16[2,576,128]{2,1,0:T(8,128)(2,1)S(1)}, bf16[2,576,128]{2,1,0:T(8,128)(2,1)S(1)}, u32[]{:S(2)}, u32[]{:S(2)}) collective-permute-start(bf16[2,576,128]{2,1,0:T(8,128)(2,1)S(1)} %pad_maximum_fusion.refs_5_), channel_id=1, source_target_pairs={{0,224},{32,0},{64,32},{96,64},{128,96},{160,128},{192,160},{224,1... | collective-permute-start | bytes 884744 | tf_op jit(solution)/shard_map/ppermute | solution.py:34
  21.1 0.2 all-to-all-done
  21.3 0.5 slice.55
  22.4 4.0 %collective-permute-done.2.refs_7_ = bf16[2,576,128]{2,1,0:T(8,128)(2,1)S(1)} collective-permute-done((bf16[2,576,128]{2,1,0:T(8,128)(2,1)S(1)}, bf16[2,576,128]{2,1,0:T(8,128)(2,1)S(1)}, u32[]{:S(2)}, u32[]{:S(2)}) %collective-permute-start.2) | collective-permute-done | bytes 294944 | tf_op jit(solution)/shard_map/ppermute | solution.py:34
  26.4 0.5 slice.56
  27.7 0.6 slice.57
  28.9 0.8 fusion.2
  29.7 0.0 copy-start.12
  29.7 0.8 broadcast_in_dim.10
  30.5 5.0 %all-to-all-start.1 = ((bf16[8,32,1024]{2,1,0:T(8,128)(2,1)}), bf16[8,32,1024]{2,1,0:T(8,128)(2,1)S(1)}, u32[]{:S(2)}, u32[]{:S(2)}) async-start(bf16[8,32,1024]{2,1,0:T(8,128)(2,1)} %broadcast_in_dim.10), calls=%async_computation.1 | async-start | bytes 1048576 | tf_op jit(solution)/shard_map/all_to_all | solution.py:23
  35.5 1.5 %collective-permute-start.8 = (bf16[2,576,128]{2,1,0:T(8,128)(2,1)S(1)}, bf16[2,576,128]{2,1,0:T(8,128)(2,1)}, u32[]{:S(2)}, u32[]{:S(2)}) collective-permute-start(bf16[2,576,128]{2,1,0:T(8,128)(2,1)S(1)} %collective-permute-done.2.refs_7_), channel_id=1, source_target_pairs={{0,32},{32,64},{64,96},{96,128},{128,160},{160,192},{192,224},{224... | collective-permute-start | bytes 884744 | tf_op jit(solution)/shard_map/ppermute | solution.py:34
  37.0 1.2 %collective-permute-start.9 = (bf16[2,576,128]{2,1,0:T(8,128)(2,1)S(1)}, bf16[2,576,128]{2,1,0:T(8,128)(2,1)}, u32[]{:S(2)}, u32[]{:S(2)}) collective-permute-start(bf16[2,576,128]{2,1,0:T(8,128)(2,1)S(1)} %collective-permute-done.3.refs_8_), channel_id=1, source_target_pairs={{0,224},{32,0},{64,32},{96,64},{128,96},{160,128},{192,160},{224,1... | collective-permute-start | bytes 884744 | tf_op jit(solution)/shard_map/ppermute | solution.py:34
  38.2 3.1 %convolution_convert_fusion.refs_2_ = bf16[128,1536]{1,0:T(8,128)(2,1)S(1)} fusion(bf16[1536,128]{1,0:T(8,128)(2,1)S(1)} %bitcast.29, bf16[1536,1536]{1,0:T(8,128)(2,1)} %param.8), kind=kOutput, calls=%fused_computation | convolution fusion | flops 604176384 | bytes 5505024 | tf_op jit(solution)/shard_map/dot_general | solution.py:233
  41.4 0.5 slice.62
  42.6 13.2 %collective-permute-done.8.refs_11_ = bf16[2,576,128]{2,1,0:T(8,128)(2,1)} collective-permute-done((bf16[2,576,128]{2,1,0:T(8,128)(2,1)S(1)}, bf16[2,576,128]{2,1,0:T(8,128)(2,1)}, u32[]{:S(2)}, u32[]{:S(2)}) %collective-permute-start.8) | collective-permute-done | bytes 294944 | tf_op jit(solution)/shard_map/ppermute | solution.py:34
  55.7 1.2 slice.63
  57.6 1.2 slice.64
  59.4 0.5 slice.61
  60.6 0.8 broadcast_in_dim.11
  61.4 4.8 %all-to-all-start.2 = ((bf16[8,32,1024]{2,1,0:T(8,128)(2,1)}), bf16[8,32,1024]{2,1,0:T(8,128)(2,1)S(1)}, u32[]{:S(2)}, u32[]{:S(2)}) async-start(bf16[8,32,1024]{2,1,0:T(8,128)(2,1)} %broadcast_in_dim.11), calls=%async_computation.2 | async-start | bytes 1048576 | tf_op jit(solution)/shard_map/all_to_all | solution.py:23
  66.2 1.8 %collective-permute-start.5 = (bf16[2,576,128]{2,1,0:T(8,128)(2,1)S(1)}, bf16[2,576,128]{2,1,0:T(8,128)(2,1)S(1)}, u32[]{:S(2)}, u32[]{:S(2)}) collective-permute-start(bf16[2,576,128]{2,1,0:T(8,128)(2,1)S(1)} %pad_maximum_fusion.refs_5_), channel_id=1, source_target_pairs={{0,8},{8,0},{1,9},{9,1},{2,10},{10,2},{3,11},{11,3},{4,12},{12,4},... | collective-permute-start | bytes 884744 | tf_op jit(solution)/shard_map/ppermute | solution.py:34
  67.9 1.7 %collective-permute-start.12 = (bf16[2,576,128]{2,1,0:T(8,128)(2,1)}, bf16[2,576,128]{2,1,0:T(8,128)(2,1)S(1)}, u32[]{:S(2)}, u32[]{:S(2)}) collective-permute-start(bf16[2,576,128]{2,1,0:T(8,128)(2,1)} %collective-permute-done.8.refs_11_), channel_id=1, source_target_pairs={{0,32},{32,64},{64,96},{96,128},{128,160},{160,192},{192,224},{224... | collective-permute-start | bytes 884744 | tf_op jit(solution)/shard_map/ppermute | solution.py:34
  69.7 1.2 %collective-permute-start.13 = (bf16[2,576,128]{2,1,0:T(8,128)(2,1)}, bf16[2,576,128]{2,1,0:T(8,128)(2,1)S(1)}, u32[]{:S(2)}, u32[]{:S(2)}) collective-permute-start(bf16[2,576,128]{2,1,0:T(8,128)(2,1)} %collective-permute-done.9.refs_12_), channel_id=1, source_target_pairs={{0,224},{32,0},{64,32},{96,64},{128,96},{160,128},{192,160},{224,1... | collective-permute-start | bytes 884744 | tf_op jit(solution)/shard_map/ppermute | solution.py:34
  70.9 0.4 collective-permute-start.4
  71.3 0.2 collective-permute-start.6
  71.4 0.0 collective-permute-done.5.refs_6_
  71.4 0.7 copy-done.4
  72.1 0.4 collective-permute-start.7
  72.5 14.3 %collective-permute-done.12.refs_6_ = bf16[2,576,128]{2,1,0:T(8,128)(2,1)S(1)} collective-permute-done((bf16[2,576,128]{2,1,0:T(8,128)(2,1)}, bf16[2,576,128]{2,1,0:T(8,128)(2,1)S(1)}, u32[]{:S(2)}, u32[]{:S(2)}) %collective-permute-start.12) | collective-permute-done | bytes 294944 | tf_op jit(solution)/shard_map/ppermute | solution.py:34
  86.8 1.5 %collective-permute-start.10 = (bf16[2,576,128]{2,1,0:T(8,128)(2,1)}, bf16[2,576,128]{2,1,0:T(8,128)(2,1)S(1)}, u32[]{:S(2)}, u32[]{:S(2)}) collective-permute-start(bf16[2,576,128]{2,1,0:T(8,128)(2,1)} %collective-permute-done.8.refs_11_), channel_id=1, source_target_pairs={{0,8},{8,0},{1,9},{9,1},{2,10},{10,2},{3,11},{11,3},{4,12},{12,4},... | collective-permute-start | bytes 884744 | tf_op jit(solution)/shard_map/ppermute | solution.py:34
  88.3 0.0 collective-permute-done.13.refs_7_
  88.3 0.0 collective-permute-start.11
  88.3 0.7 slice.58
  88.9 0.7 slice.59
  89.6 0.7 copy-done.6
  90.3 0.0 collective-permute-start.16
  90.4 0.7 copy-done.8
  91.1 2.7 %collective-permute-start.17 = (bf16[1,576,128]{2,1,0:T(8,128)(2,1)}, bf16[1,576,128]{2,1,0:T(8,128)(2,1)S(1)}, u32[]{:S(2)}, u32[]{:S(2)}) collective-permute-start(bf16[1,576,128]{2,1,0:T(8,128)(2,1)} %slice.59), channel_id=1, source_target_pairs={{0,224},{32,0},{64,32},{96,64},{128,96},{160,128},{192,160},{224,1... | collective-permute-start | bytes 442376 | tf_op jit(solution)/shard_map/ppermute | solution.py:34
  93.7 0.7 copy-done.10
  94.5 1.1 collective-permute-start.20
  95.5 0.1 pad_add_fusion.refs_0_
  95.6 0.0 collective-permute-start.14
  95.7 1.1 collective-permute-done.16.refs_10_
  96.8 1.4 %collective-permute-start.15 = (bf16[2,576,128]{2,1,0:T(8,128)(2,1)S(1)}, bf16[2,576,128]{2,1,0:T(8,128)(2,1)S(1)}, u32[]{:S(2)}, u32[]{:S(2)}) collective-permute-start(bf16[2,576,128]{2,1,0:T(8,128)(2,1)S(1)} %collective-permute-done.13.refs_7_), channel_id=1, source_target_pairs={{0,8},{8,0},{1,9},{9,1},{2,10},{10,2},{3,11},{11,3},{4,12},{12,4},... | collective-permute-start | bytes 884744 | tf_op jit(solution)/shard_map/ppermute | solution.py:34
  98.1 0.0 collective-permute-start.18
  98.1 0.5 collective-permute-start.19
  98.7 1.0 copy-done.1
  99.6 1.0 copy-done.3
  100.6 1.0 copy-done.5
  101.5 1.0 copy-done.7
  102.5 1.0 copy-done.9
  103.5 1.0 copy-done.11
  104.4 8.4 %shard_map.64 = (bf16[2,512,576]{2,1,0:T(8,128)(2,1)S(1)}, f32[2,512,128]{2,1,0:T(8,128)S(1)}, f32[2,512,128]{2,1,0:T(8,128)S(1)}, f32[2,512,512]{2,1,0:T(8,128)S(1)}) custom-call(s32[4]{0:T(128)S(1)} %pad_add_fusion.refs_0_, s32[64]{0:T(128)S(1)} %copy-done.12, bf16[128,1536]{1,0:T(8,128)(2,1)S(1)} %convolution_convert_fusion.refs_2_, ...), custom_call_target="tpu_custom_call" | custom-call | flops 4278190080 | bytes 4391184 | tf_op jit(solution)/shard_map/pallas_call | solution.py:184
  112.9 7.4 %shard_map.65 = bf16[128,1024]{1,0:T(8,128)(2,1)} custom-call(s32[4]{0:T(128)S(1)} %pad_add_fusion.refs_0_, s32[64]{0:T(128)S(1)} %copy-done.12, bf16[2,512,576]{2,1,0:T(8,128)(2,1)S(1)} %get-tuple-element.9.refs_2_, f32[2,512,128]{2,1,0:T(8,128)S(1)} %get-tuple-element.10.refs_3_, f32[2,512,128]{2,1,0:T(8,128)S(1)} %get-tuple-element.11.refs_4_, ...), custom_call_target="tpu_custom_call" | custom-call | flops 2566914048 | bytes 7143696 | tf_op jit(solution)/shard_map/pallas_call | solution.py:184
  (36 shorter events, 0.1 us)
Async XLA Ops:
  0.8 59.7 %copy-start.13 = (bf16[16,1024]{1,0:T(8,128)(2,1)S(1)}, bf16[16,1024]{1,0:T(8,128)(2,1)}, u32[]{:S(2)}) copy-start(bf16[16,1024]{1,0:T(8,128)(2,1)} %param.10) | copy-start | bytes 98308
  0.8 5.6 %collective-permute-start = (bf16[32,1024]{1,0:T(8,128)(2,1)S(1)}, bf16[32,1024]{1,0:T(8,128)(2,1)S(1)}, u32[]{:S(2)}, u32[]{:S(2)}) collective-permute-start(bf16[32,1024]{1,0:T(8,128)(2,1)S(1)} %pad_maximum_fusion.2), channel_id=1, source_target_pairs={{0,16},{16,0},{1,17},{17,1},{2,18},{18,2},{3,19},{19,3},{4,20},{20... | collective-permute-start | bytes 196616 | tf_op jit(solution)/shard_map/ppermute | solution.py:34
  4.4 10.0 %collective-permute-start.1 = (bf16[1,576,128]{2,1,0:T(8,128)(2,1)}, bf16[1,576,128]{2,1,0:T(8,128)(2,1)S(1)}, u32[]{:S(2)}, u32[]{:S(2)}) collective-permute-start(bf16[1,576,128]{2,1,0:T(8,128)(2,1)} %bitcast.30), channel_id=1, source_target_pairs={{0,16},{16,0},{1,17},{17,1},{2,18},{18,2},{3,19},{19,3},{4,20},{20... | collective-permute-start | bytes 442376 | tf_op jit(solution)/shard_map/ppermute | solution.py:34
  9.1 12.1 %all-to-all-start = ((bf16[8,192,128]{2,1,0:T(8,128)(2,1)}), bf16[8,192,128]{2,1,0:T(8,128)(2,1)S(1)}, u32[]{:S(2)}, u32[]{:S(2)}) async-start(bf16[8,192,128]{2,1,0:T(8,128)(2,1)} %broadcast_in_dim.9), calls=%async_computation | async-start | bytes 786432 | tf_op jit(solution)/shard_map/all_to_all | solution.py:23
  15.3 11.1 %collective-permute-start.2 = (bf16[2,576,128]{2,1,0:T(8,128)(2,1)S(1)}, bf16[2,576,128]{2,1,0:T(8,128)(2,1)S(1)}, u32[]{:S(2)}, u32[]{:S(2)}) collective-permute-start(bf16[2,576,128]{2,1,0:T(8,128)(2,1)S(1)} %pad_maximum_fusion.refs_5_), channel_id=1, source_target_pairs={{0,32},{32,64},{64,96},{96,128},{128,160},{160,192},{192,224},{224... | collective-permute-start | bytes 884744 | tf_op jit(solution)/shard_map/ppermute | solution.py:34
  17.0 10.6 %collective-permute-start.3 = (bf16[2,576,128]{2,1,0:T(8,128)(2,1)S(1)}, bf16[2,576,128]{2,1,0:T(8,128)(2,1)S(1)}, u32[]{:S(2)}, u32[]{:S(2)}) collective-permute-start(bf16[2,576,128]{2,1,0:T(8,128)(2,1)S(1)} %pad_maximum_fusion.refs_5_), channel_id=1, source_target_pairs={{0,224},{32,0},{64,32},{96,64},{128,96},{160,128},{192,160},{224,1... | collective-permute-start | bytes 884744 | tf_op jit(solution)/shard_map/ppermute | solution.py:34
  26.4 63.2 %copy-start = (bf16[2,576,128]{2,1,0:T(8,128)(2,1)}, bf16[2,576,128]{2,1,0:T(8,128)(2,1)S(1)}, u32[]{:S(2)}) copy-start(bf16[2,576,128]{2,1,0:T(8,128)(2,1)S(1)} %collective-permute-done.2.refs_7_) | copy-start | bytes 884740
  27.7 62.0 %copy-start.2 = (bf16[2,576,128]{2,1,0:T(8,128)(2,1)}, bf16[2,576,128]{2,1,0:T(8,128)(2,1)S(1)}, u32[]{:S(2)}) copy-start(bf16[2,576,128]{2,1,0:T(8,128)(2,1)S(1)} %collective-permute-done.3.refs_8_) | copy-start | bytes 884740
  29.7 69.0 %copy-start.12 = (s32[64]{0:T(128)S(1)}, s32[64]{0:T(128)}, u32[]{:S(2)}) copy-start(s32[64]{0:T(128)} %refs_1_.3) | copy-start | bytes 772
  30.5 28.9 %all-to-all-start.1 = ((bf16[8,32,1024]{2,1,0:T(8,128)(2,1)}), bf16[8,32,1024]{2,1,0:T(8,128)(2,1)S(1)}, u32[]{:S(2)}, u32[]{:S(2)}) async-start(bf16[8,32,1024]{2,1,0:T(8,128)(2,1)} %broadcast_in_dim.10), calls=%async_computation.1 | async-start | bytes 1048576 | tf_op jit(solution)/shard_map/all_to_all | solution.py:23
  35.5 20.2 %collective-permute-start.8 = (bf16[2,576,128]{2,1,0:T(8,128)(2,1)S(1)}, bf16[2,576,128]{2,1,0:T(8,128)(2,1)}, u32[]{:S(2)}, u32[]{:S(2)}) collective-permute-start(bf16[2,576,128]{2,1,0:T(8,128)(2,1)S(1)} %collective-permute-done.2.refs_7_), channel_id=1, source_target_pairs={{0,32},{32,64},{64,96},{96,128},{128,160},{160,192},{192,224},{224... | collective-permute-start | bytes 884744 | tf_op jit(solution)/shard_map/ppermute | solution.py:34
  37.0 20.6 %collective-permute-start.9 = (bf16[2,576,128]{2,1,0:T(8,128)(2,1)S(1)}, bf16[2,576,128]{2,1,0:T(8,128)(2,1)}, u32[]{:S(2)}, u32[]{:S(2)}) collective-permute-start(bf16[2,576,128]{2,1,0:T(8,128)(2,1)S(1)} %collective-permute-done.3.refs_8_), channel_id=1, source_target_pairs={{0,224},{32,0},{64,32},{96,64},{128,96},{160,128},{192,160},{224,1... | collective-permute-start | bytes 884744 | tf_op jit(solution)/shard_map/ppermute | solution.py:34
  61.4 33.1 %all-to-all-start.2 = ((bf16[8,32,1024]{2,1,0:T(8,128)(2,1)}), bf16[8,32,1024]{2,1,0:T(8,128)(2,1)S(1)}, u32[]{:S(2)}, u32[]{:S(2)}) async-start(bf16[8,32,1024]{2,1,0:T(8,128)(2,1)} %broadcast_in_dim.11), calls=%async_computation.2 | async-start | bytes 1048576 | tf_op jit(solution)/shard_map/all_to_all | solution.py:23
  66.2 5.3 %collective-permute-start.5 = (bf16[2,576,128]{2,1,0:T(8,128)(2,1)S(1)}, bf16[2,576,128]{2,1,0:T(8,128)(2,1)S(1)}, u32[]{:S(2)}, u32[]{:S(2)}) collective-permute-start(bf16[2,576,128]{2,1,0:T(8,128)(2,1)S(1)} %pad_maximum_fusion.refs_5_), channel_id=1, source_target_pairs={{0,8},{8,0},{1,9},{9,1},{2,10},{10,2},{3,11},{11,3},{4,12},{12,4},... | collective-permute-start | bytes 884744 | tf_op jit(solution)/shard_map/ppermute | solution.py:34
  67.9 18.8 %collective-permute-start.12 = (bf16[2,576,128]{2,1,0:T(8,128)(2,1)}, bf16[2,576,128]{2,1,0:T(8,128)(2,1)S(1)}, u32[]{:S(2)}, u32[]{:S(2)}) collective-permute-start(bf16[2,576,128]{2,1,0:T(8,128)(2,1)} %collective-permute-done.8.refs_11_), channel_id=1, source_target_pairs={{0,32},{32,64},{64,96},{96,128},{128,160},{160,192},{192,224},{224... | collective-permute-start | bytes 884744 | tf_op jit(solution)/shard_map/ppermute | solution.py:34
  69.7 18.6 %collective-permute-start.13 = (bf16[2,576,128]{2,1,0:T(8,128)(2,1)}, bf16[2,576,128]{2,1,0:T(8,128)(2,1)S(1)}, u32[]{:S(2)}, u32[]{:S(2)}) collective-permute-start(bf16[2,576,128]{2,1,0:T(8,128)(2,1)} %collective-permute-done.9.refs_12_), channel_id=1, source_target_pairs={{0,224},{32,0},{64,32},{96,64},{128,96},{160,128},{192,160},{224,1... | collective-permute-start | bytes 884744 | tf_op jit(solution)/shard_map/ppermute | solution.py:34
  70.9 27.2 %collective-permute-start.4 = (bf16[256,1024]{1,0:T(8,128)(2,1)S(1)}, bf16[256,1024]{1,0:T(8,128)(2,1)S(1)}, u32[]{:S(2)}, u32[]{:S(2)}) collective-permute-start(bf16[256,1024]{1,0:T(8,128)(2,1)S(1)} %bitcast.24), channel_id=1, source_target_pairs={{0,8},{8,0},{1,9},{9,1},{2,10},{10,2},{3,11},{11,3},{4,12},{12,4},... | collective-permute-start | bytes 1572872 | tf_op jit(solution)/shard_map/ppermute | solution.py:34
  71.3 18.3 %collective-permute-start.6 = (bf16[2,576,128]{2,1,0:T(8,128)(2,1)S(1)}, bf16[2,576,128]{2,1,0:T(8,128)(2,1)S(1)}, u32[]{:S(2)}, u32[]{:S(2)}) collective-permute-start(bf16[2,576,128]{2,1,0:T(8,128)(2,1)S(1)} %collective-permute-done.2.refs_7_), channel_id=1, source_target_pairs={{0,8},{8,0},{1,9},{9,1},{2,10},{10,2},{3,11},{11,3},{4,12},{12,4},... | collective-permute-start | bytes 884744 | tf_op jit(solution)/shard_map/ppermute | solution.py:34
  71.4 0.7 copy-start.4
  72.1 18.2 %collective-permute-start.7 = (bf16[2,576,128]{2,1,0:T(8,128)(2,1)S(1)}, bf16[2,576,128]{2,1,0:T(8,128)(2,1)S(1)}, u32[]{:S(2)}, u32[]{:S(2)}) collective-permute-start(bf16[2,576,128]{2,1,0:T(8,128)(2,1)S(1)} %collective-permute-done.3.refs_8_), channel_id=1, source_target_pairs={{0,8},{8,0},{1,9},{9,1},{2,10},{10,2},{3,11},{11,3},{4,12},{12,4},... | collective-permute-start | bytes 884744 | tf_op jit(solution)/shard_map/ppermute | solution.py:34
  86.8 6.9 %collective-permute-start.10 = (bf16[2,576,128]{2,1,0:T(8,128)(2,1)}, bf16[2,576,128]{2,1,0:T(8,128)(2,1)S(1)}, u32[]{:S(2)}, u32[]{:S(2)}) collective-permute-start(bf16[2,576,128]{2,1,0:T(8,128)(2,1)} %collective-permute-done.8.refs_11_), channel_id=1, source_target_pairs={{0,8},{8,0},{1,9},{9,1},{2,10},{10,2},{3,11},{11,3},{4,12},{12,4},... | collective-permute-start | bytes 884744 | tf_op jit(solution)/shard_map/ppermute | solution.py:34
  88.3 7.4 %collective-permute-start.11 = (bf16[2,576,128]{2,1,0:T(8,128)(2,1)}, bf16[2,576,128]{2,1,0:T(8,128)(2,1)}, u32[]{:S(2)}, u32[]{:S(2)}) collective-permute-start(bf16[2,576,128]{2,1,0:T(8,128)(2,1)} %collective-permute-done.9.refs_12_), channel_id=1, source_target_pairs={{0,8},{8,0},{1,9},{9,1},{2,10},{10,2},{3,11},{11,3},{4,12},{12,4},... | collective-permute-start | bytes 884744 | tf_op jit(solution)/shard_map/ppermute | solution.py:34
  89.6 0.7 copy-start.6
  90.3 6.4 %collective-permute-start.16 = (bf16[1,576,128]{2,1,0:T(8,128)(2,1)}, bf16[1,576,128]{2,1,0:T(8,128)(2,1)}, u32[]{:S(2)}, u32[]{:S(2)}) collective-permute-start(bf16[1,576,128]{2,1,0:T(8,128)(2,1)} %slice.58), channel_id=1, source_target_pairs={{0,32},{32,64},{64,96},{96,128},{128,160},{160,192},{192,224},{224... | collective-permute-start | bytes 442376 | tf_op jit(solution)/shard_map/ppermute | solution.py:34
  90.4 0.7 copy-start.8
  91.1 7.1 %collective-permute-start.17 = (bf16[1,576,128]{2,1,0:T(8,128)(2,1)}, bf16[1,576,128]{2,1,0:T(8,128)(2,1)S(1)}, u32[]{:S(2)}, u32[]{:S(2)}) collective-permute-start(bf16[1,576,128]{2,1,0:T(8,128)(2,1)} %slice.59), channel_id=1, source_target_pairs={{0,224},{32,0},{64,32},{96,64},{128,96},{160,128},{192,160},{224,1... | collective-permute-start | bytes 442376 | tf_op jit(solution)/shard_map/ppermute | solution.py:34
  93.7 0.7 copy-start.10
  94.5 18.4 %collective-permute-start.20 = (bf16[256,1024]{1,0:T(8,128)(2,1)S(1)}, bf16[256,1024]{1,0:T(8,128)(2,1)S(1)}, u32[]{:S(2)}, u32[]{:S(2)}) collective-permute-start(bf16[256,1024]{1,0:T(8,128)(2,1)S(1)} %bitcast.26), channel_id=1, source_target_pairs={{0,8},{8,0},{1,9},{9,1},{2,10},{10,2},{3,11},{11,3},{4,12},{12,4},... | collective-permute-start | bytes 1572872 | tf_op jit(solution)/shard_map/ppermute | solution.py:34
  95.6 17.3 %collective-permute-start.14 = (bf16[2,576,128]{2,1,0:T(8,128)(2,1)S(1)}, bf16[2,576,128]{2,1,0:T(8,128)(2,1)S(1)}, u32[]{:S(2)}, u32[]{:S(2)}) collective-permute-start(bf16[2,576,128]{2,1,0:T(8,128)(2,1)S(1)} %collective-permute-done.12.refs_6_), channel_id=1, source_target_pairs={{0,8},{8,0},{1,9},{9,1},{2,10},{10,2},{3,11},{11,3},{4,12},{12,4},... | collective-permute-start | bytes 884744 | tf_op jit(solution)/shard_map/ppermute | solution.py:34
  96.8 16.1 %collective-permute-start.15 = (bf16[2,576,128]{2,1,0:T(8,128)(2,1)S(1)}, bf16[2,576,128]{2,1,0:T(8,128)(2,1)S(1)}, u32[]{:S(2)}, u32[]{:S(2)}) collective-permute-start(bf16[2,576,128]{2,1,0:T(8,128)(2,1)S(1)} %collective-permute-done.13.refs_7_), channel_id=1, source_target_pairs={{0,8},{8,0},{1,9},{9,1},{2,10},{10,2},{3,11},{11,3},{4,12},{12,4},... | collective-permute-start | bytes 884744 | tf_op jit(solution)/shard_map/ppermute | solution.py:34
  98.1 14.7 %collective-permute-start.18 = (bf16[1,576,128]{2,1,0:T(8,128)(2,1)}, bf16[1,576,128]{2,1,0:T(8,128)(2,1)S(1)}, u32[]{:S(2)}, u32[]{:S(2)}) collective-permute-start(bf16[1,576,128]{2,1,0:T(8,128)(2,1)} %collective-permute-done.16.refs_10_), channel_id=1, source_target_pairs={{0,8},{8,0},{1,9},{9,1},{2,10},{10,2},{3,11},{11,3},{4,12},{12,4},... | collective-permute-start | bytes 442376 | tf_op jit(solution)/shard_map/ppermute | solution.py:34
  98.1 14.7 %collective-permute-start.19 = (bf16[1,576,128]{2,1,0:T(8,128)(2,1)S(1)}, bf16[1,576,128]{2,1,0:T(8,128)(2,1)S(1)}, u32[]{:S(2)}, u32[]{:S(2)}) collective-permute-start(bf16[1,576,128]{2,1,0:T(8,128)(2,1)S(1)} %collective-permute-done.17.refs_11_), channel_id=1, source_target_pairs={{0,8},{8,0},{1,9},{9,1},{2,10},{10,2},{3,11},{11,3},{4,12},{12,4},... | collective-permute-start | bytes 442376 | tf_op jit(solution)/shard_map/ppermute | solution.py:34
  98.7 1.0 copy-start.1
  99.6 1.0 copy-start.3
  100.6 1.0 copy-start.5
  101.5 1.0 copy-start.7
  102.5 1.0 copy-start.9
  103.5 1.0 copy-start.11

commit v4 on v0

v4 whole, which is shorter than its diff:
```python
import functools
import math

import jax
import jax.numpy as jnp
from jax import lax
from jax.experimental import pallas as pl
from jax.experimental.pallas import tpu as pltpu
from jax.sharding import Mesh, PartitionSpec as P

NOPE = 128
ROPE = 64
VDIM = 128
KV = 512
SPAN = 64
LANES = 128
VARIANTS = 4
MASKED = -1e30
EXP2_SCALE = (NOPE + ROPE) ** (-0.5) * math.log2(math.e)


def after(x, *done):
    for d in done:
        x = x + d[(0,) * d.ndim] * jnp.zeros((), x.dtype)
    return x


def gather_blocks(x, axes, count):
    copies = jnp.broadcast_to(x[None], (count,) + x.shape)
    return lax.all_to_all(copies, axes, 0, 0, tiled=True)


def shift(x, axis, by):
    n = lax.axis_size(axis)
    return lax.ppermute(x, axis, [(i, (i + by) % n) for i in range(n)])


def dot(a, b):
    return jnp.dot(a, b, preferred_element_type=jnp.float32)


def dot_t(a, b):
    return lax.dot_general(a, b, (((1,), (1,)), ((), ())), preferred_element_type=jnp.float32)


def weave(xh, core, own_ref, oth_ref, offset, dst_ref):
    rows = 16
    for i in range(dst_ref.shape[0] // (2 * rows)):
        pair = (i // 2) * 2 + (xh if i % 2 == 0 else 1 - xh)
        at = pl.multiple_of((2 * pair + core) * rows, rows)
        ot = pl.multiple_of((2 * pair + 1 - core) * rows, rows)
        src = slice(2 * i * rows + offset, 2 * i * rows + offset + rows)
        dst_ref[pl.ds(at, rows), :] = own_ref[src, :]
        dst_ref[pl.ds(ot, rows), :] = oth_ref[src, :]


def attend_rows(q_ref, lo_ref, hi_ref, mix_ref, c, slot, rows, variant):
    q = q_ref[slot, rows, :]
    count = lo_ref.shape[1]
    step = count // VARIANTS
    within = lax.broadcasted_iota(jnp.int32, (q.shape[0], 1), 0) % SPAN
    lane = lax.broadcasted_iota(jnp.int32, (1, step), 1)
    if slot == 0:
        open_lo, n_lo = step * variant, step * (variant + 1)
        s_lo = dot(q, lo_ref[:, :n_lo])
        seen = lane + open_lo <= c * SPAN + within
        parts = [jnp.where(seen, s_lo[:, open_lo:], MASKED)]
        if open_lo:
            parts = [s_lo[:, :open_lo]] + parts
    else:
        first = step * variant
        s_hi = dot(q, hi_ref[:, first:])
        at = lane % SPAN - (lane + first) // SPAN * SPAN
        seen = at <= within - c * SPAN
        parts = [dot(q, lo_ref[...]), jnp.where(seen, s_hi[:, :step], MASKED)]
        if first + step < count:
            parts.append(s_hi[:, step:])
    s = jnp.concatenate(parts, axis=1)
    high = jnp.max(s, axis=1, keepdims=True)
    w = jnp.exp2((s - high) * EXP2_SCALE)
    total = jnp.sum(w, axis=1, keepdims=True)
    w = w.astype(jnp.bfloat16)
    if slot == 0:
        acc = dot_t(w, lo_ref[:KV, :n_lo])
    else:
        acc = dot_t(w[:, :count], lo_ref[:KV, :]) + dot_t(w[:, count:], hi_ref[:KV, first:])
    mix_ref[slot, rows, :] = (acc / total).astype(jnp.bfloat16)


def attention_kernel(layout, heads, tile, *refs):
    refs = list(refs)
    take = lambda n: [refs.pop(0) for _ in range(n)]
    idx_ref, span_ref, query_ref, w_ref, wx_ref = take(5)
    piece_refs = take(len(layout))
    out_ref, key_ref, lo_ref, hi_ref, wk_ref, wv_ref, q_ref, mix_ref, sem = refs
    z, xh, core, slot0 = (idx_ref[i] for i in range(4))
    zs = w_ref.shape[0] // 64

    copies = []
    for (dz, which), piece in zip(layout, piece_refs):
        for j, (dx, dc) in enumerate(which):
            zz = lax.rem(z + dz + zs, zs)
            xx = 1 - xh if dx else xh
            cc = 1 - core if dc else core
            place = span_ref[2 * ((zz * 2 + xx) * 2 + cc)]
            copy = pltpu.make_async_copy(piece.at[j], key_ref.at[place], sem.at[len(copies)])
            copy.start()
            copies.append(copy)

    weave(xh, core, w_ref, wx_ref, 0, wk_ref)
    for h in range(heads):
        rows = slice(h * SPAN, (h + 1) * SPAN)
        at = h * (NOPE + ROPE)
        q_latent = dot_t(query_ref[:, at : at + NOPE], wk_ref[:, h * NOPE : (h + 1) * NOPE])
        q_latent = q_latent.astype(jnp.bfloat16)
        q_rope = query_ref[:, at + NOPE : at + NOPE + ROPE]
        for slot in range(2):
            toks = slice(slot * SPAN, (slot + 1) * SPAN)
            q_ref[slot, rows, :KV] = q_latent[toks, :]
            q_ref[slot, rows, KV:] = q_rope[toks, :]
    weave(xh, core, w_ref, wx_ref, 16, wv_ref)

    for copy in copies:
        copy.wait()
    for i in range(0, len(copies), 2):
        left, right = key_ref[i], key_ref[i + 1]
        cols = slice(i * SPAN, (i + 2) * SPAN)
        lo_ref[:, cols] = jnp.concatenate([left[:, :SPAN], right[:, :SPAN]], axis=1)
        hi_ref[:, cols] = jnp.concatenate([left[:, SPAN:], right[:, SPAN:]], axis=1)

    c = span_ref[slot0]
    group = lax.div(c, len(copies) // VARIANTS)
    for variant in range(VARIANTS):

        @pl.when(group == variant)
        def _():
            def body(i, carry):
                rows = pl.ds(pl.multiple_of(i * tile, tile), tile)
                for slot in range(2):
                    attend_rows(q_ref, lo_ref, hi_ref, mix_ref, c, slot, rows, variant)
                return carry

            lax.fori_loop(0, heads * SPAN // tile, body, 0)

    for h in range(heads):
        cols = slice(h * VDIM, (h + 1) * VDIM)
        rows = slice(h * SPAN, (h + 1) * SPAN)
        both = jnp.concatenate([mix_ref[0, rows, :], mix_ref[1, rows, :]], axis=0)
        out_ref[:, cols] = dot(both, wv_ref[:, cols]).astype(jnp.bfloat16)


def attention(layout, heads, idx, span_ids, query, w, w_x, pieces):
    rows, cols = heads * SPAN, w.shape[1]
    b16 = jnp.bfloat16
    shards = sum(p.shape[0] for p in pieces)
    args = [idx, span_ids, query, w, w_x, *pieces]
    size = sum(math.prod(a.shape) * a.dtype.itemsize for a in args)
    work = 2 * rows * shards * SPAN * 5 // 4
    vmem = pl.BlockSpec(memory_space=pltpu.VMEM)
    return pl.pallas_call(
        functools.partial(attention_kernel, layout, heads, min(rows, 256)),
        out_shape=jax.ShapeDtypeStruct((2 * SPAN, cols), b16),
        in_specs=[pl.BlockSpec(memory_space=pltpu.SMEM)] * 2
        + [vmem] * 3
        + [pl.BlockSpec(memory_space=pltpu.HBM)] * len(pieces),
        out_specs=vmem,
        scratch_shapes=[
            pltpu.VMEM((shards, KV + ROPE, 2 * SPAN), b16),
            pltpu.VMEM((KV + ROPE, shards * SPAN), b16),
            pltpu.VMEM((KV + ROPE, shards * SPAN), b16),
            pltpu.VMEM((KV, cols), b16),
            pltpu.VMEM((KV, cols), b16),
            pltpu.VMEM((2, rows, KV + ROPE), b16),
            pltpu.VMEM((2, rows, KV), b16),
            pltpu.SemaphoreType.DMA((shards,)),
        ],
        compiler_params=pltpu.CompilerParams(vmem_limit_bytes=60 << 20),
        cost_estimate=pl.CostEstimate(
            flops=2 * work * (2 * KV + ROPE), bytes_accessed=size, transcendentals=work
        ),
    )(*args)


def per_device(compressed, latent, w_uq, w_uk, w_uv, span_ids):
    toks = compressed.shape[0]
    heads = w_uk.shape[1] // NOPE
    zs, ys, xls = (lax.axis_size(a) for a in ("z", "y", "xl"))
    ctx = lax.axis_index(("z", "xh", "core"))
    idx = jnp.stack([lax.axis_index("z"), lax.axis_index("xh"), lax.axis_index("core"), 2 * ctx])

    weights = jnp.concatenate([w_uk, w_uv], axis=0)
    weights = jnp.concatenate([weights, shift(weights, "xh", 1)], axis=0)
    w = lax.all_gather(weights, "z", axis=0, tiled=True)

    features = after(compressed.T, lax.optimization_barrier(weights))
    features = gather_blocks(features, ("y", "xl"), ys * xls).reshape(-1, toks)
    query = lax.dot_general(
        features, w_uq, (((0,), (0,)), ((), ())), preferred_element_type=jnp.float32
    ).astype(jnp.bfloat16)

    shard = latent.T[None]
    here = jnp.concatenate([shard, shift(shard, "xh", 1)], axis=0)
    both, first_xh, second_xh = ((0, 0), (1, 0)), ((0, 0),), ((1, 0),)
    pieces = [(0, both, here)]
    ahead = behind = here
    for k in range(1, zs // 2):
        if k == 2:
            ahead, behind = after(ahead, features), after(behind, features)
        ahead, behind = shift(ahead, "z", 1), shift(behind, "z", -1)
        pieces += [(-k, both, ahead), (k, both, behind)]
    last = shift(after(ahead[:1], query), "z", 1), shift(after(behind[1:], query), "z", -1)
    pieces += [
        (-(zs // 2), first_xh, last[0]),
        (zs // 2, second_xh, last[1]),
    ]
    handed = [
        (dz, tuple((dx, 1) for dx, _ in which), shift(piece, "core", 1))
        for dz, which, piece in pieces
    ]
    w_x = shift(after(w, *last, *(piece for _, _, piece in handed[:-2])), "core", 1)
    pieces += handed

    layout = tuple((dz, which) for dz, which, _ in pieces)
    return attention(layout, heads, idx, span_ids, query, w, w_x, [p for _, _, p in pieces])


def solution(mesh):
    fine = Mesh(mesh.devices.reshape(8, 2, 2, 4, 2), ("z", "xh", "core", "y", "xl"))
    ctx, tp = ("z", "xh", "core"), ("y", "xl")
    placed = (P(ctx, tp), P(ctx, None), P(None, tp), P(ctx, tp), P(ctx, tp), P())
    return jax.shard_map(
        per_device, mesh=fine, in_specs=placed, out_specs=P(ctx, tp), check_vma=False
    )
```

time: 295 us -> 104 us (0.35)
  waiting for transfers between devices: 161 us -> 14 us
  other arithmetic: 53 us -> 4.75 us
  starting transfers between devices: 0.08 us -> 34.3 us
  blocking collectives: 25.2 us -> 0 us
  matrix products: 22.2 us -> 3.17 us
  Pallas kernels: 0 us -> 15.5 us
  local copies, waits for them, and re-layouts: 16.9 us -> 9.96 us
  between operations: 15.7 us -> 21.5 us
    all_gather x3 -> x1, waiting for transfers between devices: 159 us -> 0.02 us  [per_device(): w = lax.all_gather(weights, 'z', axis=0, tiled=True)]
    add x1 -> x6, other arithmetic: 35.8 us -> 2.42 us  [after(): x = x + d[(0,) * d.ndim] * jnp.zeros((), x.dtype)]
    ppermute x0 -> x20, starting transfers between devices: none -> 30 us  [shift(): return lax.ppermute(x, axis, [(i, (i + by) % n) for i in range(n)])]
    all_gather x1 -> x0, blocking collectives: 25.2 us -> none  [per_device(): lax.all_gather(compressed, 'tp', axis=1, tiled=True)]
    dot_general x7 -> x1, matrix products: 22.2 us -> 3.17 us  [per_device(): lax.dot_general(features, w_uq, (((0,), (0,)), ((), ())), preferred_eleme...]
    pallas_call x0 -> x1, Pallas kernels: none -> 15.5 us  [attention(): pl.pallas_call(functools.partial(attention_kernel, layout, heads, min(row...]
    ppermute x0 -> x20, waiting for transfers between devices: none -> 13.4 us  [shift(): return lax.ppermute(x, axis, [(i, (i + by) % n) for i in range(n)])]
    gather x4 -> x0, local copies, waits for them, and re-layouts: 7.81 us -> none  [per_device(): jnp.repeat(span_ids, span_len, total_repeat_length=total_slots) * span_len]
  transfers between devices with their start and end apart: 3 -> 22, of which waited for: 2 -> 8; matrix products, arithmetic and copies ran while one was open for 22% -> 15% of each run, Pallas kernels for 0% -> 0%
where the time goes in v4:
time: 104 us; the launch traced here: 103 us
  starting transfers between devices  34.3 us (33%)
  between operations  21.5 us (21%)
  Pallas kernels  15.5 us (15%)
  waiting for transfers between devices  14 us (13%)
  local copies, waits for them, and re-layouts  9.96 us (10%)
  other arithmetic  4.75 us (5%)
  matrix products  3.17 us (3%)
    ppermute x20, starting transfers between devices, shift(): return lax.ppermute(x, axis, [(i, (i + by) % n) for i in range(n)])  30 us
    pallas_call x1, Pallas kernels, attention(): pl.pallas_call(functools.partial(attention_kernel, layout, heads, min(row...  15.5 us
    ppermute x20, waiting for transfers between devices, shift(): return lax.ppermute(x, axis, [(i, (i + by) % n) for i in range(n)])  13.4 us
    slice x12, local copies, waits for them, and re-layouts, after(): x = x + d[(0,) * d.ndim] * jnp.zeros((), x.dtype)  6.9 us
    all_to_all x1, starting transfers between devices, gather_blocks(): return lax.all_to_all(copies, axes, 0, 0, tiled=True)  4.34 us
    dot_general x1, matrix products, per_device(): lax.dot_general(features, w_uq, (((0,), (0,)), ((), ())), preferred_eleme...  3.17 us
    add x6, other arithmetic, after(): x = x + d[(0,) * d.ndim] * jnp.zeros((), x.dtype)  2.42 us
    unnamed x42, local copies, waits for them, and re-layouts  2.27 us
  transfers between devices with their start and end apart: 22, of which 8 were waited for; matrix products, arithmetic and copies ran while one was open for 15% of the time, Pallas kernels for 0%

profile of v4, /device:TPU:1, one launch (start us, length us, event | category | flops | bytes accessed | tf_op | source)
XLA Modules:
  0.0 103.2 jit_solution(16997873626420433579)
XLA Ops:
  6.5 3.6 %collective-permute-start.1 = (bf16[1,576,128]{2,1,0:T(8,128)(2,1)}, bf16[1,576,128]{2,1,0:T(8,128)(2,1)S(1)}, u32[]{:S(2)}, u32[]{:S(2)}) collective-permute-start(bf16[1,576,128]{2,1,0:T(8,128)(2,1)} %bitcast.26), channel_id=1, source_target_pairs={{0,16},{16,0},{1,17},{17,1},{2,18},{18,2},{3,19},{19,3},{4,20},{20... | collective-permute-start | bytes 442376 | tf_op jit(solution)/shard_map/ppermute | solution.py:35
  10.1 0.8 pad_maximum_fusion.1
  10.9 0.0 collective-permute-start
  10.9 0.8 constant_dynamic-update-slice_fusion.2
  11.7 0.8 constant_dynamic-update-slice_fusion.1
  12.4 4.0 %collective-permute-done = bf16[32,1024]{1,0:T(8,128)(2,1)S(1)} collective-permute-done((bf16[32,1024]{1,0:T(8,128)(2,1)S(1)}, bf16[32,1024]{1,0:T(8,128)(2,1)S(1)}, u32[]{:S(2)}, u32[]{:S(2)}) %collective-permute-start) | collective-permute-done | bytes 65568 | tf_op jit(solution)/shard_map/ppermute | solution.py:35
  16.4 0.6 slice.58
  17.6 0.8 add_bitcast_fusion
  18.4 0.8 broadcast_in_dim.4
  19.2 4.3 %all-to-all-start = ((bf16[8,192,128]{2,1,0:T(8,128)(2,1)}), bf16[8,192,128]{2,1,0:T(8,128)(2,1)S(1)}, u32[]{:S(2)}, u32[]{:S(2)}) async-start(bf16[8,192,128]{2,1,0:T(8,128)(2,1)} %broadcast_in_dim.4), calls=%async_computation | async-start | bytes 786432 | tf_op jit(solution)/shard_map/all_to_all | solution.py:30
  23.6 0.0 all-gather.2.cloned.1.call-start
  23.6 0.0 collective-permute-done.1
  23.6 0.9 pad_maximum_fusion.refs_5_
  24.6 1.7 %collective-permute-start.2 = (bf16[2,576,128]{2,1,0:T(8,128)(2,1)S(1)}, bf16[2,576,128]{2,1,0:T(8,128)(2,1)S(1)}, u32[]{:S(2)}, u32[]{:S(2)}) collective-permute-start(bf16[2,576,128]{2,1,0:T(8,128)(2,1)S(1)} %pad_maximum_fusion.refs_5_), channel_id=1, source_target_pairs={{0,32},{32,64},{64,96},{96,128},{128,160},{160,192},{192,224},{224... | collective-permute-start | bytes 884744 | tf_op jit(solution)/shard_map/ppermute | solution.py:35
  26.3 0.0 all-gather.2.cloned.1.call-update
  26.3 4.0 %collective-permute-start.6 = (bf16[2,576,128]{2,1,0:T(8,128)(2,1)S(1)}, bf16[2,576,128]{2,1,0:T(8,128)(2,1)S(1)}, u32[]{:S(2)}, u32[]{:S(2)}) collective-permute-start(bf16[2,576,128]{2,1,0:T(8,128)(2,1)S(1)} %pad_maximum_fusion.refs_5_), channel_id=1, source_target_pairs={{0,224},{32,0},{64,32},{96,64},{128,96},{160,128},{192,160},{224,1... | collective-permute-start | bytes 884744 | tf_op jit(solution)/shard_map/ppermute | solution.py:35
  30.3 0.5 all-to-all-done
  30.9 0.5 slice.59
  32.1 4.1 %collective-permute-done.2.refs_6_ = bf16[2,576,128]{2,1,0:T(8,128)(2,1)S(1)} collective-permute-done((bf16[2,576,128]{2,1,0:T(8,128)(2,1)S(1)}, bf16[2,576,128]{2,1,0:T(8,128)(2,1)S(1)}, u32[]{:S(2)}, u32[]{:S(2)}) %collective-permute-start.2) | collective-permute-done | bytes 294944 | tf_op jit(solution)/shard_map/ppermute | solution.py:35
  36.2 0.1 collective-permute-start.3
  36.3 0.0 collective-permute-done.6.refs_7_
  36.3 2.7 %collective-permute-start.7 = (bf16[2,576,128]{2,1,0:T(8,128)(2,1)S(1)}, bf16[2,576,128]{2,1,0:T(8,128)(2,1)S(1)}, u32[]{:S(2)}, u32[]{:S(2)}) collective-permute-start(bf16[2,576,128]{2,1,0:T(8,128)(2,1)S(1)} %broadcast_add_fusion), channel_id=1, source_target_pairs={{0,224},{32,0},{64,32},{96,64},{128,96},{160,128},{192,160},{224,1... | collective-permute-start | bytes 884744 | tf_op jit(solution)/shard_map/ppermute | solution.py:35
  39.1 2.6 %collective-permute-start.10 = (bf16[2,576,128]{2,1,0:T(8,128)(2,1)S(1)}, bf16[2,576,128]{2,1,0:T(8,128)(2,1)S(1)}, u32[]{:S(2)}, u32[]{:S(2)}) collective-permute-start(bf16[2,576,128]{2,1,0:T(8,128)(2,1)S(1)} %pad_maximum_fusion.refs_5_), channel_id=1, source_target_pairs={{0,8},{8,0},{1,9},{9,1},{2,10},{10,2},{3,11},{11,3},{4,12},{12,4},... | collective-permute-start | bytes 884744 | tf_op jit(solution)/shard_map/ppermute | solution.py:35
  41.6 0.0 collective-permute-start.11
  41.6 0.5 collective-permute-start.12
  42.2 1.8 %collective-permute-done.3.refs_8_ = bf16[2,576,128]{2,1,0:T(8,128)(2,1)S(1)} collective-permute-done((bf16[2,576,128]{2,1,0:T(8,128)(2,1)S(1)}, bf16[2,576,128]{2,1,0:T(8,128)(2,1)S(1)}, u32[]{:S(2)}, u32[]{:S(2)}) %collective-permute-start.3) | collective-permute-done | bytes 294944 | tf_op jit(solution)/shard_map/ppermute | solution.py:35
  44.0 0.0 collective-permute-start.4
  44.0 1.4 %collective-permute-done.7.refs_9_ = bf16[2,576,128]{2,1,0:T(8,128)(2,1)S(1)} collective-permute-done((bf16[2,576,128]{2,1,0:T(8,128)(2,1)S(1)}, bf16[2,576,128]{2,1,0:T(8,128)(2,1)S(1)}, u32[]{:S(2)}, u32[]{:S(2)}) %collective-permute-start.7) | collective-permute-done | bytes 294944 | tf_op jit(solution)/shard_map/ppermute | solution.py:35
  45.4 3.4 %collective-permute-start.8 = (bf16[2,576,128]{2,1,0:T(8,128)(2,1)S(1)}, bf16[2,576,128]{2,1,0:T(8,128)(2,1)S(1)}, u32[]{:S(2)}, u32[]{:S(2)}) collective-permute-start(bf16[2,576,128]{2,1,0:T(8,128)(2,1)S(1)} %collective-permute-done.7.refs_9_), channel_id=1, source_target_pairs={{0,224},{32,0},{64,32},{96,64},{128,96},{160,128},{192,160},{224,1... | collective-permute-start | bytes 884744 | tf_op jit(solution)/shard_map/ppermute | solution.py:35
  48.8 3.2 %convolution_convert_fusion.refs_2_ = bf16[128,1536]{1,0:T(8,128)(2,1)S(1)} fusion(bf16[1536,128]{1,0:T(8,128)(2,1)S(1)} %bitcast.25, bf16[1536,1536]{1,0:T(8,128)(2,1)} %param.8), kind=kOutput, calls=%fused_computation | convolution fusion | flops 604176384 | bytes 5505024 | tf_op jit(solution)/shard_map/dot_general | solution.py:197
  52.0 0.6 slice.61
  53.2 0.2 collective-permute-done.4.refs_10_
  53.4 5.6 %collective-permute-start.13 = (bf16[2,576,128]{2,1,0:T(8,128)(2,1)S(1)}, bf16[2,576,128]{2,1,0:T(8,128)(2,1)S(1)}, u32[]{:S(2)}, u32[]{:S(2)}) collective-permute-start(bf16[2,576,128]{2,1,0:T(8,128)(2,1)S(1)} %collective-permute-done.3.refs_8_), channel_id=1, source_target_pairs={{0,8},{8,0},{1,9},{9,1},{2,10},{10,2},{3,11},{11,3},{4,12},{12,4},... | collective-permute-start | bytes 884744 | tf_op jit(solution)/shard_map/ppermute | solution.py:35
  59.0 0.0 collective-permute-done.10.refs_14_
  59.1 0.1 collective-permute-start.14
  59.2 0.0 collective-permute-done.11.refs_15_
  59.2 0.1 collective-permute-start.5
  59.3 0.0 collective-permute-done.12.refs_16_
  59.3 0.5 collective-permute-start.15
  59.8 0.5 collective-permute-start.16
  60.3 3.7 %collective-permute-start.9 = (bf16[1,576,128]{2,1,0:T(8,128)(2,1)S(1)}, bf16[1,576,128]{2,1,0:T(8,128)(2,1)S(1)}, u32[]{:S(2)}, u32[]{:S(2)}) collective-permute-start(bf16[1,576,128]{2,1,0:T(8,128)(2,1)S(1)} %slice_add_fusion), channel_id=1, source_target_pairs={{0,224},{32,0},{64,32},{96,64},{128,96},{160,128},{192,160},{224,1... | collective-permute-start | bytes 442376 | tf_op jit(solution)/shard_map/ppermute | solution.py:35
  64.0 0.6 slice.65
  65.2 0.6 slice.66
  66.5 0.6 slice.67
  67.8 0.5 slice.68
  68.9 0.0 collective-permute-done.14.refs_18_
  68.9 0.6 slice.69
  70.1 0.5 slice.62
  71.2 0.6 slice.64
  72.5 0.6 slice.70
  73.9 0.6 slice.71
  74.5 0.1 copy-done.15
  75.2 0.0 all-gather.2.cloned.1.call-done.refs_3_
  75.2 1.5 %add_add_fusion = bf16[512,1024]{1,0:T(8,128)(2,1)S(1)} fusion(bf16[512,1024]{1,0:T(8,128)(2,1)} %all-gather.2.cloned.1.call-done.refs_3_, bf16[]{:T(256)} %bitcast.20, bf16[]{:T(256)} %bitcast.19, bf16[]{:T(256)} %bitcast.18, bf16[]{:T(256)} %bitcast.17, bf16[]{:T(256)} %bitcast.16, bf16[]{:T(256)} %bitcast.15, bf16[]{:T(256)} %bitcast.14, bf16[]{:T(256)} %bitcast.13, ...), kind=kLoop, calls=%fused_computation.1 | loop fusion | flops 4718592 | bytes 2097170 | tf_op jit(solution)/shard_map/add | solution.py:24
  76.8 0.4 collective-permute-start.17
  77.2 0.2 collective-permute-start.18
  77.4 0.3 collective-permute-start.19
  77.7 0.6 pad_add_fusion.refs_0_
  78.3 1.7 %collective-permute-done.18.refs_21_ = bf16[1,576,128]{2,1,0:T(8,128)(2,1)S(1)} collective-permute-done((bf16[1,576,128]{2,1,0:T(8,128)(2,1)}, bf16[1,576,128]{2,1,0:T(8,128)(2,1)S(1)}, u32[]{:S(2)}, u32[]{:S(2)}) %collective-permute-start.18) | collective-permute-done | bytes 147488 | tf_op jit(solution)/shard_map/ppermute | solution.py:35
  80.0 0.2 collective-permute-done.19.refs_22_
  80.2 0.0 collective-permute-done.17.refs_4_
  80.2 0.4 copy-done.18
  80.6 0.2 copy-done.19
  80.8 15.5 %shard_map.64 = bf16[128,1024]{1,0:T(8,128)(2,1)} custom-call(s32[4]{0:T(128)} %pad_add_fusion.refs_0_, s32[64]{0:T(128)} %refs_1_.1, bf16[128,1536]{1,0:T(8,128)(2,1)} %copy-done, bf16[512,1024]{1,0:T(8,128)(2,1)} %all-gather.2.cloned.1.call-done.refs_3_, bf16[512,1024]{1,0:T(8,128)(2,1)} %collective-permute-done.17.refs_4_, ...), custom_call_target="tpu_custom_call" | custom-call | flops 5704253440 | bytes 7209232 | tf_op jit(solution)/shard_map/pallas_call | solution.py:160
  (48 shorter events, 0.2 us)
Async XLA Ops:
  6.5 17.1 %collective-permute-start.1 = (bf16[1,576,128]{2,1,0:T(8,128)(2,1)}, bf16[1,576,128]{2,1,0:T(8,128)(2,1)S(1)}, u32[]{:S(2)}, u32[]{:S(2)}) collective-permute-start(bf16[1,576,128]{2,1,0:T(8,128)(2,1)} %bitcast.26), channel_id=1, source_target_pairs={{0,16},{16,0},{1,17},{17,1},{2,18},{18,2},{3,19},{19,3},{4,20},{20... | collective-permute-start | bytes 442376 | tf_op jit(solution)/shard_map/ppermute | solution.py:35
  10.9 5.5 %collective-permute-start = (bf16[32,1024]{1,0:T(8,128)(2,1)S(1)}, bf16[32,1024]{1,0:T(8,128)(2,1)S(1)}, u32[]{:S(2)}, u32[]{:S(2)}) collective-permute-start(bf16[32,1024]{1,0:T(8,128)(2,1)S(1)} %pad_maximum_fusion.1), channel_id=1, source_target_pairs={{0,16},{16,0},{1,17},{17,1},{2,18},{18,2},{3,19},{19,3},{4,20},{20... | collective-permute-start | bytes 196616 | tf_op jit(solution)/shard_map/ppermute | solution.py:35
  16.4 9.9 %copy-start.4 = (bf16[64,1024]{1,0:T(8,128)(2,1)}, bf16[64,1024]{1,0:T(8,128)(2,1)S(1)}, u32[]{:S(2)}) copy-start(bf16[64,1024]{1,0:T(8,128)(2,1)S(1)} %constant_dynamic-update-slice_fusion) | copy-start | bytes 393220
  19.2 11.7 %all-to-all-start = ((bf16[8,192,128]{2,1,0:T(8,128)(2,1)}), bf16[8,192,128]{2,1,0:T(8,128)(2,1)S(1)}, u32[]{:S(2)}, u32[]{:S(2)}) async-start(bf16[8,192,128]{2,1,0:T(8,128)(2,1)} %broadcast_in_dim.4), calls=%async_computation | async-start | bytes 786432 | tf_op jit(solution)/shard_map/all_to_all | solution.py:30
  23.6 51.7 %all-gather.2.cloned.1.call-start = ((), (), s32[]{:S(2)}) async-start(), calls=%async_computation.1 | async-start | bytes 1179648 | tf_op jit(solution)/shard_map/all_gather | solution.py:193
  24.6 52.2 %copy-start.1 = (bf16[2,576,128]{2,1,0:T(8,128)(2,1)}, bf16[2,576,128]{2,1,0:T(8,128)(2,1)S(1)}, u32[]{:S(2)}) copy-start(bf16[2,576,128]{2,1,0:T(8,128)(2,1)S(1)} %pad_maximum_fusion.refs_5_) | copy-start | bytes 884740
  24.6 11.6 %collective-permute-start.2 = (bf16[2,576,128]{2,1,0:T(8,128)(2,1)S(1)}, bf16[2,576,128]{2,1,0:T(8,128)(2,1)S(1)}, u32[]{:S(2)}, u32[]{:S(2)}) collective-permute-start(bf16[2,576,128]{2,1,0:T(8,128)(2,1)S(1)} %pad_maximum_fusion.refs_5_), channel_id=1, source_target_pairs={{0,32},{32,64},{64,96},{96,128},{128,160},{160,192},{192,224},{224... | collective-permute-start | bytes 884744 | tf_op jit(solution)/shard_map/ppermute | solution.py:35
  26.3 10.0 %collective-permute-start.6 = (bf16[2,576,128]{2,1,0:T(8,128)(2,1)S(1)}, bf16[2,576,128]{2,1,0:T(8,128)(2,1)S(1)}, u32[]{:S(2)}, u32[]{:S(2)}) collective-permute-start(bf16[2,576,128]{2,1,0:T(8,128)(2,1)S(1)} %pad_maximum_fusion.refs_5_), channel_id=1, source_target_pairs={{0,224},{32,0},{64,32},{96,64},{128,96},{160,128},{192,160},{224,1... | collective-permute-start | bytes 884744 | tf_op jit(solution)/shard_map/ppermute | solution.py:35
  36.2 40.6 %copy-start.2 = (bf16[2,576,128]{2,1,0:T(8,128)(2,1)}, bf16[2,576,128]{2,1,0:T(8,128)(2,1)S(1)}, u32[]{:S(2)}) copy-start(bf16[2,576,128]{2,1,0:T(8,128)(2,1)S(1)} %collective-permute-done.2.refs_6_) | copy-start | bytes 884740
  36.2 7.8 %collective-permute-start.3 = (bf16[2,576,128]{2,1,0:T(8,128)(2,1)S(1)}, bf16[2,576,128]{2,1,0:T(8,128)(2,1)S(1)}, u32[]{:S(2)}, u32[]{:S(2)}) collective-permute-start(bf16[2,576,128]{2,1,0:T(8,128)(2,1)S(1)} %broadcast_add_fusion.1), channel_id=1, source_target_pairs={{0,32},{32,64},{64,96},{96,128},{128,160},{160,192},{192,224},{224... | collective-permute-start | bytes 884744 | tf_op jit(solution)/shard_map/ppermute | solution.py:35
  36.3 43.9 %copy-start.3 = (bf16[2,576,128]{2,1,0:T(8,128)(2,1)}, bf16[2,576,128]{2,1,0:T(8,128)(2,1)S(1)}, u32[]{:S(2)}) copy-start(bf16[2,576,128]{2,1,0:T(8,128)(2,1)S(1)} %collective-permute-done.6.refs_7_) | copy-start | bytes 884740
  36.3 9.1 %collective-permute-start.7 = (bf16[2,576,128]{2,1,0:T(8,128)(2,1)S(1)}, bf16[2,576,128]{2,1,0:T(8,128)(2,1)S(1)}, u32[]{:S(2)}, u32[]{:S(2)}) collective-permute-start(bf16[2,576,128]{2,1,0:T(8,128)(2,1)S(1)} %broadcast_add_fusion), channel_id=1, source_target_pairs={{0,224},{32,0},{64,32},{96,64},{128,96},{160,128},{192,160},{224,1... | collective-permute-start | bytes 884744 | tf_op jit(solution)/shard_map/ppermute | solution.py:35
  39.1 20.0 %collective-permute-start.10 = (bf16[2,576,128]{2,1,0:T(8,128)(2,1)S(1)}, bf16[2,576,128]{2,1,0:T(8,128)(2,1)S(1)}, u32[]{:S(2)}, u32[]{:S(2)}) collective-permute-start(bf16[2,576,128]{2,1,0:T(8,128)(2,1)S(1)} %pad_maximum_fusion.refs_5_), channel_id=1, source_target_pairs={{0,8},{8,0},{1,9},{9,1},{2,10},{10,2},{3,11},{11,3},{4,12},{12,4},... | collective-permute-start | bytes 884744 | tf_op jit(solution)/shard_map/ppermute | solution.py:35
  41.6 17.5 %collective-permute-start.11 = (bf16[2,576,128]{2,1,0:T(8,128)(2,1)S(1)}, bf16[2,576,128]{2,1,0:T(8,128)(2,1)S(1)}, u32[]{:S(2)}, u32[]{:S(2)}) collective-permute-start(bf16[2,576,128]{2,1,0:T(8,128)(2,1)S(1)} %collective-permute-done.2.refs_6_), channel_id=1, source_target_pairs={{0,8},{8,0},{1,9},{9,1},{2,10},{10,2},{3,11},{11,3},{4,12},{12,4},... | collective-permute-start | bytes 884744 | tf_op jit(solution)/shard_map/ppermute | solution.py:35
  41.6 17.6 %collective-permute-start.12 = (bf16[2,576,128]{2,1,0:T(8,128)(2,1)S(1)}, bf16[2,576,128]{2,1,0:T(8,128)(2,1)S(1)}, u32[]{:S(2)}, u32[]{:S(2)}) collective-permute-start(bf16[2,576,128]{2,1,0:T(8,128)(2,1)S(1)} %collective-permute-done.6.refs_7_), channel_id=1, source_target_pairs={{0,8},{8,0},{1,9},{9,1},{2,10},{10,2},{3,11},{11,3},{4,12},{12,4},... | collective-permute-start | bytes 884744 | tf_op jit(solution)/shard_map/ppermute | solution.py:35
  44.0 36.2 %copy-start.7 = (bf16[2,576,128]{2,1,0:T(8,128)(2,1)}, bf16[2,576,128]{2,1,0:T(8,128)(2,1)S(1)}, u32[]{:S(2)}) copy-start(bf16[2,576,128]{2,1,0:T(8,128)(2,1)S(1)} %collective-permute-done.3.refs_8_) | copy-start | bytes 884740
  44.0 9.4 %collective-permute-start.4 = (bf16[2,576,128]{2,1,0:T(8,128)(2,1)S(1)}, bf16[2,576,128]{2,1,0:T(8,128)(2,1)S(1)}, u32[]{:S(2)}, u32[]{:S(2)}) collective-permute-start(bf16[2,576,128]{2,1,0:T(8,128)(2,1)S(1)} %collective-permute-done.3.refs_8_), channel_id=1, source_target_pairs={{0,32},{32,64},{64,96},{96,128},{128,160},{160,192},{192,224},{224... | collective-permute-start | bytes 884744 | tf_op jit(solution)/shard_map/ppermute | solution.py:35
  45.4 34.8 %copy-start.8 = (bf16[2,576,128]{2,1,0:T(8,128)(2,1)}, bf16[2,576,128]{2,1,0:T(8,128)(2,1)S(1)}, u32[]{:S(2)}) copy-start(bf16[2,576,128]{2,1,0:T(8,128)(2,1)S(1)} %collective-permute-done.7.refs_9_) | copy-start | bytes 884740
  45.4 14.4 %collective-permute-start.8 = (bf16[2,576,128]{2,1,0:T(8,128)(2,1)S(1)}, bf16[2,576,128]{2,1,0:T(8,128)(2,1)S(1)}, u32[]{:S(2)}, u32[]{:S(2)}) collective-permute-start(bf16[2,576,128]{2,1,0:T(8,128)(2,1)S(1)} %collective-permute-done.7.refs_9_), channel_id=1, source_target_pairs={{0,224},{32,0},{64,32},{96,64},{128,96},{160,128},{192,160},{224,1... | collective-permute-start | bytes 884744 | tf_op jit(solution)/shard_map/ppermute | solution.py:35
  52.0 28.2 %copy-start = (bf16[128,1536]{1,0:T(8,128)(2,1)}, bf16[128,1536]{1,0:T(8,128)(2,1)S(1)}, u32[]{:S(2)}) copy-start(bf16[128,1536]{1,0:T(8,128)(2,1)S(1)} %convolution_convert_fusion.refs_2_) | copy-start | bytes 1179652
  53.4 26.8 %copy-start.5 = (bf16[2,576,128]{2,1,0:T(8,128)(2,1)}, bf16[2,576,128]{2,1,0:T(8,128)(2,1)S(1)}, u32[]{:S(2)}) copy-start(bf16[2,576,128]{2,1,0:T(8,128)(2,1)S(1)} %collective-permute-done.4.refs_10_) | copy-start | bytes 884740
  53.4 6.9 %collective-permute-start.13 = (bf16[2,576,128]{2,1,0:T(8,128)(2,1)S(1)}, bf16[2,576,128]{2,1,0:T(8,128)(2,1)S(1)}, u32[]{:S(2)}, u32[]{:S(2)}) collective-permute-start(bf16[2,576,128]{2,1,0:T(8,128)(2,1)S(1)} %collective-permute-done.3.refs_8_), channel_id=1, source_target_pairs={{0,8},{8,0},{1,9},{9,1},{2,10},{10,2},{3,11},{11,3},{4,12},{12,4},... | collective-permute-start | bytes 884744 | tf_op jit(solution)/shard_map/ppermute | solution.py:35
  59.0 14.8 %copy-start.9 = (bf16[2,576,128]{2,1,0:T(8,128)(2,1)}, bf16[2,576,128]{2,1,0:T(8,128)(2,1)S(1)}, u32[]{:S(2)}) copy-start(bf16[2,576,128]{2,1,0:T(8,128)(2,1)S(1)} %collective-permute-done.10.refs_14_) | copy-start | bytes 884740
  59.1 9.8 %collective-permute-start.14 = (bf16[2,576,128]{2,1,0:T(8,128)(2,1)S(1)}, bf16[2,576,128]{2,1,0:T(8,128)(2,1)S(1)}, u32[]{:S(2)}, u32[]{:S(2)}) collective-permute-start(bf16[2,576,128]{2,1,0:T(8,128)(2,1)S(1)} %collective-permute-done.7.refs_9_), channel_id=1, source_target_pairs={{0,8},{8,0},{1,9},{9,1},{2,10},{10,2},{3,11},{11,3},{4,12},{12,4},... | collective-permute-start | bytes 884744 | tf_op jit(solution)/shard_map/ppermute | solution.py:35
  59.2 15.3 %copy-start.10 = (bf16[2,576,128]{2,1,0:T(8,128)(2,1)}, bf16[2,576,128]{2,1,0:T(8,128)(2,1)S(1)}, u32[]{:S(2)}) copy-start(bf16[2,576,128]{2,1,0:T(8,128)(2,1)S(1)} %collective-permute-done.11.refs_15_) | copy-start | bytes 884740
  59.2 10.9 %collective-permute-start.5 = (bf16[1,576,128]{2,1,0:T(8,128)(2,1)S(1)}, bf16[1,576,128]{2,1,0:T(8,128)(2,1)S(1)}, u32[]{:S(2)}, u32[]{:S(2)}) collective-permute-start(bf16[1,576,128]{2,1,0:T(8,128)(2,1)S(1)} %slice_add_fusion.1), channel_id=1, source_target_pairs={{0,32},{32,64},{64,96},{96,128},{128,160},{160,192},{192,224},{224... | collective-permute-start | bytes 442376 | tf_op jit(solution)/shard_map/ppermute | solution.py:35
  59.3 15.2 %copy-start.11 = (bf16[2,576,128]{2,1,0:T(8,128)(2,1)}, bf16[2,576,128]{2,1,0:T(8,128)(2,1)S(1)}, u32[]{:S(2)}) copy-start(bf16[2,576,128]{2,1,0:T(8,128)(2,1)S(1)} %collective-permute-done.12.refs_16_) | copy-start | bytes 884740
  59.3 13.2 %collective-permute-start.15 = (bf16[2,576,128]{2,1,0:T(8,128)(2,1)S(1)}, bf16[2,576,128]{2,1,0:T(8,128)(2,1)S(1)}, u32[]{:S(2)}, u32[]{:S(2)}) collective-permute-start(bf16[2,576,128]{2,1,0:T(8,128)(2,1)S(1)} %collective-permute-done.4.refs_10_), channel_id=1, source_target_pairs={{0,8},{8,0},{1,9},{9,1},{2,10},{10,2},{3,11},{11,3},{4,12},{12,4},... | collective-permute-start | bytes 884744 | tf_op jit(solution)/shard_map/ppermute | solution.py:35
  59.8 20.5 %copy-start.6 = (bf16[2,576,128]{2,1,0:T(8,128)(2,1)}, bf16[2,576,128]{2,1,0:T(8,128)(2,1)S(1)}, u32[]{:S(2)}) copy-start(bf16[2,576,128]{2,1,0:T(8,128)(2,1)S(1)} %collective-permute-done.8.refs_11_) | copy-start | bytes 884740
  59.8 14.1 %collective-permute-start.16 = (bf16[2,576,128]{2,1,0:T(8,128)(2,1)S(1)}, bf16[2,576,128]{2,1,0:T(8,128)(2,1)S(1)}, u32[]{:S(2)}, u32[]{:S(2)}) collective-permute-start(bf16[2,576,128]{2,1,0:T(8,128)(2,1)S(1)} %collective-permute-done.8.refs_11_), channel_id=1, source_target_pairs={{0,8},{8,0},{1,9},{9,1},{2,10},{10,2},{3,11},{11,3},{4,12},{12,4},... | collective-permute-start | bytes 884744 | tf_op jit(solution)/shard_map/ppermute | solution.py:35
  60.3 14.2 %copy-start.12 = (bf16[2,576,128]{2,1,0:T(8,128)(2,1)}, bf16[2,576,128]{2,1,0:T(8,128)(2,1)S(1)}, u32[]{:S(2)}) copy-start(bf16[2,576,128]{2,1,0:T(8,128)(2,1)S(1)} %collective-permute-done.13.refs_17_) | copy-start | bytes 884740
  60.3 10.9 %collective-permute-start.9 = (bf16[1,576,128]{2,1,0:T(8,128)(2,1)S(1)}, bf16[1,576,128]{2,1,0:T(8,128)(2,1)S(1)}, u32[]{:S(2)}, u32[]{:S(2)}) collective-permute-start(bf16[1,576,128]{2,1,0:T(8,128)(2,1)S(1)} %slice_add_fusion), channel_id=1, source_target_pairs={{0,224},{32,0},{64,32},{96,64},{128,96},{160,128},{192,160},{224,1... | collective-permute-start | bytes 442376 | tf_op jit(solution)/shard_map/ppermute | solution.py:35
  68.9 5.6 %copy-start.13 = (bf16[2,576,128]{2,1,0:T(8,128)(2,1)}, bf16[2,576,128]{2,1,0:T(8,128)(2,1)S(1)}, u32[]{:S(2)}) copy-start(bf16[2,576,128]{2,1,0:T(8,128)(2,1)S(1)} %collective-permute-done.14.refs_18_) | copy-start | bytes 884740
  70.1 4.4 %copy-start.16 = (bf16[1,576,128]{2,1,0:T(8,128)(2,1)}, bf16[1,576,128]{2,1,0:T(8,128)(2,1)S(1)}, u32[]{:S(2)}) copy-start(bf16[1,576,128]{2,1,0:T(8,128)(2,1)S(1)} %collective-permute-done.5.refs_12_) | copy-start | bytes 442372
  71.2 3.3 %copy-start.17 = (bf16[1,576,128]{2,1,0:T(8,128)(2,1)}, bf16[1,576,128]{2,1,0:T(8,128)(2,1)S(1)}, u32[]{:S(2)}) copy-start(bf16[1,576,128]{2,1,0:T(8,128)(2,1)S(1)} %collective-permute-done.9.refs_13_) | copy-start | bytes 442372
  72.5 2.0 %copy-start.14 = (bf16[2,576,128]{2,1,0:T(8,128)(2,1)}, bf16[2,576,128]{2,1,0:T(8,128)(2,1)S(1)}, u32[]{:S(2)}) copy-start(bf16[2,576,128]{2,1,0:T(8,128)(2,1)S(1)} %collective-permute-done.15.refs_19_) | copy-start | bytes 884740
  73.9 0.7 copy-start.15
  76.8 3.4 %collective-permute-start.17 = (bf16[512,1024]{1,0:T(8,128)(2,1)S(1)}, bf16[512,1024]{1,0:T(8,128)(2,1)}, u32[]{:S(2)}, u32[]{:S(2)}) collective-permute-start(bf16[512,1024]{1,0:T(8,128)(2,1)S(1)} %add_add_fusion), channel_id=1, source_target_pairs={{0,8},{8,0},{1,9},{9,1},{2,10},{10,2},{3,11},{11,3},{4,12},{12,4},... | collective-permute-start | bytes 3145736 | tf_op jit(solution)/shard_map/ppermute | solution.py:35
  77.2 2.8 %collective-permute-start.18 = (bf16[1,576,128]{2,1,0:T(8,128)(2,1)}, bf16[1,576,128]{2,1,0:T(8,128)(2,1)S(1)}, u32[]{:S(2)}, u32[]{:S(2)}) collective-permute-start(bf16[1,576,128]{2,1,0:T(8,128)(2,1)} %copy-done.16), channel_id=1, source_target_pairs={{0,8},{8,0},{1,9},{9,1},{2,10},{10,2},{3,11},{11,3},{4,12},{12,4},... | collective-permute-start | bytes 442376 | tf_op jit(solution)/shard_map/ppermute | solution.py:35
  77.4 2.8 %collective-permute-start.19 = (bf16[1,576,128]{2,1,0:T(8,128)(2,1)}, bf16[1,576,128]{2,1,0:T(8,128)(2,1)S(1)}, u32[]{:S(2)}, u32[]{:S(2)}) collective-permute-start(bf16[1,576,128]{2,1,0:T(8,128)(2,1)} %copy-done.17), channel_id=1, source_target_pairs={{0,8},{8,0},{1,9},{9,1},{2,10},{10,2},{3,11},{11,3},{4,12},{12,4},... | collective-permute-start | bytes 442376 | tf_op jit(solution)/shard_map/ppermute | solution.py:35
  80.0 0.7 copy-start.18
  80.2 0.6 copy-start.19
Sparse Core Ops, SparseCore 0:
  26.4 40.6 all-gather.1

commit v5 on v4

v5 whole, which is shorter than its diff:
```python
import functools
import math

import jax
import jax.numpy as jnp
from jax import lax
from jax.experimental import pallas as pl
from jax.experimental.pallas import tpu as pltpu
from jax.sharding import Mesh, PartitionSpec as P

NOPE = 128
ROPE = 64
VDIM = 128
KV = 512
SPAN = 64
LANES = 128
VARIANTS = 4
MASKED = -1e30
EXP2_SCALE = (NOPE + ROPE) ** (-0.5) * math.log2(math.e)


def gate(values, *done):
    hbm = pl.BlockSpec(memory_space=pl.ANY)
    n = len(values)
    return pl.pallas_call(
        lambda *refs: None,
        out_shape=[jax.ShapeDtypeStruct(v.shape, v.dtype) for v in values],
        in_specs=[hbm] * (n + len(done)),
        out_specs=[hbm] * n,
        input_output_aliases={i: i for i in range(n)},
        compiler_params=pltpu.CompilerParams(vmem_limit_bytes=1 << 20),
        cost_estimate=pl.CostEstimate(flops=0, bytes_accessed=0, transcendentals=0),
    )(*values, *done)


def shift(x, axis, by):
    n = lax.axis_size(axis)
    return lax.ppermute(x, axis, [(i, (i + by) % n) for i in range(n)])


def dot(a, b):
    return jnp.dot(a, b, preferred_element_type=jnp.float32)


def dot_t(a, b):
    return lax.dot_general(a, b, (((1,), (1,)), ((), ())), preferred_element_type=jnp.float32)


def by_head(w):
    rows, cols = w.shape
    return w.reshape(rows, cols // LANES, LANES).transpose(1, 0, 2).reshape(-1, LANES)


def head_rows(w_ref, at, rows):
    return jnp.concatenate([w_ref[i, at : at + rows, :] for i in range(w_ref.shape[0])], axis=0)


def attend_rows(q_ref, lo_ref, hi_ref, mix_ref, c, slot, rows, variant):
    q = q_ref[slot, rows, :]
    count = lo_ref.shape[1]
    step = count // VARIANTS
    within = lax.broadcasted_iota(jnp.int32, (q.shape[0], 1), 0) % SPAN
    lane = lax.broadcasted_iota(jnp.int32, (1, step), 1)
    if slot == 0:
        open_lo, n_lo = step * variant, step * (variant + 1)
        s_lo = dot(q, lo_ref[:, :n_lo])
        seen = lane + open_lo <= c * SPAN + within
        parts = [jnp.where(seen, s_lo[:, open_lo:], MASKED)]
        if open_lo:
            parts = [s_lo[:, :open_lo]] + parts
    else:
        first = step * variant
        s_hi = dot(q, hi_ref[:, first:])
        at = lane % SPAN - (lane + first) // SPAN * SPAN
        seen = at <= within - c * SPAN
        parts = [dot(q, lo_ref[...]), jnp.where(seen, s_hi[:, :step], MASKED)]
        if first + step < count:
            parts.append(s_hi[:, step:])
    s = jnp.concatenate(parts, axis=1)
    high = jnp.max(s, axis=1, keepdims=True)
    w = jnp.exp2((s - high) * EXP2_SCALE)
    total = jnp.sum(w, axis=1, keepdims=True)
    w = w.astype(jnp.bfloat16)
    if slot == 0:
        acc = dot_t(w, lo_ref[:KV, :n_lo])
    else:
        acc = dot_t(w[:, :count], lo_ref[:KV, :]) + dot_t(w[:, count:], hi_ref[:KV, first:])
    mix_ref[slot, rows, :] = (acc / total).astype(jnp.bfloat16)


def attention_kernel(layout, heads, tile, *refs):
    refs = list(refs)
    take = lambda n: [refs.pop(0) for _ in range(n)]
    idx_ref, span_ref, query_ref = take(3)
    piece_refs = take(len(layout))
    out_ref, key_ref, w_ref, lo_ref, hi_ref, q_ref, mix_ref, key_sem, w_sem = refs
    z, xh, core, slot0 = (idx_ref[i] for i in range(4))
    shards, latent_rows = key_ref.shape[:2]
    zs = shards // 4
    shard_rows = KV // shards

    key_copies, w_copies = [], []
    for (dz, which), piece in zip(layout, piece_refs):
        for j, (dx, dc) in enumerate(which):
            zz = lax.rem(z + dz + zs, zs)
            xx = 1 - xh if dx else xh
            cc = 1 - core if dc else core
            shard, n = (zz * 2 + xx) * 2 + cc, len(w_copies)
            w_rows = pl.ds(latent_rows, w_ref.shape[1])
            w_copies.append(
                pltpu.make_async_copy(piece.at[j, w_rows], w_ref.at[shard], w_sem.at[n])
            )
            place = span_ref[2 * shard]
            key_rows = pl.ds(0, latent_rows)
            key_copies.append(
                pltpu.make_async_copy(piece.at[j, key_rows], key_ref.at[place], key_sem.at[n])
            )
    for copy in w_copies + key_copies:
        copy.start()
    for copy in w_copies:
        copy.wait()

    for h in range(heads):
        rows = slice(h * SPAN, (h + 1) * SPAN)
        at = h * (NOPE + ROPE)
        wk = head_rows(w_ref, h * shard_rows, shard_rows)
        q_latent = dot_t(query_ref[:, at : at + NOPE], wk).astype(jnp.bfloat16)
        q_rope = query_ref[:, at + NOPE : at + NOPE + ROPE]
        for slot in range(2):
            toks = slice(slot * SPAN, (slot + 1) * SPAN)
            q_ref[slot, rows, :KV] = q_latent[toks, :]
            q_ref[slot, rows, KV:] = q_rope[toks, :]

    for copy in key_copies:
        copy.wait()
    for i in range(0, shards, 2):
        left, right = key_ref[i], key_ref[i + 1]
        cols = slice(i * SPAN, (i + 2) * SPAN)
        lo_ref[:, cols] = jnp.concatenate([left[:, :SPAN], right[:, :SPAN]], axis=1)
        hi_ref[:, cols] = jnp.concatenate([left[:, SPAN:], right[:, SPAN:]], axis=1)

    c = span_ref[slot0]
    group = lax.div(c, shards // VARIANTS)
    for variant in range(VARIANTS):

        @pl.when(group == variant)
        def _():
            def body(i, carry):
                rows = pl.ds(pl.multiple_of(i * tile, tile), tile)
                for slot in range(2):
                    attend_rows(q_ref, lo_ref, hi_ref, mix_ref, c, slot, rows, variant)
                return carry

            lax.fori_loop(0, heads * SPAN // tile, body, 0)

    for h in range(heads):
        cols = slice(h * VDIM, (h + 1) * VDIM)
        rows = slice(h * SPAN, (h + 1) * SPAN)
        both = jnp.concatenate([mix_ref[0, rows, :], mix_ref[1, rows, :]], axis=0)
        wv = head_rows(w_ref, (heads + h) * shard_rows, shard_rows)
        out_ref[:, cols] = dot(both, wv).astype(jnp.bfloat16)


def attention(layout, heads, idx, span_ids, query, pieces):
    rows, cols = heads * SPAN, heads * VDIM
    b16 = jnp.bfloat16
    shards = sum(p.shape[0] for p in pieces)
    args = [idx, span_ids, query, *pieces]
    size = sum(math.prod(a.shape) * a.dtype.itemsize for a in args)
    work = 2 * rows * shards * SPAN * 5 // 4
    vmem = pl.BlockSpec(memory_space=pltpu.VMEM)
    return pl.pallas_call(
        functools.partial(attention_kernel, layout, heads, min(rows, 256)),
        out_shape=jax.ShapeDtypeStruct((2 * SPAN, cols), b16),
        in_specs=[pl.BlockSpec(memory_space=pltpu.SMEM)] * 2
        + [vmem]
        + [pl.BlockSpec(memory_space=pltpu.HBM)] * len(pieces),
        out_specs=vmem,
        scratch_shapes=[
            pltpu.VMEM((shards, KV + ROPE, 2 * SPAN), b16),
            pltpu.VMEM((shards, pieces[0].shape[1] - KV - ROPE, LANES), b16),
            pltpu.VMEM((KV + ROPE, shards * SPAN), b16),
            pltpu.VMEM((KV + ROPE, shards * SPAN), b16),
            pltpu.VMEM((2, rows, KV + ROPE), b16),
            pltpu.VMEM((2, rows, KV), b16),
            pltpu.SemaphoreType.DMA((shards,)),
            pltpu.SemaphoreType.DMA((shards,)),
        ],
        compiler_params=pltpu.CompilerParams(vmem_limit_bytes=60 << 20),
        cost_estimate=pl.CostEstimate(
            flops=2 * work * (2 * KV + ROPE), bytes_accessed=size, transcendentals=work
        ),
    )(*args)


def per_device(compressed, latent, w_uq, w_uk, w_uv, span_ids):
    toks = compressed.shape[0]
    heads = w_uk.shape[1] // NOPE
    zs, ys, xls = (lax.axis_size(a) for a in ("z", "y", "xl"))
    ctx = lax.axis_index(("z", "xh", "core"))
    idx = jnp.stack([lax.axis_index("z"), lax.axis_index("xh"), lax.axis_index("core"), 2 * ctx])

    shard = jnp.concatenate([latent.T, by_head(w_uk), by_head(w_uv)], axis=0)[None]
    here = jnp.concatenate([shard, shift(shard, "xh", 1)], axis=0)

    copies = jnp.broadcast_to(compressed.T[None], (ys * xls,) + compressed.T.shape)
    (copies,) = gate([copies], shard)
    features = lax.all_to_all(copies, ("y", "xl"), 0, 0, tiled=True).reshape(-1, toks)
    query = lax.dot_general(
        features, w_uq, (((0,), (0,)), ((), ())), preferred_element_type=jnp.float32
    ).astype(jnp.bfloat16)

    both, first_xh, second_xh = ((0, 0), (1, 0)), ((0, 0),), ((1, 0),)
    pieces = [(0, both, here)]
    ahead = behind = here
    for k in range(1, zs // 2):
        ahead, behind = shift(ahead, "z", 1), shift(behind, "z", -1)
        if k == 1:
            ahead, behind = gate([ahead, behind], features)
        if k == 2:
            ahead, behind = gate([ahead, behind], query)
        pieces += [(-k, both, ahead), (k, both, behind)]
    pieces += [
        (-(zs // 2), first_xh, shift(ahead[:1], "z", 1)),
        (zs // 2, second_xh, shift(behind[1:], "z", -1)),
    ]
    pieces += [
        (dz, tuple((dx, 1) for dx, _ in which), shift(piece, "core", 1))
        for dz, which, piece in pieces
    ]
    layout = tuple((dz, which) for dz, which, _ in pieces)
    return attention(layout, heads, idx, span_ids, query, [p for _, _, p in pieces])


def solution(mesh):
    fine = Mesh(mesh.devices.reshape(8, 2, 2, 4, 2), ("z", "xh", "core", "y", "xl"))
    ctx, tp = ("z", "xh", "core"), ("y", "xl")
    placed = (P(ctx, tp), P(ctx, None), P(None, tp), P(ctx, tp), P(ctx, tp), P())
    return jax.shard_map(
        per_device, mesh=fine, in_specs=placed, out_specs=P(ctx, tp), check_vma=False
    )
```

time: 104 us -> 80.6 us (0.77)
  between operations: 21.5 us -> 0.37 us
  blocking collectives: 0 us -> 12 us
  local copies, waits for them, and re-layouts: 9.96 us -> 3.19 us
  other arithmetic: 4.75 us -> 1.62 us
  starting transfers between devices: 34.3 us -> 31.5 us
  matrix products: 3.17 us -> 0.81 us
  waiting for transfers between devices: 14 us -> 15.2 us
    all_to_all x0 -> x1, blocking collectives: none -> 12 us  [per_device(): lax.all_to_all(copies, ('y', 'xl'), 0, 0, tiled=True).reshape(-1, toks)]
    slice x12 -> x2, local copies, waits for them, and re-layouts: 6.9 us -> 0.03 us  [the longest x1 0.02 us: per_device(): behind[1:]]
    all_to_all x1 -> x0, starting transfers between devices: 4.34 us -> none  [gather_blocks(): return lax.all_to_all(copies, axes, 0, 0, tiled=True)]
    add x6 -> x0, other arithmetic: 2.42 us -> none  [after(): x = x + d[(0,) * d.ndim] * jnp.zeros((), x.dtype)]
    dot_general x1, matrix products: 3.17 us -> 0.81 us  [per_device(): lax.dot_general(features, w_uq, (((0,), (0,)), ((), ())), preferred_eleme...]
    ppermute x20 -> x18, waiting for transfers between devices: 13.4 us -> 15.2 us  [shift(): return lax.ppermute(x, axis, [(i, (i + by) % n) for i in range(n)])]
    ppermute x20 -> x18, starting transfers between devices: 30 us -> 31.5 us  [shift(): return lax.ppermute(x, axis, [(i, (i + by) % n) for i in range(n)])]
    reshape x0 -> x2, local copies, waits for them, and re-layouts: none -> 1.15 us  [by_head(): w.reshape(rows, cols // LANES, LANES).transpose(1, 0, 2).reshape(-1, LANES)]
  transfers between devices with their start and end apart: 22 -> 18, of which waited for: 8 -> 6; matrix products, arithmetic and copies ran while one was open for 15% -> 3% of each run, Pallas kernels for 0% -> 0%
where the time goes in v5:
time: 80.6 us; the launch traced here: 80.4 us
  starting transfers between devices  31.5 us (39%)
  Pallas kernels  15.7 us (19%)
  waiting for transfers between devices  15.2 us (19%)
  blocking collectives  12 us (15%)
  local copies, waits for them, and re-layouts  3.19 us (4%)
  other arithmetic  1.62 us (2%)
  matrix products  0.81 us (1%)
    ppermute x18, starting transfers between devices, shift(): return lax.ppermute(x, axis, [(i, (i + by) % n) for i in range(n)])  31.5 us
    pallas_call x1, Pallas kernels, attention(): pl.pallas_call(functools.partial(attention_kernel, layout, heads, min(row...  15.7 us
    ppermute x18, waiting for transfers between devices, shift(): return lax.ppermute(x, axis, [(i, (i + by) % n) for i in range(n)])  15.2 us
    all_to_all x1, blocking collectives, per_device(): lax.all_to_all(copies, ('y', 'xl'), 0, 0, tiled=True).reshape(-1, toks)  12 us
  transfers between devices with their start and end apart: 18, of which 6 were waited for; matrix products, arithmetic and copies ran while one was open for 3% of the time, Pallas kernels for 0%

profile of v5, /device:TPU:1, one launch (start us, length us, event | category | flops | bytes accessed | tf_op | source)
XLA Modules:
  0.0 80.4 jit_solution(13710812914367868924)
XLA Ops:
  0.0 0.0 copy-start
  0.0 0.8 copy-done
  0.8 1.1 %copy_bitcast_fusion = bf16[16,8,128]{2,0,1:T(8,128)(2,1)S(1)} fusion(bf16[16,1024]{1,0:T(8,128)(2,1)} %param.10), kind=kLoop, calls=%fused_computation.3 | loop fusion | bytes 65536 | tf_op jit(solution)/shard_map/reshape | solution.py:51
  1.9 0.9 %maximum_bitcast_fusion.refs_1_ = bf16[1,832,128]{2,1,0:T(8,128)(2,1)S(1)} fusion(bf16[128,128]{1,0:T(8,128)(2,1)S(1)} %bitcast.31, bf16[128,128]{1,0:T(8,128)(2,1)S(1)} %bitcast.30, bf16[576,128]{1,0:T(8,128)(2,1)} %bitcast.29), kind=kLoop, calls=%fused_computation.2 | loop fusion | flops 638976 | bytes 425984 | tf_op jit(solution)/shard_map/broadcast_in_dim | solution.py:203
  2.8 3.7 %collective-permute-start = (bf16[1,832,128]{2,1,0:T(8,128)(2,1)S(1)}, bf16[1,832,128]{2,1,0:T(8,128)(2,1)S(1)}, u32[]{:S(2)}, u32[]{:S(2)}) collective-permute-start(bf16[1,832,128]{2,1,0:T(8,128)(2,1)S(1)} %maximum_bitcast_fusion.refs_1_), channel_id=1, source_target_pairs={{0,16},{16,0},{1,17},{17,1},{2,18},{18,2},{3,19},{19,3},{4,20},{20... | collective-permute-start | bytes 638984 | tf_op jit(solution)/shard_map/ppermute | solution.py:38
  6.5 3.9 %collective-permute-done = bf16[1,832,128]{2,1,0:T(8,128)(2,1)S(1)} collective-permute-done((bf16[1,832,128]{2,1,0:T(8,128)(2,1)S(1)}, bf16[1,832,128]{2,1,0:T(8,128)(2,1)S(1)}, u32[]{:S(2)}, u32[]{:S(2)}) %collective-permute-start) | collective-permute-done | bytes 213024 | tf_op jit(solution)/shard_map/ppermute | solution.py:38
  10.5 0.0 copy-start.7
  10.5 6.6 %collective-permute-start.2 = (bf16[2,832,128]{2,1,0:T(8,128)(2,1)S(1)}, bf16[2,832,128]{2,1,0:T(8,128)(2,1)S(1)}, u32[]{:S(2)}, u32[]{:S(2)}) collective-permute-start(bf16[2,832,128]{2,1,0:T(8,128)(2,1)S(1)} %pad_maximum_fusion.refs_3_), channel_id=1, source_target_pairs={{0,224},{32,0},{64,32},{96,64},{128,96},{160,128},{192,160},{224,1... | collective-permute-start | bytes 1277960 | tf_op jit(solution)/shard_map/ppermute | solution.py:38
  17.1 0.0 collective-permute-start.1
  17.1 0.8 %broadcast_in_dim.4.refs_0_ = bf16[8,192,128]{2,1,0:T(8,128)(2,1)S(1)} broadcast(bf16[192,128]{1,0:T(8,128)(2,1)} %bitcast.32), dimensions={1,2} | broadcast | bytes 442368 | tf_op jit(solution)/shard_map/broadcast_in_dim | solution.py:206
  18.0 12.0 %all_to_all.5 = bf16[8,192,128]{2,1,0:T(8,128)(2,1)S(1)} all-to-all(bf16[8,192,128]{2,1,0:T(8,128)(2,1)S(1)} %shard_map.64), channel_id=1, replica_groups=mesh['z'=8,'xh'=2,'core'=2,'y'=4,'xl'=2] {'y','xl'}, dimensions={0} | all-to-all | bytes 786432 | tf_op jit(solution)/shard_map/all_to_all | solution.py:208
  29.9 0.0 collective-permute-done.2.refs_1_
  29.9 0.0 collective-permute-done.1.refs_0_
  29.9 0.0 copy-start.3
  30.0 0.1 collective-permute-start.3
  30.0 2.7 %collective-permute-start.4 = (bf16[2,832,128]{2,1,0:T(8,128)(2,1)S(1)}, bf16[2,832,128]{2,1,0:T(8,128)(2,1)S(1)}, u32[]{:S(2)}, u32[]{:S(2)}) collective-permute-start(bf16[2,832,128]{2,1,0:T(8,128)(2,1)S(1)} %get-tuple-element.10.refs_5_), channel_id=1, source_target_pairs={{0,224},{32,0},{64,32},{96,64},{128,96},{160,128},{192,160},{224,1... | collective-permute-start | bytes 1277960 | tf_op jit(solution)/shard_map/ppermute | solution.py:38
  32.7 0.0 copy-done.6
  32.7 0.8 %convolution_convert_fusion.refs_2_ = bf16[128,1536]{1,0:T(8,128)(2,1)S(1)} fusion(bf16[1536,128]{1,0:T(8,128)(2,1)S(1)} %bitcast.28, bf16[1536,1536]{1,0:T(8,128)(2,1)S(1)} %copy-done.6), kind=kOutput, calls=%fused_computation | convolution fusion | flops 604176384 | bytes 5505024 | tf_op jit(solution)/shard_map/dot_general | solution.py:209
  33.5 0.0 copy-start.1
  33.5 5.9 %collective-permute-done.3.refs_0_ = bf16[2,832,128]{2,1,0:T(8,128)(2,1)S(1)} collective-permute-done((bf16[2,832,128]{2,1,0:T(8,128)(2,1)S(1)}, bf16[2,832,128]{2,1,0:T(8,128)(2,1)S(1)}, u32[]{:S(2)}, u32[]{:S(2)}) %collective-permute-start.3) | collective-permute-done | bytes 426016 | tf_op jit(solution)/shard_map/ppermute | solution.py:38
  39.4 0.0 collective-permute-done.4.refs_1_
  39.4 0.1 collective-permute-start.5
  39.5 2.7 %collective-permute-start.6 = (bf16[2,832,128]{2,1,0:T(8,128)(2,1)S(1)}, bf16[2,832,128]{2,1,0:T(8,128)(2,1)S(1)}, u32[]{:S(2)}, u32[]{:S(2)}) collective-permute-start(bf16[2,832,128]{2,1,0:T(8,128)(2,1)S(1)} %get-tuple-element.12.refs_7_), channel_id=1, source_target_pairs={{0,224},{32,0},{64,32},{96,64},{128,96},{160,128},{192,160},{224,1... | collective-permute-start | bytes 1277960 | tf_op jit(solution)/shard_map/ppermute | solution.py:38
  42.2 0.0 copy-done.7
  42.2 4.6 %collective-permute-start.9 = (bf16[2,832,128]{2,1,0:T(8,128)(2,1)S(1)}, bf16[2,832,128]{2,1,0:T(8,128)(2,1)S(1)}, u32[]{:S(2)}, u32[]{:S(2)}) collective-permute-start(bf16[2,832,128]{2,1,0:T(8,128)(2,1)S(1)} %pad_maximum_fusion.refs_3_), channel_id=1, source_target_pairs={{0,8},{8,0},{1,9},{9,1},{2,10},{10,2},{3,11},{11,3},{4,12},{12,4},... | collective-permute-start | bytes 1277960 | tf_op jit(solution)/shard_map/ppermute | solution.py:38
  46.8 0.0 collective-permute-start.10
  46.8 0.5 collective-permute-start.11
  47.3 0.4 collective-permute-done.5.refs_8_
  47.7 5.3 %collective-permute-start.12 = (bf16[2,832,128]{2,1,0:T(8,128)(2,1)S(1)}, bf16[2,832,128]{2,1,0:T(8,128)(2,1)S(1)}, u32[]{:S(2)}, u32[]{:S(2)}) collective-permute-start(bf16[2,832,128]{2,1,0:T(8,128)(2,1)S(1)} %get-tuple-element.11.refs_6_), channel_id=1, source_target_pairs={{0,8},{8,0},{1,9},{9,1},{2,10},{10,2},{3,11},{11,3},{4,12},{12,4},... | collective-permute-start | bytes 1277960 | tf_op jit(solution)/shard_map/ppermute | solution.py:38
  53.0 0.0 collective-permute-done.6.refs_9_
  53.0 0.0 copy-start.9
  53.0 0.1 collective-permute-start.13
  53.1 0.0 collective-permute-done.9.refs_12_
  53.1 0.0 copy-start.10
  53.1 0.7 collective-permute-start.7
  53.8 0.0 collective-permute-done.10.refs_13_
  53.8 2.3 %collective-permute-start.8 = (bf16[1,832,128]{2,1,0:T(8,128)(2,1)S(1)}, bf16[1,832,128]{2,1,0:T(8,128)(2,1)}, u32[]{:S(2)}, u32[]{:S(2)}) collective-permute-start(bf16[1,832,128]{2,1,0:T(8,128)(2,1)S(1)} %slice.9), channel_id=1, source_target_pairs={{0,224},{32,0},{64,32},{96,64},{128,96},{160,128},{192,160},{224,1... | collective-permute-start | bytes 638984 | tf_op jit(solution)/shard_map/ppermute | solution.py:38
  56.1 0.0 collective-permute-done.11.refs_14_
  56.1 0.8 %collective-permute-start.14 = (bf16[2,832,128]{2,1,0:T(8,128)(2,1)S(1)}, bf16[2,832,128]{2,1,0:T(8,128)(2,1)S(1)}, u32[]{:S(2)}, u32[]{:S(2)}) collective-permute-start(bf16[2,832,128]{2,1,0:T(8,128)(2,1)S(1)} %collective-permute-done.5.refs_8_), channel_id=1, source_target_pairs={{0,8},{8,0},{1,9},{9,1},{2,10},{10,2},{3,11},{11,3},{4,12},{12,4},... | collective-permute-start | bytes 1277960 | tf_op jit(solution)/shard_map/ppermute | solution.py:38
  56.9 0.0 collective-permute-done.12.refs_15_
  56.9 0.1 collective-permute-start.15
  57.1 4.0 %collective-permute-done.7.refs_10_ = bf16[1,832,128]{2,1,0:T(8,128)(2,1)} collective-permute-done((bf16[1,832,128]{2,1,0:T(8,128)(2,1)S(1)}, bf16[1,832,128]{2,1,0:T(8,128)(2,1)}, u32[]{:S(2)}, u32[]{:S(2)}) %collective-permute-start.7) | collective-permute-done | bytes 213024 | tf_op jit(solution)/shard_map/ppermute | solution.py:38
  61.1 1.2 %collective-permute-start.16 = (bf16[1,832,128]{2,1,0:T(8,128)(2,1)}, bf16[1,832,128]{2,1,0:T(8,128)(2,1)}, u32[]{:S(2)}, u32[]{:S(2)}) collective-permute-start(bf16[1,832,128]{2,1,0:T(8,128)(2,1)} %collective-permute-done.7.refs_10_), channel_id=1, source_target_pairs={{0,8},{8,0},{1,9},{9,1},{2,10},{10,2},{3,11},{11,3},{4,12},{12,4},... | collective-permute-start | bytes 638984 | tf_op jit(solution)/shard_map/ppermute | solution.py:38
  62.3 0.0 collective-permute-done.8.refs_11_
  62.3 0.0 copy-done.10
  62.3 0.1 collective-permute-start.17
  62.4 0.0 copy-done.11
  62.4 0.0 copy-done.12
  62.4 0.0 copy-done.13
  62.4 0.7 pad_add_fusion.refs_0_
  63.1 0.0 collective-permute-done.13.refs_16_
  63.1 0.7 collective-permute-done.16.refs_19_
  63.7 0.0 collective-permute-done.14.refs_17_
  63.7 0.4 collective-permute-done.17.refs_20_
  64.1 0.0 collective-permute-done.15.refs_18_
  64.1 0.0 copy-done.2
  64.1 0.0 copy-done.3
  64.1 0.0 copy-done.1
  64.1 0.0 copy-done.4
  64.1 0.0 copy-done.5
  64.1 0.0 copy-done.8
  64.2 0.0 copy-done.9
  64.2 0.3 copy-done.14
  64.5 15.7 %shard_map.67 = bf16[128,1024]{1,0:T(8,128)(2,1)} custom-call(s32[4]{0:T(128)} %pad_add_fusion.refs_0_, s32[64]{0:T(128)} %refs_1_.1, bf16[128,1536]{1,0:T(8,128)(2,1)} %copy-done.1, bf16[2,832,128]{2,1,0:T(8,128)(2,1)} %copy-done.7, bf16[2,832,128]{2,1,0:T(8,128)(2,1)} %copy-done.3, bf16[2,832,128]{2,1,0:T(8,128)(2,1)} %copy-done.2, ...), custom_call_target="tpu_custom_call" | custom-call | flops 5704253440 | bytes 7209232 | tf_op jit(solution)/shard_map/pallas_call | solution.py:172
  (16 shorter events, 0.1 us)
Async XLA Ops:
  0.0 0.8 copy-start
  0.0 32.7 %copy-start.6 = (bf16[1536,1536]{1,0:T(8,128)(2,1)S(1)}, bf16[1536,1536]{1,0:T(8,128)(2,1)}, u32[]{:S(2)}) copy-start(bf16[1536,1536]{1,0:T(8,128)(2,1)} %param.8) | copy-start | bytes 14155780
  2.8 7.6 %collective-permute-start = (bf16[1,832,128]{2,1,0:T(8,128)(2,1)S(1)}, bf16[1,832,128]{2,1,0:T(8,128)(2,1)S(1)}, u32[]{:S(2)}, u32[]{:S(2)}) collective-permute-start(bf16[1,832,128]{2,1,0:T(8,128)(2,1)S(1)} %maximum_bitcast_fusion.refs_1_), channel_id=1, source_target_pairs={{0,16},{16,0},{1,17},{17,1},{2,18},{18,2},{3,19},{19,3},{4,20},{20... | collective-permute-start | bytes 638984 | tf_op jit(solution)/shard_map/ppermute | solution.py:38
  10.5 31.7 %copy-start.7 = (bf16[2,832,128]{2,1,0:T(8,128)(2,1)}, bf16[2,832,128]{2,1,0:T(8,128)(2,1)S(1)}, u32[]{:S(2)}) copy-start(bf16[2,832,128]{2,1,0:T(8,128)(2,1)S(1)} %pad_maximum_fusion.refs_3_) | copy-start | bytes 1277956
  10.5 19.5 %collective-permute-start.2 = (bf16[2,832,128]{2,1,0:T(8,128)(2,1)S(1)}, bf16[2,832,128]{2,1,0:T(8,128)(2,1)S(1)}, u32[]{:S(2)}, u32[]{:S(2)}) collective-permute-start(bf16[2,832,128]{2,1,0:T(8,128)(2,1)S(1)} %pad_maximum_fusion.refs_3_), channel_id=1, source_target_pairs={{0,224},{32,0},{64,32},{96,64},{128,96},{160,128},{192,160},{224,1... | collective-permute-start | bytes 1277960 | tf_op jit(solution)/shard_map/ppermute | solution.py:38
  17.1 12.8 %collective-permute-start.1 = (bf16[2,832,128]{2,1,0:T(8,128)(2,1)S(1)}, bf16[2,832,128]{2,1,0:T(8,128)(2,1)S(1)}, u32[]{:S(2)}, u32[]{:S(2)}) collective-permute-start(bf16[2,832,128]{2,1,0:T(8,128)(2,1)S(1)} %pad_maximum_fusion.refs_3_), channel_id=1, source_target_pairs={{0,32},{32,64},{64,96},{96,128},{128,160},{160,192},{192,224},{224... | collective-permute-start | bytes 1277960 | tf_op jit(solution)/shard_map/ppermute | solution.py:38
  29.9 34.2 %copy-start.2 = (bf16[2,832,128]{2,1,0:T(8,128)(2,1)}, bf16[2,832,128]{2,1,0:T(8,128)(2,1)S(1)}, u32[]{:S(2)}) copy-start(bf16[2,832,128]{2,1,0:T(8,128)(2,1)S(1)} %get-tuple-element.10.refs_5_) | copy-start | bytes 1277956
  29.9 34.2 %copy-start.3 = (bf16[2,832,128]{2,1,0:T(8,128)(2,1)}, bf16[2,832,128]{2,1,0:T(8,128)(2,1)S(1)}, u32[]{:S(2)}) copy-start(bf16[2,832,128]{2,1,0:T(8,128)(2,1)S(1)} %get-tuple-element.9.refs_4_) | copy-start | bytes 1277956
  30.0 9.4 %collective-permute-start.3 = (bf16[2,832,128]{2,1,0:T(8,128)(2,1)S(1)}, bf16[2,832,128]{2,1,0:T(8,128)(2,1)S(1)}, u32[]{:S(2)}, u32[]{:S(2)}) collective-permute-start(bf16[2,832,128]{2,1,0:T(8,128)(2,1)S(1)} %get-tuple-element.9.refs_4_), channel_id=1, source_target_pairs={{0,32},{32,64},{64,96},{96,128},{128,160},{160,192},{192,224},{224... | collective-permute-start | bytes 1277960 | tf_op jit(solution)/shard_map/ppermute | solution.py:38
  30.0 9.4 %collective-permute-start.4 = (bf16[2,832,128]{2,1,0:T(8,128)(2,1)S(1)}, bf16[2,832,128]{2,1,0:T(8,128)(2,1)S(1)}, u32[]{:S(2)}, u32[]{:S(2)}) collective-permute-start(bf16[2,832,128]{2,1,0:T(8,128)(2,1)S(1)} %get-tuple-element.10.refs_5_), channel_id=1, source_target_pairs={{0,224},{32,0},{64,32},{96,64},{128,96},{160,128},{192,160},{224,1... | collective-permute-start | bytes 1277960 | tf_op jit(solution)/shard_map/ppermute | solution.py:38
  33.5 30.6 %copy-start.1 = (bf16[128,1536]{1,0:T(8,128)(2,1)}, bf16[128,1536]{1,0:T(8,128)(2,1)S(1)}, u32[]{:S(2)}) copy-start(bf16[128,1536]{1,0:T(8,128)(2,1)S(1)} %convolution_convert_fusion.refs_2_) | copy-start | bytes 1179652
  39.4 24.7 %copy-start.4 = (bf16[2,832,128]{2,1,0:T(8,128)(2,1)}, bf16[2,832,128]{2,1,0:T(8,128)(2,1)S(1)}, u32[]{:S(2)}) copy-start(bf16[2,832,128]{2,1,0:T(8,128)(2,1)S(1)} %get-tuple-element.11.refs_6_) | copy-start | bytes 1277956
  39.4 24.7 %copy-start.5 = (bf16[2,832,128]{2,1,0:T(8,128)(2,1)}, bf16[2,832,128]{2,1,0:T(8,128)(2,1)S(1)}, u32[]{:S(2)}) copy-start(bf16[2,832,128]{2,1,0:T(8,128)(2,1)S(1)} %get-tuple-element.12.refs_7_) | copy-start | bytes 1277956
  39.4 8.3 %collective-permute-start.5 = (bf16[2,832,128]{2,1,0:T(8,128)(2,1)S(1)}, bf16[2,832,128]{2,1,0:T(8,128)(2,1)S(1)}, u32[]{:S(2)}, u32[]{:S(2)}) collective-permute-start(bf16[2,832,128]{2,1,0:T(8,128)(2,1)S(1)} %get-tuple-element.11.refs_6_), channel_id=1, source_target_pairs={{0,32},{32,64},{64,96},{96,128},{128,160},{160,192},{192,224},{224... | collective-permute-start | bytes 1277960 | tf_op jit(solution)/shard_map/ppermute | solution.py:38
  39.5 13.5 %collective-permute-start.6 = (bf16[2,832,128]{2,1,0:T(8,128)(2,1)S(1)}, bf16[2,832,128]{2,1,0:T(8,128)(2,1)S(1)}, u32[]{:S(2)}, u32[]{:S(2)}) collective-permute-start(bf16[2,832,128]{2,1,0:T(8,128)(2,1)S(1)} %get-tuple-element.12.refs_7_), channel_id=1, source_target_pairs={{0,224},{32,0},{64,32},{96,64},{128,96},{160,128},{192,160},{224,1... | collective-permute-start | bytes 1277960 | tf_op jit(solution)/shard_map/ppermute | solution.py:38
  42.2 10.9 %collective-permute-start.9 = (bf16[2,832,128]{2,1,0:T(8,128)(2,1)S(1)}, bf16[2,832,128]{2,1,0:T(8,128)(2,1)S(1)}, u32[]{:S(2)}, u32[]{:S(2)}) collective-permute-start(bf16[2,832,128]{2,1,0:T(8,128)(2,1)S(1)} %pad_maximum_fusion.refs_3_), channel_id=1, source_target_pairs={{0,8},{8,0},{1,9},{9,1},{2,10},{10,2},{3,11},{11,3},{4,12},{12,4},... | collective-permute-start | bytes 1277960 | tf_op jit(solution)/shard_map/ppermute | solution.py:38
  46.8 7.0 %collective-permute-start.10 = (bf16[2,832,128]{2,1,0:T(8,128)(2,1)S(1)}, bf16[2,832,128]{2,1,0:T(8,128)(2,1)S(1)}, u32[]{:S(2)}, u32[]{:S(2)}) collective-permute-start(bf16[2,832,128]{2,1,0:T(8,128)(2,1)S(1)} %get-tuple-element.9.refs_4_), channel_id=1, source_target_pairs={{0,8},{8,0},{1,9},{9,1},{2,10},{10,2},{3,11},{11,3},{4,12},{12,4},... | collective-permute-start | bytes 1277960 | tf_op jit(solution)/shard_map/ppermute | solution.py:38
  46.8 9.3 %collective-permute-start.11 = (bf16[2,832,128]{2,1,0:T(8,128)(2,1)S(1)}, bf16[2,832,128]{2,1,0:T(8,128)(2,1)S(1)}, u32[]{:S(2)}, u32[]{:S(2)}) collective-permute-start(bf16[2,832,128]{2,1,0:T(8,128)(2,1)S(1)} %get-tuple-element.10.refs_5_), channel_id=1, source_target_pairs={{0,8},{8,0},{1,9},{9,1},{2,10},{10,2},{3,11},{11,3},{4,12},{12,4},... | collective-permute-start | bytes 1277960 | tf_op jit(solution)/shard_map/ppermute | solution.py:38
  47.7 16.5 %copy-start.8 = (bf16[2,832,128]{2,1,0:T(8,128)(2,1)}, bf16[2,832,128]{2,1,0:T(8,128)(2,1)S(1)}, u32[]{:S(2)}) copy-start(bf16[2,832,128]{2,1,0:T(8,128)(2,1)S(1)} %collective-permute-done.5.refs_8_) | copy-start | bytes 1277956
  47.7 9.3 %collective-permute-start.12 = (bf16[2,832,128]{2,1,0:T(8,128)(2,1)S(1)}, bf16[2,832,128]{2,1,0:T(8,128)(2,1)S(1)}, u32[]{:S(2)}, u32[]{:S(2)}) collective-permute-start(bf16[2,832,128]{2,1,0:T(8,128)(2,1)S(1)} %get-tuple-element.11.refs_6_), channel_id=1, source_target_pairs={{0,8},{8,0},{1,9},{9,1},{2,10},{10,2},{3,11},{11,3},{4,12},{12,4},... | collective-permute-start | bytes 1277960 | tf_op jit(solution)/shard_map/ppermute | solution.py:38
  53.0 11.2 %copy-start.9 = (bf16[2,832,128]{2,1,0:T(8,128)(2,1)}, bf16[2,832,128]{2,1,0:T(8,128)(2,1)S(1)}, u32[]{:S(2)}) copy-start(bf16[2,832,128]{2,1,0:T(8,128)(2,1)S(1)} %collective-permute-done.6.refs_9_) | copy-start | bytes 1277956
  53.0 10.1 %collective-permute-start.13 = (bf16[2,832,128]{2,1,0:T(8,128)(2,1)S(1)}, bf16[2,832,128]{2,1,0:T(8,128)(2,1)}, u32[]{:S(2)}, u32[]{:S(2)}) collective-permute-start(bf16[2,832,128]{2,1,0:T(8,128)(2,1)S(1)} %get-tuple-element.12.refs_7_), channel_id=1, source_target_pairs={{0,8},{8,0},{1,9},{9,1},{2,10},{10,2},{3,11},{11,3},{4,12},{12,4},... | collective-permute-start | bytes 1277960 | tf_op jit(solution)/shard_map/ppermute | solution.py:38
  53.1 9.2 %copy-start.10 = (bf16[2,832,128]{2,1,0:T(8,128)(2,1)}, bf16[2,832,128]{2,1,0:T(8,128)(2,1)S(1)}, u32[]{:S(2)}) copy-start(bf16[2,832,128]{2,1,0:T(8,128)(2,1)S(1)} %collective-permute-done.9.refs_12_) | copy-start | bytes 1277956
  53.1 8.0 %collective-permute-start.7 = (bf16[1,832,128]{2,1,0:T(8,128)(2,1)S(1)}, bf16[1,832,128]{2,1,0:T(8,128)(2,1)}, u32[]{:S(2)}, u32[]{:S(2)}) collective-permute-start(bf16[1,832,128]{2,1,0:T(8,128)(2,1)S(1)} %slice.8), channel_id=1, source_target_pairs={{0,32},{32,64},{64,96},{96,128},{128,160},{160,192},{192,224},{224... | collective-permute-start | bytes 638984 | tf_op jit(solution)/shard_map/ppermute | solution.py:38
  53.8 8.6 %copy-start.11 = (bf16[2,832,128]{2,1,0:T(8,128)(2,1)}, bf16[2,832,128]{2,1,0:T(8,128)(2,1)S(1)}, u32[]{:S(2)}) copy-start(bf16[2,832,128]{2,1,0:T(8,128)(2,1)S(1)} %collective-permute-done.10.refs_13_) | copy-start | bytes 1277956
  53.8 8.5 %collective-permute-start.8 = (bf16[1,832,128]{2,1,0:T(8,128)(2,1)S(1)}, bf16[1,832,128]{2,1,0:T(8,128)(2,1)}, u32[]{:S(2)}, u32[]{:S(2)}) collective-permute-start(bf16[1,832,128]{2,1,0:T(8,128)(2,1)S(1)} %slice.9), channel_id=1, source_target_pairs={{0,224},{32,0},{64,32},{96,64},{128,96},{160,128},{192,160},{224,1... | collective-permute-start | bytes 638984 | tf_op jit(solution)/shard_map/ppermute | solution.py:38
  56.1 6.3 %copy-start.12 = (bf16[2,832,128]{2,1,0:T(8,128)(2,1)}, bf16[2,832,128]{2,1,0:T(8,128)(2,1)S(1)}, u32[]{:S(2)}) copy-start(bf16[2,832,128]{2,1,0:T(8,128)(2,1)S(1)} %collective-permute-done.11.refs_14_) | copy-start | bytes 1277956
  56.1 7.6 %collective-permute-start.14 = (bf16[2,832,128]{2,1,0:T(8,128)(2,1)S(1)}, bf16[2,832,128]{2,1,0:T(8,128)(2,1)S(1)}, u32[]{:S(2)}, u32[]{:S(2)}) collective-permute-start(bf16[2,832,128]{2,1,0:T(8,128)(2,1)S(1)} %collective-permute-done.5.refs_8_), channel_id=1, source_target_pairs={{0,8},{8,0},{1,9},{9,1},{2,10},{10,2},{3,11},{11,3},{4,12},{12,4},... | collective-permute-start | bytes 1277960 | tf_op jit(solution)/shard_map/ppermute | solution.py:38
  56.9 5.5 %copy-start.13 = (bf16[2,832,128]{2,1,0:T(8,128)(2,1)}, bf16[2,832,128]{2,1,0:T(8,128)(2,1)S(1)}, u32[]{:S(2)}) copy-start(bf16[2,832,128]{2,1,0:T(8,128)(2,1)S(1)} %collective-permute-done.12.refs_15_) | copy-start | bytes 1277956
  56.9 7.2 %collective-permute-start.15 = (bf16[2,832,128]{2,1,0:T(8,128)(2,1)S(1)}, bf16[2,832,128]{2,1,0:T(8,128)(2,1)}, u32[]{:S(2)}, u32[]{:S(2)}) collective-permute-start(bf16[2,832,128]{2,1,0:T(8,128)(2,1)S(1)} %collective-permute-done.6.refs_9_), channel_id=1, source_target_pairs={{0,8},{8,0},{1,9},{9,1},{2,10},{10,2},{3,11},{11,3},{4,12},{12,4},... | collective-permute-start | bytes 1277960 | tf_op jit(solution)/shard_map/ppermute | solution.py:38
  61.1 2.7 %collective-permute-start.16 = (bf16[1,832,128]{2,1,0:T(8,128)(2,1)}, bf16[1,832,128]{2,1,0:T(8,128)(2,1)}, u32[]{:S(2)}, u32[]{:S(2)}) collective-permute-start(bf16[1,832,128]{2,1,0:T(8,128)(2,1)} %collective-permute-done.7.refs_10_), channel_id=1, source_target_pairs={{0,8},{8,0},{1,9},{9,1},{2,10},{10,2},{3,11},{11,3},{4,12},{12,4},... | collective-permute-start | bytes 638984 | tf_op jit(solution)/shard_map/ppermute | solution.py:38
  62.3 1.8 %collective-permute-start.17 = (bf16[1,832,128]{2,1,0:T(8,128)(2,1)}, bf16[1,832,128]{2,1,0:T(8,128)(2,1)}, u32[]{:S(2)}, u32[]{:S(2)}) collective-permute-start(bf16[1,832,128]{2,1,0:T(8,128)(2,1)} %collective-permute-done.8.refs_11_), channel_id=1, source_target_pairs={{0,8},{8,0},{1,9},{9,1},{2,10},{10,2},{3,11},{11,3},{4,12},{12,4},... | collective-permute-start | bytes 638984 | tf_op jit(solution)/shard_map/ppermute | solution.py:38
  63.7 0.8 copy-start.14

commit v6 on v5

--- a/solution.py
+++ b/solution.py
@@ -200,11 +200,16 @@
     ctx = lax.axis_index(("z", "xh", "core"))
     idx = jnp.stack([lax.axis_index("z"), lax.axis_index("xh"), lax.axis_index("core"), 2 * ctx])
 
-    shard = jnp.concatenate([latent.T, by_head(w_uk), by_head(w_uv)], axis=0)[None]
-    here = jnp.concatenate([shard, shift(shard, "xh", 1)], axis=0)
+    own = latent.T
+    across = lax.ppermute(own, ("xh", "xl"), [(0, 3), (3, 0), (1, 2), (2, 1)])
+    weights = jnp.concatenate([by_head(w_uk), by_head(w_uv)], axis=0)
+    weights_x = shift(weights, "xh", 1)
+    here = jnp.stack(
+        [jnp.concatenate([own, weights], axis=0), jnp.concatenate([across, weights_x], axis=0)]
+    )
 
     copies = jnp.broadcast_to(compressed.T[None], (ys * xls,) + compressed.T.shape)
-    (copies,) = gate([copies], shard)
+    (copies,) = gate([copies], weights)
     features = lax.all_to_all(copies, ("y", "xl"), 0, 0, tiled=True).reshape(-1, toks)
     query = lax.dot_general(
         features, w_uq, (((0,), (0,)), ((), ())), preferred_element_type=jnp.float32
@@ -216,8 +221,6 @@
     for k in range(1, zs // 2):
         ahead, behind = shift(ahead, "z", 1), shift(behind, "z", -1)
         if k == 1:
-            ahead, behind = gate([ahead, behind], features)
-        if k == 2:
             ahead, behind = gate([ahead, behind], query)
         pieces += [(-k, both, ahead), (k, both, behind)]
     pieces += [

time: 80.6 us -> 79.8 us (0.990)
  blocking collectives: 12 us -> 0 us
  waiting for transfers between devices: 15.2 us -> 22 us
  starting transfers between devices: 31.5 us -> 33.9 us
  matrix products: 0.81 us -> 3.14 us
    all_to_all x1 -> x0, blocking collectives: 12 us -> none  [per_device(): lax.all_to_all(copies, ('y', 'xl'), 0, 0, tiled=True).reshape(-1, toks)]
    ppermute x18, waiting for transfers between devices: 15.2 us -> 21.2 us  [shift(): return lax.ppermute(x, axis, [(i, (i + by) % n) for i in range(n)])]
    ppermute x18, starting transfers between devices: 31.5 us -> 26.3 us  [shift(): return lax.ppermute(x, axis, [(i, (i + by) % n) for i in range(n)])]
    all_to_all x0 -> x1, starting transfers between devices: none -> 4.22 us  [per_device(): lax.all_to_all(copies, ('y', 'xl'), 0, 0, tiled=True).reshape(-1, toks)]
    ppermute x0 -> x1, starting transfers between devices: none -> 3.31 us  [per_device(): across = lax.ppermute(own, ('xh', 'xl'), [(0, 3), (3, 0), (1, 2), (2, 1)])]
    dot_general x1, matrix products: 0.81 us -> 3.14 us  [per_device(): lax.dot_general(features, w_uq, (((0,), (0,)), ((), ())), preferred_eleme...]
    unnamed x30 -> x26, local copies, waits for them, and re-layouts: 1.15 us -> 0.05 us
    another operation x0 -> x3, other arithmetic: none -> 0.98 us  [per_device(): jnp.stack([jnp.concatenate([own, weights], axis=0), jnp.concatenate([acro...]
  transfers between devices with their start and end apart: 18 -> 20, of which waited for: 6 -> 8; matrix products, arithmetic and copies ran while one was open for 3% -> 9% of each run, Pallas kernels for 0% -> 0%
where the time goes in v6:
time: 79.8 us; the launch traced here: 79.6 us
  starting transfers between devices  33.9 us (42%)
  waiting for transfers between devices  22 us (28%)
  Pallas kernels  16 us (20%)
  matrix products  3.14 us (4%)
  local copies, waits for them, and re-layouts  2.45 us (3%)
  other arithmetic  1.64 us (2%)
    ppermute x18, starting transfers between devices, shift(): return lax.ppermute(x, axis, [(i, (i + by) % n) for i in range(n)])  26.3 us
    ppermute x18, waiting for transfers between devices, shift(): return lax.ppermute(x, axis, [(i, (i + by) % n) for i in range(n)])  21.2 us
    pallas_call x1, Pallas kernels, attention(): pl.pallas_call(functools.partial(attention_kernel, layout, heads, min(row...  16 us
    all_to_all x1, starting transfers between devices, per_device(): lax.all_to_all(copies, ('y', 'xl'), 0, 0, tiled=True).reshape(-1, toks)  4.22 us
    ppermute x1, starting transfers between devices, per_device(): across = lax.ppermute(own, ('xh', 'xl'), [(0, 3), (3, 0), (1, 2), (2, 1)])  3.31 us
    dot_general x1, matrix products, per_device(): lax.dot_general(features, w_uq, (((0,), (0,)), ((), ())), preferred_eleme...  3.14 us
    broadcast_in_dim x1, local copies, waits for them, and re-layouts, per_device(): jnp.broadcast_to(compressed.T[None], (ys * xls,) + compressed.T.shape)  1.6 us
  transfers between devices with their start and end apart: 20, of which 8 were waited for; matrix products, arithmetic and copies ran while one was open for 9% of the time, Pallas kernels for 0%

profile of v6, /device:TPU:1, one launch (start us, length us, event | category | flops | bytes accessed | tf_op | source)
XLA Modules:
  0.0 79.6 jit_solution(14114286719368984338)
XLA Ops:
  0.0 0.0 copy-start
  0.0 3.3 %collective-permute-start = (bf16[576,128]{1,0:T(8,128)(2,1)}, bf16[576,128]{1,0:T(8,128)(2,1)S(1)}, u32[]{:S(2)}, u32[]{:S(2)}) collective-permute-start(bf16[576,128]{1,0:T(8,128)(2,1)} %bitcast.34), channel_id=1, source_target_pairs={{0,17},{17,0},{1,16},{16,1},{2,19},{19,2},{3,18},{18,3},{4,21},{21... | collective-permute-start | bytes 442376 | tf_op jit(solution)/shard_map/ppermute | solution.py:204
  3.3 0.0 copy-done
  3.3 0.8 copy_bitcast_fusion
  4.1 1.1 %collective-permute-start.1 = (bf16[256,128]{1,0:T(8,128)(2,1)S(1)}, bf16[256,128]{1,0:T(8,128)(2,1)S(1)}, u32[]{:S(2)}, u32[]{:S(2)}) collective-permute-start(bf16[256,128]{1,0:T(8,128)(2,1)S(1)} %pad_maximum_fusion.1.refs_1_), channel_id=1, source_target_pairs={{0,16},{16,0},{1,17},{17,1},{2,18},{18,2},{3,19},{19,3},{4,20},{20... | collective-permute-start | bytes 196616 | tf_op jit(solution)/shard_map/ppermute | solution.py:38
  5.2 1.6 %broadcast_in_dim.2.refs_0_ = bf16[8,192,128]{2,1,0:T(8,128)(2,1)} broadcast(bf16[192,128]{1,0:T(8,128)(2,1)} %bitcast.36), dimensions={1,2} | broadcast | bytes 442368 | tf_op jit(solution)/shard_map/broadcast_in_dim | solution.py:211
  6.8 4.2 %all-to-all-start = ((bf16[8,192,128]{2,1,0:T(8,128)(2,1)}), bf16[8,192,128]{2,1,0:T(8,128)(2,1)S(1)}, u32[]{:S(2)}, u32[]{:S(2)}) async-start(bf16[8,192,128]{2,1,0:T(8,128)(2,1)} %shard_map.64), calls=%async_computation | async-start | bytes 786432 | tf_op jit(solution)/shard_map/all_to_all | solution.py:213
  11.0 0.9 %maximum_bitcast_fusion = bf16[1,832,128]{2,1,0:T(8,128)(2,1)S(1)} fusion(bf16[128,128]{1,0:T(8,128)(2,1)S(1)} %bitcast.33, bf16[128,128]{1,0:T(8,128)(2,1)S(1)} %bitcast.31, bf16[576,128]{1,0:T(8,128)(2,1)} %bitcast.35), kind=kLoop, calls=%fused_computation.2 | loop fusion | flops 638976 | bytes 425984 | tf_op jit(solution)/shard_map/stack | solution.py:207
  11.9 0.0 collective-permute-done.1
  12.0 0.0 collective-permute-done
  12.0 0.0 copy-start.4
  12.1 5.7 %collective-permute-start.3 = (bf16[2,832,128]{2,1,0:T(8,128)(2,1)S(1)}, bf16[2,832,128]{2,1,0:T(8,128)(2,1)S(1)}, u32[]{:S(2)}, u32[]{:S(2)}) collective-permute-start(bf16[2,832,128]{2,1,0:T(8,128)(2,1)S(1)} %pad_maximum_fusion.refs_3_), channel_id=1, source_target_pairs={{0,224},{32,0},{64,32},{96,64},{128,96},{160,128},{192,160},{224,1... | collective-permute-start | bytes 1277960 | tf_op jit(solution)/shard_map/ppermute | solution.py:38
  17.7 0.0 collective-permute-start.2
  17.7 0.8 all-to-all-done
  18.5 3.1 %convolution_convert_fusion.refs_2_ = bf16[128,1536]{1,0:T(8,128)(2,1)S(1)} fusion(bf16[1536,128]{1,0:T(8,128)(2,1)S(1)} %bitcast.29, bf16[1536,1536]{1,0:T(8,128)(2,1)} %param.8), kind=kOutput, calls=%fused_computation | convolution fusion | flops 604176384 | bytes 5505024 | tf_op jit(solution)/shard_map/dot_general | solution.py:214
  21.6 0.0 copy-start.1
  21.7 3.9 %collective-permute-done.3.refs_1_ = bf16[2,832,128]{2,1,0:T(8,128)(2,1)S(1)} collective-permute-done((bf16[2,832,128]{2,1,0:T(8,128)(2,1)S(1)}, bf16[2,832,128]{2,1,0:T(8,128)(2,1)S(1)}, u32[]{:S(2)}, u32[]{:S(2)}) %collective-permute-start.3) | collective-permute-done | bytes 426016 | tf_op jit(solution)/shard_map/ppermute | solution.py:38
  25.6 3.1 %collective-permute-done.2.refs_0_ = bf16[2,832,128]{2,1,0:T(8,128)(2,1)S(1)} collective-permute-done((bf16[2,832,128]{2,1,0:T(8,128)(2,1)S(1)}, bf16[2,832,128]{2,1,0:T(8,128)(2,1)S(1)}, u32[]{:S(2)}, u32[]{:S(2)}) %collective-permute-start.2) | collective-permute-done | bytes 426016 | tf_op jit(solution)/shard_map/ppermute | solution.py:38
  28.7 0.0 collective-permute-start.4
  28.7 2.7 %collective-permute-start.5 = (bf16[2,832,128]{2,1,0:T(8,128)(2,1)S(1)}, bf16[2,832,128]{2,1,0:T(8,128)(2,1)}, u32[]{:S(2)}, u32[]{:S(2)}) collective-permute-start(bf16[2,832,128]{2,1,0:T(8,128)(2,1)S(1)} %get-tuple-element.8.refs_5_), channel_id=1, source_target_pairs={{0,224},{32,0},{64,32},{96,64},{128,96},{160,128},{192,160},{224,1... | collective-permute-start | bytes 1277960 | tf_op jit(solution)/shard_map/ppermute | solution.py:38
  31.4 7.4 %collective-permute-done.4.refs_6_ = bf16[2,832,128]{2,1,0:T(8,128)(2,1)S(1)} collective-permute-done((bf16[2,832,128]{2,1,0:T(8,128)(2,1)S(1)}, bf16[2,832,128]{2,1,0:T(8,128)(2,1)S(1)}, u32[]{:S(2)}, u32[]{:S(2)}) %collective-permute-start.4) | collective-permute-done | bytes 426016 | tf_op jit(solution)/shard_map/ppermute | solution.py:38
  38.8 0.0 collective-permute-start.6
  38.8 0.0 collective-permute-done.5.refs_7_
  38.8 2.7 %collective-permute-start.7 = (bf16[2,832,128]{2,1,0:T(8,128)(2,1)}, bf16[2,832,128]{2,1,0:T(8,128)(2,1)S(1)}, u32[]{:S(2)}, u32[]{:S(2)}) collective-permute-start(bf16[2,832,128]{2,1,0:T(8,128)(2,1)} %collective-permute-done.5.refs_7_), channel_id=1, source_target_pairs={{0,224},{32,0},{64,32},{96,64},{128,96},{160,128},{192,160},{224,1... | collective-permute-start | bytes 1277960 | tf_op jit(solution)/shard_map/ppermute | solution.py:38
  41.5 3.9 %collective-permute-start.10 = (bf16[2,832,128]{2,1,0:T(8,128)(2,1)S(1)}, bf16[2,832,128]{2,1,0:T(8,128)(2,1)S(1)}, u32[]{:S(2)}, u32[]{:S(2)}) collective-permute-start(bf16[2,832,128]{2,1,0:T(8,128)(2,1)S(1)} %pad_maximum_fusion.refs_3_), channel_id=1, source_target_pairs={{0,8},{8,0},{1,9},{9,1},{2,10},{10,2},{3,11},{11,3},{4,12},{12,4},... | collective-permute-start | bytes 1277960 | tf_op jit(solution)/shard_map/ppermute | solution.py:38
  45.4 0.0 collective-permute-start.11
  45.4 0.5 collective-permute-start.12
  45.9 2.0 %collective-permute-done.6.refs_8_ = bf16[2,832,128]{2,1,0:T(8,128)(2,1)S(1)} collective-permute-done((bf16[2,832,128]{2,1,0:T(8,128)(2,1)S(1)}, bf16[2,832,128]{2,1,0:T(8,128)(2,1)S(1)}, u32[]{:S(2)}, u32[]{:S(2)}) %collective-permute-start.6) | collective-permute-done | bytes 426016 | tf_op jit(solution)/shard_map/ppermute | solution.py:38
  48.0 4.3 %collective-permute-start.13 = (bf16[2,832,128]{2,1,0:T(8,128)(2,1)S(1)}, bf16[2,832,128]{2,1,0:T(8,128)(2,1)S(1)}, u32[]{:S(2)}, u32[]{:S(2)}) collective-permute-start(bf16[2,832,128]{2,1,0:T(8,128)(2,1)S(1)} %collective-permute-done.4.refs_6_), channel_id=1, source_target_pairs={{0,8},{8,0},{1,9},{9,1},{2,10},{10,2},{3,11},{11,3},{4,12},{12,4},... | collective-permute-start | bytes 1277960 | tf_op jit(solution)/shard_map/ppermute | solution.py:38
  52.3 0.0 collective-permute-done.7.refs_9_
  52.3 0.0 copy-start.6
  52.3 0.1 collective-permute-start.14
  52.4 0.0 collective-permute-done.10.refs_12_
  52.4 0.0 copy-start.8
  52.4 0.1 collective-permute-start.8
  52.5 0.0 collective-permute-done.11.refs_13_
  52.5 0.0 copy-start.9
  52.5 2.8 %collective-permute-start.9 = (bf16[1,832,128]{2,1,0:T(8,128)(2,1)S(1)}, bf16[1,832,128]{2,1,0:T(8,128)(2,1)}, u32[]{:S(2)}, u32[]{:S(2)}) collective-permute-start(bf16[1,832,128]{2,1,0:T(8,128)(2,1)S(1)} %slice.9), channel_id=1, source_target_pairs={{0,224},{32,0},{64,32},{96,64},{128,96},{160,128},{192,160},{224,1... | collective-permute-start | bytes 638984 | tf_op jit(solution)/shard_map/ppermute | solution.py:38
  55.4 0.0 collective-permute-done.12.refs_14_
  55.4 0.9 %collective-permute-start.15 = (bf16[2,832,128]{2,1,0:T(8,128)(2,1)S(1)}, bf16[2,832,128]{2,1,0:T(8,128)(2,1)}, u32[]{:S(2)}, u32[]{:S(2)}) collective-permute-start(bf16[2,832,128]{2,1,0:T(8,128)(2,1)S(1)} %collective-permute-done.6.refs_8_), channel_id=1, source_target_pairs={{0,8},{8,0},{1,9},{9,1},{2,10},{10,2},{3,11},{11,3},{4,12},{12,4},... | collective-permute-start | bytes 1277960 | tf_op jit(solution)/shard_map/ppermute | solution.py:38
  56.2 0.0 collective-permute-done.13.refs_15_
  56.2 0.3 collective-permute-start.16
  56.5 3.7 %collective-permute-done.8.refs_10_ = bf16[1,832,128]{2,1,0:T(8,128)(2,1)S(1)} collective-permute-done((bf16[1,832,128]{2,1,0:T(8,128)(2,1)S(1)}, bf16[1,832,128]{2,1,0:T(8,128)(2,1)S(1)}, u32[]{:S(2)}, u32[]{:S(2)}) %collective-permute-start.8) | collective-permute-done | bytes 213024 | tf_op jit(solution)/shard_map/ppermute | solution.py:38
  60.2 1.3 %collective-permute-start.17 = (bf16[1,832,128]{2,1,0:T(8,128)(2,1)S(1)}, bf16[1,832,128]{2,1,0:T(8,128)(2,1)}, u32[]{:S(2)}, u32[]{:S(2)}) collective-permute-start(bf16[1,832,128]{2,1,0:T(8,128)(2,1)S(1)} %collective-permute-done.8.refs_10_), channel_id=1, source_target_pairs={{0,8},{8,0},{1,9},{9,1},{2,10},{10,2},{3,11},{11,3},{4,12},{12,4},... | collective-permute-start | bytes 638984 | tf_op jit(solution)/shard_map/ppermute | solution.py:38
  61.5 0.0 collective-permute-done.9.refs_11_
  61.5 0.0 copy-done.8
  61.5 0.1 collective-permute-start.18
  61.6 0.0 copy-done.9
  61.6 0.0 copy-done.10
  61.6 0.0 copy-done.11
  61.6 0.7 pad_add_fusion.refs_0_
  62.2 0.0 collective-permute-done.14.refs_16_
  62.2 0.5 collective-permute-done.17.refs_19_
  62.7 0.6 collective-permute-done.18.refs_20_
  63.3 0.0 collective-permute-done.15.refs_17_
  63.3 0.0 collective-permute-done.16.refs_18_
  63.3 0.0 copy-done.4
  63.3 0.0 copy-done.1
  63.3 0.0 copy-done.2
  63.3 0.0 copy-done.3
  63.3 0.0 copy-done.7
  63.3 0.0 copy-done.5
  63.3 0.0 copy-done.6
  63.4 16.0 %shard_map.66 = bf16[128,1024]{1,0:T(8,128)(2,1)} custom-call(s32[4]{0:T(128)} %pad_add_fusion.refs_0_, s32[64]{0:T(128)} %refs_1_.1, bf16[128,1536]{1,0:T(8,128)(2,1)} %copy-done.1, bf16[2,832,128]{2,1,0:T(8,128)(2,1)} %copy-done.4, bf16[2,832,128]{2,1,0:T(8,128)(2,1)} %copy-done.3, bf16[2,832,128]{2,1,0:T(8,128)(2,1)} %copy-done.2, ...), custom_call_target="tpu_custom_call" | custom-call | flops 5704253440 | bytes 7209232 | tf_op jit(solution)/shard_map/pallas_call | solution.py:172
  (16 shorter events, 0.1 us)
Async XLA Ops:
  0.0 3.3 %copy-start = (bf16[16,1024]{1,0:T(8,128)(2,1)S(1)}, bf16[16,1024]{1,0:T(8,128)(2,1)}, u32[]{:S(2)}) copy-start(bf16[16,1024]{1,0:T(8,128)(2,1)} %param.9) | copy-start | bytes 98308
  0.0 12.0 %collective-permute-start = (bf16[576,128]{1,0:T(8,128)(2,1)}, bf16[576,128]{1,0:T(8,128)(2,1)S(1)}, u32[]{:S(2)}, u32[]{:S(2)}) collective-permute-start(bf16[576,128]{1,0:T(8,128)(2,1)} %bitcast.34), channel_id=1, source_target_pairs={{0,17},{17,0},{1,16},{16,1},{2,19},{19,2},{3,18},{18,3},{4,21},{21... | collective-permute-start | bytes 442376 | tf_op jit(solution)/shard_map/ppermute | solution.py:204
  4.1 7.8 %collective-permute-start.1 = (bf16[256,128]{1,0:T(8,128)(2,1)S(1)}, bf16[256,128]{1,0:T(8,128)(2,1)S(1)}, u32[]{:S(2)}, u32[]{:S(2)}) collective-permute-start(bf16[256,128]{1,0:T(8,128)(2,1)S(1)} %pad_maximum_fusion.1.refs_1_), channel_id=1, source_target_pairs={{0,16},{16,0},{1,17},{17,1},{2,18},{18,2},{3,19},{19,3},{4,20},{20... | collective-permute-start | bytes 196616 | tf_op jit(solution)/shard_map/ppermute | solution.py:38
  6.8 11.7 %all-to-all-start = ((bf16[8,192,128]{2,1,0:T(8,128)(2,1)}), bf16[8,192,128]{2,1,0:T(8,128)(2,1)S(1)}, u32[]{:S(2)}, u32[]{:S(2)}) async-start(bf16[8,192,128]{2,1,0:T(8,128)(2,1)} %shard_map.64), calls=%async_computation | async-start | bytes 786432 | tf_op jit(solution)/shard_map/all_to_all | solution.py:213
  12.0 51.2 %copy-start.4 = (bf16[2,832,128]{2,1,0:T(8,128)(2,1)}, bf16[2,832,128]{2,1,0:T(8,128)(2,1)S(1)}, u32[]{:S(2)}) copy-start(bf16[2,832,128]{2,1,0:T(8,128)(2,1)S(1)} %pad_maximum_fusion.refs_3_) | copy-start | bytes 1277956
  12.1 13.5 %collective-permute-start.3 = (bf16[2,832,128]{2,1,0:T(8,128)(2,1)S(1)}, bf16[2,832,128]{2,1,0:T(8,128)(2,1)S(1)}, u32[]{:S(2)}, u32[]{:S(2)}) collective-permute-start(bf16[2,832,128]{2,1,0:T(8,128)(2,1)S(1)} %pad_maximum_fusion.refs_3_), channel_id=1, source_target_pairs={{0,224},{32,0},{64,32},{96,64},{128,96},{160,128},{192,160},{224,1... | collective-permute-start | bytes 1277960 | tf_op jit(solution)/shard_map/ppermute | solution.py:38
  17.7 11.0 %collective-permute-start.2 = (bf16[2,832,128]{2,1,0:T(8,128)(2,1)S(1)}, bf16[2,832,128]{2,1,0:T(8,128)(2,1)S(1)}, u32[]{:S(2)}, u32[]{:S(2)}) collective-permute-start(bf16[2,832,128]{2,1,0:T(8,128)(2,1)S(1)} %pad_maximum_fusion.refs_3_), channel_id=1, source_target_pairs={{0,32},{32,64},{64,96},{96,128},{128,160},{160,192},{192,224},{224... | collective-permute-start | bytes 1277960 | tf_op jit(solution)/shard_map/ppermute | solution.py:38
  21.6 41.6 %copy-start.1 = (bf16[128,1536]{1,0:T(8,128)(2,1)}, bf16[128,1536]{1,0:T(8,128)(2,1)S(1)}, u32[]{:S(2)}) copy-start(bf16[128,1536]{1,0:T(8,128)(2,1)S(1)} %convolution_convert_fusion.refs_2_) | copy-start | bytes 1179652
  28.7 34.6 %copy-start.2 = (bf16[2,832,128]{2,1,0:T(8,128)(2,1)}, bf16[2,832,128]{2,1,0:T(8,128)(2,1)S(1)}, u32[]{:S(2)}) copy-start(bf16[2,832,128]{2,1,0:T(8,128)(2,1)S(1)} %get-tuple-element.8.refs_5_) | copy-start | bytes 1277956
  28.7 34.6 %copy-start.3 = (bf16[2,832,128]{2,1,0:T(8,128)(2,1)}, bf16[2,832,128]{2,1,0:T(8,128)(2,1)S(1)}, u32[]{:S(2)}) copy-start(bf16[2,832,128]{2,1,0:T(8,128)(2,1)S(1)} %get-tuple-element.7.refs_4_) | copy-start | bytes 1277956
  28.7 10.1 %collective-permute-start.4 = (bf16[2,832,128]{2,1,0:T(8,128)(2,1)S(1)}, bf16[2,832,128]{2,1,0:T(8,128)(2,1)S(1)}, u32[]{:S(2)}, u32[]{:S(2)}) collective-permute-start(bf16[2,832,128]{2,1,0:T(8,128)(2,1)S(1)} %get-tuple-element.7.refs_4_), channel_id=1, source_target_pairs={{0,32},{32,64},{64,96},{96,128},{128,160},{160,192},{192,224},{224... | collective-permute-start | bytes 1277960 | tf_op jit(solution)/shard_map/ppermute | solution.py:38
  28.7 10.1 %collective-permute-start.5 = (bf16[2,832,128]{2,1,0:T(8,128)(2,1)S(1)}, bf16[2,832,128]{2,1,0:T(8,128)(2,1)}, u32[]{:S(2)}, u32[]{:S(2)}) collective-permute-start(bf16[2,832,128]{2,1,0:T(8,128)(2,1)S(1)} %get-tuple-element.8.refs_5_), channel_id=1, source_target_pairs={{0,224},{32,0},{64,32},{96,64},{128,96},{160,128},{192,160},{224,1... | collective-permute-start | bytes 1277960 | tf_op jit(solution)/shard_map/ppermute | solution.py:38
  38.8 24.5 %copy-start.7 = (bf16[2,832,128]{2,1,0:T(8,128)(2,1)}, bf16[2,832,128]{2,1,0:T(8,128)(2,1)S(1)}, u32[]{:S(2)}) copy-start(bf16[2,832,128]{2,1,0:T(8,128)(2,1)S(1)} %collective-permute-done.4.refs_6_) | copy-start | bytes 1277956
  38.8 9.2 %collective-permute-start.6 = (bf16[2,832,128]{2,1,0:T(8,128)(2,1)S(1)}, bf16[2,832,128]{2,1,0:T(8,128)(2,1)S(1)}, u32[]{:S(2)}, u32[]{:S(2)}) collective-permute-start(bf16[2,832,128]{2,1,0:T(8,128)(2,1)S(1)} %collective-permute-done.4.refs_6_), channel_id=1, source_target_pairs={{0,32},{32,64},{64,96},{96,128},{128,160},{160,192},{192,224},{224... | collective-permute-start | bytes 1277960 | tf_op jit(solution)/shard_map/ppermute | solution.py:38
  38.8 13.5 %collective-permute-start.7 = (bf16[2,832,128]{2,1,0:T(8,128)(2,1)}, bf16[2,832,128]{2,1,0:T(8,128)(2,1)S(1)}, u32[]{:S(2)}, u32[]{:S(2)}) collective-permute-start(bf16[2,832,128]{2,1,0:T(8,128)(2,1)} %collective-permute-done.5.refs_7_), channel_id=1, source_target_pairs={{0,224},{32,0},{64,32},{96,64},{128,96},{160,128},{192,160},{224,1... | collective-permute-start | bytes 1277960 | tf_op jit(solution)/shard_map/ppermute | solution.py:38
  41.5 10.9 %collective-permute-start.10 = (bf16[2,832,128]{2,1,0:T(8,128)(2,1)S(1)}, bf16[2,832,128]{2,1,0:T(8,128)(2,1)S(1)}, u32[]{:S(2)}, u32[]{:S(2)}) collective-permute-start(bf16[2,832,128]{2,1,0:T(8,128)(2,1)S(1)} %pad_maximum_fusion.refs_3_), channel_id=1, source_target_pairs={{0,8},{8,0},{1,9},{9,1},{2,10},{10,2},{3,11},{11,3},{4,12},{12,4},... | collective-permute-start | bytes 1277960 | tf_op jit(solution)/shard_map/ppermute | solution.py:38
  45.4 7.1 %collective-permute-start.11 = (bf16[2,832,128]{2,1,0:T(8,128)(2,1)S(1)}, bf16[2,832,128]{2,1,0:T(8,128)(2,1)S(1)}, u32[]{:S(2)}, u32[]{:S(2)}) collective-permute-start(bf16[2,832,128]{2,1,0:T(8,128)(2,1)S(1)} %get-tuple-element.7.refs_4_), channel_id=1, source_target_pairs={{0,8},{8,0},{1,9},{9,1},{2,10},{10,2},{3,11},{11,3},{4,12},{12,4},... | collective-permute-start | bytes 1277960 | tf_op jit(solution)/shard_map/ppermute | solution.py:38
  45.4 10.0 %collective-permute-start.12 = (bf16[2,832,128]{2,1,0:T(8,128)(2,1)S(1)}, bf16[2,832,128]{2,1,0:T(8,128)(2,1)S(1)}, u32[]{:S(2)}, u32[]{:S(2)}) collective-permute-start(bf16[2,832,128]{2,1,0:T(8,128)(2,1)S(1)} %get-tuple-element.8.refs_5_), channel_id=1, source_target_pairs={{0,8},{8,0},{1,9},{9,1},{2,10},{10,2},{3,11},{11,3},{4,12},{12,4},... | collective-permute-start | bytes 1277960 | tf_op jit(solution)/shard_map/ppermute | solution.py:38
  48.0 15.4 %copy-start.5 = (bf16[2,832,128]{2,1,0:T(8,128)(2,1)}, bf16[2,832,128]{2,1,0:T(8,128)(2,1)S(1)}, u32[]{:S(2)}) copy-start(bf16[2,832,128]{2,1,0:T(8,128)(2,1)S(1)} %collective-permute-done.6.refs_8_) | copy-start | bytes 1277956
  48.0 8.3 %collective-permute-start.13 = (bf16[2,832,128]{2,1,0:T(8,128)(2,1)S(1)}, bf16[2,832,128]{2,1,0:T(8,128)(2,1)S(1)}, u32[]{:S(2)}, u32[]{:S(2)}) collective-permute-start(bf16[2,832,128]{2,1,0:T(8,128)(2,1)S(1)} %collective-permute-done.4.refs_6_), channel_id=1, source_target_pairs={{0,8},{8,0},{1,9},{9,1},{2,10},{10,2},{3,11},{11,3},{4,12},{12,4},... | collective-permute-start | bytes 1277960 | tf_op jit(solution)/shard_map/ppermute | solution.py:38
  52.3 11.1 %copy-start.6 = (bf16[2,832,128]{2,1,0:T(8,128)(2,1)}, bf16[2,832,128]{2,1,0:T(8,128)(2,1)S(1)}, u32[]{:S(2)}) copy-start(bf16[2,832,128]{2,1,0:T(8,128)(2,1)S(1)} %collective-permute-done.7.refs_9_) | copy-start | bytes 1277956
  52.3 9.9 %collective-permute-start.14 = (bf16[2,832,128]{2,1,0:T(8,128)(2,1)}, bf16[2,832,128]{2,1,0:T(8,128)(2,1)}, u32[]{:S(2)}, u32[]{:S(2)}) collective-permute-start(bf16[2,832,128]{2,1,0:T(8,128)(2,1)} %collective-permute-done.5.refs_7_), channel_id=1, source_target_pairs={{0,8},{8,0},{1,9},{9,1},{2,10},{10,2},{3,11},{11,3},{4,12},{12,4},... | collective-permute-start | bytes 1277960 | tf_op jit(solution)/shard_map/ppermute | solution.py:38
  52.4 9.0 %copy-start.8 = (bf16[2,832,128]{2,1,0:T(8,128)(2,1)}, bf16[2,832,128]{2,1,0:T(8,128)(2,1)S(1)}, u32[]{:S(2)}) copy-start(bf16[2,832,128]{2,1,0:T(8,128)(2,1)S(1)} %collective-permute-done.10.refs_12_) | copy-start | bytes 1277956
  52.4 7.8 %collective-permute-start.8 = (bf16[1,832,128]{2,1,0:T(8,128)(2,1)S(1)}, bf16[1,832,128]{2,1,0:T(8,128)(2,1)S(1)}, u32[]{:S(2)}, u32[]{:S(2)}) collective-permute-start(bf16[1,832,128]{2,1,0:T(8,128)(2,1)S(1)} %slice.8), channel_id=1, source_target_pairs={{0,32},{32,64},{64,96},{96,128},{128,160},{160,192},{192,224},{224... | collective-permute-start | bytes 638984 | tf_op jit(solution)/shard_map/ppermute | solution.py:38
  52.5 9.0 %copy-start.9 = (bf16[2,832,128]{2,1,0:T(8,128)(2,1)}, bf16[2,832,128]{2,1,0:T(8,128)(2,1)S(1)}, u32[]{:S(2)}) copy-start(bf16[2,832,128]{2,1,0:T(8,128)(2,1)S(1)} %collective-permute-done.11.refs_13_) | copy-start | bytes 1277956
  52.5 8.9 %collective-permute-start.9 = (bf16[1,832,128]{2,1,0:T(8,128)(2,1)S(1)}, bf16[1,832,128]{2,1,0:T(8,128)(2,1)}, u32[]{:S(2)}, u32[]{:S(2)}) collective-permute-start(bf16[1,832,128]{2,1,0:T(8,128)(2,1)S(1)} %slice.9), channel_id=1, source_target_pairs={{0,224},{32,0},{64,32},{96,64},{128,96},{160,128},{192,160},{224,1... | collective-permute-start | bytes 638984 | tf_op jit(solution)/shard_map/ppermute | solution.py:38
  55.4 6.2 %copy-start.10 = (bf16[2,832,128]{2,1,0:T(8,128)(2,1)}, bf16[2,832,128]{2,1,0:T(8,128)(2,1)S(1)}, u32[]{:S(2)}) copy-start(bf16[2,832,128]{2,1,0:T(8,128)(2,1)S(1)} %collective-permute-done.12.refs_14_) | copy-start | bytes 1277956
  55.4 7.9 %collective-permute-start.15 = (bf16[2,832,128]{2,1,0:T(8,128)(2,1)S(1)}, bf16[2,832,128]{2,1,0:T(8,128)(2,1)}, u32[]{:S(2)}, u32[]{:S(2)}) collective-permute-start(bf16[2,832,128]{2,1,0:T(8,128)(2,1)S(1)} %collective-permute-done.6.refs_8_), channel_id=1, source_target_pairs={{0,8},{8,0},{1,9},{9,1},{2,10},{10,2},{3,11},{11,3},{4,12},{12,4},... | collective-permute-start | bytes 1277960 | tf_op jit(solution)/shard_map/ppermute | solution.py:38
  56.2 5.3 %copy-start.11 = (bf16[2,832,128]{2,1,0:T(8,128)(2,1)}, bf16[2,832,128]{2,1,0:T(8,128)(2,1)S(1)}, u32[]{:S(2)}) copy-start(bf16[2,832,128]{2,1,0:T(8,128)(2,1)S(1)} %collective-permute-done.13.refs_15_) | copy-start | bytes 1277956
  56.2 7.0 %collective-permute-start.16 = (bf16[2,832,128]{2,1,0:T(8,128)(2,1)S(1)}, bf16[2,832,128]{2,1,0:T(8,128)(2,1)}, u32[]{:S(2)}, u32[]{:S(2)}) collective-permute-start(bf16[2,832,128]{2,1,0:T(8,128)(2,1)S(1)} %collective-permute-done.7.refs_9_), channel_id=1, source_target_pairs={{0,8},{8,0},{1,9},{9,1},{2,10},{10,2},{3,11},{11,3},{4,12},{12,4},... | collective-permute-start | bytes 1277960 | tf_op jit(solution)/shard_map/ppermute | solution.py:38
  60.2 3.1 %copy-start.12 = (bf16[1,832,128]{2,1,0:T(8,128)(2,1)}, bf16[1,832,128]{2,1,0:T(8,128)(2,1)S(1)}, u32[]{:S(2)}) copy-start(bf16[1,832,128]{2,1,0:T(8,128)(2,1)S(1)} %collective-permute-done.8.refs_10_) | copy-start | bytes 638980
  60.2 2.5 %collective-permute-start.17 = (bf16[1,832,128]{2,1,0:T(8,128)(2,1)S(1)}, bf16[1,832,128]{2,1,0:T(8,128)(2,1)}, u32[]{:S(2)}, u32[]{:S(2)}) collective-permute-start(bf16[1,832,128]{2,1,0:T(8,128)(2,1)S(1)} %collective-permute-done.8.refs_10_), channel_id=1, source_target_pairs={{0,8},{8,0},{1,9},{9,1},{2,10},{10,2},{3,11},{11,3},{4,12},{12,4},... | collective-permute-start | bytes 638984 | tf_op jit(solution)/shard_map/ppermute | solution.py:38
  61.5 1.8 %collective-permute-start.18 = (bf16[1,832,128]{2,1,0:T(8,128)(2,1)}, bf16[1,832,128]{2,1,0:T(8,128)(2,1)}, u32[]{:S(2)}, u32[]{:S(2)}) collective-permute-start(bf16[1,832,128]{2,1,0:T(8,128)(2,1)} %collective-permute-done.9.refs_11_), channel_id=1, source_target_pairs={{0,8},{8,0},{1,9},{9,1},{2,10},{10,2},{3,11},{11,3},{4,12},{12,4},... | collective-permute-start | bytes 638984 | tf_op jit(solution)/shard_map/ppermute | solution.py:38

commit v7 on v6

--- a/solution.py
+++ b/solution.py
@@ -15,6 +15,8 @@
 SPAN = 64
 LANES = 128
 VARIANTS = 4
+PREPARE_VMEM = 40 << 20
+ATTENTION_VMEM = 28 << 20
 MASKED = -1e30
 EXP2_SCALE = (NOPE + ROPE) ** (-0.5) * math.log2(math.e)
 
@@ -88,35 +90,62 @@
     mix_ref[slot, rows, :] = (acc / total).astype(jnp.bfloat16)
 
 
-def attention_kernel(layout, heads, tile, *refs):
-    refs = list(refs)
-    take = lambda n: [refs.pop(0) for _ in range(n)]
-    idx_ref, span_ref, query_ref = take(3)
-    piece_refs = take(len(layout))
-    out_ref, key_ref, w_ref, lo_ref, hi_ref, q_ref, mix_ref, key_sem, w_sem = refs
-    z, xh, core, slot0 = (idx_ref[i] for i in range(4))
+def fetch(layout, idx_ref, span_ref, piece_refs, key_ref, w_ref, key_sem, w_sem):
+    z, xh, core = (idx_ref[i] for i in range(3))
     shards, latent_rows = key_ref.shape[:2]
     zs = shards // 4
-    shard_rows = KV // shards
-
-    key_copies, w_copies = [], []
+    key_copies, w_copies, places = [], [], []
     for (dz, which), piece in zip(layout, piece_refs):
         for j, (dx, dc) in enumerate(which):
             zz = lax.rem(z + dz + zs, zs)
             xx = 1 - xh if dx else xh
             cc = 1 - core if dc else core
-            shard, n = (zz * 2 + xx) * 2 + cc, len(w_copies)
+            shard, n = (zz * 2 + xx) * 2 + cc, len(places)
+            places.append(span_ref[2 * shard])
             w_rows = pl.ds(latent_rows, w_ref.shape[1])
             w_copies.append(
                 pltpu.make_async_copy(piece.at[j, w_rows], w_ref.at[shard], w_sem.at[n])
             )
-            place = span_ref[2 * shard]
             key_rows = pl.ds(0, latent_rows)
             key_copies.append(
-                pltpu.make_async_copy(piece.at[j, key_rows], key_ref.at[place], key_sem.at[n])
+                pltpu.make_async_copy(piece.at[j, key_rows], key_ref.at[places[n]], key_sem.at[n])
             )
     for copy in w_copies + key_copies:
         copy.start()
+    return key_copies, w_copies, places
+
+
+def pair_up(key_ref, lo_ref, hi_ref, pair):
+    left, right = key_ref[2 * pair], key_ref[2 * pair + 1]
+    cols = pl.ds(pl.multiple_of(pair * 2 * SPAN, 2 * SPAN), 2 * SPAN)
+    lo_ref[:, cols] = jnp.concatenate([left[:, :SPAN], right[:, :SPAN]], axis=1)
+    hi_ref[:, cols] = jnp.concatenate([left[:, SPAN:], right[:, SPAN:]], axis=1)
+
+
+def prepare_kernel(layout, *refs):
+    idx_ref, span_ref, *piece_refs = refs[: 2 + len(layout)]
+    key_ref, w_ref, lo_ref, hi_ref, token_ref, key_sem, w_sem = refs[2 + len(layout) :]
+    token_ref[...] = jnp.zeros_like(token_ref)
+    key_copies, w_copies, _ = fetch(
+        layout, idx_ref, span_ref, piece_refs, key_ref, w_ref, key_sem, w_sem
+    )
+    for copy in key_copies:
+        copy.wait()
+    for pair in range(key_ref.shape[0] // 2):
+        pair_up(key_ref, lo_ref, hi_ref, pair)
+    for copy in w_copies:
+        copy.wait()
+
+
+def attention_kernel(layout, heads, tile, *refs):
+    idx_ref, span_ref, query_ref, _, _, _, _, *refs = refs
+    piece_refs, refs = refs[: len(layout)], refs[len(layout) :]
+    out_ref, key_ref, w_ref, lo_ref, hi_ref, q_ref, mix_ref, key_sem, w_sem = refs
+    shards = key_ref.shape[0]
+    shard_rows = KV // shards
+    key_copies, w_copies, places = fetch(
+        layout, idx_ref, span_ref, piece_refs, key_ref, w_ref, key_sem, w_sem
+    )
     for copy in w_copies:
         copy.wait()
 
@@ -133,13 +162,10 @@
 
     for copy in key_copies:
         copy.wait()
-    for i in range(0, shards, 2):
-        left, right = key_ref[i], key_ref[i + 1]
-        cols = slice(i * SPAN, (i + 2) * SPAN)
-        lo_ref[:, cols] = jnp.concatenate([left[:, :SPAN], right[:, :SPAN]], axis=1)
-        hi_ref[:, cols] = jnp.concatenate([left[:, SPAN:], right[:, SPAN:]], axis=1)
-
-    c = span_ref[slot0]
+    for place in places:
+        pair_up(key_ref, lo_ref, hi_ref, lax.div(place, 2))
+
+    c = span_ref[idx_ref[3]]
     group = lax.div(c, shards // VARIANTS)
     for variant in range(VARIANTS):
 
@@ -161,36 +187,67 @@
         out_ref[:, cols] = dot(both, wv).astype(jnp.bfloat16)
 
 
-def attention(layout, heads, idx, span_ids, query, pieces):
-    rows, cols = heads * SPAN, heads * VDIM
-    b16 = jnp.bfloat16
-    shards = sum(p.shape[0] for p in pieces)
-    args = [idx, span_ids, query, *pieces]
-    size = sum(math.prod(a.shape) * a.dtype.itemsize for a in args)
+VMEM = pl.BlockSpec(memory_space=pltpu.VMEM)
+SMEM = pl.BlockSpec(memory_space=pltpu.SMEM)
+ANY = pl.BlockSpec(memory_space=pl.ANY)
+
+
+def nbytes(arrays):
+    return sum(math.prod(a.shape) * a.dtype.itemsize for a in arrays)
+
+
+def prepare(idx, span_ids, pieces):
+    layout = tuple((dz, which) for dz, which, _ in pieces)
+    pieces = [piece for _, _, piece in pieces]
+    shards, weight_rows = span_ids.shape[0] // 2, pieces[0].shape[1] - KV - ROPE
+    count = sum(p.shape[0] for p in pieces)
+    held = [
+        jax.ShapeDtypeStruct(shape, jnp.bfloat16)
+        for shape in (
+            (shards, KV + ROPE, 2 * SPAN),
+            (shards, weight_rows, LANES),
+            (KV + ROPE, shards * SPAN),
+            (KV + ROPE, shards * SPAN),
+            (16, LANES),
+        )
+    ]
+    return pl.pallas_call(
+        functools.partial(prepare_kernel, layout),
+        out_shape=held,
+        in_specs=[SMEM] * 2 + [ANY] * len(pieces),
+        out_specs=[VMEM] * 5,
+        scratch_shapes=[pltpu.SemaphoreType.DMA((count,)), pltpu.SemaphoreType.DMA((count,))],
+        compiler_params=pltpu.CompilerParams(vmem_limit_bytes=PREPARE_VMEM),
+        cost_estimate=pl.CostEstimate(flops=0, bytes_accessed=2 * nbytes(held), transcendentals=0),
+    )(idx, span_ids, *pieces)
+
+
+def attention(heads, idx, span_ids, query, held, pieces):
+    layout = tuple((dz, which) for dz, which, _ in pieces)
+    pieces = [piece for _, _, piece in pieces]
+    rows, cols, shards = heads * SPAN, heads * VDIM, span_ids.shape[0] // 2
+    count = sum(p.shape[0] for p in pieces)
+    args = [idx, span_ids, query, *held, *pieces]
     work = 2 * rows * shards * SPAN * 5 // 4
-    vmem = pl.BlockSpec(memory_space=pltpu.VMEM)
-    return pl.pallas_call(
+    shape = jax.ShapeDtypeStruct
+    out, *_ = pl.pallas_call(
         functools.partial(attention_kernel, layout, heads, min(rows, 256)),
-        out_shape=jax.ShapeDtypeStruct((2 * SPAN, cols), b16),
-        in_specs=[pl.BlockSpec(memory_space=pltpu.SMEM)] * 2
-        + [vmem]
-        + [pl.BlockSpec(memory_space=pltpu.HBM)] * len(pieces),
-        out_specs=vmem,
+        out_shape=[shape((2 * SPAN, cols), query.dtype), *[shape(a.shape, a.dtype) for a in held]],
+        in_specs=[SMEM] * 2 + [VMEM] * 5 + [ANY] * len(pieces),
+        out_specs=[VMEM] * 5,
+        input_output_aliases={3 + i: 1 + i for i in range(4)},
         scratch_shapes=[
-            pltpu.VMEM((shards, KV + ROPE, 2 * SPAN), b16),
-            pltpu.VMEM((shards, pieces[0].shape[1] - KV - ROPE, LANES), b16),
-            pltpu.VMEM((KV + ROPE, shards * SPAN), b16),
-            pltpu.VMEM((KV + ROPE, shards * SPAN), b16),
-            pltpu.VMEM((2, rows, KV + ROPE), b16),
-            pltpu.VMEM((2, rows, KV), b16),
-            pltpu.SemaphoreType.DMA((shards,)),
-            pltpu.SemaphoreType.DMA((shards,)),
+            pltpu.VMEM((2, rows, KV + ROPE), query.dtype),
+            pltpu.VMEM((2, rows, KV), query.dtype),
+            pltpu.SemaphoreType.DMA((count,)),
+            pltpu.SemaphoreType.DMA((count,)),
         ],
-        compiler_params=pltpu.CompilerParams(vmem_limit_bytes=60 << 20),
+        compiler_params=pltpu.CompilerParams(vmem_limit_bytes=ATTENTION_VMEM),
         cost_estimate=pl.CostEstimate(
-            flops=2 * work * (2 * KV + ROPE), bytes_accessed=size, transcendentals=work
+            flops=2 * work * (2 * KV + ROPE), bytes_accessed=nbytes(args), transcendentals=work
         ),
     )(*args)
+    return out
 
 
 def per_device(compressed, latent, w_uq, w_uk, w_uv, span_ids):
@@ -209,7 +266,7 @@
     )
 
     copies = jnp.broadcast_to(compressed.T[None], (ys * xls,) + compressed.T.shape)
-    (copies,) = gate([copies], weights)
+    (copies,) = gate([copies], here)
     features = lax.all_to_all(copies, ("y", "xl"), 0, 0, tiled=True).reshape(-1, toks)
     query = lax.dot_general(
         features, w_uq, (((0,), (0,)), ((), ())), preferred_element_type=jnp.float32
@@ -220,19 +277,19 @@
     ahead = behind = here
     for k in range(1, zs // 2):
         ahead, behind = shift(ahead, "z", 1), shift(behind, "z", -1)
-        if k == 1:
+        if k == 2:
             ahead, behind = gate([ahead, behind], query)
         pieces += [(-k, both, ahead), (k, both, behind)]
-    pieces += [
-        (-(zs // 2), first_xh, shift(ahead[:1], "z", 1)),
-        (zs // 2, second_xh, shift(behind[1:], "z", -1)),
+    hand = lambda some: [
+        (dz, tuple((dx, 1) for dx, _ in which), shift(piece, "core", 1))
+        for dz, which, piece in some
     ]
-    pieces += [
-        (dz, tuple((dx, 1) for dx, _ in which), shift(piece, "core", 1))
-        for dz, which, piece in pieces
-    ]
-    layout = tuple((dz, which) for dz, which, _ in pieces)
-    return attention(layout, heads, idx, span_ids, query, [p for _, _, p in pieces])
+    early = pieces + hand(pieces)
+    last = [shift(ahead[:1], "z", 1), shift(behind[1:], "z", -1)]
+    *held, token = prepare(idx, span_ids, early)
+    last = gate(last, token)
+    late = [(-(zs // 2), first_xh, last[0]), (zs // 2, second_xh, last[1])]
+    return attention(heads, idx, span_ids, query, held, late + hand(late))
 
 
 def solution(mesh):

time: 79.8 us -> 87.6 us (1.098)
  waiting for transfers between devices: 22 us -> 5.99 us
  local copies, waits for them, and re-layouts: 2.45 us -> 11.4 us
  Pallas kernels: 16 us -> 24.6 us
  starting transfers between devices: 33.9 us -> 40.3 us
    ppermute x18, waiting for transfers between devices: 21.2 us -> 5.98 us  [shift(): return lax.ppermute(x, axis, [(i, (i + by) % n) for i in range(n)])]
    pallas_call x0 -> x1, Pallas kernels: none -> 12.8 us  [prepare(): pl.pallas_call(functools.partial(prepare_kernel, layout), out_shape=held,...]
    unnamed x26 -> x18, local copies, waits for them, and re-layouts: 0.05 us -> 7.65 us
    ppermute x18, starting transfers between devices: 26.3 us -> 32.7 us  [shift(): return lax.ppermute(x, axis, [(i, (i + by) % n) for i in range(n)])]
    pallas_call x1, Pallas kernels: 16 us -> 11.9 us  [attention(): pl.pallas_call(functools.partial(attention_kernel, layout, heads, min(row...]
    slice x2, local copies, waits for them, and re-layouts: 0.03 us -> 1.42 us  [per_device(): last = [shift(ahead[:1], 'z', 1), shift(behind[1:], 'z', -1)]]
  transfers between devices with their start and end apart: 20 -> 20, of which waited for: 8 -> 5; matrix products, arithmetic and copies ran while one was open for 9% -> 9% of each run, Pallas kernels for 0% -> 15%
where the time goes in v7:
time: 87.6 us; the launch traced here: 86.9 us
  starting transfers between devices  40.3 us (46%)
  Pallas kernels  24.6 us (28%)
  local copies, waits for them, and re-layouts  11.4 us (13%)
  waiting for transfers between devices  5.99 us (7%)
  matrix products  3.16 us (4%)
  other arithmetic  1.06 us (1%)
    ppermute x18, starting transfers between devices, shift(): return lax.ppermute(x, axis, [(i, (i + by) % n) for i in range(n)])  32.7 us
    pallas_call x1, Pallas kernels, prepare(): pl.pallas_call(functools.partial(prepare_kernel, layout), out_shape=held,...  12.8 us
    pallas_call x1, Pallas kernels, attention(): pl.pallas_call(functools.partial(attention_kernel, layout, heads, min(row...  11.9 us
    unnamed x18, local copies, waits for them, and re-layouts  7.65 us
    ppermute x18, waiting for transfers between devices, shift(): return lax.ppermute(x, axis, [(i, (i + by) % n) for i in range(n)])  5.98 us
    all_to_all x1, starting transfers between devices, per_device(): lax.all_to_all(copies, ('y', 'xl'), 0, 0, tiled=True).reshape(-1, toks)  4.32 us
    ppermute x1, starting transfers between devices, per_device(): across = lax.ppermute(own, ('xh', 'xl'), [(0, 3), (3, 0), (1, 2), (2, 1)])  3.31 us
    dot_general x1, matrix products, per_device(): lax.dot_general(features, w_uq, (((0,), (0,)), ((), ())), preferred_eleme...  3.16 us
  transfers between devices with their start and end apart: 20, of which 5 were waited for; matrix products, arithmetic and copies ran while one was open for 9% of the time, Pallas kernels for 15%

profile of v7, /device:TPU:1, one launch (start us, length us, event | category | flops | bytes accessed | tf_op | source)
XLA Modules:
  0.0 86.9 jit_solution(5690360954979798046)
XLA Ops:
  0.0 0.0 copy-start
  0.0 3.3 %collective-permute-start = (bf16[576,128]{1,0:T(8,128)(2,1)}, bf16[576,128]{1,0:T(8,128)(2,1)S(1)}, u32[]{:S(2)}, u32[]{:S(2)}) collective-permute-start(bf16[576,128]{1,0:T(8,128)(2,1)} %bitcast.34), channel_id=1, source_target_pairs={{0,17},{17,0},{1,16},{16,1},{2,19},{19,2},{3,18},{18,3},{4,21},{21... | collective-permute-start | bytes 442376 | tf_op jit(solution)/shard_map/ppermute | solution.py:261
  3.3 0.0 copy-done
  3.3 0.8 copy_bitcast_fusion
  4.1 1.1 %collective-permute-start.1 = (bf16[256,128]{1,0:T(8,128)(2,1)S(1)}, bf16[256,128]{1,0:T(8,128)(2,1)S(1)}, u32[]{:S(2)}, u32[]{:S(2)}) collective-permute-start(bf16[256,128]{1,0:T(8,128)(2,1)S(1)} %pad_maximum_fusion.1), channel_id=1, source_target_pairs={{0,16},{16,0},{1,17},{17,1},{2,18},{18,2},{3,19},{19,3},{4,20},{20... | collective-permute-start | bytes 196616 | tf_op jit(solution)/shard_map/ppermute | solution.py:40
  5.2 0.9 %maximum_bitcast_fusion = bf16[1,832,128]{2,1,0:T(8,128)(2,1)S(1)} fusion(bf16[128,128]{1,0:T(8,128)(2,1)S(1)} %bitcast.33, bf16[128,128]{1,0:T(8,128)(2,1)S(1)} %bitcast.31, bf16[576,128]{1,0:T(8,128)(2,1)} %bitcast.35), kind=kLoop, calls=%fused_computation.2 | loop fusion | flops 638976 | bytes 425984 | tf_op jit(solution)/shard_map/stack | solution.py:264
  6.1 2.8 %collective-permute-done.1 = bf16[256,128]{1,0:T(8,128)(2,1)S(1)} collective-permute-done((bf16[256,128]{1,0:T(8,128)(2,1)S(1)}, bf16[256,128]{1,0:T(8,128)(2,1)S(1)}, u32[]{:S(2)}, u32[]{:S(2)}) %collective-permute-start.1) | collective-permute-done | bytes 65568 | tf_op jit(solution)/shard_map/ppermute | solution.py:40
  8.9 0.0 collective-permute-done
  9.0 5.5 %collective-permute-start.3 = (bf16[2,832,128]{2,1,0:T(8,128)(2,1)S(1)}, bf16[2,832,128]{2,1,0:T(8,128)(2,1)S(1)}, u32[]{:S(2)}, u32[]{:S(2)}) collective-permute-start(bf16[2,832,128]{2,1,0:T(8,128)(2,1)S(1)} %pad_maximum_fusion.refs_1_.refs_2_), channel_id=1, source_target_pairs={{0,224},{32,0},{64,32},{96,64},{128,96},{160,128},{192,160},{224,1... | collective-permute-start | bytes 1277960 | tf_op jit(solution)/shard_map/ppermute | solution.py:40
  14.5 0.0 collective-permute-start.2
  14.5 1.6 %broadcast_in_dim.2.refs_0_ = bf16[8,192,128]{2,1,0:T(8,128)(2,1)} broadcast(bf16[192,128]{1,0:T(8,128)(2,1)} %bitcast.36), dimensions={1,2} | broadcast | bytes 442368 | tf_op jit(solution)/shard_map/broadcast_in_dim | solution.py:268
  16.1 0.0 copy-start.7
  16.1 4.3 %all-to-all-start = ((bf16[8,192,128]{2,1,0:T(8,128)(2,1)}), bf16[8,192,128]{2,1,0:T(8,128)(2,1)S(1)}, u32[]{:S(2)}, u32[]{:S(2)}) async-start(bf16[8,192,128]{2,1,0:T(8,128)(2,1)} %shard_map.64), calls=%async_computation | async-start | bytes 786432 | tf_op jit(solution)/shard_map/all_to_all | solution.py:270
  20.5 1.1 %collective-permute-done.3.refs_4_ = bf16[2,832,128]{2,1,0:T(8,128)(2,1)S(1)} collective-permute-done((bf16[2,832,128]{2,1,0:T(8,128)(2,1)S(1)}, bf16[2,832,128]{2,1,0:T(8,128)(2,1)S(1)}, u32[]{:S(2)}, u32[]{:S(2)}) %collective-permute-start.3) | collective-permute-done | bytes 426016 | tf_op jit(solution)/shard_map/ppermute | solution.py:40
  21.5 3.4 %collective-permute-start.5 = (bf16[2,832,128]{2,1,0:T(8,128)(2,1)S(1)}, bf16[2,832,128]{2,1,0:T(8,128)(2,1)S(1)}, u32[]{:S(2)}, u32[]{:S(2)}) collective-permute-start(bf16[2,832,128]{2,1,0:T(8,128)(2,1)S(1)} %collective-permute-done.3.refs_4_), channel_id=1, source_target_pairs={{0,224},{32,0},{64,32},{96,64},{128,96},{160,128},{192,160},{224,1... | collective-permute-start | bytes 1277960 | tf_op jit(solution)/shard_map/ppermute | solution.py:40
  24.9 0.0 collective-permute-done.2.refs_3_
  25.0 0.0 collective-permute-start.4
  25.0 3.3 %collective-permute-start.8 = (bf16[2,832,128]{2,1,0:T(8,128)(2,1)S(1)}, bf16[2,832,128]{2,1,0:T(8,128)(2,1)}, u32[]{:S(2)}, u32[]{:S(2)}) collective-permute-start(bf16[2,832,128]{2,1,0:T(8,128)(2,1)S(1)} %pad_maximum_fusion.refs_1_.refs_2_), channel_id=1, source_target_pairs={{0,8},{8,0},{1,9},{9,1},{2,10},{10,2},{3,11},{11,3},{4,12},{12,4},... | collective-permute-start | bytes 1277960 | tf_op jit(solution)/shard_map/ppermute | solution.py:40
  28.3 0.0 all-to-all-done
  28.3 3.2 %convolution_convert_fusion.refs_2_ = bf16[128,1536]{1,0:T(8,128)(2,1)S(1)} fusion(bf16[1536,128]{1,0:T(8,128)(2,1)S(1)} %bitcast.29, bf16[1536,1536]{1,0:T(8,128)(2,1)} %param.8), kind=kOutput, calls=%fused_computation | convolution fusion | flops 604176384 | bytes 5505024 | tf_op jit(solution)/shard_map/dot_general | solution.py:271
  31.4 2.9 %collective-permute-start.10 = (bf16[2,832,128]{2,1,0:T(8,128)(2,1)S(1)}, bf16[2,832,128]{2,1,0:T(8,128)(2,1)S(1)}, u32[]{:S(2)}, u32[]{:S(2)}) collective-permute-start(bf16[2,832,128]{2,1,0:T(8,128)(2,1)S(1)} %collective-permute-done.3.refs_4_), channel_id=1, source_target_pairs={{0,8},{8,0},{1,9},{9,1},{2,10},{10,2},{3,11},{11,3},{4,12},{12,4},... | collective-permute-start | bytes 1277960 | tf_op jit(solution)/shard_map/ppermute | solution.py:40
  34.4 0.0 collective-permute-done.5.refs_1_
  34.4 0.0 collective-permute-done.4.refs_0_
  34.4 0.0 collective-permute-start.6
  34.4 3.0 %collective-permute-start.7 = (bf16[2,832,128]{2,1,0:T(8,128)(2,1)S(1)}, bf16[2,832,128]{2,1,0:T(8,128)(2,1)S(1)}, u32[]{:S(2)}, u32[]{:S(2)}) collective-permute-start(bf16[2,832,128]{2,1,0:T(8,128)(2,1)S(1)} %get-tuple-element.16.refs_6_), channel_id=1, source_target_pairs={{0,224},{32,0},{64,32},{96,64},{128,96},{160,128},{192,160},{224,1... | collective-permute-start | bytes 1277960 | tf_op jit(solution)/shard_map/ppermute | solution.py:40
  37.4 4.2 %collective-permute-start.9 = (bf16[2,832,128]{2,1,0:T(8,128)(2,1)S(1)}, bf16[2,832,128]{2,1,0:T(8,128)(2,1)S(1)}, u32[]{:S(2)}, u32[]{:S(2)}) collective-permute-start(bf16[2,832,128]{2,1,0:T(8,128)(2,1)S(1)} %collective-permute-done.2.refs_3_), channel_id=1, source_target_pairs={{0,8},{8,0},{1,9},{9,1},{2,10},{10,2},{3,11},{11,3},{4,12},{12,4},... | collective-permute-start | bytes 1277960 | tf_op jit(solution)/shard_map/ppermute | solution.py:40
  41.6 0.0 collective-permute-done.8.refs_9_
  41.6 0.0 collective-permute-start.11
  41.6 0.0 collective-permute-done.10.refs_11_
  41.6 0.0 copy-start.1
  41.7 0.8 copy-done.1
  42.4 0.5 collective-permute-start.12
  42.9 0.5 collective-permute-done.6.refs_7_
  43.4 4.7 %collective-permute-start.13 = (bf16[2,832,128]{2,1,0:T(8,128)(2,1)S(1)}, bf16[2,832,128]{2,1,0:T(8,128)(2,1)}, u32[]{:S(2)}, u32[]{:S(2)}) collective-permute-start(bf16[2,832,128]{2,1,0:T(8,128)(2,1)S(1)} %collective-permute-done.6.refs_7_), channel_id=1, source_target_pairs={{0,8},{8,0},{1,9},{9,1},{2,10},{10,2},{3,11},{11,3},{4,12},{12,4},... | collective-permute-start | bytes 1277960 | tf_op jit(solution)/shard_map/ppermute | solution.py:40
  48.1 0.0 collective-permute-done.7.refs_8_
  48.1 0.0 collective-permute-start.14
  48.1 0.7 slice.8
  48.8 0.7 slice.9
  49.5 0.0 collective-permute-done.9.refs_10_
  49.5 0.8 copy-done.3
  50.3 0.0 collective-permute-start.15
  50.3 0.0 collective-permute-done.11.refs_12_
  50.3 0.0 copy-start.5
  50.3 0.8 copy-done.5
  51.1 2.8 %collective-permute-start.16 = (bf16[1,832,128]{2,1,0:T(8,128)(2,1)}, bf16[1,832,128]{2,1,0:T(8,128)(2,1)}, u32[]{:S(2)}, u32[]{:S(2)}) collective-permute-start(bf16[1,832,128]{2,1,0:T(8,128)(2,1)} %slice.9), channel_id=1, source_target_pairs={{0,224},{32,0},{64,32},{96,64},{128,96},{160,128},{192,160},{224,1... | collective-permute-start | bytes 638984 | tf_op jit(solution)/shard_map/ppermute | solution.py:40
  53.8 0.1 pad_add_fusion.refs_0_
  53.9 0.0 collective-permute-done.12.refs_13_
  53.9 0.0 collective-permute-done.13.refs_14_
  53.9 0.0 collective-permute-done.14.refs_15_
  53.9 0.0 copy-done.7
  53.9 0.0 copy-start.2
  53.9 1.0 %copy-done.2 = bf16[2,832,128]{2,1,0:T(8,128)(2,1)S(1)} copy-done((bf16[2,832,128]{2,1,0:T(8,128)(2,1)S(1)}, bf16[2,832,128]{2,1,0:T(8,128)(2,1)}, u32[]{:S(2)}) %copy-start.2) | copy-done | bytes 426008
  54.9 0.0 copy-start.4
  54.9 1.0 %copy-done.4 = bf16[2,832,128]{2,1,0:T(8,128)(2,1)S(1)} copy-done((bf16[2,832,128]{2,1,0:T(8,128)(2,1)S(1)}, bf16[2,832,128]{2,1,0:T(8,128)(2,1)}, u32[]{:S(2)}) %copy-start.4) | copy-done | bytes 426008
  55.9 1.0 %copy-done.6 = bf16[2,832,128]{2,1,0:T(8,128)(2,1)S(1)} copy-done((bf16[2,832,128]{2,1,0:T(8,128)(2,1)S(1)}, bf16[2,832,128]{2,1,0:T(8,128)(2,1)}, u32[]{:S(2)}) %copy-start.6) | copy-done | bytes 426008
  56.9 12.8 %shard_map.66 = (bf16[32,576,128]{2,1,0:T(8,128)(2,1)}, bf16[32,256,128]{2,1,0:T(8,128)(2,1)S(1)}, bf16[576,2048]{1,0:T(8,128)(2,1)S(1)}, bf16[576,2048]{1,0:T(8,128)(2,1)S(1)}, bf16[16,128]{1,0:T(8,128)(2,1)S(1)}) custom-call(s32[4]{0:T(128)S(1)} %pad_add_fusion.refs_0_, s32[64]{0:T(128)S(1)} %copy-done.7, ...), custom_call_target="tpu_custom_call" | custom-call | bytes 23076864 | tf_op jit(solution)/shard_map/pallas_call | solution.py:214
  69.7 0.0 collective-permute-done.15.refs_0_
  69.7 0.0 collective-permute-done.16.refs_1_
  69.7 1.1 %collective-permute-start.17 = (bf16[1,832,128]{2,1,0:T(8,128)(2,1)}, bf16[1,832,128]{2,1,0:T(8,128)(2,1)S(1)}, u32[]{:S(2)}, u32[]{:S(2)}) collective-permute-start(bf16[1,832,128]{2,1,0:T(8,128)(2,1)} %get-tuple-element.22.refs_7_), channel_id=1, source_target_pairs={{0,8},{8,0},{1,9},{9,1},{2,10},{10,2},{3,11},{11,3},{4,12},{12,4},... | collective-permute-start | bytes 638984 | tf_op jit(solution)/shard_map/ppermute | solution.py:40
  70.8 0.1 collective-permute-start.18
  70.9 1.2 %collective-permute-done.17.refs_9_ = bf16[1,832,128]{2,1,0:T(8,128)(2,1)S(1)} collective-permute-done((bf16[1,832,128]{2,1,0:T(8,128)(2,1)}, bf16[1,832,128]{2,1,0:T(8,128)(2,1)S(1)}, u32[]{:S(2)}, u32[]{:S(2)}) %collective-permute-start.17) | collective-permute-done | bytes 213024 | tf_op jit(solution)/shard_map/ppermute | solution.py:40
  72.1 0.4 collective-permute-done.18.refs_10_
  72.5 2.3 %copy-done.8 = bf16[32,576,128]{2,1,0:T(8,128)(2,1)S(1)} copy-done((bf16[32,576,128]{2,1,0:T(8,128)(2,1)S(1)}, bf16[32,576,128]{2,1,0:T(8,128)(2,1)}, u32[]{:S(2)}) %copy-start.8) | copy-done | bytes 4718616
  74.8 11.9 %shard_map.68 = (bf16[128,1024]{1,0:T(8,128)(2,1)}, bf16[32,576,128]{2,1,0:T(8,128)(2,1)S(1)}, bf16[32,256,128]{2,1,0:T(8,128)(2,1)S(1)}, bf16[576,2048]{1,0:T(8,128)(2,1)S(1)}, bf16[576,2048]{1,0:T(8,128)(2,1)S(1)}) custom-call(s32[4]{0:T(128)S(1)} %pad_add_fusion.refs_0_, ...), custom_call_target="tpu_custom_call", output_to_operand_aliasing={{1}: (3, {}), {2}: (4, {}), {3}: (5, {}), {4}: (6, {})} | custom-call | flops 5704253440 | bytes 12779792 | tf_op jit(solution)/shard_map/pallas_call | solution.py:233
  (10 shorter events, 0.1 us)
Async XLA Ops:
  0.0 3.3 %copy-start = (bf16[16,1024]{1,0:T(8,128)(2,1)S(1)}, bf16[16,1024]{1,0:T(8,128)(2,1)}, u32[]{:S(2)}) copy-start(bf16[16,1024]{1,0:T(8,128)(2,1)} %param.9) | copy-start | bytes 98308
  0.0 8.9 %collective-permute-start = (bf16[576,128]{1,0:T(8,128)(2,1)}, bf16[576,128]{1,0:T(8,128)(2,1)S(1)}, u32[]{:S(2)}, u32[]{:S(2)}) collective-permute-start(bf16[576,128]{1,0:T(8,128)(2,1)} %bitcast.34), channel_id=1, source_target_pairs={{0,17},{17,0},{1,16},{16,1},{2,19},{19,2},{3,18},{18,3},{4,21},{21... | collective-permute-start | bytes 442376 | tf_op jit(solution)/shard_map/ppermute | solution.py:261
  4.1 4.8 %collective-permute-start.1 = (bf16[256,128]{1,0:T(8,128)(2,1)S(1)}, bf16[256,128]{1,0:T(8,128)(2,1)S(1)}, u32[]{:S(2)}, u32[]{:S(2)}) collective-permute-start(bf16[256,128]{1,0:T(8,128)(2,1)S(1)} %pad_maximum_fusion.1), channel_id=1, source_target_pairs={{0,16},{16,0},{1,17},{17,1},{2,18},{18,2},{3,19},{19,3},{4,20},{20... | collective-permute-start | bytes 196616 | tf_op jit(solution)/shard_map/ppermute | solution.py:40
  9.0 12.5 %collective-permute-start.3 = (bf16[2,832,128]{2,1,0:T(8,128)(2,1)S(1)}, bf16[2,832,128]{2,1,0:T(8,128)(2,1)S(1)}, u32[]{:S(2)}, u32[]{:S(2)}) collective-permute-start(bf16[2,832,128]{2,1,0:T(8,128)(2,1)S(1)} %pad_maximum_fusion.refs_1_.refs_2_), channel_id=1, source_target_pairs={{0,224},{32,0},{64,32},{96,64},{128,96},{160,128},{192,160},{224,1... | collective-permute-start | bytes 1277960 | tf_op jit(solution)/shard_map/ppermute | solution.py:40
  14.5 10.4 %collective-permute-start.2 = (bf16[2,832,128]{2,1,0:T(8,128)(2,1)S(1)}, bf16[2,832,128]{2,1,0:T(8,128)(2,1)S(1)}, u32[]{:S(2)}, u32[]{:S(2)}) collective-permute-start(bf16[2,832,128]{2,1,0:T(8,128)(2,1)S(1)} %pad_maximum_fusion.refs_1_.refs_2_), channel_id=1, source_target_pairs={{0,32},{32,64},{64,96},{96,128},{128,160},{160,192},{192,224},{224... | collective-permute-start | bytes 1277960 | tf_op jit(solution)/shard_map/ppermute | solution.py:40
  16.1 37.8 %copy-start.7 = (s32[64]{0:T(128)S(1)}, s32[64]{0:T(128)}, u32[]{:S(2)}) copy-start(s32[64]{0:T(128)} %refs_1_.3) | copy-start | bytes 772
  16.1 12.1 %all-to-all-start = ((bf16[8,192,128]{2,1,0:T(8,128)(2,1)}), bf16[8,192,128]{2,1,0:T(8,128)(2,1)S(1)}, u32[]{:S(2)}, u32[]{:S(2)}) async-start(bf16[8,192,128]{2,1,0:T(8,128)(2,1)} %shard_map.64), calls=%async_computation | async-start | bytes 786432 | tf_op jit(solution)/shard_map/all_to_all | solution.py:270
  21.5 12.8 %collective-permute-start.5 = (bf16[2,832,128]{2,1,0:T(8,128)(2,1)S(1)}, bf16[2,832,128]{2,1,0:T(8,128)(2,1)S(1)}, u32[]{:S(2)}, u32[]{:S(2)}) collective-permute-start(bf16[2,832,128]{2,1,0:T(8,128)(2,1)S(1)} %collective-permute-done.3.refs_4_), channel_id=1, source_target_pairs={{0,224},{32,0},{64,32},{96,64},{128,96},{160,128},{192,160},{224,1... | collective-permute-start | bytes 1277960 | tf_op jit(solution)/shard_map/ppermute | solution.py:40
  25.0 9.4 %collective-permute-start.4 = (bf16[2,832,128]{2,1,0:T(8,128)(2,1)S(1)}, bf16[2,832,128]{2,1,0:T(8,128)(2,1)S(1)}, u32[]{:S(2)}, u32[]{:S(2)}) collective-permute-start(bf16[2,832,128]{2,1,0:T(8,128)(2,1)S(1)} %collective-permute-done.2.refs_3_), channel_id=1, source_target_pairs={{0,32},{32,64},{64,96},{96,128},{128,160},{160,192},{192,224},{224... | collective-permute-start | bytes 1277960 | tf_op jit(solution)/shard_map/ppermute | solution.py:40
  25.0 16.7 %collective-permute-start.8 = (bf16[2,832,128]{2,1,0:T(8,128)(2,1)S(1)}, bf16[2,832,128]{2,1,0:T(8,128)(2,1)}, u32[]{:S(2)}, u32[]{:S(2)}) collective-permute-start(bf16[2,832,128]{2,1,0:T(8,128)(2,1)S(1)} %pad_maximum_fusion.refs_1_.refs_2_), channel_id=1, source_target_pairs={{0,8},{8,0},{1,9},{9,1},{2,10},{10,2},{3,11},{11,3},{4,12},{12,4},... | collective-permute-start | bytes 1277960 | tf_op jit(solution)/shard_map/ppermute | solution.py:40
  31.4 10.2 %collective-permute-start.10 = (bf16[2,832,128]{2,1,0:T(8,128)(2,1)S(1)}, bf16[2,832,128]{2,1,0:T(8,128)(2,1)S(1)}, u32[]{:S(2)}, u32[]{:S(2)}) collective-permute-start(bf16[2,832,128]{2,1,0:T(8,128)(2,1)S(1)} %collective-permute-done.3.refs_4_), channel_id=1, source_target_pairs={{0,8},{8,0},{1,9},{9,1},{2,10},{10,2},{3,11},{11,3},{4,12},{12,4},... | collective-permute-start | bytes 1277960 | tf_op jit(solution)/shard_map/ppermute | solution.py:40
  34.4 9.1 %collective-permute-start.6 = (bf16[2,832,128]{2,1,0:T(8,128)(2,1)S(1)}, bf16[2,832,128]{2,1,0:T(8,128)(2,1)S(1)}, u32[]{:S(2)}, u32[]{:S(2)}) collective-permute-start(bf16[2,832,128]{2,1,0:T(8,128)(2,1)S(1)} %get-tuple-element.15.refs_5_), channel_id=1, source_target_pairs={{0,32},{32,64},{64,96},{96,128},{128,160},{160,192},{192,224},{224... | collective-permute-start | bytes 1277960 | tf_op jit(solution)/shard_map/ppermute | solution.py:40
  34.4 13.7 %collective-permute-start.7 = (bf16[2,832,128]{2,1,0:T(8,128)(2,1)S(1)}, bf16[2,832,128]{2,1,0:T(8,128)(2,1)S(1)}, u32[]{:S(2)}, u32[]{:S(2)}) collective-permute-start(bf16[2,832,128]{2,1,0:T(8,128)(2,1)S(1)} %get-tuple-element.16.refs_6_), channel_id=1, source_target_pairs={{0,224},{32,0},{64,32},{96,64},{128,96},{160,128},{192,160},{224,1... | collective-permute-start | bytes 1277960 | tf_op jit(solution)/shard_map/ppermute | solution.py:40
  37.4 12.1 %collective-permute-start.9 = (bf16[2,832,128]{2,1,0:T(8,128)(2,1)S(1)}, bf16[2,832,128]{2,1,0:T(8,128)(2,1)S(1)}, u32[]{:S(2)}, u32[]{:S(2)}) collective-permute-start(bf16[2,832,128]{2,1,0:T(8,128)(2,1)S(1)} %collective-permute-done.2.refs_3_), channel_id=1, source_target_pairs={{0,8},{8,0},{1,9},{9,1},{2,10},{10,2},{3,11},{11,3},{4,12},{12,4},... | collective-permute-start | bytes 1277960 | tf_op jit(solution)/shard_map/ppermute | solution.py:40
  41.6 8.6 %collective-permute-start.11 = (bf16[2,832,128]{2,1,0:T(8,128)(2,1)S(1)}, bf16[2,832,128]{2,1,0:T(8,128)(2,1)S(1)}, u32[]{:S(2)}, u32[]{:S(2)}) collective-permute-start(bf16[2,832,128]{2,1,0:T(8,128)(2,1)S(1)} %get-tuple-element.15.refs_5_), channel_id=1, source_target_pairs={{0,8},{8,0},{1,9},{9,1},{2,10},{10,2},{3,11},{11,3},{4,12},{12,4},... | collective-permute-start | bytes 1277960 | tf_op jit(solution)/shard_map/ppermute | solution.py:40
  41.6 0.8 copy-start.1
  42.4 11.5 %collective-permute-start.12 = (bf16[2,832,128]{2,1,0:T(8,128)(2,1)S(1)}, bf16[2,832,128]{2,1,0:T(8,128)(2,1)}, u32[]{:S(2)}, u32[]{:S(2)}) collective-permute-start(bf16[2,832,128]{2,1,0:T(8,128)(2,1)S(1)} %get-tuple-element.16.refs_6_), channel_id=1, source_target_pairs={{0,8},{8,0},{1,9},{9,1},{2,10},{10,2},{3,11},{11,3},{4,12},{12,4},... | collective-permute-start | bytes 1277960 | tf_op jit(solution)/shard_map/ppermute | solution.py:40
  43.4 10.5 %collective-permute-start.13 = (bf16[2,832,128]{2,1,0:T(8,128)(2,1)S(1)}, bf16[2,832,128]{2,1,0:T(8,128)(2,1)}, u32[]{:S(2)}, u32[]{:S(2)}) collective-permute-start(bf16[2,832,128]{2,1,0:T(8,128)(2,1)S(1)} %collective-permute-done.6.refs_7_), channel_id=1, source_target_pairs={{0,8},{8,0},{1,9},{9,1},{2,10},{10,2},{3,11},{11,3},{4,12},{12,4},... | collective-permute-start | bytes 1277960 | tf_op jit(solution)/shard_map/ppermute | solution.py:40
  48.1 5.8 %collective-permute-start.14 = (bf16[2,832,128]{2,1,0:T(8,128)(2,1)S(1)}, bf16[2,832,128]{2,1,0:T(8,128)(2,1)}, u32[]{:S(2)}, u32[]{:S(2)}) collective-permute-start(bf16[2,832,128]{2,1,0:T(8,128)(2,1)S(1)} %collective-permute-done.7.refs_8_), channel_id=1, source_target_pairs={{0,8},{8,0},{1,9},{9,1},{2,10},{10,2},{3,11},{11,3},{4,12},{12,4},... | collective-permute-start | bytes 1277960 | tf_op jit(solution)/shard_map/ppermute | solution.py:40
  49.5 0.8 copy-start.3
  50.3 19.4 %collective-permute-start.15 = (bf16[1,832,128]{2,1,0:T(8,128)(2,1)}, bf16[1,832,128]{2,1,0:T(8,128)(2,1)}, u32[]{:S(2)}, u32[]{:S(2)}) collective-permute-start(bf16[1,832,128]{2,1,0:T(8,128)(2,1)} %slice.8), channel_id=1, source_target_pairs={{0,32},{32,64},{64,96},{96,128},{128,160},{160,192},{192,224},{224... | collective-permute-start | bytes 638984 | tf_op jit(solution)/shard_map/ppermute | solution.py:40
  50.3 0.8 copy-start.5
  51.1 18.6 %collective-permute-start.16 = (bf16[1,832,128]{2,1,0:T(8,128)(2,1)}, bf16[1,832,128]{2,1,0:T(8,128)(2,1)}, u32[]{:S(2)}, u32[]{:S(2)}) collective-permute-start(bf16[1,832,128]{2,1,0:T(8,128)(2,1)} %slice.9), channel_id=1, source_target_pairs={{0,224},{32,0},{64,32},{96,64},{128,96},{160,128},{192,160},{224,1... | collective-permute-start | bytes 638984 | tf_op jit(solution)/shard_map/ppermute | solution.py:40
  53.9 1.0 %copy-start.2 = (bf16[2,832,128]{2,1,0:T(8,128)(2,1)S(1)}, bf16[2,832,128]{2,1,0:T(8,128)(2,1)}, u32[]{:S(2)}) copy-start(bf16[2,832,128]{2,1,0:T(8,128)(2,1)} %copy-done.1) | copy-start | bytes 1277956
  54.9 1.0 %copy-start.4 = (bf16[2,832,128]{2,1,0:T(8,128)(2,1)S(1)}, bf16[2,832,128]{2,1,0:T(8,128)(2,1)}, u32[]{:S(2)}) copy-start(bf16[2,832,128]{2,1,0:T(8,128)(2,1)} %copy-done.3) | copy-start | bytes 1277956
  55.9 1.0 %copy-start.6 = (bf16[2,832,128]{2,1,0:T(8,128)(2,1)S(1)}, bf16[2,832,128]{2,1,0:T(8,128)(2,1)}, u32[]{:S(2)}) copy-start(bf16[2,832,128]{2,1,0:T(8,128)(2,1)} %copy-done.5) | copy-start | bytes 1277956
  69.7 2.4 %collective-permute-start.17 = (bf16[1,832,128]{2,1,0:T(8,128)(2,1)}, bf16[1,832,128]{2,1,0:T(8,128)(2,1)S(1)}, u32[]{:S(2)}, u32[]{:S(2)}) collective-permute-start(bf16[1,832,128]{2,1,0:T(8,128)(2,1)} %get-tuple-element.22.refs_7_), channel_id=1, source_target_pairs={{0,8},{8,0},{1,9},{9,1},{2,10},{10,2},{3,11},{11,3},{4,12},{12,4},... | collective-permute-start | bytes 638984 | tf_op jit(solution)/shard_map/ppermute | solution.py:40
  70.8 1.7 %collective-permute-start.18 = (bf16[1,832,128]{2,1,0:T(8,128)(2,1)}, bf16[1,832,128]{2,1,0:T(8,128)(2,1)S(1)}, u32[]{:S(2)}, u32[]{:S(2)}) collective-permute-start(bf16[1,832,128]{2,1,0:T(8,128)(2,1)} %get-tuple-element.23.refs_8_), channel_id=1, source_target_pairs={{0,8},{8,0},{1,9},{9,1},{2,10},{10,2},{3,11},{11,3},{4,12},{12,4},... | collective-permute-start | bytes 638984 | tf_op jit(solution)/shard_map/ppermute | solution.py:40
  72.5 2.3 %copy-start.8 = (bf16[32,576,128]{2,1,0:T(8,128)(2,1)S(1)}, bf16[32,576,128]{2,1,0:T(8,128)(2,1)}, u32[]{:S(2)}) copy-start(bf16[32,576,128]{2,1,0:T(8,128)(2,1)} %get-tuple-element.17.refs_3_) | copy-start | bytes 14155780

commit v8 on v6

--- a/solution.py
+++ b/solution.py
@@ -51,8 +51,9 @@
     return w.reshape(rows, cols // LANES, LANES).transpose(1, 0, 2).reshape(-1, LANES)
 
 
-def head_rows(w_ref, at, rows):
-    return jnp.concatenate([w_ref[i, at : at + rows, :] for i in range(w_ref.shape[0])], axis=0)
+def head_rows(w_ref, which, at, rows):
+    shards = range(w_ref.shape[1])
+    return jnp.concatenate([w_ref[which, i, at : at + rows, :] for i in shards], axis=0)
 
 
 def attend_rows(q_ref, lo_ref, hi_ref, mix_ref, c, slot, rows, variant):
@@ -99,31 +100,33 @@
     zs = shards // 4
     shard_rows = KV // shards
 
-    key_copies, w_copies = [], []
+    key_copies, wk_copies, wv_copies = [], [], []
     for (dz, which), piece in zip(layout, piece_refs):
         for j, (dx, dc) in enumerate(which):
             zz = lax.rem(z + dz + zs, zs)
             xx = 1 - xh if dx else xh
             cc = 1 - core if dc else core
-            shard, n = (zz * 2 + xx) * 2 + cc, len(w_copies)
-            w_rows = pl.ds(latent_rows, w_ref.shape[1])
-            w_copies.append(
-                pltpu.make_async_copy(piece.at[j, w_rows], w_ref.at[shard], w_sem.at[n])
-            )
+            shard, n = (zz * 2 + xx) * 2 + cc, len(key_copies)
+            rows = w_ref.shape[2]
+            for i, w_copies in enumerate((wk_copies, wv_copies)):
+                src = piece.at[j, pl.ds(latent_rows + i * rows, rows)]
+                w_copies.append(
+                    pltpu.make_async_copy(src, w_ref.at[i, shard], w_sem.at[i, n])
+                )
             place = span_ref[2 * shard]
             key_rows = pl.ds(0, latent_rows)
             key_copies.append(
                 pltpu.make_async_copy(piece.at[j, key_rows], key_ref.at[place], key_sem.at[n])
             )
-    for copy in w_copies + key_copies:
+    for copy in wk_copies + key_copies + wv_copies:
         copy.start()
-    for copy in w_copies:
+    for copy in wk_copies:
         copy.wait()
 
     for h in range(heads):
         rows = slice(h * SPAN, (h + 1) * SPAN)
         at = h * (NOPE + ROPE)
-        wk = head_rows(w_ref, h * shard_rows, shard_rows)
+        wk = head_rows(w_ref, 0, h * shard_rows, shard_rows)
         q_latent = dot_t(query_ref[:, at : at + NOPE], wk).astype(jnp.bfloat16)
         q_rope = query_ref[:, at + NOPE : at + NOPE + ROPE]
         for slot in range(2):
@@ -153,11 +156,13 @@
 
             lax.fori_loop(0, heads * SPAN // tile, body, 0)
 
+    for copy in wv_copies:
+        copy.wait()
     for h in range(heads):
         cols = slice(h * VDIM, (h + 1) * VDIM)
         rows = slice(h * SPAN, (h + 1) * SPAN)
         both = jnp.concatenate([mix_ref[0, rows, :], mix_ref[1, rows, :]], axis=0)
-        wv = head_rows(w_ref, (heads + h) * shard_rows, shard_rows)
+        wv = head_rows(w_ref, 1, h * shard_rows, shard_rows)
         out_ref[:, cols] = dot(both, wv).astype(jnp.bfloat16)
 
 
@@ -178,13 +183,13 @@
         out_specs=vmem,
         scratch_shapes=[
             pltpu.VMEM((shards, KV + ROPE, 2 * SPAN), b16),
-            pltpu.VMEM((shards, pieces[0].shape[1] - KV - ROPE, LANES), b16),
+            pltpu.VMEM((2, shards, (pieces[0].shape[1] - KV - ROPE) // 2, LANES), b16),
             pltpu.VMEM((KV + ROPE, shards * SPAN), b16),
             pltpu.VMEM((KV + ROPE, shards * SPAN), b16),
             pltpu.VMEM((2, rows, KV + ROPE), b16),
             pltpu.VMEM((2, rows, KV), b16),
             pltpu.SemaphoreType.DMA((shards,)),
-            pltpu.SemaphoreType.DMA((shards,)),
+            pltpu.SemaphoreType.DMA((2, shards)),
         ],
         compiler_params=pltpu.CompilerParams(vmem_limit_bytes=60 << 20),
         cost_estimate=pl.CostEstimate(
@@ -209,28 +214,37 @@
     )
 
     copies = jnp.broadcast_to(compressed.T[None], (ys * xls,) + compressed.T.shape)
-    (copies,) = gate([copies], weights)
+    (copies,) = gate([copies], here)
     features = lax.all_to_all(copies, ("y", "xl"), 0, 0, tiled=True).reshape(-1, toks)
     query = lax.dot_general(
         features, w_uq, (((0,), (0,)), ((), ())), preferred_element_type=jnp.float32
     ).astype(jnp.bfloat16)
 
     both, first_xh, second_xh = ((0, 0), (1, 0)), ((0, 0),), ((1, 0),)
+    hand = lambda some: [
+        (dz, tuple((dx, 1) for dx, _ in which), shift(piece, "core", 1))
+        for dz, which, piece in some
+    ]
+    half = zs // 2
     pieces = [(0, both, here)]
     ahead = behind = here
-    for k in range(1, zs // 2):
+    for k in range(1, half):
         ahead, behind = shift(ahead, "z", 1), shift(behind, "z", -1)
-        if k == 1:
+        if k == half - 2:
             ahead, behind = gate([ahead, behind], query)
-        pieces += [(-k, both, ahead), (k, both, behind)]
-    pieces += [
-        (-(zs // 2), first_xh, shift(ahead[:1], "z", 1)),
-        (zs // 2, second_xh, shift(behind[1:], "z", -1)),
+        if k < half - 1:
+            pieces += [(-k, both, ahead), (k, both, behind)]
+    pieces += hand(pieces)
+    last = gate([ahead[:1], behind[1:]], *(piece for _, _, piece in pieces[len(pieces) // 2 :]))
+    last = [shift(last[0], "z", 1), shift(last[1], "z", -1)]
+    ahead, behind = gate([ahead, behind], *last)
+    late = [
+        (1 - half, both, ahead),
+        (half - 1, both, behind),
+        (-half, first_xh, last[0]),
+        (half, second_xh, last[1]),
     ]
-    pieces += [
-        (dz, tuple((dx, 1) for dx, _ in which), shift(piece, "core", 1))
-        for dz, which, piece in pieces
-    ]
+    pieces += late + hand(late)
     layout = tuple((dz, which) for dz, which, _ in pieces)
     return attention(layout, heads, idx, span_ids, query, [p for _, _, p in pieces])
 

time: 79.8 us -> 78.2 us (0.980)
  waiting for transfers between devices: 22 us -> 18.7 us
  starting transfers between devices: 33.9 us -> 35.7 us
    ppermute x18, waiting for transfers between devices: 21.2 us -> 16.4 us  [shift(): return lax.ppermute(x, axis, [(i, (i + by) % n) for i in range(n)])]
    ppermute x18, starting transfers between devices: 26.3 us -> 28.2 us  [shift(): return lax.ppermute(x, axis, [(i, (i + by) % n) for i in range(n)])]
    all_to_all x1, waiting for transfers between devices: 0.78 us -> 2.22 us  [per_device(): lax.all_to_all(copies, ('y', 'xl'), 0, 0, tiled=True).reshape(-1, toks)]
  transfers between devices with their start and end apart: 20 -> 20, of which waited for: 8 -> 11; matrix products, arithmetic and copies ran while one was open for 9% -> 9% of each run, Pallas kernels for 0% -> 0%
where the time goes in v8:
time: 78.2 us; the launch traced here: 77.7 us
  starting transfers between devices  35.7 us (46%)
  waiting for transfers between devices  18.7 us (24%)
  Pallas kernels  15.7 us (20%)
  matrix products  3.14 us (4%)
  local copies, waits for them, and re-layouts  2.48 us (3%)
  other arithmetic  1.6 us (2%)
    ppermute x18, starting transfers between devices, shift(): return lax.ppermute(x, axis, [(i, (i + by) % n) for i in range(n)])  28.2 us
    ppermute x18, waiting for transfers between devices, shift(): return lax.ppermute(x, axis, [(i, (i + by) % n) for i in range(n)])  16.4 us
    pallas_call x1, Pallas kernels, attention(): pl.pallas_call(functools.partial(attention_kernel, layout, heads, min(row...  15.7 us
    all_to_all x1, starting transfers between devices, per_device(): lax.all_to_all(copies, ('y', 'xl'), 0, 0, tiled=True).reshape(-1, toks)  4.19 us
    ppermute x1, starting transfers between devices, per_device(): across = lax.ppermute(own, ('xh', 'xl'), [(0, 3), (3, 0), (1, 2), (2, 1)])  3.31 us
    dot_general x1, matrix products, per_device(): lax.dot_general(features, w_uq, (((0,), (0,)), ((), ())), preferred_eleme...  3.14 us
    all_to_all x1, waiting for transfers between devices, per_device(): lax.all_to_all(copies, ('y', 'xl'), 0, 0, tiled=True).reshape(-1, toks)  2.22 us
    broadcast_in_dim x1, local copies, waits for them, and re-layouts, per_device(): jnp.broadcast_to(compressed.T[None], (ys * xls,) + compressed.T.shape)  1.62 us
  transfers between devices with their start and end apart: 20, of which 11 were waited for; matrix products, arithmetic and copies ran while one was open for 9% of the time, Pallas kernels for 0%

profile of v8, /device:TPU:1, one launch (start us, length us, event | category | flops | bytes accessed | tf_op | source)
XLA Modules:
  0.0 77.7 jit_solution(185853259374014067)
XLA Ops:
  0.0 0.0 copy-start
  0.0 3.3 %collective-permute-start = (bf16[576,128]{1,0:T(8,128)(2,1)}, bf16[576,128]{1,0:T(8,128)(2,1)S(1)}, u32[]{:S(2)}, u32[]{:S(2)}) collective-permute-start(bf16[576,128]{1,0:T(8,128)(2,1)} %bitcast.34), channel_id=1, source_target_pairs={{0,17},{17,0},{1,16},{16,1},{2,19},{19,2},{3,18},{18,3},{4,21},{21... | collective-permute-start | bytes 442376 | tf_op jit(solution)/shard_map/ppermute | solution.py:209
  3.3 0.0 copy-done
  3.3 0.8 copy_bitcast_fusion
  4.1 1.1 %collective-permute-start.1 = (bf16[256,128]{1,0:T(8,128)(2,1)S(1)}, bf16[256,128]{1,0:T(8,128)(2,1)S(1)}, u32[]{:S(2)}, u32[]{:S(2)}) collective-permute-start(bf16[256,128]{1,0:T(8,128)(2,1)S(1)} %pad_maximum_fusion.1), channel_id=1, source_target_pairs={{0,16},{16,0},{1,17},{17,1},{2,18},{18,2},{3,19},{19,3},{4,20},{20... | collective-permute-start | bytes 196616 | tf_op jit(solution)/shard_map/ppermute | solution.py:38
  5.2 0.9 %maximum_bitcast_fusion = bf16[1,832,128]{2,1,0:T(8,128)(2,1)S(1)} fusion(bf16[128,128]{1,0:T(8,128)(2,1)S(1)} %bitcast.33, bf16[128,128]{1,0:T(8,128)(2,1)S(1)} %bitcast.31, bf16[576,128]{1,0:T(8,128)(2,1)} %bitcast.35), kind=kLoop, calls=%fused_computation.2 | loop fusion | flops 638976 | bytes 425984 | tf_op jit(solution)/shard_map/stack | solution.py:212
  6.1 2.8 %collective-permute-done.1 = bf16[256,128]{1,0:T(8,128)(2,1)S(1)} collective-permute-done((bf16[256,128]{1,0:T(8,128)(2,1)S(1)}, bf16[256,128]{1,0:T(8,128)(2,1)S(1)}, u32[]{:S(2)}, u32[]{:S(2)}) %collective-permute-start.1) | collective-permute-done | bytes 65568 | tf_op jit(solution)/shard_map/ppermute | solution.py:38
  8.9 0.0 collective-permute-done
  9.0 0.0 copy-start.1
  9.0 5.5 %collective-permute-start.3 = (bf16[2,832,128]{2,1,0:T(8,128)(2,1)S(1)}, bf16[2,832,128]{2,1,0:T(8,128)(2,1)S(1)}, u32[]{:S(2)}, u32[]{:S(2)}) collective-permute-start(bf16[2,832,128]{2,1,0:T(8,128)(2,1)S(1)} %pad_maximum_fusion.refs_1_.refs_3_), channel_id=1, source_target_pairs={{0,224},{32,0},{64,32},{96,64},{128,96},{160,128},{192,160},{224,1... | collective-permute-start | bytes 1277960 | tf_op jit(solution)/shard_map/ppermute | solution.py:38
  14.5 0.0 collective-permute-start.2
  14.5 1.6 %broadcast_in_dim.2.refs_0_ = bf16[8,192,128]{2,1,0:T(8,128)(2,1)} broadcast(bf16[192,128]{1,0:T(8,128)(2,1)} %bitcast.36), dimensions={1,2} | broadcast | bytes 442368 | tf_op jit(solution)/shard_map/broadcast_in_dim | solution.py:216
  16.2 4.2 %all-to-all-start = ((bf16[8,192,128]{2,1,0:T(8,128)(2,1)}), bf16[8,192,128]{2,1,0:T(8,128)(2,1)S(1)}, u32[]{:S(2)}, u32[]{:S(2)}) async-start(bf16[8,192,128]{2,1,0:T(8,128)(2,1)} %shard_map.64), calls=%async_computation | async-start | bytes 786432 | tf_op jit(solution)/shard_map/all_to_all | solution.py:218
  20.4 1.2 %collective-permute-done.3.refs_5_ = bf16[2,832,128]{2,1,0:T(8,128)(2,1)S(1)} collective-permute-done((bf16[2,832,128]{2,1,0:T(8,128)(2,1)S(1)}, bf16[2,832,128]{2,1,0:T(8,128)(2,1)S(1)}, u32[]{:S(2)}, u32[]{:S(2)}) %collective-permute-start.3) | collective-permute-done | bytes 426016 | tf_op jit(solution)/shard_map/ppermute | solution.py:38
  21.5 3.4 %collective-permute-start.5 = (bf16[2,832,128]{2,1,0:T(8,128)(2,1)S(1)}, bf16[2,832,128]{2,1,0:T(8,128)(2,1)}, u32[]{:S(2)}, u32[]{:S(2)}) collective-permute-start(bf16[2,832,128]{2,1,0:T(8,128)(2,1)S(1)} %collective-permute-done.3.refs_5_), channel_id=1, source_target_pairs={{0,224},{32,0},{64,32},{96,64},{128,96},{160,128},{192,160},{224,1... | collective-permute-start | bytes 1277960 | tf_op jit(solution)/shard_map/ppermute | solution.py:38
  25.0 0.0 collective-permute-done.2.refs_4_
  25.0 0.0 collective-permute-start.4
  25.0 2.2 %all-to-all-done = bf16[8,192,128]{2,1,0:T(8,128)(2,1)S(1)} async-done(((bf16[8,192,128]{2,1,0:T(8,128)(2,1)}), bf16[8,192,128]{2,1,0:T(8,128)(2,1)S(1)}, u32[]{:S(2)}, u32[]{:S(2)}) %all-to-all-start) | async-done | bytes 393248 | tf_op jit(solution)/shard_map/all_to_all | solution.py:218
  27.2 3.1 %convolution_convert_fusion.refs_2_ = bf16[128,1536]{1,0:T(8,128)(2,1)S(1)} fusion(bf16[1536,128]{1,0:T(8,128)(2,1)S(1)} %bitcast.29, bf16[1536,1536]{1,0:T(8,128)(2,1)} %param.8), kind=kOutput, calls=%fused_computation | convolution fusion | flops 604176384 | bytes 5505024 | tf_op jit(solution)/shard_map/dot_general | solution.py:219
  30.3 0.0 copy-start.2
  30.4 0.7 collective-permute-done.5.refs_1_
  31.0 0.0 copy-done.13
  31.0 3.1 %collective-permute-done.4.refs_0_ = bf16[2,832,128]{2,1,0:T(8,128)(2,1)S(1)} collective-permute-done((bf16[2,832,128]{2,1,0:T(8,128)(2,1)S(1)}, bf16[2,832,128]{2,1,0:T(8,128)(2,1)S(1)}, u32[]{:S(2)}, u32[]{:S(2)}) %collective-permute-start.4) | collective-permute-done | bytes 426016 | tf_op jit(solution)/shard_map/ppermute | solution.py:38
  34.2 0.0 collective-permute-start.11
  34.2 2.7 %collective-permute-start.12 = (bf16[2,832,128]{2,1,0:T(8,128)(2,1)}, bf16[2,832,128]{2,1,0:T(8,128)(2,1)S(1)}, u32[]{:S(2)}, u32[]{:S(2)}) collective-permute-start(bf16[2,832,128]{2,1,0:T(8,128)(2,1)} %get-tuple-element.12.refs_7_), channel_id=1, source_target_pairs={{0,224},{32,0},{64,32},{96,64},{128,96},{160,128},{192,160},{224,1... | collective-permute-start | bytes 1277960 | tf_op jit(solution)/shard_map/ppermute | solution.py:38
  36.9 4.8 %collective-permute-start.6 = (bf16[2,832,128]{2,1,0:T(8,128)(2,1)S(1)}, bf16[2,832,128]{2,1,0:T(8,128)(2,1)S(1)}, u32[]{:S(2)}, u32[]{:S(2)}) collective-permute-start(bf16[2,832,128]{2,1,0:T(8,128)(2,1)S(1)} %pad_maximum_fusion.refs_1_.refs_3_), channel_id=1, source_target_pairs={{0,8},{8,0},{1,9},{9,1},{2,10},{10,2},{3,11},{11,3},{4,12},{12,4},... | collective-permute-start | bytes 1277960 | tf_op jit(solution)/shard_map/ppermute | solution.py:38
  41.6 0.0 collective-permute-start.8
  41.7 0.5 collective-permute-start.7
  42.2 0.2 collective-permute-done.11.refs_0_
  42.4 5.4 %collective-permute-start.9 = (bf16[2,832,128]{2,1,0:T(8,128)(2,1)}, bf16[2,832,128]{2,1,0:T(8,128)(2,1)S(1)}, u32[]{:S(2)}, u32[]{:S(2)}) collective-permute-start(bf16[2,832,128]{2,1,0:T(8,128)(2,1)} %copy-done.10), channel_id=1, source_target_pairs={{0,8},{8,0},{1,9},{9,1},{2,10},{10,2},{3,11},{11,3},{4,12},{12,4},... | collective-permute-start | bytes 1277960 | tf_op jit(solution)/shard_map/ppermute | solution.py:38
  47.8 0.0 collective-permute-done.12.refs_1_
  47.8 0.0 collective-permute-start.10
  47.8 0.0 collective-permute-done.6.refs_2_.refs_8_
  47.8 0.0 copy-start.5
  47.8 0.0 collective-permute-done.8.refs_4_.refs_10_
  47.9 0.0 collective-permute-done.7.refs_3_.refs_9_
  47.9 1.5 %collective-permute-done.9.refs_5_.refs_11_ = bf16[2,832,128]{2,1,0:T(8,128)(2,1)S(1)} collective-permute-done((bf16[2,832,128]{2,1,0:T(8,128)(2,1)}, bf16[2,832,128]{2,1,0:T(8,128)(2,1)S(1)}, u32[]{:S(2)}, u32[]{:S(2)}) %collective-permute-start.9) | collective-permute-done | bytes 426016 | tf_op jit(solution)/shard_map/ppermute | solution.py:38
  49.4 0.6 collective-permute-done.10.refs_6_.refs_12_
  50.0 0.0 collective-permute-start.13
  50.0 2.7 %collective-permute-start.14 = (bf16[1,832,128]{2,1,0:T(8,128)(2,1)S(1)}, bf16[1,832,128]{2,1,0:T(8,128)(2,1)S(1)}, u32[]{:S(2)}, u32[]{:S(2)}) collective-permute-start(bf16[1,832,128]{2,1,0:T(8,128)(2,1)S(1)} %get-tuple-element.14), channel_id=1, source_target_pairs={{0,224},{32,0},{64,32},{96,64},{128,96},{160,128},{192,160},{224,1... | collective-permute-start | bytes 638984 | tf_op jit(solution)/shard_map/ppermute | solution.py:38
  52.6 5.0 %collective-permute-done.13.refs_2_.refs_15_ = bf16[1,832,128]{2,1,0:T(8,128)(2,1)S(1)} collective-permute-done((bf16[1,832,128]{2,1,0:T(8,128)(2,1)S(1)}, bf16[1,832,128]{2,1,0:T(8,128)(2,1)S(1)}, u32[]{:S(2)}, u32[]{:S(2)}) %collective-permute-start.13) | collective-permute-done | bytes 213024 | tf_op jit(solution)/shard_map/ppermute | solution.py:38
  57.7 0.0 collective-permute-done.14.refs_3_.refs_16_
  57.7 0.0 copy-start.3
  57.7 0.0 copy-start.4
  57.7 1.3 %collective-permute-start.15 = (bf16[2,832,128]{2,1,0:T(8,128)(2,1)S(1)}, bf16[2,832,128]{2,1,0:T(8,128)(2,1)}, u32[]{:S(2)}, u32[]{:S(2)}) collective-permute-start(bf16[2,832,128]{2,1,0:T(8,128)(2,1)S(1)} %get-tuple-element.15.refs_13_), channel_id=1, source_target_pairs={{0,8},{8,0},{1,9},{9,1},{2,10},{10,2},{3,11},{11,3},{4,12},{12,4},... | collective-permute-start | bytes 1277960 | tf_op jit(solution)/shard_map/ppermute | solution.py:38
  59.0 0.0 copy-done.9
  59.0 0.3 collective-permute-start.16
  59.3 0.2 collective-permute-start.17
  59.5 0.3 collective-permute-start.18
  59.8 0.6 pad_add_fusion.refs_0_
  60.4 1.0 %collective-permute-done.17.refs_19_ = bf16[1,832,128]{2,1,0:T(8,128)(2,1)} collective-permute-done((bf16[1,832,128]{2,1,0:T(8,128)(2,1)S(1)}, bf16[1,832,128]{2,1,0:T(8,128)(2,1)}, u32[]{:S(2)}, u32[]{:S(2)}) %collective-permute-start.17) | collective-permute-done | bytes 213024 | tf_op jit(solution)/shard_map/ppermute | solution.py:38
  61.4 0.3 collective-permute-done.18.refs_20_
  61.7 0.0 collective-permute-done.15.refs_17_
  61.7 0.0 collective-permute-done.16.refs_18_
  61.7 0.0 copy-done.2
  61.7 0.0 copy-done.5
  61.7 0.0 copy-done.6
  61.8 0.0 copy-done.7
  61.8 0.0 copy-done.8
  61.8 0.0 copy-done.11
  61.8 0.0 copy-done.12
  61.8 0.0 copy-done.3
  61.8 0.0 copy-done.4
  61.8 15.7 %shard_map.68 = bf16[128,1024]{1,0:T(8,128)(2,1)} custom-call(s32[4]{0:T(128)} %pad_add_fusion.refs_0_, s32[64]{0:T(128)} %refs_1_.1, bf16[128,1536]{1,0:T(8,128)(2,1)} %copy-done.2, bf16[2,832,128]{2,1,0:T(8,128)(2,1)} %copy-done.1, bf16[2,832,128]{2,1,0:T(8,128)(2,1)} %copy-done.14, bf16[2,832,128]{2,1,0:T(8,128)(2,1)} %copy-done.13, ...), custom_call_target="tpu_custom_call" | custom-call | flops 5704253440 | bytes 7209232 | tf_op jit(solution)/shard_map/pallas_call | solution.py:177
  (22 shorter events, 0.1 us)
Async XLA Ops:
  0.0 3.3 %copy-start = (bf16[16,1024]{1,0:T(8,128)(2,1)S(1)}, bf16[16,1024]{1,0:T(8,128)(2,1)}, u32[]{:S(2)}) copy-start(bf16[16,1024]{1,0:T(8,128)(2,1)} %param.9) | copy-start | bytes 98308
  0.0 8.9 %collective-permute-start = (bf16[576,128]{1,0:T(8,128)(2,1)}, bf16[576,128]{1,0:T(8,128)(2,1)S(1)}, u32[]{:S(2)}, u32[]{:S(2)}) collective-permute-start(bf16[576,128]{1,0:T(8,128)(2,1)} %bitcast.34), channel_id=1, source_target_pairs={{0,17},{17,0},{1,16},{16,1},{2,19},{19,2},{3,18},{18,3},{4,21},{21... | collective-permute-start | bytes 442376 | tf_op jit(solution)/shard_map/ppermute | solution.py:209
  4.1 4.8 %collective-permute-start.1 = (bf16[256,128]{1,0:T(8,128)(2,1)S(1)}, bf16[256,128]{1,0:T(8,128)(2,1)S(1)}, u32[]{:S(2)}, u32[]{:S(2)}) collective-permute-start(bf16[256,128]{1,0:T(8,128)(2,1)S(1)} %pad_maximum_fusion.1), channel_id=1, source_target_pairs={{0,16},{16,0},{1,17},{17,1},{2,18},{18,2},{3,19},{19,3},{4,20},{20... | collective-permute-start | bytes 196616 | tf_op jit(solution)/shard_map/ppermute | solution.py:38
  9.0 38.8 %copy-start.1 = (bf16[2,832,128]{2,1,0:T(8,128)(2,1)}, bf16[2,832,128]{2,1,0:T(8,128)(2,1)S(1)}, u32[]{:S(2)}) copy-start(bf16[2,832,128]{2,1,0:T(8,128)(2,1)S(1)} %pad_maximum_fusion.refs_1_.refs_3_) | copy-start | bytes 1277956
  9.0 12.5 %collective-permute-start.3 = (bf16[2,832,128]{2,1,0:T(8,128)(2,1)S(1)}, bf16[2,832,128]{2,1,0:T(8,128)(2,1)S(1)}, u32[]{:S(2)}, u32[]{:S(2)}) collective-permute-start(bf16[2,832,128]{2,1,0:T(8,128)(2,1)S(1)} %pad_maximum_fusion.refs_1_.refs_3_), channel_id=1, source_target_pairs={{0,224},{32,0},{64,32},{96,64},{128,96},{160,128},{192,160},{224,1... | collective-permute-start | bytes 1277960 | tf_op jit(solution)/shard_map/ppermute | solution.py:38
  14.5 10.4 %collective-permute-start.2 = (bf16[2,832,128]{2,1,0:T(8,128)(2,1)S(1)}, bf16[2,832,128]{2,1,0:T(8,128)(2,1)S(1)}, u32[]{:S(2)}, u32[]{:S(2)}) collective-permute-start(bf16[2,832,128]{2,1,0:T(8,128)(2,1)S(1)} %pad_maximum_fusion.refs_1_.refs_3_), channel_id=1, source_target_pairs={{0,32},{32,64},{64,96},{96,128},{128,160},{160,192},{192,224},{224... | collective-permute-start | bytes 1277960 | tf_op jit(solution)/shard_map/ppermute | solution.py:38
  16.2 11.0 %all-to-all-start = ((bf16[8,192,128]{2,1,0:T(8,128)(2,1)}), bf16[8,192,128]{2,1,0:T(8,128)(2,1)S(1)}, u32[]{:S(2)}, u32[]{:S(2)}) async-start(bf16[8,192,128]{2,1,0:T(8,128)(2,1)} %shard_map.64), calls=%async_computation | async-start | bytes 786432 | tf_op jit(solution)/shard_map/all_to_all | solution.py:218
  21.5 9.5 %copy-start.13 = (bf16[2,832,128]{2,1,0:T(8,128)(2,1)}, bf16[2,832,128]{2,1,0:T(8,128)(2,1)S(1)}, u32[]{:S(2)}) copy-start(bf16[2,832,128]{2,1,0:T(8,128)(2,1)S(1)} %collective-permute-done.3.refs_5_) | copy-start | bytes 1277956
  21.5 9.5 %collective-permute-start.5 = (bf16[2,832,128]{2,1,0:T(8,128)(2,1)S(1)}, bf16[2,832,128]{2,1,0:T(8,128)(2,1)}, u32[]{:S(2)}, u32[]{:S(2)}) collective-permute-start(bf16[2,832,128]{2,1,0:T(8,128)(2,1)S(1)} %collective-permute-done.3.refs_5_), channel_id=1, source_target_pairs={{0,224},{32,0},{64,32},{96,64},{128,96},{160,128},{192,160},{224,1... | collective-permute-start | bytes 1277960 | tf_op jit(solution)/shard_map/ppermute | solution.py:38
  25.0 6.1 %copy-start.14 = (bf16[2,832,128]{2,1,0:T(8,128)(2,1)}, bf16[2,832,128]{2,1,0:T(8,128)(2,1)S(1)}, u32[]{:S(2)}) copy-start(bf16[2,832,128]{2,1,0:T(8,128)(2,1)S(1)} %collective-permute-done.2.refs_4_) | copy-start | bytes 1277956
  25.0 9.2 %collective-permute-start.4 = (bf16[2,832,128]{2,1,0:T(8,128)(2,1)S(1)}, bf16[2,832,128]{2,1,0:T(8,128)(2,1)S(1)}, u32[]{:S(2)}, u32[]{:S(2)}) collective-permute-start(bf16[2,832,128]{2,1,0:T(8,128)(2,1)S(1)} %collective-permute-done.2.refs_4_), channel_id=1, source_target_pairs={{0,32},{32,64},{64,96},{96,128},{128,160},{160,192},{192,224},{224... | collective-permute-start | bytes 1277960 | tf_op jit(solution)/shard_map/ppermute | solution.py:38
  30.3 31.4 %copy-start.2 = (bf16[128,1536]{1,0:T(8,128)(2,1)}, bf16[128,1536]{1,0:T(8,128)(2,1)S(1)}, u32[]{:S(2)}) copy-start(bf16[128,1536]{1,0:T(8,128)(2,1)S(1)} %convolution_convert_fusion.refs_2_) | copy-start | bytes 1179652
  34.2 8.0 %copy-start.10 = (bf16[2,832,128]{2,1,0:T(8,128)(2,1)}, bf16[2,832,128]{2,1,0:T(8,128)(2,1)S(1)}, u32[]{:S(2)}) copy-start(bf16[2,832,128]{2,1,0:T(8,128)(2,1)S(1)} %get-tuple-element.11.refs_6_) | copy-start | bytes 1277956
  34.2 8.2 %collective-permute-start.11 = (bf16[2,832,128]{2,1,0:T(8,128)(2,1)S(1)}, bf16[2,832,128]{2,1,0:T(8,128)(2,1)S(1)}, u32[]{:S(2)}, u32[]{:S(2)}) collective-permute-start(bf16[2,832,128]{2,1,0:T(8,128)(2,1)S(1)} %get-tuple-element.11.refs_6_), channel_id=1, source_target_pairs={{0,32},{32,64},{64,96},{96,128},{128,160},{160,192},{192,224},{224... | collective-permute-start | bytes 1277960 | tf_op jit(solution)/shard_map/ppermute | solution.py:38
  34.2 13.6 %collective-permute-start.12 = (bf16[2,832,128]{2,1,0:T(8,128)(2,1)}, bf16[2,832,128]{2,1,0:T(8,128)(2,1)S(1)}, u32[]{:S(2)}, u32[]{:S(2)}) collective-permute-start(bf16[2,832,128]{2,1,0:T(8,128)(2,1)} %get-tuple-element.12.refs_7_), channel_id=1, source_target_pairs={{0,224},{32,0},{64,32},{96,64},{128,96},{160,128},{192,160},{224,1... | collective-permute-start | bytes 1277960 | tf_op jit(solution)/shard_map/ppermute | solution.py:38
  36.9 11.0 %collective-permute-start.6 = (bf16[2,832,128]{2,1,0:T(8,128)(2,1)S(1)}, bf16[2,832,128]{2,1,0:T(8,128)(2,1)S(1)}, u32[]{:S(2)}, u32[]{:S(2)}) collective-permute-start(bf16[2,832,128]{2,1,0:T(8,128)(2,1)S(1)} %pad_maximum_fusion.refs_1_.refs_3_), channel_id=1, source_target_pairs={{0,8},{8,0},{1,9},{9,1},{2,10},{10,2},{3,11},{11,3},{4,12},{12,4},... | collective-permute-start | bytes 1277960 | tf_op jit(solution)/shard_map/ppermute | solution.py:38
  41.6 6.2 %collective-permute-start.8 = (bf16[2,832,128]{2,1,0:T(8,128)(2,1)}, bf16[2,832,128]{2,1,0:T(8,128)(2,1)S(1)}, u32[]{:S(2)}, u32[]{:S(2)}) collective-permute-start(bf16[2,832,128]{2,1,0:T(8,128)(2,1)} %copy-done.13), channel_id=1, source_target_pairs={{0,8},{8,0},{1,9},{9,1},{2,10},{10,2},{3,11},{11,3},{4,12},{12,4},... | collective-permute-start | bytes 1277960 | tf_op jit(solution)/shard_map/ppermute | solution.py:38
  41.7 6.2 %collective-permute-start.7 = (bf16[2,832,128]{2,1,0:T(8,128)(2,1)}, bf16[2,832,128]{2,1,0:T(8,128)(2,1)S(1)}, u32[]{:S(2)}, u32[]{:S(2)}) collective-permute-start(bf16[2,832,128]{2,1,0:T(8,128)(2,1)} %copy-done.14), channel_id=1, source_target_pairs={{0,8},{8,0},{1,9},{9,1},{2,10},{10,2},{3,11},{11,3},{4,12},{12,4},... | collective-permute-start | bytes 1277960 | tf_op jit(solution)/shard_map/ppermute | solution.py:38
  42.4 7.0 %collective-permute-start.9 = (bf16[2,832,128]{2,1,0:T(8,128)(2,1)}, bf16[2,832,128]{2,1,0:T(8,128)(2,1)S(1)}, u32[]{:S(2)}, u32[]{:S(2)}) collective-permute-start(bf16[2,832,128]{2,1,0:T(8,128)(2,1)} %copy-done.10), channel_id=1, source_target_pairs={{0,8},{8,0},{1,9},{9,1},{2,10},{10,2},{3,11},{11,3},{4,12},{12,4},... | collective-permute-start | bytes 1277960 | tf_op jit(solution)/shard_map/ppermute | solution.py:38
  47.8 2.2 %collective-permute-start.10 = (bf16[2,832,128]{2,1,0:T(8,128)(2,1)}, bf16[2,832,128]{2,1,0:T(8,128)(2,1)S(1)}, u32[]{:S(2)}, u32[]{:S(2)}) collective-permute-start(bf16[2,832,128]{2,1,0:T(8,128)(2,1)} %get-tuple-element.12.refs_7_), channel_id=1, source_target_pairs={{0,8},{8,0},{1,9},{9,1},{2,10},{10,2},{3,11},{11,3},{4,12},{12,4},... | collective-permute-start | bytes 1277960 | tf_op jit(solution)/shard_map/ppermute | solution.py:38
  47.8 13.9 %copy-start.5 = (bf16[2,832,128]{2,1,0:T(8,128)(2,1)}, bf16[2,832,128]{2,1,0:T(8,128)(2,1)S(1)}, u32[]{:S(2)}) copy-start(bf16[2,832,128]{2,1,0:T(8,128)(2,1)S(1)} %collective-permute-done.6.refs_2_.refs_8_) | copy-start | bytes 1277956
  47.8 13.9 %copy-start.6 = (bf16[2,832,128]{2,1,0:T(8,128)(2,1)}, bf16[2,832,128]{2,1,0:T(8,128)(2,1)S(1)}, u32[]{:S(2)}) copy-start(bf16[2,832,128]{2,1,0:T(8,128)(2,1)S(1)} %collective-permute-done.8.refs_4_.refs_10_) | copy-start | bytes 1277956
  47.9 13.9 %copy-start.7 = (bf16[2,832,128]{2,1,0:T(8,128)(2,1)}, bf16[2,832,128]{2,1,0:T(8,128)(2,1)S(1)}, u32[]{:S(2)}) copy-start(bf16[2,832,128]{2,1,0:T(8,128)(2,1)S(1)} %collective-permute-done.7.refs_3_.refs_9_) | copy-start | bytes 1277956
  49.4 12.4 %copy-start.8 = (bf16[2,832,128]{2,1,0:T(8,128)(2,1)}, bf16[2,832,128]{2,1,0:T(8,128)(2,1)S(1)}, u32[]{:S(2)}) copy-start(bf16[2,832,128]{2,1,0:T(8,128)(2,1)S(1)} %collective-permute-done.9.refs_5_.refs_11_) | copy-start | bytes 1277956
  50.0 9.0 %copy-start.9 = (bf16[2,832,128]{2,1,0:T(8,128)(2,1)}, bf16[2,832,128]{2,1,0:T(8,128)(2,1)S(1)}, u32[]{:S(2)}) copy-start(bf16[2,832,128]{2,1,0:T(8,128)(2,1)S(1)} %collective-permute-done.10.refs_6_.refs_12_) | copy-start | bytes 1277956
  50.0 7.7 %collective-permute-start.13 = (bf16[1,832,128]{2,1,0:T(8,128)(2,1)S(1)}, bf16[1,832,128]{2,1,0:T(8,128)(2,1)S(1)}, u32[]{:S(2)}, u32[]{:S(2)}) collective-permute-start(bf16[1,832,128]{2,1,0:T(8,128)(2,1)S(1)} %get-tuple-element.13), channel_id=1, source_target_pairs={{0,32},{32,64},{64,96},{96,128},{128,160},{160,192},{192,224},{224... | collective-permute-start | bytes 638984 | tf_op jit(solution)/shard_map/ppermute | solution.py:38
  50.0 7.7 %collective-permute-start.14 = (bf16[1,832,128]{2,1,0:T(8,128)(2,1)S(1)}, bf16[1,832,128]{2,1,0:T(8,128)(2,1)S(1)}, u32[]{:S(2)}, u32[]{:S(2)}) collective-permute-start(bf16[1,832,128]{2,1,0:T(8,128)(2,1)S(1)} %get-tuple-element.14), channel_id=1, source_target_pairs={{0,224},{32,0},{64,32},{96,64},{128,96},{160,128},{192,160},{224,1... | collective-permute-start | bytes 638984 | tf_op jit(solution)/shard_map/ppermute | solution.py:38
  57.6 4.1 %copy-start.11 = (bf16[1,832,128]{2,1,0:T(8,128)(2,1)}, bf16[1,832,128]{2,1,0:T(8,128)(2,1)S(1)}, u32[]{:S(2)}) copy-start(bf16[1,832,128]{2,1,0:T(8,128)(2,1)S(1)} %collective-permute-done.13.refs_2_.refs_15_) | copy-start | bytes 638980
  57.7 4.1 %copy-start.12 = (bf16[1,832,128]{2,1,0:T(8,128)(2,1)}, bf16[1,832,128]{2,1,0:T(8,128)(2,1)S(1)}, u32[]{:S(2)}) copy-start(bf16[1,832,128]{2,1,0:T(8,128)(2,1)S(1)} %collective-permute-done.14.refs_3_.refs_16_) | copy-start | bytes 638980
  57.7 4.1 %copy-start.3 = (bf16[2,832,128]{2,1,0:T(8,128)(2,1)}, bf16[2,832,128]{2,1,0:T(8,128)(2,1)S(1)}, u32[]{:S(2)}) copy-start(bf16[2,832,128]{2,1,0:T(8,128)(2,1)S(1)} %get-tuple-element.15.refs_13_) | copy-start | bytes 1277956
  57.7 4.1 %copy-start.4 = (bf16[2,832,128]{2,1,0:T(8,128)(2,1)}, bf16[2,832,128]{2,1,0:T(8,128)(2,1)S(1)}, u32[]{:S(2)}) copy-start(bf16[2,832,128]{2,1,0:T(8,128)(2,1)S(1)} %get-tuple-element.16.refs_14_) | copy-start | bytes 1277956
  57.7 4.0 %collective-permute-start.15 = (bf16[2,832,128]{2,1,0:T(8,128)(2,1)S(1)}, bf16[2,832,128]{2,1,0:T(8,128)(2,1)}, u32[]{:S(2)}, u32[]{:S(2)}) collective-permute-start(bf16[2,832,128]{2,1,0:T(8,128)(2,1)S(1)} %get-tuple-element.15.refs_13_), channel_id=1, source_target_pairs={{0,8},{8,0},{1,9},{9,1},{2,10},{10,2},{3,11},{11,3},{4,12},{12,4},... | collective-permute-start | bytes 1277960 | tf_op jit(solution)/shard_map/ppermute | solution.py:38
  59.0 2.8 %collective-permute-start.16 = (bf16[2,832,128]{2,1,0:T(8,128)(2,1)S(1)}, bf16[2,832,128]{2,1,0:T(8,128)(2,1)}, u32[]{:S(2)}, u32[]{:S(2)}) collective-permute-start(bf16[2,832,128]{2,1,0:T(8,128)(2,1)S(1)} %get-tuple-element.16.refs_14_), channel_id=1, source_target_pairs={{0,8},{8,0},{1,9},{9,1},{2,10},{10,2},{3,11},{11,3},{4,12},{12,4},... | collective-permute-start | bytes 1277960 | tf_op jit(solution)/shard_map/ppermute | solution.py:38
  59.3 2.1 %collective-permute-start.17 = (bf16[1,832,128]{2,1,0:T(8,128)(2,1)S(1)}, bf16[1,832,128]{2,1,0:T(8,128)(2,1)}, u32[]{:S(2)}, u32[]{:S(2)}) collective-permute-start(bf16[1,832,128]{2,1,0:T(8,128)(2,1)S(1)} %collective-permute-done.13.refs_2_.refs_15_), channel_id=1, source_target_pairs={{0,8},{8,0},{1,9},{9,1},{2,10},{10,2},{3,11},{11,3},{4,12},{12,4},... | collective-permute-start | bytes 638984 | tf_op jit(solution)/shard_map/ppermute | solution.py:38
  59.5 2.2 %collective-permute-start.18 = (bf16[1,832,128]{2,1,0:T(8,128)(2,1)S(1)}, bf16[1,832,128]{2,1,0:T(8,128)(2,1)}, u32[]{:S(2)}, u32[]{:S(2)}) collective-permute-start(bf16[1,832,128]{2,1,0:T(8,128)(2,1)S(1)} %collective-permute-done.14.refs_3_.refs_16_), channel_id=1, source_target_pairs={{0,8},{8,0},{1,9},{9,1},{2,10},{10,2},{3,11},{11,3},{4,12},{12,4},... | collective-permute-start | bytes 638984 | tf_op jit(solution)/shard_map/ppermute | solution.py:38

commit v9 on v8

--- a/solution.py
+++ b/solution.py
@@ -226,24 +226,19 @@
         for dz, which, piece in some
     ]
     half = zs // 2
-    pieces = [(0, both, here)]
+    pieces, late = [(0, both, here)], []
     ahead = behind = here
     for k in range(1, half):
         ahead, behind = shift(ahead, "z", 1), shift(behind, "z", -1)
         if k == half - 2:
             ahead, behind = gate([ahead, behind], query)
-        if k < half - 1:
-            pieces += [(-k, both, ahead), (k, both, behind)]
+        (pieces if k < half - 2 else late).extend([(-k, both, ahead), (k, both, behind)])
     pieces += hand(pieces)
     last = gate([ahead[:1], behind[1:]], *(piece for _, _, piece in pieces[len(pieces) // 2 :]))
+    moved = gate([piece for _, _, piece in late], *last)
+    late = [(dz, which, piece) for (dz, which, _), piece in zip(late, moved)]
     last = [shift(last[0], "z", 1), shift(last[1], "z", -1)]
-    ahead, behind = gate([ahead, behind], *last)
-    late = [
-        (1 - half, both, ahead),
-        (half - 1, both, behind),
-        (-half, first_xh, last[0]),
-        (half, second_xh, last[1]),
-    ]
+    late += [(-half, first_xh, last[0]), (half, second_xh, last[1])]
     pieces += late + hand(late)
     layout = tuple((dz, which) for dz, which, _ in pieces)
     return attention(layout, heads, idx, span_ids, query, [p for _, _, p in pieces])

time: 78.2 us -> 76 us (0.972)
  waiting for transfers between devices: 18.7 us -> 13.8 us
  starting transfers between devices: 35.7 us -> 37.1 us
  local copies, waits for them, and re-layouts: 2.48 us -> 3.83 us
    ppermute x18, waiting for transfers between devices: 16.4 us -> 11.6 us  [shift(): return lax.ppermute(x, axis, [(i, (i + by) % n) for i in range(n)])]
    ppermute x18, starting transfers between devices: 28.2 us -> 29.6 us  [shift(): return lax.ppermute(x, axis, [(i, (i + by) % n) for i in range(n)])]
    unnamed x30, local copies, waits for them, and re-layouts: 0.06 us -> 1.4 us
where the time goes in v9:
time: 76 us; the launch traced here: 75.7 us
  starting transfers between devices  37.1 us (49%)
  Pallas kernels  15.9 us (21%)
  waiting for transfers between devices  13.8 us (18%)
  local copies, waits for them, and re-layouts  3.83 us (5%)
  matrix products  3.14 us (4%)
  other arithmetic  1.6 us (2%)
    ppermute x18, starting transfers between devices, shift(): return lax.ppermute(x, axis, [(i, (i + by) % n) for i in range(n)])  29.6 us
    pallas_call x1, Pallas kernels, attention(): pl.pallas_call(functools.partial(attention_kernel, layout, heads, min(row...  15.9 us
    ppermute x18, waiting for transfers between devices, shift(): return lax.ppermute(x, axis, [(i, (i + by) % n) for i in range(n)])  11.6 us
    all_to_all x1, starting transfers between devices, per_device(): lax.all_to_all(copies, ('y', 'xl'), 0, 0, tiled=True).reshape(-1, toks)  4.19 us
    ppermute x1, starting transfers between devices, per_device(): across = lax.ppermute(own, ('xh', 'xl'), [(0, 3), (3, 0), (1, 2), (2, 1)])  3.31 us
    dot_general x1, matrix products, per_device(): lax.dot_general(features, w_uq, (((0,), (0,)), ((), ())), preferred_eleme...  3.14 us
    all_to_all x1, waiting for transfers between devices, per_device(): lax.all_to_all(copies, ('y', 'xl'), 0, 0, tiled=True).reshape(-1, toks)  2.22 us
    broadcast_in_dim x1, local copies, waits for them, and re-layouts, per_device(): jnp.broadcast_to(compressed.T[None], (ys * xls,) + compressed.T.shape)  1.62 us
  transfers between devices with their start and end apart: 20, of which 11 were waited for; matrix products, arithmetic and copies ran while one was open for 9% of the time, Pallas kernels for 0%

profile of v9, /device:TPU:1, one launch (start us, length us, event | category | flops | bytes accessed | tf_op | source)
XLA Modules:
  0.0 75.7 jit_solution(9829249489017715004)
XLA Ops:
  0.0 0.0 copy-start
  0.0 3.3 %collective-permute-start = (bf16[576,128]{1,0:T(8,128)(2,1)}, bf16[576,128]{1,0:T(8,128)(2,1)S(1)}, u32[]{:S(2)}, u32[]{:S(2)}) collective-permute-start(bf16[576,128]{1,0:T(8,128)(2,1)} %bitcast.34), channel_id=1, source_target_pairs={{0,17},{17,0},{1,16},{16,1},{2,19},{19,2},{3,18},{18,3},{4,21},{21... | collective-permute-start | bytes 442376 | tf_op jit(solution)/shard_map/ppermute | solution.py:209
  3.3 0.0 copy-done
  3.3 0.8 %copy_bitcast_fusion = bf16[16,8,128]{2,0,1:T(8,128)(2,1)S(1)} fusion(bf16[16,1024]{1,0:T(8,128)(2,1)} %param.10), kind=kLoop, calls=%fused_computation.5 | loop fusion | bytes 65536 | tf_op jit(solution)/shard_map/reshape | solution.py:51
  4.1 1.1 %collective-permute-start.1 = (bf16[256,128]{1,0:T(8,128)(2,1)S(1)}, bf16[256,128]{1,0:T(8,128)(2,1)S(1)}, u32[]{:S(2)}, u32[]{:S(2)}) collective-permute-start(bf16[256,128]{1,0:T(8,128)(2,1)S(1)} %pad_maximum_fusion.1), channel_id=1, source_target_pairs={{0,16},{16,0},{1,17},{17,1},{2,18},{18,2},{3,19},{19,3},{4,20},{20... | collective-permute-start | bytes 196616 | tf_op jit(solution)/shard_map/ppermute | solution.py:38
  5.2 0.9 %maximum_bitcast_fusion = bf16[1,832,128]{2,1,0:T(8,128)(2,1)S(1)} fusion(bf16[128,128]{1,0:T(8,128)(2,1)S(1)} %bitcast.33, bf16[128,128]{1,0:T(8,128)(2,1)S(1)} %bitcast.31, bf16[576,128]{1,0:T(8,128)(2,1)} %bitcast.35), kind=kLoop, calls=%fused_computation.2 | loop fusion | flops 638976 | bytes 425984 | tf_op jit(solution)/shard_map/stack | solution.py:212
  6.1 2.8 %collective-permute-done.1 = bf16[256,128]{1,0:T(8,128)(2,1)S(1)} collective-permute-done((bf16[256,128]{1,0:T(8,128)(2,1)S(1)}, bf16[256,128]{1,0:T(8,128)(2,1)S(1)}, u32[]{:S(2)}, u32[]{:S(2)}) %collective-permute-start.1) | collective-permute-done | bytes 65568 | tf_op jit(solution)/shard_map/ppermute | solution.py:38
  8.9 0.0 collective-permute-done
  9.0 0.0 copy-start.1
  9.0 5.5 %collective-permute-start.3 = (bf16[2,832,128]{2,1,0:T(8,128)(2,1)S(1)}, bf16[2,832,128]{2,1,0:T(8,128)(2,1)S(1)}, u32[]{:S(2)}, u32[]{:S(2)}) collective-permute-start(bf16[2,832,128]{2,1,0:T(8,128)(2,1)S(1)} %pad_maximum_fusion.refs_1_.refs_3_), channel_id=1, source_target_pairs={{0,224},{32,0},{64,32},{96,64},{128,96},{160,128},{192,160},{224,1... | collective-permute-start | bytes 1277960 | tf_op jit(solution)/shard_map/ppermute | solution.py:38
  14.5 0.0 collective-permute-start.2
  14.5 1.6 %broadcast_in_dim.2.refs_0_ = bf16[8,192,128]{2,1,0:T(8,128)(2,1)} broadcast(bf16[192,128]{1,0:T(8,128)(2,1)} %bitcast.36), dimensions={1,2} | broadcast | bytes 442368 | tf_op jit(solution)/shard_map/broadcast_in_dim | solution.py:216
  16.2 4.2 %all-to-all-start = ((bf16[8,192,128]{2,1,0:T(8,128)(2,1)}), bf16[8,192,128]{2,1,0:T(8,128)(2,1)S(1)}, u32[]{:S(2)}, u32[]{:S(2)}) async-start(bf16[8,192,128]{2,1,0:T(8,128)(2,1)} %shard_map.64), calls=%async_computation | async-start | bytes 786432 | tf_op jit(solution)/shard_map/all_to_all | solution.py:218
  20.4 1.2 %collective-permute-done.3.refs_5_ = bf16[2,832,128]{2,1,0:T(8,128)(2,1)S(1)} collective-permute-done((bf16[2,832,128]{2,1,0:T(8,128)(2,1)S(1)}, bf16[2,832,128]{2,1,0:T(8,128)(2,1)S(1)}, u32[]{:S(2)}, u32[]{:S(2)}) %collective-permute-start.3) | collective-permute-done | bytes 426016 | tf_op jit(solution)/shard_map/ppermute | solution.py:38
  21.5 3.4 %collective-permute-start.8 = (bf16[2,832,128]{2,1,0:T(8,128)(2,1)S(1)}, bf16[2,832,128]{2,1,0:T(8,128)(2,1)S(1)}, u32[]{:S(2)}, u32[]{:S(2)}) collective-permute-start(bf16[2,832,128]{2,1,0:T(8,128)(2,1)S(1)} %collective-permute-done.3.refs_5_), channel_id=1, source_target_pairs={{0,224},{32,0},{64,32},{96,64},{128,96},{160,128},{192,160},{224,1... | collective-permute-start | bytes 1277960 | tf_op jit(solution)/shard_map/ppermute | solution.py:38
  25.0 0.0 collective-permute-done.2.refs_4_
  25.0 0.0 collective-permute-start.7
  25.0 2.2 %all-to-all-done = bf16[8,192,128]{2,1,0:T(8,128)(2,1)S(1)} async-done(((bf16[8,192,128]{2,1,0:T(8,128)(2,1)}), bf16[8,192,128]{2,1,0:T(8,128)(2,1)S(1)}, u32[]{:S(2)}, u32[]{:S(2)}) %all-to-all-start) | async-done | bytes 393248 | tf_op jit(solution)/shard_map/all_to_all | solution.py:218
  27.2 3.1 %convolution_convert_fusion.refs_2_ = bf16[128,1536]{1,0:T(8,128)(2,1)S(1)} fusion(bf16[1536,128]{1,0:T(8,128)(2,1)S(1)} %bitcast.29, bf16[1536,1536]{1,0:T(8,128)(2,1)} %param.8), kind=kOutput, calls=%fused_computation | convolution fusion | flops 604176384 | bytes 5505024 | tf_op jit(solution)/shard_map/dot_general | solution.py:219
  30.3 0.0 copy-start.4
  30.4 0.7 collective-permute-done.8.refs_1_
  31.0 3.1 %collective-permute-done.7.refs_0_ = bf16[2,832,128]{2,1,0:T(8,128)(2,1)S(1)} collective-permute-done((bf16[2,832,128]{2,1,0:T(8,128)(2,1)S(1)}, bf16[2,832,128]{2,1,0:T(8,128)(2,1)S(1)}, u32[]{:S(2)}, u32[]{:S(2)}) %collective-permute-start.7) | collective-permute-done | bytes 426016 | tf_op jit(solution)/shard_map/ppermute | solution.py:38
  34.2 0.0 copy-done.10
  34.2 0.0 collective-permute-start.9
  34.2 0.0 copy-done.11
  34.2 2.7 %collective-permute-start.10 = (bf16[2,832,128]{2,1,0:T(8,128)(2,1)S(1)}, bf16[2,832,128]{2,1,0:T(8,128)(2,1)S(1)}, u32[]{:S(2)}, u32[]{:S(2)}) collective-permute-start(bf16[2,832,128]{2,1,0:T(8,128)(2,1)S(1)} %get-tuple-element.14.refs_1_), channel_id=1, source_target_pairs={{0,224},{32,0},{64,32},{96,64},{128,96},{160,128},{192,160},{224,1... | collective-permute-start | bytes 1277960 | tf_op jit(solution)/shard_map/ppermute | solution.py:38
  36.9 4.8 %collective-permute-start.4 = (bf16[2,832,128]{2,1,0:T(8,128)(2,1)S(1)}, bf16[2,832,128]{2,1,0:T(8,128)(2,1)S(1)}, u32[]{:S(2)}, u32[]{:S(2)}) collective-permute-start(bf16[2,832,128]{2,1,0:T(8,128)(2,1)S(1)} %pad_maximum_fusion.refs_1_.refs_3_), channel_id=1, source_target_pairs={{0,8},{8,0},{1,9},{9,1},{2,10},{10,2},{3,11},{11,3},{4,12},{12,4},... | collective-permute-start | bytes 1277960 | tf_op jit(solution)/shard_map/ppermute | solution.py:38
  41.7 0.0 collective-permute-start.6
  41.7 0.5 collective-permute-start.5
  42.2 0.2 collective-permute-done.9.refs_2_
  42.4 0.0 copy-done.1
  42.4 0.0 collective-permute-done.10.refs_3_
  42.4 1.2 %collective-permute-done.4.refs_2_.refs_6_ = bf16[2,832,128]{2,1,0:T(8,128)(2,1)S(1)} collective-permute-done((bf16[2,832,128]{2,1,0:T(8,128)(2,1)S(1)}, bf16[2,832,128]{2,1,0:T(8,128)(2,1)S(1)}, u32[]{:S(2)}, u32[]{:S(2)}) %collective-permute-start.4) | collective-permute-done | bytes 426016 | tf_op jit(solution)/shard_map/ppermute | solution.py:38
  43.6 0.2 collective-permute-done.6.refs_4_.refs_8_
  43.9 0.6 collective-permute-done.5.refs_3_.refs_7_
  44.5 0.0 collective-permute-start.11
  44.5 2.7 %collective-permute-start.12 = (bf16[1,832,128]{2,1,0:T(8,128)(2,1)S(1)}, bf16[1,832,128]{2,1,0:T(8,128)(2,1)}, u32[]{:S(2)}, u32[]{:S(2)}) collective-permute-start(bf16[1,832,128]{2,1,0:T(8,128)(2,1)S(1)} %get-tuple-element.16.refs_5_), channel_id=1, source_target_pairs={{0,224},{32,0},{64,32},{96,64},{128,96},{160,128},{192,160},{224,1... | collective-permute-start | bytes 638984 | tf_op jit(solution)/shard_map/ppermute | solution.py:38
  47.2 4.2 %collective-permute-start.13 = (bf16[2,832,128]{2,1,0:T(8,128)(2,1)S(1)}, bf16[2,832,128]{2,1,0:T(8,128)(2,1)S(1)}, u32[]{:S(2)}, u32[]{:S(2)}) collective-permute-start(bf16[2,832,128]{2,1,0:T(8,128)(2,1)S(1)} %get-tuple-element.17.refs_9_), channel_id=1, source_target_pairs={{0,8},{8,0},{1,9},{9,1},{2,10},{10,2},{3,11},{11,3},{4,12},{12,4},... | collective-permute-start | bytes 1277960 | tf_op jit(solution)/shard_map/ppermute | solution.py:38
  51.3 0.1 collective-permute-start.14
  51.5 0.0 collective-permute-done.11.refs_13_
  51.5 3.6 %collective-permute-start.17 = (bf16[1,832,128]{2,1,0:T(8,128)(2,1)S(1)}, bf16[1,832,128]{2,1,0:T(8,128)(2,1)S(1)}, u32[]{:S(2)}, u32[]{:S(2)}) collective-permute-start(bf16[1,832,128]{2,1,0:T(8,128)(2,1)S(1)} %collective-permute-done.11.refs_13_), channel_id=1, source_target_pairs={{0,8},{8,0},{1,9},{9,1},{2,10},{10,2},{3,11},{11,3},{4,12},{12,4},... | collective-permute-start | bytes 638984 | tf_op jit(solution)/shard_map/ppermute | solution.py:38
  55.0 0.0 collective-permute-start.15
  55.0 0.0 collective-permute-done.12.refs_14_
  55.0 0.0 copy-done.9
  55.0 0.0 copy-done.13
  55.0 0.7 collective-permute-start.16
  55.7 0.7 collective-permute-done.17.refs_19_
  56.4 0.7 copy-done.14
  57.1 0.4 collective-permute-start.18
  57.4 0.6 pad_add_fusion.refs_0_
  58.0 0.8 %collective-permute-done.18.refs_20_ = bf16[1,832,128]{2,1,0:T(8,128)(2,1)} collective-permute-done((bf16[1,832,128]{2,1,0:T(8,128)(2,1)}, bf16[1,832,128]{2,1,0:T(8,128)(2,1)}, u32[]{:S(2)}, u32[]{:S(2)}) %collective-permute-start.18) | collective-permute-done | bytes 213024 | tf_op jit(solution)/shard_map/ppermute | solution.py:38
  58.9 0.0 collective-permute-done.13.refs_15_
  58.9 0.0 collective-permute-done.14.refs_16_
  58.9 0.0 collective-permute-done.15.refs_17_
  58.9 0.0 collective-permute-done.16.refs_18_
  58.9 0.0 copy-done.4
  58.9 0.0 copy-done.7
  58.9 0.0 copy-done.8
  58.9 0.0 copy-done.2
  58.9 0.0 copy-done.3
  58.9 0.0 copy-done.5
  59.0 0.0 copy-done.6
  59.0 0.7 copy-done.12
  59.6 15.9 %shard_map.68 = bf16[128,1024]{1,0:T(8,128)(2,1)} custom-call(s32[4]{0:T(128)} %pad_add_fusion.refs_0_, s32[64]{0:T(128)} %refs_1_.1, bf16[128,1536]{1,0:T(8,128)(2,1)} %copy-done.4, bf16[2,832,128]{2,1,0:T(8,128)(2,1)} %copy-done.1, bf16[2,832,128]{2,1,0:T(8,128)(2,1)} %copy-done.11, bf16[2,832,128]{2,1,0:T(8,128)(2,1)} %copy-done.10, ...), custom_call_target="tpu_custom_call" | custom-call | flops 5704253440 | bytes 7209232 | tf_op jit(solution)/shard_map/pallas_call | solution.py:177
  (22 shorter events, 0.1 us)
Async XLA Ops:
  0.0 3.3 %copy-start = (bf16[16,1024]{1,0:T(8,128)(2,1)S(1)}, bf16[16,1024]{1,0:T(8,128)(2,1)}, u32[]{:S(2)}) copy-start(bf16[16,1024]{1,0:T(8,128)(2,1)} %param.9) | copy-start | bytes 98308
  0.0 8.9 %collective-permute-start = (bf16[576,128]{1,0:T(8,128)(2,1)}, bf16[576,128]{1,0:T(8,128)(2,1)S(1)}, u32[]{:S(2)}, u32[]{:S(2)}) collective-permute-start(bf16[576,128]{1,0:T(8,128)(2,1)} %bitcast.34), channel_id=1, source_target_pairs={{0,17},{17,0},{1,16},{16,1},{2,19},{19,2},{3,18},{18,3},{4,21},{21... | collective-permute-start | bytes 442376 | tf_op jit(solution)/shard_map/ppermute | solution.py:209
  4.1 4.8 %collective-permute-start.1 = (bf16[256,128]{1,0:T(8,128)(2,1)S(1)}, bf16[256,128]{1,0:T(8,128)(2,1)S(1)}, u32[]{:S(2)}, u32[]{:S(2)}) collective-permute-start(bf16[256,128]{1,0:T(8,128)(2,1)S(1)} %pad_maximum_fusion.1), channel_id=1, source_target_pairs={{0,16},{16,0},{1,17},{17,1},{2,18},{18,2},{3,19},{19,3},{4,20},{20... | collective-permute-start | bytes 196616 | tf_op jit(solution)/shard_map/ppermute | solution.py:38
  9.0 33.4 %copy-start.1 = (bf16[2,832,128]{2,1,0:T(8,128)(2,1)}, bf16[2,832,128]{2,1,0:T(8,128)(2,1)S(1)}, u32[]{:S(2)}) copy-start(bf16[2,832,128]{2,1,0:T(8,128)(2,1)S(1)} %pad_maximum_fusion.refs_1_.refs_3_) | copy-start | bytes 1277956
  9.0 12.5 %collective-permute-start.3 = (bf16[2,832,128]{2,1,0:T(8,128)(2,1)S(1)}, bf16[2,832,128]{2,1,0:T(8,128)(2,1)S(1)}, u32[]{:S(2)}, u32[]{:S(2)}) collective-permute-start(bf16[2,832,128]{2,1,0:T(8,128)(2,1)S(1)} %pad_maximum_fusion.refs_1_.refs_3_), channel_id=1, source_target_pairs={{0,224},{32,0},{64,32},{96,64},{128,96},{160,128},{192,160},{224,1... | collective-permute-start | bytes 1277960 | tf_op jit(solution)/shard_map/ppermute | solution.py:38
  14.5 10.4 %collective-permute-start.2 = (bf16[2,832,128]{2,1,0:T(8,128)(2,1)S(1)}, bf16[2,832,128]{2,1,0:T(8,128)(2,1)S(1)}, u32[]{:S(2)}, u32[]{:S(2)}) collective-permute-start(bf16[2,832,128]{2,1,0:T(8,128)(2,1)S(1)} %pad_maximum_fusion.refs_1_.refs_3_), channel_id=1, source_target_pairs={{0,32},{32,64},{64,96},{96,128},{128,160},{160,192},{192,224},{224... | collective-permute-start | bytes 1277960 | tf_op jit(solution)/shard_map/ppermute | solution.py:38
  16.2 11.0 %all-to-all-start = ((bf16[8,192,128]{2,1,0:T(8,128)(2,1)}), bf16[8,192,128]{2,1,0:T(8,128)(2,1)S(1)}, u32[]{:S(2)}, u32[]{:S(2)}) async-start(bf16[8,192,128]{2,1,0:T(8,128)(2,1)} %shard_map.64), calls=%async_computation | async-start | bytes 786432 | tf_op jit(solution)/shard_map/all_to_all | solution.py:218
  21.5 12.6 %copy-start.10 = (bf16[2,832,128]{2,1,0:T(8,128)(2,1)}, bf16[2,832,128]{2,1,0:T(8,128)(2,1)S(1)}, u32[]{:S(2)}) copy-start(bf16[2,832,128]{2,1,0:T(8,128)(2,1)S(1)} %collective-permute-done.3.refs_5_) | copy-start | bytes 1277956
  21.5 9.5 %collective-permute-start.8 = (bf16[2,832,128]{2,1,0:T(8,128)(2,1)S(1)}, bf16[2,832,128]{2,1,0:T(8,128)(2,1)S(1)}, u32[]{:S(2)}, u32[]{:S(2)}) collective-permute-start(bf16[2,832,128]{2,1,0:T(8,128)(2,1)S(1)} %collective-permute-done.3.refs_5_), channel_id=1, source_target_pairs={{0,224},{32,0},{64,32},{96,64},{128,96},{160,128},{192,160},{224,1... | collective-permute-start | bytes 1277960 | tf_op jit(solution)/shard_map/ppermute | solution.py:38
  25.0 9.2 %copy-start.11 = (bf16[2,832,128]{2,1,0:T(8,128)(2,1)}, bf16[2,832,128]{2,1,0:T(8,128)(2,1)S(1)}, u32[]{:S(2)}) copy-start(bf16[2,832,128]{2,1,0:T(8,128)(2,1)S(1)} %collective-permute-done.2.refs_4_) | copy-start | bytes 1277956
  25.0 9.2 %collective-permute-start.7 = (bf16[2,832,128]{2,1,0:T(8,128)(2,1)S(1)}, bf16[2,832,128]{2,1,0:T(8,128)(2,1)S(1)}, u32[]{:S(2)}, u32[]{:S(2)}) collective-permute-start(bf16[2,832,128]{2,1,0:T(8,128)(2,1)S(1)} %collective-permute-done.2.refs_4_), channel_id=1, source_target_pairs={{0,32},{32,64},{64,96},{96,128},{128,160},{160,192},{192,224},{224... | collective-permute-start | bytes 1277960 | tf_op jit(solution)/shard_map/ppermute | solution.py:38
  30.3 28.5 %copy-start.4 = (bf16[128,1536]{1,0:T(8,128)(2,1)}, bf16[128,1536]{1,0:T(8,128)(2,1)S(1)}, u32[]{:S(2)}) copy-start(bf16[128,1536]{1,0:T(8,128)(2,1)S(1)} %convolution_convert_fusion.refs_2_) | copy-start | bytes 1179652
  34.2 8.2 %collective-permute-start.9 = (bf16[2,832,128]{2,1,0:T(8,128)(2,1)S(1)}, bf16[2,832,128]{2,1,0:T(8,128)(2,1)S(1)}, u32[]{:S(2)}, u32[]{:S(2)}) collective-permute-start(bf16[2,832,128]{2,1,0:T(8,128)(2,1)S(1)} %get-tuple-element.13.refs_0_), channel_id=1, source_target_pairs={{0,32},{32,64},{64,96},{96,128},{128,160},{160,192},{192,224},{224... | collective-permute-start | bytes 1277960 | tf_op jit(solution)/shard_map/ppermute | solution.py:38
  34.2 8.2 %collective-permute-start.10 = (bf16[2,832,128]{2,1,0:T(8,128)(2,1)S(1)}, bf16[2,832,128]{2,1,0:T(8,128)(2,1)S(1)}, u32[]{:S(2)}, u32[]{:S(2)}) collective-permute-start(bf16[2,832,128]{2,1,0:T(8,128)(2,1)S(1)} %get-tuple-element.14.refs_1_), channel_id=1, source_target_pairs={{0,224},{32,0},{64,32},{96,64},{128,96},{160,128},{192,160},{224,1... | collective-permute-start | bytes 1277960 | tf_op jit(solution)/shard_map/ppermute | solution.py:38
  36.9 6.8 %collective-permute-start.4 = (bf16[2,832,128]{2,1,0:T(8,128)(2,1)S(1)}, bf16[2,832,128]{2,1,0:T(8,128)(2,1)S(1)}, u32[]{:S(2)}, u32[]{:S(2)}) collective-permute-start(bf16[2,832,128]{2,1,0:T(8,128)(2,1)S(1)} %pad_maximum_fusion.refs_1_.refs_3_), channel_id=1, source_target_pairs={{0,8},{8,0},{1,9},{9,1},{2,10},{10,2},{3,11},{11,3},{4,12},{12,4},... | collective-permute-start | bytes 1277960 | tf_op jit(solution)/shard_map/ppermute | solution.py:38
  41.7 2.2 %collective-permute-start.6 = (bf16[2,832,128]{2,1,0:T(8,128)(2,1)}, bf16[2,832,128]{2,1,0:T(8,128)(2,1)S(1)}, u32[]{:S(2)}, u32[]{:S(2)}) collective-permute-start(bf16[2,832,128]{2,1,0:T(8,128)(2,1)} %copy-done.10), channel_id=1, source_target_pairs={{0,8},{8,0},{1,9},{9,1},{2,10},{10,2},{3,11},{11,3},{4,12},{12,4},... | collective-permute-start | bytes 1277960 | tf_op jit(solution)/shard_map/ppermute | solution.py:38
  41.7 2.8 %collective-permute-start.5 = (bf16[2,832,128]{2,1,0:T(8,128)(2,1)}, bf16[2,832,128]{2,1,0:T(8,128)(2,1)S(1)}, u32[]{:S(2)}, u32[]{:S(2)}) collective-permute-start(bf16[2,832,128]{2,1,0:T(8,128)(2,1)} %copy-done.11), channel_id=1, source_target_pairs={{0,8},{8,0},{1,9},{9,1},{2,10},{10,2},{3,11},{11,3},{4,12},{12,4},... | collective-permute-start | bytes 1277960 | tf_op jit(solution)/shard_map/ppermute | solution.py:38
  43.6 15.3 %copy-start.7 = (bf16[2,832,128]{2,1,0:T(8,128)(2,1)}, bf16[2,832,128]{2,1,0:T(8,128)(2,1)S(1)}, u32[]{:S(2)}) copy-start(bf16[2,832,128]{2,1,0:T(8,128)(2,1)S(1)} %collective-permute-done.4.refs_2_.refs_6_) | copy-start | bytes 1277956
  43.9 15.0 %copy-start.8 = (bf16[2,832,128]{2,1,0:T(8,128)(2,1)}, bf16[2,832,128]{2,1,0:T(8,128)(2,1)S(1)}, u32[]{:S(2)}) copy-start(bf16[2,832,128]{2,1,0:T(8,128)(2,1)S(1)} %collective-permute-done.6.refs_4_.refs_8_) | copy-start | bytes 1277956
  44.5 10.6 %copy-start.9 = (bf16[2,832,128]{2,1,0:T(8,128)(2,1)}, bf16[2,832,128]{2,1,0:T(8,128)(2,1)S(1)}, u32[]{:S(2)}) copy-start(bf16[2,832,128]{2,1,0:T(8,128)(2,1)S(1)} %collective-permute-done.5.refs_3_.refs_7_) | copy-start | bytes 1277956
  44.5 7.0 %collective-permute-start.11 = (bf16[1,832,128]{2,1,0:T(8,128)(2,1)S(1)}, bf16[1,832,128]{2,1,0:T(8,128)(2,1)S(1)}, u32[]{:S(2)}, u32[]{:S(2)}) collective-permute-start(bf16[1,832,128]{2,1,0:T(8,128)(2,1)S(1)} %get-tuple-element.15.refs_4_), channel_id=1, source_target_pairs={{0,32},{32,64},{64,96},{96,128},{128,160},{160,192},{192,224},{224... | collective-permute-start | bytes 638984 | tf_op jit(solution)/shard_map/ppermute | solution.py:38
  44.5 10.5 %collective-permute-start.12 = (bf16[1,832,128]{2,1,0:T(8,128)(2,1)S(1)}, bf16[1,832,128]{2,1,0:T(8,128)(2,1)}, u32[]{:S(2)}, u32[]{:S(2)}) collective-permute-start(bf16[1,832,128]{2,1,0:T(8,128)(2,1)S(1)} %get-tuple-element.16.refs_5_), channel_id=1, source_target_pairs={{0,224},{32,0},{64,32},{96,64},{128,96},{160,128},{192,160},{224,1... | collective-permute-start | bytes 638984 | tf_op jit(solution)/shard_map/ppermute | solution.py:38
  47.2 11.8 %copy-start.2 = (bf16[2,832,128]{2,1,0:T(8,128)(2,1)}, bf16[2,832,128]{2,1,0:T(8,128)(2,1)S(1)}, u32[]{:S(2)}) copy-start(bf16[2,832,128]{2,1,0:T(8,128)(2,1)S(1)} %get-tuple-element.18.refs_10_) | copy-start | bytes 1277956
  47.2 11.8 %copy-start.3 = (bf16[2,832,128]{2,1,0:T(8,128)(2,1)}, bf16[2,832,128]{2,1,0:T(8,128)(2,1)S(1)}, u32[]{:S(2)}) copy-start(bf16[2,832,128]{2,1,0:T(8,128)(2,1)S(1)} %get-tuple-element.17.refs_9_) | copy-start | bytes 1277956
  47.2 11.8 %copy-start.5 = (bf16[2,832,128]{2,1,0:T(8,128)(2,1)}, bf16[2,832,128]{2,1,0:T(8,128)(2,1)S(1)}, u32[]{:S(2)}) copy-start(bf16[2,832,128]{2,1,0:T(8,128)(2,1)S(1)} %get-tuple-element.19.refs_11_) | copy-start | bytes 1277956
  47.2 11.8 %copy-start.6 = (bf16[2,832,128]{2,1,0:T(8,128)(2,1)}, bf16[2,832,128]{2,1,0:T(8,128)(2,1)S(1)}, u32[]{:S(2)}) copy-start(bf16[2,832,128]{2,1,0:T(8,128)(2,1)S(1)} %get-tuple-element.20.refs_12_) | copy-start | bytes 1277956
  47.2 11.7 %collective-permute-start.13 = (bf16[2,832,128]{2,1,0:T(8,128)(2,1)S(1)}, bf16[2,832,128]{2,1,0:T(8,128)(2,1)S(1)}, u32[]{:S(2)}, u32[]{:S(2)}) collective-permute-start(bf16[2,832,128]{2,1,0:T(8,128)(2,1)S(1)} %get-tuple-element.17.refs_9_), channel_id=1, source_target_pairs={{0,8},{8,0},{1,9},{9,1},{2,10},{10,2},{3,11},{11,3},{4,12},{12,4},... | collective-permute-start | bytes 1277960 | tf_op jit(solution)/shard_map/ppermute | solution.py:38
  51.3 7.5 %collective-permute-start.14 = (bf16[2,832,128]{2,1,0:T(8,128)(2,1)S(1)}, bf16[2,832,128]{2,1,0:T(8,128)(2,1)}, u32[]{:S(2)}, u32[]{:S(2)}) collective-permute-start(bf16[2,832,128]{2,1,0:T(8,128)(2,1)S(1)} %get-tuple-element.18.refs_10_), channel_id=1, source_target_pairs={{0,8},{8,0},{1,9},{9,1},{2,10},{10,2},{3,11},{11,3},{4,12},{12,4},... | collective-permute-start | bytes 1277960 | tf_op jit(solution)/shard_map/ppermute | solution.py:38
  51.5 3.6 %copy-start.13 = (bf16[1,832,128]{2,1,0:T(8,128)(2,1)}, bf16[1,832,128]{2,1,0:T(8,128)(2,1)S(1)}, u32[]{:S(2)}) copy-start(bf16[1,832,128]{2,1,0:T(8,128)(2,1)S(1)} %collective-permute-done.11.refs_13_) | copy-start | bytes 638980
  51.5 4.9 %collective-permute-start.17 = (bf16[1,832,128]{2,1,0:T(8,128)(2,1)S(1)}, bf16[1,832,128]{2,1,0:T(8,128)(2,1)S(1)}, u32[]{:S(2)}, u32[]{:S(2)}) collective-permute-start(bf16[1,832,128]{2,1,0:T(8,128)(2,1)S(1)} %collective-permute-done.11.refs_13_), channel_id=1, source_target_pairs={{0,8},{8,0},{1,9},{9,1},{2,10},{10,2},{3,11},{11,3},{4,12},{12,4},... | collective-permute-start | bytes 638984 | tf_op jit(solution)/shard_map/ppermute | solution.py:38
  55.0 3.8 %collective-permute-start.15 = (bf16[2,832,128]{2,1,0:T(8,128)(2,1)S(1)}, bf16[2,832,128]{2,1,0:T(8,128)(2,1)}, u32[]{:S(2)}, u32[]{:S(2)}) collective-permute-start(bf16[2,832,128]{2,1,0:T(8,128)(2,1)S(1)} %get-tuple-element.19.refs_11_), channel_id=1, source_target_pairs={{0,8},{8,0},{1,9},{9,1},{2,10},{10,2},{3,11},{11,3},{4,12},{12,4},... | collective-permute-start | bytes 1277960 | tf_op jit(solution)/shard_map/ppermute | solution.py:38
  55.0 3.8 %collective-permute-start.16 = (bf16[2,832,128]{2,1,0:T(8,128)(2,1)S(1)}, bf16[2,832,128]{2,1,0:T(8,128)(2,1)}, u32[]{:S(2)}, u32[]{:S(2)}) collective-permute-start(bf16[2,832,128]{2,1,0:T(8,128)(2,1)S(1)} %get-tuple-element.20.refs_12_), channel_id=1, source_target_pairs={{0,8},{8,0},{1,9},{9,1},{2,10},{10,2},{3,11},{11,3},{4,12},{12,4},... | collective-permute-start | bytes 1277960 | tf_op jit(solution)/shard_map/ppermute | solution.py:38
  56.4 0.7 copy-start.14
  57.1 1.8 %collective-permute-start.18 = (bf16[1,832,128]{2,1,0:T(8,128)(2,1)}, bf16[1,832,128]{2,1,0:T(8,128)(2,1)}, u32[]{:S(2)}, u32[]{:S(2)}) collective-permute-start(bf16[1,832,128]{2,1,0:T(8,128)(2,1)} %collective-permute-done.12.refs_14_), channel_id=1, source_target_pairs={{0,8},{8,0},{1,9},{9,1},{2,10},{10,2},{3,11},{11,3},{4,12},{12,4},... | collective-permute-start | bytes 638984 | tf_op jit(solution)/shard_map/ppermute | solution.py:38
  58.9 0.8 %copy-start.12 = (bf16[2,832,128]{2,1,0:T(8,128)(2,1)}, bf16[2,832,128]{2,1,0:T(8,128)(2,1)S(1)}, u32[]{:S(2)}) copy-start(bf16[2,832,128]{2,1,0:T(8,128)(2,1)S(1)} %collective-permute-done.13.refs_15_) | copy-start | bytes 1277956

commit v10 on v9

--- a/solution.py
+++ b/solution.py
@@ -191,7 +191,7 @@
             pltpu.SemaphoreType.DMA((shards,)),
             pltpu.SemaphoreType.DMA((2, shards)),
         ],
-        compiler_params=pltpu.CompilerParams(vmem_limit_bytes=60 << 20),
+        compiler_params=pltpu.CompilerParams(vmem_limit_bytes=36 << 20),
         cost_estimate=pl.CostEstimate(
             flops=2 * work * (2 * KV + ROPE), bytes_accessed=size, transcendentals=work
         ),
@@ -214,7 +214,7 @@
     )
 
     copies = jnp.broadcast_to(compressed.T[None], (ys * xls,) + compressed.T.shape)
-    (copies,) = gate([copies], here)
+    (copies,) = gate([copies], here, idx)
     features = lax.all_to_all(copies, ("y", "xl"), 0, 0, tiled=True).reshape(-1, toks)
     query = lax.dot_general(
         features, w_uq, (((0,), (0,)), ((), ())), preferred_element_type=jnp.float32

time: 76 us -> 82.2 us (1.082)
  Pallas kernels: 15.9 us -> 23.9 us
  local copies, waits for them, and re-layouts: 3.83 us -> 2.4 us
    pallas_call x1, Pallas kernels: 15.9 us -> 23.9 us  [attention(): pl.pallas_call(functools.partial(attention_kernel, layout, heads, min(row...]
    unnamed x30 -> x4, local copies, waits for them, and re-layouts: 1.4 us -> 0.01 us
  transfers between devices with their start and end apart: 20 -> 20, of which waited for: 11 -> 11; matrix products, arithmetic and copies ran while one was open for 9% -> 8% of each run, Pallas kernels for 0% -> 0%
where the time goes in v10:
time: 82.2 us; the launch traced here: 81.8 us
  starting transfers between devices  37.1 us (45%)
  Pallas kernels  23.9 us (29%)
  waiting for transfers between devices  13.8 us (17%)
  matrix products  3.17 us (4%)
  local copies, waits for them, and re-layouts  2.4 us (3%)
  other arithmetic  1.06 us (1%)
    ppermute x18, starting transfers between devices, shift(): return lax.ppermute(x, axis, [(i, (i + by) % n) for i in range(n)])  29.6 us
    pallas_call x1, Pallas kernels, attention(): pl.pallas_call(functools.partial(attention_kernel, layout, heads, min(row...  23.9 us
    ppermute x18, waiting for transfers between devices, shift(): return lax.ppermute(x, axis, [(i, (i + by) % n) for i in range(n)])  11.6 us
    all_to_all x1, starting transfers between devices, per_device(): lax.all_to_all(copies, ('y', 'xl'), 0, 0, tiled=True).reshape(-1, toks)  4.19 us
    ppermute x1, starting transfers between devices, per_device(): across = lax.ppermute(own, ('xh', 'xl'), [(0, 3), (3, 0), (1, 2), (2, 1)])  3.31 us
    dot_general x1, matrix products, per_device(): lax.dot_general(features, w_uq, (((0,), (0,)), ((), ())), preferred_eleme...  3.17 us
    all_to_all x1, waiting for transfers between devices, per_device(): lax.all_to_all(copies, ('y', 'xl'), 0, 0, tiled=True).reshape(-1, toks)  2.27 us
  transfers between devices with their start and end apart: 20, of which 11 were waited for; matrix products, arithmetic and copies ran while one was open for 8% of the time, Pallas kernels for 0%

profile of v10, /device:TPU:1, one launch (start us, length us, event | category | flops | bytes accessed | tf_op | source)
XLA Modules:
  0.0 81.8 jit_solution(17341621359710789397)
XLA Ops:
  0.0 0.0 copy-start
  0.0 3.3 %collective-permute-start = (bf16[576,128]{1,0:T(8,128)(2,1)}, bf16[576,128]{1,0:T(8,128)(2,1)S(1)}, u32[]{:S(2)}, u32[]{:S(2)}) collective-permute-start(bf16[576,128]{1,0:T(8,128)(2,1)} %bitcast.34), channel_id=1, source_target_pairs={{0,17},{17,0},{1,16},{16,1},{2,19},{19,2},{3,18},{18,3},{4,21},{21... | collective-permute-start | bytes 442376 | tf_op jit(solution)/shard_map/ppermute | solution.py:209
  3.3 0.0 copy-done
  3.3 0.8 copy_bitcast_fusion
  4.1 1.1 %collective-permute-start.1 = (bf16[256,128]{1,0:T(8,128)(2,1)S(1)}, bf16[256,128]{1,0:T(8,128)(2,1)S(1)}, u32[]{:S(2)}, u32[]{:S(2)}) collective-permute-start(bf16[256,128]{1,0:T(8,128)(2,1)S(1)} %pad_maximum_fusion.1), channel_id=1, source_target_pairs={{0,16},{16,0},{1,17},{17,1},{2,18},{18,2},{3,19},{19,3},{4,20},{20... | collective-permute-start | bytes 196616 | tf_op jit(solution)/shard_map/ppermute | solution.py:38
  5.2 0.9 %maximum_bitcast_fusion = bf16[1,832,128]{2,1,0:T(8,128)(2,1)S(1)} fusion(bf16[128,128]{1,0:T(8,128)(2,1)S(1)} %bitcast.33, bf16[128,128]{1,0:T(8,128)(2,1)S(1)} %bitcast.31, bf16[576,128]{1,0:T(8,128)(2,1)} %bitcast.35), kind=kLoop, calls=%fused_computation.2 | loop fusion | flops 638976 | bytes 425984 | tf_op jit(solution)/shard_map/stack | solution.py:212
  6.1 2.8 %collective-permute-done.1 = bf16[256,128]{1,0:T(8,128)(2,1)S(1)} collective-permute-done((bf16[256,128]{1,0:T(8,128)(2,1)S(1)}, bf16[256,128]{1,0:T(8,128)(2,1)S(1)}, u32[]{:S(2)}, u32[]{:S(2)}) %collective-permute-start.1) | collective-permute-done | bytes 65568 | tf_op jit(solution)/shard_map/ppermute | solution.py:38
  8.9 0.0 collective-permute-done
  9.0 5.5 %collective-permute-start.3 = (bf16[2,832,128]{2,1,0:T(8,128)(2,1)S(1)}, bf16[2,832,128]{2,1,0:T(8,128)(2,1)S(1)}, u32[]{:S(2)}, u32[]{:S(2)}) collective-permute-start(bf16[2,832,128]{2,1,0:T(8,128)(2,1)S(1)} %pad_maximum_fusion.refs_1_.refs_3_), channel_id=1, source_target_pairs={{0,224},{32,0},{64,32},{96,64},{128,96},{160,128},{192,160},{224,1... | collective-permute-start | bytes 1277960 | tf_op jit(solution)/shard_map/ppermute | solution.py:38
  14.5 0.0 collective-permute-start.2
  14.5 0.1 pad_add_fusion.refs_2_.refs_0_
  14.6 1.6 %broadcast_in_dim.2.refs_0_ = bf16[8,192,128]{2,1,0:T(8,128)(2,1)} broadcast(bf16[192,128]{1,0:T(8,128)(2,1)} %bitcast.36), dimensions={1,2} | broadcast | bytes 442368 | tf_op jit(solution)/shard_map/broadcast_in_dim | solution.py:216
  16.2 4.2 %all-to-all-start = ((bf16[8,192,128]{2,1,0:T(8,128)(2,1)}), bf16[8,192,128]{2,1,0:T(8,128)(2,1)S(1)}, u32[]{:S(2)}, u32[]{:S(2)}) async-start(bf16[8,192,128]{2,1,0:T(8,128)(2,1)} %shard_map.64), calls=%async_computation | async-start | bytes 786432 | tf_op jit(solution)/shard_map/all_to_all | solution.py:218
  20.4 1.1 %collective-permute-done.3.refs_5_ = bf16[2,832,128]{2,1,0:T(8,128)(2,1)S(1)} collective-permute-done((bf16[2,832,128]{2,1,0:T(8,128)(2,1)S(1)}, bf16[2,832,128]{2,1,0:T(8,128)(2,1)S(1)}, u32[]{:S(2)}, u32[]{:S(2)}) %collective-permute-start.3) | collective-permute-done | bytes 426016 | tf_op jit(solution)/shard_map/ppermute | solution.py:38
  21.5 3.4 %collective-permute-start.8 = (bf16[2,832,128]{2,1,0:T(8,128)(2,1)S(1)}, bf16[2,832,128]{2,1,0:T(8,128)(2,1)S(1)}, u32[]{:S(2)}, u32[]{:S(2)}) collective-permute-start(bf16[2,832,128]{2,1,0:T(8,128)(2,1)S(1)} %collective-permute-done.3.refs_5_), channel_id=1, source_target_pairs={{0,224},{32,0},{64,32},{96,64},{128,96},{160,128},{192,160},{224,1... | collective-permute-start | bytes 1277960 | tf_op jit(solution)/shard_map/ppermute | solution.py:38
  24.9 0.0 collective-permute-done.2.refs_4_
  25.0 0.0 collective-permute-start.7
  25.0 2.3 %all-to-all-done = bf16[8,192,128]{2,1,0:T(8,128)(2,1)S(1)} async-done(((bf16[8,192,128]{2,1,0:T(8,128)(2,1)}), bf16[8,192,128]{2,1,0:T(8,128)(2,1)S(1)}, u32[]{:S(2)}, u32[]{:S(2)}) %all-to-all-start) | async-done | bytes 393248 | tf_op jit(solution)/shard_map/all_to_all | solution.py:218
  27.2 0.0 copy-start.1
  27.2 3.2 %convolution_convert_fusion.refs_2_ = bf16[128,1536]{1,0:T(8,128)(2,1)S(1)} fusion(bf16[1536,128]{1,0:T(8,128)(2,1)S(1)} %bitcast.29, bf16[1536,1536]{1,0:T(8,128)(2,1)} %param.8), kind=kOutput, calls=%fused_computation | convolution fusion | flops 604176384 | bytes 5505024 | tf_op jit(solution)/shard_map/dot_general | solution.py:219
  30.4 0.6 collective-permute-done.8.refs_1_
  31.0 3.1 %collective-permute-done.7.refs_0_ = bf16[2,832,128]{2,1,0:T(8,128)(2,1)S(1)} collective-permute-done((bf16[2,832,128]{2,1,0:T(8,128)(2,1)S(1)}, bf16[2,832,128]{2,1,0:T(8,128)(2,1)S(1)}, u32[]{:S(2)}, u32[]{:S(2)}) %collective-permute-start.7) | collective-permute-done | bytes 426016 | tf_op jit(solution)/shard_map/ppermute | solution.py:38
  34.2 0.0 collective-permute-start.9
  34.2 2.7 %collective-permute-start.10 = (bf16[2,832,128]{2,1,0:T(8,128)(2,1)S(1)}, bf16[2,832,128]{2,1,0:T(8,128)(2,1)S(1)}, u32[]{:S(2)}, u32[]{:S(2)}) collective-permute-start(bf16[2,832,128]{2,1,0:T(8,128)(2,1)S(1)} %get-tuple-element.14.refs_1_), channel_id=1, source_target_pairs={{0,224},{32,0},{64,32},{96,64},{128,96},{160,128},{192,160},{224,1... | collective-permute-start | bytes 1277960 | tf_op jit(solution)/shard_map/ppermute | solution.py:38
  36.8 4.8 %collective-permute-start.4 = (bf16[2,832,128]{2,1,0:T(8,128)(2,1)S(1)}, bf16[2,832,128]{2,1,0:T(8,128)(2,1)S(1)}, u32[]{:S(2)}, u32[]{:S(2)}) collective-permute-start(bf16[2,832,128]{2,1,0:T(8,128)(2,1)S(1)} %pad_maximum_fusion.refs_1_.refs_3_), channel_id=1, source_target_pairs={{0,8},{8,0},{1,9},{9,1},{2,10},{10,2},{3,11},{11,3},{4,12},{12,4},... | collective-permute-start | bytes 1277960 | tf_op jit(solution)/shard_map/ppermute | solution.py:38
  41.6 0.0 collective-permute-start.6
  41.6 0.5 collective-permute-start.5
  42.1 0.2 collective-permute-done.9.refs_2_
  42.4 0.0 collective-permute-done.10.refs_3_
  42.4 0.6 collective-permute-done.4.refs_2_.refs_6_
  43.0 0.6 collective-permute-done.6.refs_4_.refs_8_
  43.6 0.6 collective-permute-done.5.refs_3_.refs_7_
  44.2 0.0 collective-permute-start.11
  44.3 2.7 %collective-permute-start.12 = (bf16[1,832,128]{2,1,0:T(8,128)(2,1)S(1)}, bf16[1,832,128]{2,1,0:T(8,128)(2,1)S(1)}, u32[]{:S(2)}, u32[]{:S(2)}) collective-permute-start(bf16[1,832,128]{2,1,0:T(8,128)(2,1)S(1)} %get-tuple-element.16.refs_5_), channel_id=1, source_target_pairs={{0,224},{32,0},{64,32},{96,64},{128,96},{160,128},{192,160},{224,1... | collective-permute-start | bytes 638984 | tf_op jit(solution)/shard_map/ppermute | solution.py:38
  46.9 4.3 %collective-permute-start.13 = (bf16[2,832,128]{2,1,0:T(8,128)(2,1)S(1)}, bf16[2,832,128]{2,1,0:T(8,128)(2,1)S(1)}, u32[]{:S(2)}, u32[]{:S(2)}) collective-permute-start(bf16[2,832,128]{2,1,0:T(8,128)(2,1)S(1)} %get-tuple-element.17.refs_9_), channel_id=1, source_target_pairs={{0,8},{8,0},{1,9},{9,1},{2,10},{10,2},{3,11},{11,3},{4,12},{12,4},... | collective-permute-start | bytes 1277960 | tf_op jit(solution)/shard_map/ppermute | solution.py:38
  51.2 0.0 collective-permute-start.14
  51.2 0.0 collective-permute-done.11.refs_13_
  51.2 3.8 %collective-permute-start.17 = (bf16[1,832,128]{2,1,0:T(8,128)(2,1)S(1)}, bf16[1,832,128]{2,1,0:T(8,128)(2,1)S(1)}, u32[]{:S(2)}, u32[]{:S(2)}) collective-permute-start(bf16[1,832,128]{2,1,0:T(8,128)(2,1)S(1)} %collective-permute-done.11.refs_13_), channel_id=1, source_target_pairs={{0,8},{8,0},{1,9},{9,1},{2,10},{10,2},{3,11},{11,3},{4,12},{12,4},... | collective-permute-start | bytes 638984 | tf_op jit(solution)/shard_map/ppermute | solution.py:38
  55.0 0.0 collective-permute-start.15
  55.0 0.0 collective-permute-done.12.refs_14_
  55.0 0.5 collective-permute-start.16
  55.5 0.6 collective-permute-done.17.refs_19_
  56.1 0.4 collective-permute-start.18
  56.4 1.2 %collective-permute-done.18.refs_20_ = bf16[1,832,128]{2,1,0:T(8,128)(2,1)S(1)} collective-permute-done((bf16[1,832,128]{2,1,0:T(8,128)(2,1)S(1)}, bf16[1,832,128]{2,1,0:T(8,128)(2,1)S(1)}, u32[]{:S(2)}, u32[]{:S(2)}) %collective-permute-start.18) | collective-permute-done | bytes 213024 | tf_op jit(solution)/shard_map/ppermute | solution.py:38
  57.6 0.0 collective-permute-done.13.refs_15_
  57.7 0.0 collective-permute-done.14.refs_16_
  57.7 0.0 collective-permute-done.15.refs_17_
  57.7 0.0 collective-permute-done.16.refs_18_
  57.7 0.0 copy-done.1
  57.7 23.9 %shard_map.68 = bf16[128,1024]{1,0:T(8,128)(2,1)} custom-call(s32[4]{0:T(128)S(1)} %pad_add_fusion.refs_2_.refs_0_, s32[64]{0:T(128)S(1)} %copy-done.1, bf16[128,1536]{1,0:T(8,128)(2,1)S(1)} %convolution_convert_fusion.refs_2_, bf16[2,832,128]{2,1,0:T(8,128)(2,1)S(1)} %pad_maximum_fusion.refs_1_.refs_3_, ...), custom_call_target="tpu_custom_call" | custom-call | flops 5704253440 | bytes 7209232 | tf_op jit(solution)/shard_map/pallas_call | solution.py:177
  (10 shorter events, 0.1 us)
Async XLA Ops:
  0.0 3.3 %copy-start = (bf16[16,1024]{1,0:T(8,128)(2,1)S(1)}, bf16[16,1024]{1,0:T(8,128)(2,1)}, u32[]{:S(2)}) copy-start(bf16[16,1024]{1,0:T(8,128)(2,1)} %param.9) | copy-start | bytes 98308
  0.0 8.9 %collective-permute-start = (bf16[576,128]{1,0:T(8,128)(2,1)}, bf16[576,128]{1,0:T(8,128)(2,1)S(1)}, u32[]{:S(2)}, u32[]{:S(2)}) collective-permute-start(bf16[576,128]{1,0:T(8,128)(2,1)} %bitcast.34), channel_id=1, source_target_pairs={{0,17},{17,0},{1,16},{16,1},{2,19},{19,2},{3,18},{18,3},{4,21},{21... | collective-permute-start | bytes 442376 | tf_op jit(solution)/shard_map/ppermute | solution.py:209
  4.1 4.8 %collective-permute-start.1 = (bf16[256,128]{1,0:T(8,128)(2,1)S(1)}, bf16[256,128]{1,0:T(8,128)(2,1)S(1)}, u32[]{:S(2)}, u32[]{:S(2)}) collective-permute-start(bf16[256,128]{1,0:T(8,128)(2,1)S(1)} %pad_maximum_fusion.1), channel_id=1, source_target_pairs={{0,16},{16,0},{1,17},{17,1},{2,18},{18,2},{3,19},{19,3},{4,20},{20... | collective-permute-start | bytes 196616 | tf_op jit(solution)/shard_map/ppermute | solution.py:38
  9.0 12.5 %collective-permute-start.3 = (bf16[2,832,128]{2,1,0:T(8,128)(2,1)S(1)}, bf16[2,832,128]{2,1,0:T(8,128)(2,1)S(1)}, u32[]{:S(2)}, u32[]{:S(2)}) collective-permute-start(bf16[2,832,128]{2,1,0:T(8,128)(2,1)S(1)} %pad_maximum_fusion.refs_1_.refs_3_), channel_id=1, source_target_pairs={{0,224},{32,0},{64,32},{96,64},{128,96},{160,128},{192,160},{224,1... | collective-permute-start | bytes 1277960 | tf_op jit(solution)/shard_map/ppermute | solution.py:38
  14.5 10.4 %collective-permute-start.2 = (bf16[2,832,128]{2,1,0:T(8,128)(2,1)S(1)}, bf16[2,832,128]{2,1,0:T(8,128)(2,1)S(1)}, u32[]{:S(2)}, u32[]{:S(2)}) collective-permute-start(bf16[2,832,128]{2,1,0:T(8,128)(2,1)S(1)} %pad_maximum_fusion.refs_1_.refs_3_), channel_id=1, source_target_pairs={{0,32},{32,64},{64,96},{96,128},{128,160},{160,192},{192,224},{224... | collective-permute-start | bytes 1277960 | tf_op jit(solution)/shard_map/ppermute | solution.py:38
  16.2 11.0 %all-to-all-start = ((bf16[8,192,128]{2,1,0:T(8,128)(2,1)}), bf16[8,192,128]{2,1,0:T(8,128)(2,1)S(1)}, u32[]{:S(2)}, u32[]{:S(2)}) async-start(bf16[8,192,128]{2,1,0:T(8,128)(2,1)} %shard_map.64), calls=%async_computation | async-start | bytes 786432 | tf_op jit(solution)/shard_map/all_to_all | solution.py:218
  21.5 9.5 %collective-permute-start.8 = (bf16[2,832,128]{2,1,0:T(8,128)(2,1)S(1)}, bf16[2,832,128]{2,1,0:T(8,128)(2,1)S(1)}, u32[]{:S(2)}, u32[]{:S(2)}) collective-permute-start(bf16[2,832,128]{2,1,0:T(8,128)(2,1)S(1)} %collective-permute-done.3.refs_5_), channel_id=1, source_target_pairs={{0,224},{32,0},{64,32},{96,64},{128,96},{160,128},{192,160},{224,1... | collective-permute-start | bytes 1277960 | tf_op jit(solution)/shard_map/ppermute | solution.py:38
  25.0 9.2 %collective-permute-start.7 = (bf16[2,832,128]{2,1,0:T(8,128)(2,1)S(1)}, bf16[2,832,128]{2,1,0:T(8,128)(2,1)S(1)}, u32[]{:S(2)}, u32[]{:S(2)}) collective-permute-start(bf16[2,832,128]{2,1,0:T(8,128)(2,1)S(1)} %collective-permute-done.2.refs_4_), channel_id=1, source_target_pairs={{0,32},{32,64},{64,96},{96,128},{128,160},{160,192},{192,224},{224... | collective-permute-start | bytes 1277960 | tf_op jit(solution)/shard_map/ppermute | solution.py:38
  27.2 30.4 %copy-start.1 = (s32[64]{0:T(128)S(1)}, s32[64]{0:T(128)}, u32[]{:S(2)}) copy-start(s32[64]{0:T(128)} %refs_1_.1) | copy-start | bytes 772
  34.2 8.2 %collective-permute-start.9 = (bf16[2,832,128]{2,1,0:T(8,128)(2,1)S(1)}, bf16[2,832,128]{2,1,0:T(8,128)(2,1)S(1)}, u32[]{:S(2)}, u32[]{:S(2)}) collective-permute-start(bf16[2,832,128]{2,1,0:T(8,128)(2,1)S(1)} %get-tuple-element.13.refs_0_), channel_id=1, source_target_pairs={{0,32},{32,64},{64,96},{96,128},{128,160},{160,192},{192,224},{224... | collective-permute-start | bytes 1277960 | tf_op jit(solution)/shard_map/ppermute | solution.py:38
  34.2 8.2 %collective-permute-start.10 = (bf16[2,832,128]{2,1,0:T(8,128)(2,1)S(1)}, bf16[2,832,128]{2,1,0:T(8,128)(2,1)S(1)}, u32[]{:S(2)}, u32[]{:S(2)}) collective-permute-start(bf16[2,832,128]{2,1,0:T(8,128)(2,1)S(1)} %get-tuple-element.14.refs_1_), channel_id=1, source_target_pairs={{0,224},{32,0},{64,32},{96,64},{128,96},{160,128},{192,160},{224,1... | collective-permute-start | bytes 1277960 | tf_op jit(solution)/shard_map/ppermute | solution.py:38
  36.8 6.2 %collective-permute-start.4 = (bf16[2,832,128]{2,1,0:T(8,128)(2,1)S(1)}, bf16[2,832,128]{2,1,0:T(8,128)(2,1)S(1)}, u32[]{:S(2)}, u32[]{:S(2)}) collective-permute-start(bf16[2,832,128]{2,1,0:T(8,128)(2,1)S(1)} %pad_maximum_fusion.refs_1_.refs_3_), channel_id=1, source_target_pairs={{0,8},{8,0},{1,9},{9,1},{2,10},{10,2},{3,11},{11,3},{4,12},{12,4},... | collective-permute-start | bytes 1277960 | tf_op jit(solution)/shard_map/ppermute | solution.py:38
  41.6 2.0 %collective-permute-start.6 = (bf16[2,832,128]{2,1,0:T(8,128)(2,1)S(1)}, bf16[2,832,128]{2,1,0:T(8,128)(2,1)S(1)}, u32[]{:S(2)}, u32[]{:S(2)}) collective-permute-start(bf16[2,832,128]{2,1,0:T(8,128)(2,1)S(1)} %collective-permute-done.3.refs_5_), channel_id=1, source_target_pairs={{0,8},{8,0},{1,9},{9,1},{2,10},{10,2},{3,11},{11,3},{4,12},{12,4},... | collective-permute-start | bytes 1277960 | tf_op jit(solution)/shard_map/ppermute | solution.py:38
  41.6 2.6 %collective-permute-start.5 = (bf16[2,832,128]{2,1,0:T(8,128)(2,1)S(1)}, bf16[2,832,128]{2,1,0:T(8,128)(2,1)S(1)}, u32[]{:S(2)}, u32[]{:S(2)}) collective-permute-start(bf16[2,832,128]{2,1,0:T(8,128)(2,1)S(1)} %collective-permute-done.2.refs_4_), channel_id=1, source_target_pairs={{0,8},{8,0},{1,9},{9,1},{2,10},{10,2},{3,11},{11,3},{4,12},{12,4},... | collective-permute-start | bytes 1277960 | tf_op jit(solution)/shard_map/ppermute | solution.py:38
  44.2 7.0 %collective-permute-start.11 = (bf16[1,832,128]{2,1,0:T(8,128)(2,1)S(1)}, bf16[1,832,128]{2,1,0:T(8,128)(2,1)S(1)}, u32[]{:S(2)}, u32[]{:S(2)}) collective-permute-start(bf16[1,832,128]{2,1,0:T(8,128)(2,1)S(1)} %get-tuple-element.15.refs_4_), channel_id=1, source_target_pairs={{0,32},{32,64},{64,96},{96,128},{128,160},{160,192},{192,224},{224... | collective-permute-start | bytes 638984 | tf_op jit(solution)/shard_map/ppermute | solution.py:38
  44.3 10.7 %collective-permute-start.12 = (bf16[1,832,128]{2,1,0:T(8,128)(2,1)S(1)}, bf16[1,832,128]{2,1,0:T(8,128)(2,1)S(1)}, u32[]{:S(2)}, u32[]{:S(2)}) collective-permute-start(bf16[1,832,128]{2,1,0:T(8,128)(2,1)S(1)} %get-tuple-element.16.refs_5_), channel_id=1, source_target_pairs={{0,224},{32,0},{64,32},{96,64},{128,96},{160,128},{192,160},{224,1... | collective-permute-start | bytes 638984 | tf_op jit(solution)/shard_map/ppermute | solution.py:38
  46.9 10.7 %collective-permute-start.13 = (bf16[2,832,128]{2,1,0:T(8,128)(2,1)S(1)}, bf16[2,832,128]{2,1,0:T(8,128)(2,1)S(1)}, u32[]{:S(2)}, u32[]{:S(2)}) collective-permute-start(bf16[2,832,128]{2,1,0:T(8,128)(2,1)S(1)} %get-tuple-element.17.refs_9_), channel_id=1, source_target_pairs={{0,8},{8,0},{1,9},{9,1},{2,10},{10,2},{3,11},{11,3},{4,12},{12,4},... | collective-permute-start | bytes 1277960 | tf_op jit(solution)/shard_map/ppermute | solution.py:38
  51.2 6.5 %collective-permute-start.14 = (bf16[2,832,128]{2,1,0:T(8,128)(2,1)S(1)}, bf16[2,832,128]{2,1,0:T(8,128)(2,1)S(1)}, u32[]{:S(2)}, u32[]{:S(2)}) collective-permute-start(bf16[2,832,128]{2,1,0:T(8,128)(2,1)S(1)} %get-tuple-element.18.refs_10_), channel_id=1, source_target_pairs={{0,8},{8,0},{1,9},{9,1},{2,10},{10,2},{3,11},{11,3},{4,12},{12,4},... | collective-permute-start | bytes 1277960 | tf_op jit(solution)/shard_map/ppermute | solution.py:38
  51.2 4.8 %collective-permute-start.17 = (bf16[1,832,128]{2,1,0:T(8,128)(2,1)S(1)}, bf16[1,832,128]{2,1,0:T(8,128)(2,1)S(1)}, u32[]{:S(2)}, u32[]{:S(2)}) collective-permute-start(bf16[1,832,128]{2,1,0:T(8,128)(2,1)S(1)} %collective-permute-done.11.refs_13_), channel_id=1, source_target_pairs={{0,8},{8,0},{1,9},{9,1},{2,10},{10,2},{3,11},{11,3},{4,12},{12,4},... | collective-permute-start | bytes 638984 | tf_op jit(solution)/shard_map/ppermute | solution.py:38
  55.0 2.7 %collective-permute-start.15 = (bf16[2,832,128]{2,1,0:T(8,128)(2,1)S(1)}, bf16[2,832,128]{2,1,0:T(8,128)(2,1)S(1)}, u32[]{:S(2)}, u32[]{:S(2)}) collective-permute-start(bf16[2,832,128]{2,1,0:T(8,128)(2,1)S(1)} %get-tuple-element.19.refs_11_), channel_id=1, source_target_pairs={{0,8},{8,0},{1,9},{9,1},{2,10},{10,2},{3,11},{11,3},{4,12},{12,4},... | collective-permute-start | bytes 1277960 | tf_op jit(solution)/shard_map/ppermute | solution.py:38
  55.0 2.7 %collective-permute-start.16 = (bf16[2,832,128]{2,1,0:T(8,128)(2,1)S(1)}, bf16[2,832,128]{2,1,0:T(8,128)(2,1)S(1)}, u32[]{:S(2)}, u32[]{:S(2)}) collective-permute-start(bf16[2,832,128]{2,1,0:T(8,128)(2,1)S(1)} %get-tuple-element.20.refs_12_), channel_id=1, source_target_pairs={{0,8},{8,0},{1,9},{9,1},{2,10},{10,2},{3,11},{11,3},{4,12},{12,4},... | collective-permute-start | bytes 1277960 | tf_op jit(solution)/shard_map/ppermute | solution.py:38
  56.1 1.6 %collective-permute-start.18 = (bf16[1,832,128]{2,1,0:T(8,128)(2,1)S(1)}, bf16[1,832,128]{2,1,0:T(8,128)(2,1)S(1)}, u32[]{:S(2)}, u32[]{:S(2)}) collective-permute-start(bf16[1,832,128]{2,1,0:T(8,128)(2,1)S(1)} %collective-permute-done.12.refs_14_), channel_id=1, source_target_pairs={{0,8},{8,0},{1,9},{9,1},{2,10},{10,2},{3,11},{11,3},{4,12},{12,4},... | collective-permute-start | bytes 638984 | tf_op jit(solution)/shard_map/ppermute | solution.py:38

commit v11 on v10

--- a/solution.py
+++ b/solution.py
@@ -94,34 +94,34 @@
     take = lambda n: [refs.pop(0) for _ in range(n)]
     idx_ref, span_ref, query_ref = take(3)
     piece_refs = take(len(layout))
-    out_ref, key_ref, w_ref, lo_ref, hi_ref, q_ref, mix_ref, key_sem, w_sem = refs
+    out_ref, key_ref, w_ref, lo_ref, hi_ref, q_ref, mix_ref = refs
     z, xh, core, slot0 = (idx_ref[i] for i in range(4))
     shards, latent_rows = key_ref.shape[:2]
     zs = shards // 4
     shard_rows = KV // shards
 
-    key_copies, wk_copies, wv_copies = [], [], []
-    for (dz, which), piece in zip(layout, piece_refs):
-        for j, (dx, dc) in enumerate(which):
-            zz = lax.rem(z + dz + zs, zs)
-            xx = 1 - xh if dx else xh
-            cc = 1 - core if dc else core
-            shard, n = (zz * 2 + xx) * 2 + cc, len(key_copies)
-            rows = w_ref.shape[2]
-            for i, w_copies in enumerate((wk_copies, wv_copies)):
-                src = piece.at[j, pl.ds(latent_rows + i * rows, rows)]
-                w_copies.append(
-                    pltpu.make_async_copy(src, w_ref.at[i, shard], w_sem.at[i, n])
-                )
-            place = span_ref[2 * shard]
-            key_rows = pl.ds(0, latent_rows)
-            key_copies.append(
-                pltpu.make_async_copy(piece.at[j, key_rows], key_ref.at[place], key_sem.at[n])
-            )
-    for copy in wk_copies + key_copies + wv_copies:
-        copy.start()
-    for copy in wk_copies:
-        copy.wait()
+    parts, w_rows = 4, w_ref.shape[2]
+
+    def sort(part, carry):
+        def quarter(rows):
+            size = rows // parts
+            return pl.ds(pl.multiple_of(part * size, size), size), size
+
+        keys, _ = quarter(latent_rows)
+        some, size = quarter(w_rows)
+        for (dz, which), piece in zip(layout, piece_refs):
+            for j, (dx, dc) in enumerate(which):
+                zz = lax.rem(z + dz + zs, zs)
+                xx = 1 - xh if dx else xh
+                cc = 1 - core if dc else core
+                shard = (zz * 2 + xx) * 2 + cc
+                key_ref[span_ref[2 * shard], keys, :] = piece[j, keys, :]
+                for i in range(2):
+                    at = pl.multiple_of(latent_rows + i * w_rows + part * size, size)
+                    w_ref[i, shard, some, :] = piece[j, pl.ds(at, size), :]
+        return carry
+
+    lax.fori_loop(0, parts, sort, 0)
 
     for h in range(heads):
         rows = slice(h * SPAN, (h + 1) * SPAN)
@@ -134,8 +134,6 @@
             q_ref[slot, rows, :KV] = q_latent[toks, :]
             q_ref[slot, rows, KV:] = q_rope[toks, :]
 
-    for copy in key_copies:
-        copy.wait()
     for i in range(0, shards, 2):
         left, right = key_ref[i], key_ref[i + 1]
         cols = slice(i * SPAN, (i + 2) * SPAN)
@@ -156,8 +154,6 @@
 
             lax.fori_loop(0, heads * SPAN // tile, body, 0)
 
-    for copy in wv_copies:
-        copy.wait()
     for h in range(heads):
         cols = slice(h * VDIM, (h + 1) * VDIM)
         rows = slice(h * SPAN, (h + 1) * SPAN)
@@ -179,7 +175,7 @@
         out_shape=jax.ShapeDtypeStruct((2 * SPAN, cols), b16),
         in_specs=[pl.BlockSpec(memory_space=pltpu.SMEM)] * 2
         + [vmem]
-        + [pl.BlockSpec(memory_space=pltpu.HBM)] * len(pieces),
+        + [vmem] * len(pieces),
         out_specs=vmem,
         scratch_shapes=[
             pltpu.VMEM((shards, KV + ROPE, 2 * SPAN), b16),
@@ -188,8 +184,6 @@
             pltpu.VMEM((KV + ROPE, shards * SPAN), b16),
             pltpu.VMEM((2, rows, KV + ROPE), b16),
             pltpu.VMEM((2, rows, KV), b16),
-            pltpu.SemaphoreType.DMA((shards,)),
-            pltpu.SemaphoreType.DMA((2, shards)),
         ],
         compiler_params=pltpu.CompilerParams(vmem_limit_bytes=36 << 20),
         cost_estimate=pl.CostEstimate(

time: 82.2 us -> 70.6 us (0.86)
  Pallas kernels: 23.9 us -> 12.4 us
    pallas_call x1, Pallas kernels: 23.9 us -> 12.4 us  [attention(): pl.pallas_call(functools.partial(attention_kernel, layout, heads, min(row...]
  transfers between devices with their start and end apart: 20 -> 20, of which waited for: 11 -> 11; matrix products, arithmetic and copies ran while one was open for 8% -> 9% of each run, Pallas kernels for 0% -> 0%
where the time goes in v11:
time: 70.6 us; the launch traced here: 70.1 us
  starting transfers between devices  37.1 us (53%)
  waiting for transfers between devices  13.8 us (20%)
  Pallas kernels  12.4 us (18%)
  matrix products  3.17 us (4%)
  local copies, waits for them, and re-layouts  2.4 us (3%)
  other arithmetic  1.06 us (2%)
    ppermute x18, starting transfers between devices, shift(): return lax.ppermute(x, axis, [(i, (i + by) % n) for i in range(n)])  29.6 us
    pallas_call x1, Pallas kernels, attention(): pl.pallas_call(functools.partial(attention_kernel, layout, heads, min(row...  12.4 us
    ppermute x18, waiting for transfers between devices, shift(): return lax.ppermute(x, axis, [(i, (i + by) % n) for i in range(n)])  11.6 us
    all_to_all x1, starting transfers between devices, per_device(): lax.all_to_all(copies, ('y', 'xl'), 0, 0, tiled=True).reshape(-1, toks)  4.19 us
    ppermute x1, starting transfers between devices, per_device(): across = lax.ppermute(own, ('xh', 'xl'), [(0, 3), (3, 0), (1, 2), (2, 1)])  3.31 us
    dot_general x1, matrix products, per_device(): lax.dot_general(features, w_uq, (((0,), (0,)), ((), ())), preferred_eleme...  3.17 us
    all_to_all x1, waiting for transfers between devices, per_device(): lax.all_to_all(copies, ('y', 'xl'), 0, 0, tiled=True).reshape(-1, toks)  2.27 us
    broadcast_in_dim x1, local copies, waits for them, and re-layouts, per_device(): jnp.broadcast_to(compressed.T[None], (ys * xls,) + compressed.T.shape)  1.59 us
  transfers between devices with their start and end apart: 20, of which 11 were waited for; matrix products, arithmetic and copies ran while one was open for 9% of the time, Pallas kernels for 0%

profile of v11, /device:TPU:1, one launch (start us, length us, event | category | flops | bytes accessed | tf_op | source)
XLA Modules:
  0.0 70.1 jit_solution(14264378770669351135)
XLA Ops:
  0.0 0.0 copy-start
  0.0 3.3 %collective-permute-start = (bf16[576,128]{1,0:T(8,128)(2,1)}, bf16[576,128]{1,0:T(8,128)(2,1)S(1)}, u32[]{:S(2)}, u32[]{:S(2)}) collective-permute-start(bf16[576,128]{1,0:T(8,128)(2,1)} %bitcast.34), channel_id=1, source_target_pairs={{0,17},{17,0},{1,16},{16,1},{2,19},{19,2},{3,18},{18,3},{4,21},{21... | collective-permute-start | bytes 442376 | tf_op jit(solution)/shard_map/ppermute | solution.py:203
  3.3 0.0 copy-done
  3.3 0.8 %copy_bitcast_fusion = bf16[16,8,128]{2,0,1:T(8,128)(2,1)S(1)} fusion(bf16[16,1024]{1,0:T(8,128)(2,1)} %param.10), kind=kLoop, calls=%fused_computation.5 | loop fusion | bytes 65536 | tf_op jit(solution)/shard_map/reshape | solution.py:51
  4.1 1.1 %collective-permute-start.1 = (bf16[256,128]{1,0:T(8,128)(2,1)S(1)}, bf16[256,128]{1,0:T(8,128)(2,1)S(1)}, u32[]{:S(2)}, u32[]{:S(2)}) collective-permute-start(bf16[256,128]{1,0:T(8,128)(2,1)S(1)} %pad_maximum_fusion.1), channel_id=1, source_target_pairs={{0,16},{16,0},{1,17},{17,1},{2,18},{18,2},{3,19},{19,3},{4,20},{20... | collective-permute-start | bytes 196616 | tf_op jit(solution)/shard_map/ppermute | solution.py:38
  5.2 0.9 %maximum_bitcast_fusion = bf16[1,832,128]{2,1,0:T(8,128)(2,1)S(1)} fusion(bf16[128,128]{1,0:T(8,128)(2,1)S(1)} %bitcast.33, bf16[128,128]{1,0:T(8,128)(2,1)S(1)} %bitcast.31, bf16[576,128]{1,0:T(8,128)(2,1)} %bitcast.35), kind=kLoop, calls=%fused_computation.2 | loop fusion | flops 638976 | bytes 425984 | tf_op jit(solution)/shard_map/stack | solution.py:206
  6.1 2.8 %collective-permute-done.1 = bf16[256,128]{1,0:T(8,128)(2,1)S(1)} collective-permute-done((bf16[256,128]{1,0:T(8,128)(2,1)S(1)}, bf16[256,128]{1,0:T(8,128)(2,1)S(1)}, u32[]{:S(2)}, u32[]{:S(2)}) %collective-permute-start.1) | collective-permute-done | bytes 65568 | tf_op jit(solution)/shard_map/ppermute | solution.py:38
  8.9 0.0 collective-permute-done
  9.0 5.5 %collective-permute-start.3 = (bf16[2,832,128]{2,1,0:T(8,128)(2,1)S(1)}, bf16[2,832,128]{2,1,0:T(8,128)(2,1)S(1)}, u32[]{:S(2)}, u32[]{:S(2)}) collective-permute-start(bf16[2,832,128]{2,1,0:T(8,128)(2,1)S(1)} %pad_maximum_fusion.refs_1_.refs_3_), channel_id=1, source_target_pairs={{0,224},{32,0},{64,32},{96,64},{128,96},{160,128},{192,160},{224,1... | collective-permute-start | bytes 1277960 | tf_op jit(solution)/shard_map/ppermute | solution.py:38
  14.5 0.0 collective-permute-start.2
  14.5 0.1 pad_add_fusion.refs_2_.refs_0_
  14.6 1.6 %broadcast_in_dim.2.refs_0_ = bf16[8,192,128]{2,1,0:T(8,128)(2,1)} broadcast(bf16[192,128]{1,0:T(8,128)(2,1)} %bitcast.36), dimensions={1,2} | broadcast | bytes 442368 | tf_op jit(solution)/shard_map/broadcast_in_dim | solution.py:210
  16.2 4.2 %all-to-all-start = ((bf16[8,192,128]{2,1,0:T(8,128)(2,1)}), bf16[8,192,128]{2,1,0:T(8,128)(2,1)S(1)}, u32[]{:S(2)}, u32[]{:S(2)}) async-start(bf16[8,192,128]{2,1,0:T(8,128)(2,1)} %shard_map.64), calls=%async_computation | async-start | bytes 786432 | tf_op jit(solution)/shard_map/all_to_all | solution.py:212
  20.4 1.1 %collective-permute-done.3.refs_5_ = bf16[2,832,128]{2,1,0:T(8,128)(2,1)S(1)} collective-permute-done((bf16[2,832,128]{2,1,0:T(8,128)(2,1)S(1)}, bf16[2,832,128]{2,1,0:T(8,128)(2,1)S(1)}, u32[]{:S(2)}, u32[]{:S(2)}) %collective-permute-start.3) | collective-permute-done | bytes 426016 | tf_op jit(solution)/shard_map/ppermute | solution.py:38
  21.5 3.4 %collective-permute-start.8 = (bf16[2,832,128]{2,1,0:T(8,128)(2,1)S(1)}, bf16[2,832,128]{2,1,0:T(8,128)(2,1)S(1)}, u32[]{:S(2)}, u32[]{:S(2)}) collective-permute-start(bf16[2,832,128]{2,1,0:T(8,128)(2,1)S(1)} %collective-permute-done.3.refs_5_), channel_id=1, source_target_pairs={{0,224},{32,0},{64,32},{96,64},{128,96},{160,128},{192,160},{224,1... | collective-permute-start | bytes 1277960 | tf_op jit(solution)/shard_map/ppermute | solution.py:38
  24.9 0.0 collective-permute-done.2.refs_4_
  25.0 0.0 collective-permute-start.7
  25.0 2.3 %all-to-all-done = bf16[8,192,128]{2,1,0:T(8,128)(2,1)S(1)} async-done(((bf16[8,192,128]{2,1,0:T(8,128)(2,1)}), bf16[8,192,128]{2,1,0:T(8,128)(2,1)S(1)}, u32[]{:S(2)}, u32[]{:S(2)}) %all-to-all-start) | async-done | bytes 393248 | tf_op jit(solution)/shard_map/all_to_all | solution.py:212
  27.2 0.0 copy-start.1
  27.2 3.2 %convolution_convert_fusion.refs_2_ = bf16[128,1536]{1,0:T(8,128)(2,1)S(1)} fusion(bf16[1536,128]{1,0:T(8,128)(2,1)S(1)} %bitcast.29, bf16[1536,1536]{1,0:T(8,128)(2,1)} %param.8), kind=kOutput, calls=%fused_computation | convolution fusion | flops 604176384 | bytes 5505024 | tf_op jit(solution)/shard_map/dot_general | solution.py:213
  30.4 0.6 collective-permute-done.8.refs_1_
  31.0 3.1 %collective-permute-done.7.refs_0_ = bf16[2,832,128]{2,1,0:T(8,128)(2,1)S(1)} collective-permute-done((bf16[2,832,128]{2,1,0:T(8,128)(2,1)S(1)}, bf16[2,832,128]{2,1,0:T(8,128)(2,1)S(1)}, u32[]{:S(2)}, u32[]{:S(2)}) %collective-permute-start.7) | collective-permute-done | bytes 426016 | tf_op jit(solution)/shard_map/ppermute | solution.py:38
  34.2 0.0 collective-permute-start.9
  34.2 2.7 %collective-permute-start.10 = (bf16[2,832,128]{2,1,0:T(8,128)(2,1)S(1)}, bf16[2,832,128]{2,1,0:T(8,128)(2,1)S(1)}, u32[]{:S(2)}, u32[]{:S(2)}) collective-permute-start(bf16[2,832,128]{2,1,0:T(8,128)(2,1)S(1)} %get-tuple-element.14.refs_1_), channel_id=1, source_target_pairs={{0,224},{32,0},{64,32},{96,64},{128,96},{160,128},{192,160},{224,1... | collective-permute-start | bytes 1277960 | tf_op jit(solution)/shard_map/ppermute | solution.py:38
  36.8 4.8 %collective-permute-start.4 = (bf16[2,832,128]{2,1,0:T(8,128)(2,1)S(1)}, bf16[2,832,128]{2,1,0:T(8,128)(2,1)S(1)}, u32[]{:S(2)}, u32[]{:S(2)}) collective-permute-start(bf16[2,832,128]{2,1,0:T(8,128)(2,1)S(1)} %pad_maximum_fusion.refs_1_.refs_3_), channel_id=1, source_target_pairs={{0,8},{8,0},{1,9},{9,1},{2,10},{10,2},{3,11},{11,3},{4,12},{12,4},... | collective-permute-start | bytes 1277960 | tf_op jit(solution)/shard_map/ppermute | solution.py:38
  41.6 0.0 collective-permute-start.6
  41.6 0.5 collective-permute-start.5
  42.1 0.2 collective-permute-done.9.refs_2_
  42.4 0.0 collective-permute-done.10.refs_3_
  42.4 0.6 collective-permute-done.4.refs_2_.refs_6_
  43.0 0.6 collective-permute-done.6.refs_4_.refs_8_
  43.6 0.6 collective-permute-done.5.refs_3_.refs_7_
  44.2 0.0 collective-permute-start.11
  44.3 2.7 %collective-permute-start.12 = (bf16[1,832,128]{2,1,0:T(8,128)(2,1)S(1)}, bf16[1,832,128]{2,1,0:T(8,128)(2,1)S(1)}, u32[]{:S(2)}, u32[]{:S(2)}) collective-permute-start(bf16[1,832,128]{2,1,0:T(8,128)(2,1)S(1)} %get-tuple-element.16.refs_5_), channel_id=1, source_target_pairs={{0,224},{32,0},{64,32},{96,64},{128,96},{160,128},{192,160},{224,1... | collective-permute-start | bytes 638984 | tf_op jit(solution)/shard_map/ppermute | solution.py:38
  46.9 4.3 %collective-permute-start.13 = (bf16[2,832,128]{2,1,0:T(8,128)(2,1)S(1)}, bf16[2,832,128]{2,1,0:T(8,128)(2,1)S(1)}, u32[]{:S(2)}, u32[]{:S(2)}) collective-permute-start(bf16[2,832,128]{2,1,0:T(8,128)(2,1)S(1)} %get-tuple-element.17.refs_9_), channel_id=1, source_target_pairs={{0,8},{8,0},{1,9},{9,1},{2,10},{10,2},{3,11},{11,3},{4,12},{12,4},... | collective-permute-start | bytes 1277960 | tf_op jit(solution)/shard_map/ppermute | solution.py:38
  51.2 0.0 collective-permute-start.14
  51.2 0.0 collective-permute-done.11.refs_13_
  51.2 3.8 %collective-permute-start.17 = (bf16[1,832,128]{2,1,0:T(8,128)(2,1)S(1)}, bf16[1,832,128]{2,1,0:T(8,128)(2,1)S(1)}, u32[]{:S(2)}, u32[]{:S(2)}) collective-permute-start(bf16[1,832,128]{2,1,0:T(8,128)(2,1)S(1)} %collective-permute-done.11.refs_13_), channel_id=1, source_target_pairs={{0,8},{8,0},{1,9},{9,1},{2,10},{10,2},{3,11},{11,3},{4,12},{12,4},... | collective-permute-start | bytes 638984 | tf_op jit(solution)/shard_map/ppermute | solution.py:38
  55.0 0.0 collective-permute-start.15
  55.0 0.0 collective-permute-done.12.refs_14_
  55.0 0.5 collective-permute-start.16
  55.5 0.6 collective-permute-done.17.refs_19_
  56.1 0.4 collective-permute-start.18
  56.4 1.2 %collective-permute-done.18.refs_20_ = bf16[1,832,128]{2,1,0:T(8,128)(2,1)S(1)} collective-permute-done((bf16[1,832,128]{2,1,0:T(8,128)(2,1)S(1)}, bf16[1,832,128]{2,1,0:T(8,128)(2,1)S(1)}, u32[]{:S(2)}, u32[]{:S(2)}) %collective-permute-start.18) | collective-permute-done | bytes 213024 | tf_op jit(solution)/shard_map/ppermute | solution.py:38
  57.6 0.0 collective-permute-done.13.refs_15_
  57.7 0.0 collective-permute-done.14.refs_16_
  57.7 0.0 collective-permute-done.15.refs_17_
  57.7 0.0 collective-permute-done.16.refs_18_
  57.7 0.0 copy-done.1
  57.7 12.4 %shard_map.68 = bf16[128,1024]{1,0:T(8,128)(2,1)} custom-call(s32[4]{0:T(128)S(1)} %pad_add_fusion.refs_2_.refs_0_, s32[64]{0:T(128)S(1)} %copy-done.1, bf16[128,1536]{1,0:T(8,128)(2,1)S(1)} %convolution_convert_fusion.refs_2_, bf16[2,832,128]{2,1,0:T(8,128)(2,1)S(1)} %pad_maximum_fusion.refs_1_.refs_3_, ...), custom_call_target="tpu_custom_call" | custom-call | flops 5704253440 | bytes 7209232 | tf_op jit(solution)/shard_map/pallas_call | solution.py:173
  (10 shorter events, 0.1 us)
Async XLA Ops:
  0.0 3.3 %copy-start = (bf16[16,1024]{1,0:T(8,128)(2,1)S(1)}, bf16[16,1024]{1,0:T(8,128)(2,1)}, u32[]{:S(2)}) copy-start(bf16[16,1024]{1,0:T(8,128)(2,1)} %param.9) | copy-start | bytes 98308
  0.0 8.9 %collective-permute-start = (bf16[576,128]{1,0:T(8,128)(2,1)}, bf16[576,128]{1,0:T(8,128)(2,1)S(1)}, u32[]{:S(2)}, u32[]{:S(2)}) collective-permute-start(bf16[576,128]{1,0:T(8,128)(2,1)} %bitcast.34), channel_id=1, source_target_pairs={{0,17},{17,0},{1,16},{16,1},{2,19},{19,2},{3,18},{18,3},{4,21},{21... | collective-permute-start | bytes 442376 | tf_op jit(solution)/shard_map/ppermute | solution.py:203
  4.1 4.8 %collective-permute-start.1 = (bf16[256,128]{1,0:T(8,128)(2,1)S(1)}, bf16[256,128]{1,0:T(8,128)(2,1)S(1)}, u32[]{:S(2)}, u32[]{:S(2)}) collective-permute-start(bf16[256,128]{1,0:T(8,128)(2,1)S(1)} %pad_maximum_fusion.1), channel_id=1, source_target_pairs={{0,16},{16,0},{1,17},{17,1},{2,18},{18,2},{3,19},{19,3},{4,20},{20... | collective-permute-start | bytes 196616 | tf_op jit(solution)/shard_map/ppermute | solution.py:38
  9.0 12.5 %collective-permute-start.3 = (bf16[2,832,128]{2,1,0:T(8,128)(2,1)S(1)}, bf16[2,832,128]{2,1,0:T(8,128)(2,1)S(1)}, u32[]{:S(2)}, u32[]{:S(2)}) collective-permute-start(bf16[2,832,128]{2,1,0:T(8,128)(2,1)S(1)} %pad_maximum_fusion.refs_1_.refs_3_), channel_id=1, source_target_pairs={{0,224},{32,0},{64,32},{96,64},{128,96},{160,128},{192,160},{224,1... | collective-permute-start | bytes 1277960 | tf_op jit(solution)/shard_map/ppermute | solution.py:38
  14.5 10.4 %collective-permute-start.2 = (bf16[2,832,128]{2,1,0:T(8,128)(2,1)S(1)}, bf16[2,832,128]{2,1,0:T(8,128)(2,1)S(1)}, u32[]{:S(2)}, u32[]{:S(2)}) collective-permute-start(bf16[2,832,128]{2,1,0:T(8,128)(2,1)S(1)} %pad_maximum_fusion.refs_1_.refs_3_), channel_id=1, source_target_pairs={{0,32},{32,64},{64,96},{96,128},{128,160},{160,192},{192,224},{224... | collective-permute-start | bytes 1277960 | tf_op jit(solution)/shard_map/ppermute | solution.py:38
  16.2 11.0 %all-to-all-start = ((bf16[8,192,128]{2,1,0:T(8,128)(2,1)}), bf16[8,192,128]{2,1,0:T(8,128)(2,1)S(1)}, u32[]{:S(2)}, u32[]{:S(2)}) async-start(bf16[8,192,128]{2,1,0:T(8,128)(2,1)} %shard_map.64), calls=%async_computation | async-start | bytes 786432 | tf_op jit(solution)/shard_map/all_to_all | solution.py:212
  21.5 9.5 %collective-permute-start.8 = (bf16[2,832,128]{2,1,0:T(8,128)(2,1)S(1)}, bf16[2,832,128]{2,1,0:T(8,128)(2,1)S(1)}, u32[]{:S(2)}, u32[]{:S(2)}) collective-permute-start(bf16[2,832,128]{2,1,0:T(8,128)(2,1)S(1)} %collective-permute-done.3.refs_5_), channel_id=1, source_target_pairs={{0,224},{32,0},{64,32},{96,64},{128,96},{160,128},{192,160},{224,1... | collective-permute-start | bytes 1277960 | tf_op jit(solution)/shard_map/ppermute | solution.py:38
  25.0 9.2 %collective-permute-start.7 = (bf16[2,832,128]{2,1,0:T(8,128)(2,1)S(1)}, bf16[2,832,128]{2,1,0:T(8,128)(2,1)S(1)}, u32[]{:S(2)}, u32[]{:S(2)}) collective-permute-start(bf16[2,832,128]{2,1,0:T(8,128)(2,1)S(1)} %collective-permute-done.2.refs_4_), channel_id=1, source_target_pairs={{0,32},{32,64},{64,96},{96,128},{128,160},{160,192},{192,224},{224... | collective-permute-start | bytes 1277960 | tf_op jit(solution)/shard_map/ppermute | solution.py:38
  27.2 30.4 %copy-start.1 = (s32[64]{0:T(128)S(1)}, s32[64]{0:T(128)}, u32[]{:S(2)}) copy-start(s32[64]{0:T(128)} %refs_1_.1) | copy-start | bytes 772
  34.2 8.2 %collective-permute-start.9 = (bf16[2,832,128]{2,1,0:T(8,128)(2,1)S(1)}, bf16[2,832,128]{2,1,0:T(8,128)(2,1)S(1)}, u32[]{:S(2)}, u32[]{:S(2)}) collective-permute-start(bf16[2,832,128]{2,1,0:T(8,128)(2,1)S(1)} %get-tuple-element.13.refs_0_), channel_id=1, source_target_pairs={{0,32},{32,64},{64,96},{96,128},{128,160},{160,192},{192,224},{224... | collective-permute-start | bytes 1277960 | tf_op jit(solution)/shard_map/ppermute | solution.py:38
  34.2 8.2 %collective-permute-start.10 = (bf16[2,832,128]{2,1,0:T(8,128)(2,1)S(1)}, bf16[2,832,128]{2,1,0:T(8,128)(2,1)S(1)}, u32[]{:S(2)}, u32[]{:S(2)}) collective-permute-start(bf16[2,832,128]{2,1,0:T(8,128)(2,1)S(1)} %get-tuple-element.14.refs_1_), channel_id=1, source_target_pairs={{0,224},{32,0},{64,32},{96,64},{128,96},{160,128},{192,160},{224,1... | collective-permute-start | bytes 1277960 | tf_op jit(solution)/shard_map/ppermute | solution.py:38
  36.8 6.2 %collective-permute-start.4 = (bf16[2,832,128]{2,1,0:T(8,128)(2,1)S(1)}, bf16[2,832,128]{2,1,0:T(8,128)(2,1)S(1)}, u32[]{:S(2)}, u32[]{:S(2)}) collective-permute-start(bf16[2,832,128]{2,1,0:T(8,128)(2,1)S(1)} %pad_maximum_fusion.refs_1_.refs_3_), channel_id=1, source_target_pairs={{0,8},{8,0},{1,9},{9,1},{2,10},{10,2},{3,11},{11,3},{4,12},{12,4},... | collective-permute-start | bytes 1277960 | tf_op jit(solution)/shard_map/ppermute | solution.py:38
  41.6 2.0 %collective-permute-start.6 = (bf16[2,832,128]{2,1,0:T(8,128)(2,1)S(1)}, bf16[2,832,128]{2,1,0:T(8,128)(2,1)S(1)}, u32[]{:S(2)}, u32[]{:S(2)}) collective-permute-start(bf16[2,832,128]{2,1,0:T(8,128)(2,1)S(1)} %collective-permute-done.3.refs_5_), channel_id=1, source_target_pairs={{0,8},{8,0},{1,9},{9,1},{2,10},{10,2},{3,11},{11,3},{4,12},{12,4},... | collective-permute-start | bytes 1277960 | tf_op jit(solution)/shard_map/ppermute | solution.py:38
  41.6 2.6 %collective-permute-start.5 = (bf16[2,832,128]{2,1,0:T(8,128)(2,1)S(1)}, bf16[2,832,128]{2,1,0:T(8,128)(2,1)S(1)}, u32[]{:S(2)}, u32[]{:S(2)}) collective-permute-start(bf16[2,832,128]{2,1,0:T(8,128)(2,1)S(1)} %collective-permute-done.2.refs_4_), channel_id=1, source_target_pairs={{0,8},{8,0},{1,9},{9,1},{2,10},{10,2},{3,11},{11,3},{4,12},{12,4},... | collective-permute-start | bytes 1277960 | tf_op jit(solution)/shard_map/ppermute | solution.py:38
  44.2 7.0 %collective-permute-start.11 = (bf16[1,832,128]{2,1,0:T(8,128)(2,1)S(1)}, bf16[1,832,128]{2,1,0:T(8,128)(2,1)S(1)}, u32[]{:S(2)}, u32[]{:S(2)}) collective-permute-start(bf16[1,832,128]{2,1,0:T(8,128)(2,1)S(1)} %get-tuple-element.15.refs_4_), channel_id=1, source_target_pairs={{0,32},{32,64},{64,96},{96,128},{128,160},{160,192},{192,224},{224... | collective-permute-start | bytes 638984 | tf_op jit(solution)/shard_map/ppermute | solution.py:38
  44.3 10.7 %collective-permute-start.12 = (bf16[1,832,128]{2,1,0:T(8,128)(2,1)S(1)}, bf16[1,832,128]{2,1,0:T(8,128)(2,1)S(1)}, u32[]{:S(2)}, u32[]{:S(2)}) collective-permute-start(bf16[1,832,128]{2,1,0:T(8,128)(2,1)S(1)} %get-tuple-element.16.refs_5_), channel_id=1, source_target_pairs={{0,224},{32,0},{64,32},{96,64},{128,96},{160,128},{192,160},{224,1... | collective-permute-start | bytes 638984 | tf_op jit(solution)/shard_map/ppermute | solution.py:38
  46.9 10.7 %collective-permute-start.13 = (bf16[2,832,128]{2,1,0:T(8,128)(2,1)S(1)}, bf16[2,832,128]{2,1,0:T(8,128)(2,1)S(1)}, u32[]{:S(2)}, u32[]{:S(2)}) collective-permute-start(bf16[2,832,128]{2,1,0:T(8,128)(2,1)S(1)} %get-tuple-element.17.refs_9_), channel_id=1, source_target_pairs={{0,8},{8,0},{1,9},{9,1},{2,10},{10,2},{3,11},{11,3},{4,12},{12,4},... | collective-permute-start | bytes 1277960 | tf_op jit(solution)/shard_map/ppermute | solution.py:38
  51.2 6.5 %collective-permute-start.14 = (bf16[2,832,128]{2,1,0:T(8,128)(2,1)S(1)}, bf16[2,832,128]{2,1,0:T(8,128)(2,1)S(1)}, u32[]{:S(2)}, u32[]{:S(2)}) collective-permute-start(bf16[2,832,128]{2,1,0:T(8,128)(2,1)S(1)} %get-tuple-element.18.refs_10_), channel_id=1, source_target_pairs={{0,8},{8,0},{1,9},{9,1},{2,10},{10,2},{3,11},{11,3},{4,12},{12,4},... | collective-permute-start | bytes 1277960 | tf_op jit(solution)/shard_map/ppermute | solution.py:38
  51.2 4.8 %collective-permute-start.17 = (bf16[1,832,128]{2,1,0:T(8,128)(2,1)S(1)}, bf16[1,832,128]{2,1,0:T(8,128)(2,1)S(1)}, u32[]{:S(2)}, u32[]{:S(2)}) collective-permute-start(bf16[1,832,128]{2,1,0:T(8,128)(2,1)S(1)} %collective-permute-done.11.refs_13_), channel_id=1, source_target_pairs={{0,8},{8,0},{1,9},{9,1},{2,10},{10,2},{3,11},{11,3},{4,12},{12,4},... | collective-permute-start | bytes 638984 | tf_op jit(solution)/shard_map/ppermute | solution.py:38
  55.0 2.7 %collective-permute-start.15 = (bf16[2,832,128]{2,1,0:T(8,128)(2,1)S(1)}, bf16[2,832,128]{2,1,0:T(8,128)(2,1)S(1)}, u32[]{:S(2)}, u32[]{:S(2)}) collective-permute-start(bf16[2,832,128]{2,1,0:T(8,128)(2,1)S(1)} %get-tuple-element.19.refs_11_), channel_id=1, source_target_pairs={{0,8},{8,0},{1,9},{9,1},{2,10},{10,2},{3,11},{11,3},{4,12},{12,4},... | collective-permute-start | bytes 1277960 | tf_op jit(solution)/shard_map/ppermute | solution.py:38
  55.0 2.7 %collective-permute-start.16 = (bf16[2,832,128]{2,1,0:T(8,128)(2,1)S(1)}, bf16[2,832,128]{2,1,0:T(8,128)(2,1)S(1)}, u32[]{:S(2)}, u32[]{:S(2)}) collective-permute-start(bf16[2,832,128]{2,1,0:T(8,128)(2,1)S(1)} %get-tuple-element.20.refs_12_), channel_id=1, source_target_pairs={{0,8},{8,0},{1,9},{9,1},{2,10},{10,2},{3,11},{11,3},{4,12},{12,4},... | collective-permute-start | bytes 1277960 | tf_op jit(solution)/shard_map/ppermute | solution.py:38
  56.1 1.6 %collective-permute-start.18 = (bf16[1,832,128]{2,1,0:T(8,128)(2,1)S(1)}, bf16[1,832,128]{2,1,0:T(8,128)(2,1)S(1)}, u32[]{:S(2)}, u32[]{:S(2)}) collective-permute-start(bf16[1,832,128]{2,1,0:T(8,128)(2,1)S(1)} %collective-permute-done.12.refs_14_), channel_id=1, source_target_pairs={{0,8},{8,0},{1,9},{9,1},{2,10},{10,2},{3,11},{11,3},{4,12},{12,4},... | collective-permute-start | bytes 638984 | tf_op jit(solution)/shard_map/ppermute | solution.py:38

commit v12 on v11

--- a/solution.py
+++ b/solution.py
@@ -100,25 +100,25 @@
     zs = shards // 4
     shard_rows = KV // shards
 
-    parts, w_rows = 4, w_ref.shape[2]
+    moves = []
+    for (dz, which), piece in zip(layout, piece_refs):
+        zz = lax.rem(z + dz + zs, zs)
+        for j, (dx, dc) in enumerate(which):
+            xx = 1 - xh if dx else xh
+            cc = 1 - core if dc else core
+            shard = (zz * 2 + xx) * 2 + cc
+            moves.append((piece, j, shard, span_ref[2 * shard]))
+    parts, w_rows = 2, w_ref.shape[2]
+    key_size, w_size = latent_rows // parts, w_rows // parts
 
     def sort(part, carry):
-        def quarter(rows):
-            size = rows // parts
-            return pl.ds(pl.multiple_of(part * size, size), size), size
-
-        keys, _ = quarter(latent_rows)
-        some, size = quarter(w_rows)
-        for (dz, which), piece in zip(layout, piece_refs):
-            for j, (dx, dc) in enumerate(which):
-                zz = lax.rem(z + dz + zs, zs)
-                xx = 1 - xh if dx else xh
-                cc = 1 - core if dc else core
-                shard = (zz * 2 + xx) * 2 + cc
-                key_ref[span_ref[2 * shard], keys, :] = piece[j, keys, :]
-                for i in range(2):
-                    at = pl.multiple_of(latent_rows + i * w_rows + part * size, size)
-                    w_ref[i, shard, some, :] = piece[j, pl.ds(at, size), :]
+        keys = pl.ds(pl.multiple_of(part * key_size, key_size), key_size)
+        some = pl.ds(pl.multiple_of(part * w_size, w_size), w_size)
+        for piece, j, shard, place in moves:
+            key_ref[place, keys, :] = piece[j, keys, :]
+            for i in range(2):
+                at = pl.multiple_of(latent_rows + i * w_rows + part * w_size, w_size)
+                w_ref[i, shard, some, :] = piece[j, pl.ds(at, w_size), :]
         return carry
 
     lax.fori_loop(0, parts, sort, 0)

time: 70.6 us -> 70.5 us (level)
  no operation moved by 1% of the time
where the time goes in v12:
time: 70.5 us; the launch traced here: 70.1 us
  starting transfers between devices  37.1 us (53%)
  waiting for transfers between devices  13.8 us (20%)
  Pallas kernels  12.5 us (18%)
  matrix products  3.17 us (4%)
  local copies, waits for them, and re-layouts  2.4 us (3%)
  other arithmetic  1.06 us (2%)
    ppermute x18, starting transfers between devices, shift(): return lax.ppermute(x, axis, [(i, (i + by) % n) for i in range(n)])  29.6 us
    pallas_call x1, Pallas kernels, attention(): pl.pallas_call(functools.partial(attention_kernel, layout, heads, min(row...  12.5 us
    ppermute x18, waiting for transfers between devices, shift(): return lax.ppermute(x, axis, [(i, (i + by) % n) for i in range(n)])  11.6 us
    all_to_all x1, starting transfers between devices, per_device(): lax.all_to_all(copies, ('y', 'xl'), 0, 0, tiled=True).reshape(-1, toks)  4.19 us
    ppermute x1, starting transfers between devices, per_device(): across = lax.ppermute(own, ('xh', 'xl'), [(0, 3), (3, 0), (1, 2), (2, 1)])  3.31 us
    dot_general x1, matrix products, per_device(): lax.dot_general(features, w_uq, (((0,), (0,)), ((), ())), preferred_eleme...  3.17 us
    all_to_all x1, waiting for transfers between devices, per_device(): lax.all_to_all(copies, ('y', 'xl'), 0, 0, tiled=True).reshape(-1, toks)  2.27 us
    broadcast_in_dim x1, local copies, waits for them, and re-layouts, per_device(): jnp.broadcast_to(compressed.T[None], (ys * xls,) + compressed.T.shape)  1.59 us
  transfers between devices with their start and end apart: 20, of which 11 were waited for; matrix products, arithmetic and copies ran while one was open for 9% of the time, Pallas kernels for 0%

profile of v12, /device:TPU:1, one launch (start us, length us, event | category | flops | bytes accessed | tf_op | source)
XLA Modules:
  0.0 70.1 jit_solution(15653771209102587032)
XLA Ops:
  0.0 0.0 copy-start
  0.0 3.3 %collective-permute-start = (bf16[576,128]{1,0:T(8,128)(2,1)}, bf16[576,128]{1,0:T(8,128)(2,1)S(1)}, u32[]{:S(2)}, u32[]{:S(2)}) collective-permute-start(bf16[576,128]{1,0:T(8,128)(2,1)} %bitcast.34), channel_id=1, source_target_pairs={{0,17},{17,0},{1,16},{16,1},{2,19},{19,2},{3,18},{18,3},{4,21},{21... | collective-permute-start | bytes 442376 | tf_op jit(solution)/shard_map/ppermute | solution.py:203
  3.3 0.0 copy-done
  3.3 0.8 %copy_bitcast_fusion = bf16[16,8,128]{2,0,1:T(8,128)(2,1)S(1)} fusion(bf16[16,1024]{1,0:T(8,128)(2,1)} %param.10), kind=kLoop, calls=%fused_computation.5 | loop fusion | bytes 65536 | tf_op jit(solution)/shard_map/reshape | solution.py:51
  4.1 1.1 %collective-permute-start.1 = (bf16[256,128]{1,0:T(8,128)(2,1)S(1)}, bf16[256,128]{1,0:T(8,128)(2,1)S(1)}, u32[]{:S(2)}, u32[]{:S(2)}) collective-permute-start(bf16[256,128]{1,0:T(8,128)(2,1)S(1)} %pad_maximum_fusion.1), channel_id=1, source_target_pairs={{0,16},{16,0},{1,17},{17,1},{2,18},{18,2},{3,19},{19,3},{4,20},{20... | collective-permute-start | bytes 196616 | tf_op jit(solution)/shard_map/ppermute | solution.py:38
  5.2 0.9 %maximum_bitcast_fusion = bf16[1,832,128]{2,1,0:T(8,128)(2,1)S(1)} fusion(bf16[128,128]{1,0:T(8,128)(2,1)S(1)} %bitcast.33, bf16[128,128]{1,0:T(8,128)(2,1)S(1)} %bitcast.31, bf16[576,128]{1,0:T(8,128)(2,1)} %bitcast.35), kind=kLoop, calls=%fused_computation.2 | loop fusion | flops 638976 | bytes 425984 | tf_op jit(solution)/shard_map/stack | solution.py:206
  6.1 2.8 %collective-permute-done.1 = bf16[256,128]{1,0:T(8,128)(2,1)S(1)} collective-permute-done((bf16[256,128]{1,0:T(8,128)(2,1)S(1)}, bf16[256,128]{1,0:T(8,128)(2,1)S(1)}, u32[]{:S(2)}, u32[]{:S(2)}) %collective-permute-start.1) | collective-permute-done | bytes 65568 | tf_op jit(solution)/shard_map/ppermute | solution.py:38
  8.9 0.0 collective-permute-done
  9.0 5.5 %collective-permute-start.3 = (bf16[2,832,128]{2,1,0:T(8,128)(2,1)S(1)}, bf16[2,832,128]{2,1,0:T(8,128)(2,1)S(1)}, u32[]{:S(2)}, u32[]{:S(2)}) collective-permute-start(bf16[2,832,128]{2,1,0:T(8,128)(2,1)S(1)} %pad_maximum_fusion.refs_1_.refs_3_), channel_id=1, source_target_pairs={{0,224},{32,0},{64,32},{96,64},{128,96},{160,128},{192,160},{224,1... | collective-permute-start | bytes 1277960 | tf_op jit(solution)/shard_map/ppermute | solution.py:38
  14.5 0.0 collective-permute-start.2
  14.5 0.1 pad_add_fusion.refs_2_.refs_0_
  14.6 1.6 %broadcast_in_dim.2.refs_0_ = bf16[8,192,128]{2,1,0:T(8,128)(2,1)} broadcast(bf16[192,128]{1,0:T(8,128)(2,1)} %bitcast.36), dimensions={1,2} | broadcast | bytes 442368 | tf_op jit(solution)/shard_map/broadcast_in_dim | solution.py:210
  16.2 4.2 %all-to-all-start = ((bf16[8,192,128]{2,1,0:T(8,128)(2,1)}), bf16[8,192,128]{2,1,0:T(8,128)(2,1)S(1)}, u32[]{:S(2)}, u32[]{:S(2)}) async-start(bf16[8,192,128]{2,1,0:T(8,128)(2,1)} %shard_map.64), calls=%async_computation | async-start | bytes 786432 | tf_op jit(solution)/shard_map/all_to_all | solution.py:212
  20.4 1.1 %collective-permute-done.3.refs_5_ = bf16[2,832,128]{2,1,0:T(8,128)(2,1)S(1)} collective-permute-done((bf16[2,832,128]{2,1,0:T(8,128)(2,1)S(1)}, bf16[2,832,128]{2,1,0:T(8,128)(2,1)S(1)}, u32[]{:S(2)}, u32[]{:S(2)}) %collective-permute-start.3) | collective-permute-done | bytes 426016 | tf_op jit(solution)/shard_map/ppermute | solution.py:38
  21.5 3.4 %collective-permute-start.8 = (bf16[2,832,128]{2,1,0:T(8,128)(2,1)S(1)}, bf16[2,832,128]{2,1,0:T(8,128)(2,1)S(1)}, u32[]{:S(2)}, u32[]{:S(2)}) collective-permute-start(bf16[2,832,128]{2,1,0:T(8,128)(2,1)S(1)} %collective-permute-done.3.refs_5_), channel_id=1, source_target_pairs={{0,224},{32,0},{64,32},{96,64},{128,96},{160,128},{192,160},{224,1... | collective-permute-start | bytes 1277960 | tf_op jit(solution)/shard_map/ppermute | solution.py:38
  24.9 0.0 collective-permute-done.2.refs_4_
  25.0 0.0 collective-permute-start.7
  25.0 2.3 %all-to-all-done = bf16[8,192,128]{2,1,0:T(8,128)(2,1)S(1)} async-done(((bf16[8,192,128]{2,1,0:T(8,128)(2,1)}), bf16[8,192,128]{2,1,0:T(8,128)(2,1)S(1)}, u32[]{:S(2)}, u32[]{:S(2)}) %all-to-all-start) | async-done | bytes 393248 | tf_op jit(solution)/shard_map/all_to_all | solution.py:212
  27.2 0.0 copy-start.1
  27.2 3.2 %convolution_convert_fusion.refs_2_ = bf16[128,1536]{1,0:T(8,128)(2,1)S(1)} fusion(bf16[1536,128]{1,0:T(8,128)(2,1)S(1)} %bitcast.29, bf16[1536,1536]{1,0:T(8,128)(2,1)} %param.8), kind=kOutput, calls=%fused_computation | convolution fusion | flops 604176384 | bytes 5505024 | tf_op jit(solution)/shard_map/dot_general | solution.py:213
  30.4 0.6 collective-permute-done.8.refs_1_
  31.0 3.1 %collective-permute-done.7.refs_0_ = bf16[2,832,128]{2,1,0:T(8,128)(2,1)S(1)} collective-permute-done((bf16[2,832,128]{2,1,0:T(8,128)(2,1)S(1)}, bf16[2,832,128]{2,1,0:T(8,128)(2,1)S(1)}, u32[]{:S(2)}, u32[]{:S(2)}) %collective-permute-start.7) | collective-permute-done | bytes 426016 | tf_op jit(solution)/shard_map/ppermute | solution.py:38
  34.2 0.0 collective-permute-start.9
  34.2 2.7 %collective-permute-start.10 = (bf16[2,832,128]{2,1,0:T(8,128)(2,1)S(1)}, bf16[2,832,128]{2,1,0:T(8,128)(2,1)S(1)}, u32[]{:S(2)}, u32[]{:S(2)}) collective-permute-start(bf16[2,832,128]{2,1,0:T(8,128)(2,1)S(1)} %get-tuple-element.14.refs_1_), channel_id=1, source_target_pairs={{0,224},{32,0},{64,32},{96,64},{128,96},{160,128},{192,160},{224,1... | collective-permute-start | bytes 1277960 | tf_op jit(solution)/shard_map/ppermute | solution.py:38
  36.8 4.8 %collective-permute-start.4 = (bf16[2,832,128]{2,1,0:T(8,128)(2,1)S(1)}, bf16[2,832,128]{2,1,0:T(8,128)(2,1)S(1)}, u32[]{:S(2)}, u32[]{:S(2)}) collective-permute-start(bf16[2,832,128]{2,1,0:T(8,128)(2,1)S(1)} %pad_maximum_fusion.refs_1_.refs_3_), channel_id=1, source_target_pairs={{0,8},{8,0},{1,9},{9,1},{2,10},{10,2},{3,11},{11,3},{4,12},{12,4},... | collective-permute-start | bytes 1277960 | tf_op jit(solution)/shard_map/ppermute | solution.py:38
  41.6 0.0 collective-permute-start.6
  41.6 0.5 collective-permute-start.5
  42.1 0.2 collective-permute-done.9.refs_2_
  42.4 0.0 collective-permute-done.10.refs_3_
  42.4 0.6 collective-permute-done.4.refs_2_.refs_6_
  43.0 0.6 collective-permute-done.6.refs_4_.refs_8_
  43.6 0.6 collective-permute-done.5.refs_3_.refs_7_
  44.2 0.0 collective-permute-start.11
  44.3 2.7 %collective-permute-start.12 = (bf16[1,832,128]{2,1,0:T(8,128)(2,1)S(1)}, bf16[1,832,128]{2,1,0:T(8,128)(2,1)S(1)}, u32[]{:S(2)}, u32[]{:S(2)}) collective-permute-start(bf16[1,832,128]{2,1,0:T(8,128)(2,1)S(1)} %get-tuple-element.16.refs_5_), channel_id=1, source_target_pairs={{0,224},{32,0},{64,32},{96,64},{128,96},{160,128},{192,160},{224,1... | collective-permute-start | bytes 638984 | tf_op jit(solution)/shard_map/ppermute | solution.py:38
  46.9 4.3 %collective-permute-start.13 = (bf16[2,832,128]{2,1,0:T(8,128)(2,1)S(1)}, bf16[2,832,128]{2,1,0:T(8,128)(2,1)S(1)}, u32[]{:S(2)}, u32[]{:S(2)}) collective-permute-start(bf16[2,832,128]{2,1,0:T(8,128)(2,1)S(1)} %get-tuple-element.17.refs_9_), channel_id=1, source_target_pairs={{0,8},{8,0},{1,9},{9,1},{2,10},{10,2},{3,11},{11,3},{4,12},{12,4},... | collective-permute-start | bytes 1277960 | tf_op jit(solution)/shard_map/ppermute | solution.py:38
  51.2 0.0 collective-permute-start.14
  51.2 0.0 collective-permute-done.11.refs_13_
  51.2 3.8 %collective-permute-start.17 = (bf16[1,832,128]{2,1,0:T(8,128)(2,1)S(1)}, bf16[1,832,128]{2,1,0:T(8,128)(2,1)S(1)}, u32[]{:S(2)}, u32[]{:S(2)}) collective-permute-start(bf16[1,832,128]{2,1,0:T(8,128)(2,1)S(1)} %collective-permute-done.11.refs_13_), channel_id=1, source_target_pairs={{0,8},{8,0},{1,9},{9,1},{2,10},{10,2},{3,11},{11,3},{4,12},{12,4},... | collective-permute-start | bytes 638984 | tf_op jit(solution)/shard_map/ppermute | solution.py:38
  55.0 0.0 collective-permute-start.15
  55.0 0.0 collective-permute-done.12.refs_14_
  55.0 0.5 collective-permute-start.16
  55.5 0.6 collective-permute-done.17.refs_19_
  56.1 0.4 collective-permute-start.18
  56.4 1.2 %collective-permute-done.18.refs_20_ = bf16[1,832,128]{2,1,0:T(8,128)(2,1)S(1)} collective-permute-done((bf16[1,832,128]{2,1,0:T(8,128)(2,1)S(1)}, bf16[1,832,128]{2,1,0:T(8,128)(2,1)S(1)}, u32[]{:S(2)}, u32[]{:S(2)}) %collective-permute-start.18) | collective-permute-done | bytes 213024 | tf_op jit(solution)/shard_map/ppermute | solution.py:38
  57.6 0.0 collective-permute-done.13.refs_15_
  57.7 0.0 collective-permute-done.14.refs_16_
  57.7 0.0 collective-permute-done.15.refs_17_
  57.7 0.0 collective-permute-done.16.refs_18_
  57.7 0.0 copy-done.1
  57.7 12.5 %shard_map.68 = bf16[128,1024]{1,0:T(8,128)(2,1)} custom-call(s32[4]{0:T(128)S(1)} %pad_add_fusion.refs_2_.refs_0_, s32[64]{0:T(128)S(1)} %copy-done.1, bf16[128,1536]{1,0:T(8,128)(2,1)S(1)} %convolution_convert_fusion.refs_2_, bf16[2,832,128]{2,1,0:T(8,128)(2,1)S(1)} %pad_maximum_fusion.refs_1_.refs_3_, ...), custom_call_target="tpu_custom_call" | custom-call | flops 5704253440 | bytes 7209232 | tf_op jit(solution)/shard_map/pallas_call | solution.py:173
  (10 shorter events, 0.1 us)
Async XLA Ops:
  0.0 3.3 %copy-start = (bf16[16,1024]{1,0:T(8,128)(2,1)S(1)}, bf16[16,1024]{1,0:T(8,128)(2,1)}, u32[]{:S(2)}) copy-start(bf16[16,1024]{1,0:T(8,128)(2,1)} %param.9) | copy-start | bytes 98308
  0.0 8.9 %collective-permute-start = (bf16[576,128]{1,0:T(8,128)(2,1)}, bf16[576,128]{1,0:T(8,128)(2,1)S(1)}, u32[]{:S(2)}, u32[]{:S(2)}) collective-permute-start(bf16[576,128]{1,0:T(8,128)(2,1)} %bitcast.34), channel_id=1, source_target_pairs={{0,17},{17,0},{1,16},{16,1},{2,19},{19,2},{3,18},{18,3},{4,21},{21... | collective-permute-start | bytes 442376 | tf_op jit(solution)/shard_map/ppermute | solution.py:203
  4.1 4.8 %collective-permute-start.1 = (bf16[256,128]{1,0:T(8,128)(2,1)S(1)}, bf16[256,128]{1,0:T(8,128)(2,1)S(1)}, u32[]{:S(2)}, u32[]{:S(2)}) collective-permute-start(bf16[256,128]{1,0:T(8,128)(2,1)S(1)} %pad_maximum_fusion.1), channel_id=1, source_target_pairs={{0,16},{16,0},{1,17},{17,1},{2,18},{18,2},{3,19},{19,3},{4,20},{20... | collective-permute-start | bytes 196616 | tf_op jit(solution)/shard_map/ppermute | solution.py:38
  9.0 12.5 %collective-permute-start.3 = (bf16[2,832,128]{2,1,0:T(8,128)(2,1)S(1)}, bf16[2,832,128]{2,1,0:T(8,128)(2,1)S(1)}, u32[]{:S(2)}, u32[]{:S(2)}) collective-permute-start(bf16[2,832,128]{2,1,0:T(8,128)(2,1)S(1)} %pad_maximum_fusion.refs_1_.refs_3_), channel_id=1, source_target_pairs={{0,224},{32,0},{64,32},{96,64},{128,96},{160,128},{192,160},{224,1... | collective-permute-start | bytes 1277960 | tf_op jit(solution)/shard_map/ppermute | solution.py:38
  14.5 10.4 %collective-permute-start.2 = (bf16[2,832,128]{2,1,0:T(8,128)(2,1)S(1)}, bf16[2,832,128]{2,1,0:T(8,128)(2,1)S(1)}, u32[]{:S(2)}, u32[]{:S(2)}) collective-permute-start(bf16[2,832,128]{2,1,0:T(8,128)(2,1)S(1)} %pad_maximum_fusion.refs_1_.refs_3_), channel_id=1, source_target_pairs={{0,32},{32,64},{64,96},{96,128},{128,160},{160,192},{192,224},{224... | collective-permute-start | bytes 1277960 | tf_op jit(solution)/shard_map/ppermute | solution.py:38
  16.2 11.0 %all-to-all-start = ((bf16[8,192,128]{2,1,0:T(8,128)(2,1)}), bf16[8,192,128]{2,1,0:T(8,128)(2,1)S(1)}, u32[]{:S(2)}, u32[]{:S(2)}) async-start(bf16[8,192,128]{2,1,0:T(8,128)(2,1)} %shard_map.64), calls=%async_computation | async-start | bytes 786432 | tf_op jit(solution)/shard_map/all_to_all | solution.py:212
  21.5 9.5 %collective-permute-start.8 = (bf16[2,832,128]{2,1,0:T(8,128)(2,1)S(1)}, bf16[2,832,128]{2,1,0:T(8,128)(2,1)S(1)}, u32[]{:S(2)}, u32[]{:S(2)}) collective-permute-start(bf16[2,832,128]{2,1,0:T(8,128)(2,1)S(1)} %collective-permute-done.3.refs_5_), channel_id=1, source_target_pairs={{0,224},{32,0},{64,32},{96,64},{128,96},{160,128},{192,160},{224,1... | collective-permute-start | bytes 1277960 | tf_op jit(solution)/shard_map/ppermute | solution.py:38
  25.0 9.2 %collective-permute-start.7 = (bf16[2,832,128]{2,1,0:T(8,128)(2,1)S(1)}, bf16[2,832,128]{2,1,0:T(8,128)(2,1)S(1)}, u32[]{:S(2)}, u32[]{:S(2)}) collective-permute-start(bf16[2,832,128]{2,1,0:T(8,128)(2,1)S(1)} %collective-permute-done.2.refs_4_), channel_id=1, source_target_pairs={{0,32},{32,64},{64,96},{96,128},{128,160},{160,192},{192,224},{224... | collective-permute-start | bytes 1277960 | tf_op jit(solution)/shard_map/ppermute | solution.py:38
  27.2 30.4 %copy-start.1 = (s32[64]{0:T(128)S(1)}, s32[64]{0:T(128)}, u32[]{:S(2)}) copy-start(s32[64]{0:T(128)} %refs_1_.1) | copy-start | bytes 772
  34.2 8.2 %collective-permute-start.9 = (bf16[2,832,128]{2,1,0:T(8,128)(2,1)S(1)}, bf16[2,832,128]{2,1,0:T(8,128)(2,1)S(1)}, u32[]{:S(2)}, u32[]{:S(2)}) collective-permute-start(bf16[2,832,128]{2,1,0:T(8,128)(2,1)S(1)} %get-tuple-element.13.refs_0_), channel_id=1, source_target_pairs={{0,32},{32,64},{64,96},{96,128},{128,160},{160,192},{192,224},{224... | collective-permute-start | bytes 1277960 | tf_op jit(solution)/shard_map/ppermute | solution.py:38
  34.2 8.2 %collective-permute-start.10 = (bf16[2,832,128]{2,1,0:T(8,128)(2,1)S(1)}, bf16[2,832,128]{2,1,0:T(8,128)(2,1)S(1)}, u32[]{:S(2)}, u32[]{:S(2)}) collective-permute-start(bf16[2,832,128]{2,1,0:T(8,128)(2,1)S(1)} %get-tuple-element.14.refs_1_), channel_id=1, source_target_pairs={{0,224},{32,0},{64,32},{96,64},{128,96},{160,128},{192,160},{224,1... | collective-permute-start | bytes 1277960 | tf_op jit(solution)/shard_map/ppermute | solution.py:38
  36.8 6.2 %collective-permute-start.4 = (bf16[2,832,128]{2,1,0:T(8,128)(2,1)S(1)}, bf16[2,832,128]{2,1,0:T(8,128)(2,1)S(1)}, u32[]{:S(2)}, u32[]{:S(2)}) collective-permute-start(bf16[2,832,128]{2,1,0:T(8,128)(2,1)S(1)} %pad_maximum_fusion.refs_1_.refs_3_), channel_id=1, source_target_pairs={{0,8},{8,0},{1,9},{9,1},{2,10},{10,2},{3,11},{11,3},{4,12},{12,4},... | collective-permute-start | bytes 1277960 | tf_op jit(solution)/shard_map/ppermute | solution.py:38
  41.6 2.0 %collective-permute-start.6 = (bf16[2,832,128]{2,1,0:T(8,128)(2,1)S(1)}, bf16[2,832,128]{2,1,0:T(8,128)(2,1)S(1)}, u32[]{:S(2)}, u32[]{:S(2)}) collective-permute-start(bf16[2,832,128]{2,1,0:T(8,128)(2,1)S(1)} %collective-permute-done.3.refs_5_), channel_id=1, source_target_pairs={{0,8},{8,0},{1,9},{9,1},{2,10},{10,2},{3,11},{11,3},{4,12},{12,4},... | collective-permute-start | bytes 1277960 | tf_op jit(solution)/shard_map/ppermute | solution.py:38
  41.6 2.6 %collective-permute-start.5 = (bf16[2,832,128]{2,1,0:T(8,128)(2,1)S(1)}, bf16[2,832,128]{2,1,0:T(8,128)(2,1)S(1)}, u32[]{:S(2)}, u32[]{:S(2)}) collective-permute-start(bf16[2,832,128]{2,1,0:T(8,128)(2,1)S(1)} %collective-permute-done.2.refs_4_), channel_id=1, source_target_pairs={{0,8},{8,0},{1,9},{9,1},{2,10},{10,2},{3,11},{11,3},{4,12},{12,4},... | collective-permute-start | bytes 1277960 | tf_op jit(solution)/shard_map/ppermute | solution.py:38
  44.2 7.0 %collective-permute-start.11 = (bf16[1,832,128]{2,1,0:T(8,128)(2,1)S(1)}, bf16[1,832,128]{2,1,0:T(8,128)(2,1)S(1)}, u32[]{:S(2)}, u32[]{:S(2)}) collective-permute-start(bf16[1,832,128]{2,1,0:T(8,128)(2,1)S(1)} %get-tuple-element.15.refs_4_), channel_id=1, source_target_pairs={{0,32},{32,64},{64,96},{96,128},{128,160},{160,192},{192,224},{224... | collective-permute-start | bytes 638984 | tf_op jit(solution)/shard_map/ppermute | solution.py:38
  44.3 10.7 %collective-permute-start.12 = (bf16[1,832,128]{2,1,0:T(8,128)(2,1)S(1)}, bf16[1,832,128]{2,1,0:T(8,128)(2,1)S(1)}, u32[]{:S(2)}, u32[]{:S(2)}) collective-permute-start(bf16[1,832,128]{2,1,0:T(8,128)(2,1)S(1)} %get-tuple-element.16.refs_5_), channel_id=1, source_target_pairs={{0,224},{32,0},{64,32},{96,64},{128,96},{160,128},{192,160},{224,1... | collective-permute-start | bytes 638984 | tf_op jit(solution)/shard_map/ppermute | solution.py:38
  46.9 10.7 %collective-permute-start.13 = (bf16[2,832,128]{2,1,0:T(8,128)(2,1)S(1)}, bf16[2,832,128]{2,1,0:T(8,128)(2,1)S(1)}, u32[]{:S(2)}, u32[]{:S(2)}) collective-permute-start(bf16[2,832,128]{2,1,0:T(8,128)(2,1)S(1)} %get-tuple-element.17.refs_9_), channel_id=1, source_target_pairs={{0,8},{8,0},{1,9},{9,1},{2,10},{10,2},{3,11},{11,3},{4,12},{12,4},... | collective-permute-start | bytes 1277960 | tf_op jit(solution)/shard_map/ppermute | solution.py:38
  51.2 6.5 %collective-permute-start.14 = (bf16[2,832,128]{2,1,0:T(8,128)(2,1)S(1)}, bf16[2,832,128]{2,1,0:T(8,128)(2,1)S(1)}, u32[]{:S(2)}, u32[]{:S(2)}) collective-permute-start(bf16[2,832,128]{2,1,0:T(8,128)(2,1)S(1)} %get-tuple-element.18.refs_10_), channel_id=1, source_target_pairs={{0,8},{8,0},{1,9},{9,1},{2,10},{10,2},{3,11},{11,3},{4,12},{12,4},... | collective-permute-start | bytes 1277960 | tf_op jit(solution)/shard_map/ppermute | solution.py:38
  51.2 4.8 %collective-permute-start.17 = (bf16[1,832,128]{2,1,0:T(8,128)(2,1)S(1)}, bf16[1,832,128]{2,1,0:T(8,128)(2,1)S(1)}, u32[]{:S(2)}, u32[]{:S(2)}) collective-permute-start(bf16[1,832,128]{2,1,0:T(8,128)(2,1)S(1)} %collective-permute-done.11.refs_13_), channel_id=1, source_target_pairs={{0,8},{8,0},{1,9},{9,1},{2,10},{10,2},{3,11},{11,3},{4,12},{12,4},... | collective-permute-start | bytes 638984 | tf_op jit(solution)/shard_map/ppermute | solution.py:38
  55.0 2.7 %collective-permute-start.15 = (bf16[2,832,128]{2,1,0:T(8,128)(2,1)S(1)}, bf16[2,832,128]{2,1,0:T(8,128)(2,1)S(1)}, u32[]{:S(2)}, u32[]{:S(2)}) collective-permute-start(bf16[2,832,128]{2,1,0:T(8,128)(2,1)S(1)} %get-tuple-element.19.refs_11_), channel_id=1, source_target_pairs={{0,8},{8,0},{1,9},{9,1},{2,10},{10,2},{3,11},{11,3},{4,12},{12,4},... | collective-permute-start | bytes 1277960 | tf_op jit(solution)/shard_map/ppermute | solution.py:38
  55.0 2.7 %collective-permute-start.16 = (bf16[2,832,128]{2,1,0:T(8,128)(2,1)S(1)}, bf16[2,832,128]{2,1,0:T(8,128)(2,1)S(1)}, u32[]{:S(2)}, u32[]{:S(2)}) collective-permute-start(bf16[2,832,128]{2,1,0:T(8,128)(2,1)S(1)} %get-tuple-element.20.refs_12_), channel_id=1, source_target_pairs={{0,8},{8,0},{1,9},{9,1},{2,10},{10,2},{3,11},{11,3},{4,12},{12,4},... | collective-permute-start | bytes 1277960 | tf_op jit(solution)/shard_map/ppermute | solution.py:38
  56.1 1.6 %collective-permute-start.18 = (bf16[1,832,128]{2,1,0:T(8,128)(2,1)S(1)}, bf16[1,832,128]{2,1,0:T(8,128)(2,1)S(1)}, u32[]{:S(2)}, u32[]{:S(2)}) collective-permute-start(bf16[1,832,128]{2,1,0:T(8,128)(2,1)S(1)} %collective-permute-done.12.refs_14_), channel_id=1, source_target_pairs={{0,8},{8,0},{1,9},{9,1},{2,10},{10,2},{3,11},{11,3},{4,12},{12,4},... | collective-permute-start | bytes 638984 | tf_op jit(solution)/shard_map/ppermute | solution.py:38

commit v13 on v12

--- a/solution.py
+++ b/solution.py
@@ -86,7 +86,7 @@
         acc = dot_t(w, lo_ref[:KV, :n_lo])
     else:
         acc = dot_t(w[:, :count], lo_ref[:KV, :]) + dot_t(w[:, count:], hi_ref[:KV, first:])
-    mix_ref[slot, rows, :] = (acc / total).astype(jnp.bfloat16)
+    mix_ref[slot, rows, :] = (acc * (1.0 / total)).astype(jnp.bfloat16)
 
 
 def attention_kernel(layout, heads, tile, *refs):

time: 70.5 us -> 70.5 us (level)
  no operation moved by 1% of the time
where the time goes in v13:
time: 70.5 us; the launch traced here: 70.1 us
  starting transfers between devices  37.1 us (53%)
  waiting for transfers between devices  13.8 us (20%)
  Pallas kernels  12.5 us (18%)
  matrix products  3.17 us (4%)
  local copies, waits for them, and re-layouts  2.4 us (3%)
  other arithmetic  1.06 us (2%)
    ppermute x18, starting transfers between devices, shift(): return lax.ppermute(x, axis, [(i, (i + by) % n) for i in range(n)])  29.6 us
    pallas_call x1, Pallas kernels, attention(): pl.pallas_call(functools.partial(attention_kernel, layout, heads, min(row...  12.5 us
    ppermute x18, waiting for transfers between devices, shift(): return lax.ppermute(x, axis, [(i, (i + by) % n) for i in range(n)])  11.6 us
    all_to_all x1, starting transfers between devices, per_device(): lax.all_to_all(copies, ('y', 'xl'), 0, 0, tiled=True).reshape(-1, toks)  4.19 us
    ppermute x1, starting transfers between devices, per_device(): across = lax.ppermute(own, ('xh', 'xl'), [(0, 3), (3, 0), (1, 2), (2, 1)])  3.31 us
    dot_general x1, matrix products, per_device(): lax.dot_general(features, w_uq, (((0,), (0,)), ((), ())), preferred_eleme...  3.17 us
    all_to_all x1, waiting for transfers between devices, per_device(): lax.all_to_all(copies, ('y', 'xl'), 0, 0, tiled=True).reshape(-1, toks)  2.27 us
    broadcast_in_dim x1, local copies, waits for them, and re-layouts, per_device(): jnp.broadcast_to(compressed.T[None], (ys * xls,) + compressed.T.shape)  1.59 us
  transfers between devices with their start and end apart: 20, of which 11 were waited for; matrix products, arithmetic and copies ran while one was open for 9% of the time, Pallas kernels for 0%

profile of v13, /device:TPU:1, one launch (start us, length us, event | category | flops | bytes accessed | tf_op | source)
XLA Modules:
  0.0 70.1 jit_solution(15653771209102587032)
XLA Ops:
  0.0 0.0 copy-start
  0.0 3.3 %collective-permute-start = (bf16[576,128]{1,0:T(8,128)(2,1)}, bf16[576,128]{1,0:T(8,128)(2,1)S(1)}, u32[]{:S(2)}, u32[]{:S(2)}) collective-permute-start(bf16[576,128]{1,0:T(8,128)(2,1)} %bitcast.34), channel_id=1, source_target_pairs={{0,17},{17,0},{1,16},{16,1},{2,19},{19,2},{3,18},{18,3},{4,21},{21... | collective-permute-start | bytes 442376 | tf_op jit(solution)/shard_map/ppermute | solution.py:203
  3.3 0.0 copy-done
  3.3 0.8 %copy_bitcast_fusion = bf16[16,8,128]{2,0,1:T(8,128)(2,1)S(1)} fusion(bf16[16,1024]{1,0:T(8,128)(2,1)} %param.10), kind=kLoop, calls=%fused_computation.5 | loop fusion | bytes 65536 | tf_op jit(solution)/shard_map/reshape | solution.py:51
  4.1 1.1 %collective-permute-start.1 = (bf16[256,128]{1,0:T(8,128)(2,1)S(1)}, bf16[256,128]{1,0:T(8,128)(2,1)S(1)}, u32[]{:S(2)}, u32[]{:S(2)}) collective-permute-start(bf16[256,128]{1,0:T(8,128)(2,1)S(1)} %pad_maximum_fusion.1), channel_id=1, source_target_pairs={{0,16},{16,0},{1,17},{17,1},{2,18},{18,2},{3,19},{19,3},{4,20},{20... | collective-permute-start | bytes 196616 | tf_op jit(solution)/shard_map/ppermute | solution.py:38
  5.2 0.9 %maximum_bitcast_fusion = bf16[1,832,128]{2,1,0:T(8,128)(2,1)S(1)} fusion(bf16[128,128]{1,0:T(8,128)(2,1)S(1)} %bitcast.33, bf16[128,128]{1,0:T(8,128)(2,1)S(1)} %bitcast.31, bf16[576,128]{1,0:T(8,128)(2,1)} %bitcast.35), kind=kLoop, calls=%fused_computation.2 | loop fusion | flops 638976 | bytes 425984 | tf_op jit(solution)/shard_map/stack | solution.py:206
  6.1 2.8 %collective-permute-done.1 = bf16[256,128]{1,0:T(8,128)(2,1)S(1)} collective-permute-done((bf16[256,128]{1,0:T(8,128)(2,1)S(1)}, bf16[256,128]{1,0:T(8,128)(2,1)S(1)}, u32[]{:S(2)}, u32[]{:S(2)}) %collective-permute-start.1) | collective-permute-done | bytes 65568 | tf_op jit(solution)/shard_map/ppermute | solution.py:38
  8.9 0.0 collective-permute-done
  9.0 5.5 %collective-permute-start.3 = (bf16[2,832,128]{2,1,0:T(8,128)(2,1)S(1)}, bf16[2,832,128]{2,1,0:T(8,128)(2,1)S(1)}, u32[]{:S(2)}, u32[]{:S(2)}) collective-permute-start(bf16[2,832,128]{2,1,0:T(8,128)(2,1)S(1)} %pad_maximum_fusion.refs_1_.refs_3_), channel_id=1, source_target_pairs={{0,224},{32,0},{64,32},{96,64},{128,96},{160,128},{192,160},{224,1... | collective-permute-start | bytes 1277960 | tf_op jit(solution)/shard_map/ppermute | solution.py:38
  14.5 0.0 collective-permute-start.2
  14.5 0.1 pad_add_fusion.refs_2_.refs_0_
  14.6 1.6 %broadcast_in_dim.2.refs_0_ = bf16[8,192,128]{2,1,0:T(8,128)(2,1)} broadcast(bf16[192,128]{1,0:T(8,128)(2,1)} %bitcast.36), dimensions={1,2} | broadcast | bytes 442368 | tf_op jit(solution)/shard_map/broadcast_in_dim | solution.py:210
  16.2 4.2 %all-to-all-start = ((bf16[8,192,128]{2,1,0:T(8,128)(2,1)}), bf16[8,192,128]{2,1,0:T(8,128)(2,1)S(1)}, u32[]{:S(2)}, u32[]{:S(2)}) async-start(bf16[8,192,128]{2,1,0:T(8,128)(2,1)} %shard_map.64), calls=%async_computation | async-start | bytes 786432 | tf_op jit(solution)/shard_map/all_to_all | solution.py:212
  20.4 1.1 %collective-permute-done.3.refs_5_ = bf16[2,832,128]{2,1,0:T(8,128)(2,1)S(1)} collective-permute-done((bf16[2,832,128]{2,1,0:T(8,128)(2,1)S(1)}, bf16[2,832,128]{2,1,0:T(8,128)(2,1)S(1)}, u32[]{:S(2)}, u32[]{:S(2)}) %collective-permute-start.3) | collective-permute-done | bytes 426016 | tf_op jit(solution)/shard_map/ppermute | solution.py:38
  21.5 3.4 %collective-permute-start.8 = (bf16[2,832,128]{2,1,0:T(8,128)(2,1)S(1)}, bf16[2,832,128]{2,1,0:T(8,128)(2,1)S(1)}, u32[]{:S(2)}, u32[]{:S(2)}) collective-permute-start(bf16[2,832,128]{2,1,0:T(8,128)(2,1)S(1)} %collective-permute-done.3.refs_5_), channel_id=1, source_target_pairs={{0,224},{32,0},{64,32},{96,64},{128,96},{160,128},{192,160},{224,1... | collective-permute-start | bytes 1277960 | tf_op jit(solution)/shard_map/ppermute | solution.py:38
  24.9 0.0 collective-permute-done.2.refs_4_
  25.0 0.0 collective-permute-start.7
  25.0 2.3 %all-to-all-done = bf16[8,192,128]{2,1,0:T(8,128)(2,1)S(1)} async-done(((bf16[8,192,128]{2,1,0:T(8,128)(2,1)}), bf16[8,192,128]{2,1,0:T(8,128)(2,1)S(1)}, u32[]{:S(2)}, u32[]{:S(2)}) %all-to-all-start) | async-done | bytes 393248 | tf_op jit(solution)/shard_map/all_to_all | solution.py:212
  27.2 0.0 copy-start.1
  27.2 3.2 %convolution_convert_fusion.refs_2_ = bf16[128,1536]{1,0:T(8,128)(2,1)S(1)} fusion(bf16[1536,128]{1,0:T(8,128)(2,1)S(1)} %bitcast.29, bf16[1536,1536]{1,0:T(8,128)(2,1)} %param.8), kind=kOutput, calls=%fused_computation | convolution fusion | flops 604176384 | bytes 5505024 | tf_op jit(solution)/shard_map/dot_general | solution.py:213
  30.4 0.6 collective-permute-done.8.refs_1_
  31.0 3.1 %collective-permute-done.7.refs_0_ = bf16[2,832,128]{2,1,0:T(8,128)(2,1)S(1)} collective-permute-done((bf16[2,832,128]{2,1,0:T(8,128)(2,1)S(1)}, bf16[2,832,128]{2,1,0:T(8,128)(2,1)S(1)}, u32[]{:S(2)}, u32[]{:S(2)}) %collective-permute-start.7) | collective-permute-done | bytes 426016 | tf_op jit(solution)/shard_map/ppermute | solution.py:38
  34.2 0.0 collective-permute-start.9
  34.2 2.7 %collective-permute-start.10 = (bf16[2,832,128]{2,1,0:T(8,128)(2,1)S(1)}, bf16[2,832,128]{2,1,0:T(8,128)(2,1)S(1)}, u32[]{:S(2)}, u32[]{:S(2)}) collective-permute-start(bf16[2,832,128]{2,1,0:T(8,128)(2,1)S(1)} %get-tuple-element.14.refs_1_), channel_id=1, source_target_pairs={{0,224},{32,0},{64,32},{96,64},{128,96},{160,128},{192,160},{224,1... | collective-permute-start | bytes 1277960 | tf_op jit(solution)/shard_map/ppermute | solution.py:38
  36.8 4.8 %collective-permute-start.4 = (bf16[2,832,128]{2,1,0:T(8,128)(2,1)S(1)}, bf16[2,832,128]{2,1,0:T(8,128)(2,1)S(1)}, u32[]{:S(2)}, u32[]{:S(2)}) collective-permute-start(bf16[2,832,128]{2,1,0:T(8,128)(2,1)S(1)} %pad_maximum_fusion.refs_1_.refs_3_), channel_id=1, source_target_pairs={{0,8},{8,0},{1,9},{9,1},{2,10},{10,2},{3,11},{11,3},{4,12},{12,4},... | collective-permute-start | bytes 1277960 | tf_op jit(solution)/shard_map/ppermute | solution.py:38
  41.6 0.0 collective-permute-start.6
  41.6 0.5 collective-permute-start.5
  42.1 0.2 collective-permute-done.9.refs_2_
  42.4 0.0 collective-permute-done.10.refs_3_
  42.4 0.6 collective-permute-done.4.refs_2_.refs_6_
  43.0 0.6 collective-permute-done.6.refs_4_.refs_8_
  43.6 0.6 collective-permute-done.5.refs_3_.refs_7_
  44.2 0.0 collective-permute-start.11
  44.3 2.7 %collective-permute-start.12 = (bf16[1,832,128]{2,1,0:T(8,128)(2,1)S(1)}, bf16[1,832,128]{2,1,0:T(8,128)(2,1)S(1)}, u32[]{:S(2)}, u32[]{:S(2)}) collective-permute-start(bf16[1,832,128]{2,1,0:T(8,128)(2,1)S(1)} %get-tuple-element.16.refs_5_), channel_id=1, source_target_pairs={{0,224},{32,0},{64,32},{96,64},{128,96},{160,128},{192,160},{224,1... | collective-permute-start | bytes 638984 | tf_op jit(solution)/shard_map/ppermute | solution.py:38
  46.9 4.3 %collective-permute-start.13 = (bf16[2,832,128]{2,1,0:T(8,128)(2,1)S(1)}, bf16[2,832,128]{2,1,0:T(8,128)(2,1)S(1)}, u32[]{:S(2)}, u32[]{:S(2)}) collective-permute-start(bf16[2,832,128]{2,1,0:T(8,128)(2,1)S(1)} %get-tuple-element.17.refs_9_), channel_id=1, source_target_pairs={{0,8},{8,0},{1,9},{9,1},{2,10},{10,2},{3,11},{11,3},{4,12},{12,4},... | collective-permute-start | bytes 1277960 | tf_op jit(solution)/shard_map/ppermute | solution.py:38
  51.2 0.0 collective-permute-start.14
  51.2 0.0 collective-permute-done.11.refs_13_
  51.2 3.8 %collective-permute-start.17 = (bf16[1,832,128]{2,1,0:T(8,128)(2,1)S(1)}, bf16[1,832,128]{2,1,0:T(8,128)(2,1)S(1)}, u32[]{:S(2)}, u32[]{:S(2)}) collective-permute-start(bf16[1,832,128]{2,1,0:T(8,128)(2,1)S(1)} %collective-permute-done.11.refs_13_), channel_id=1, source_target_pairs={{0,8},{8,0},{1,9},{9,1},{2,10},{10,2},{3,11},{11,3},{4,12},{12,4},... | collective-permute-start | bytes 638984 | tf_op jit(solution)/shard_map/ppermute | solution.py:38
  55.0 0.0 collective-permute-start.15
  55.0 0.0 collective-permute-done.12.refs_14_
  55.0 0.5 collective-permute-start.16
  55.5 0.6 collective-permute-done.17.refs_19_
  56.1 0.4 collective-permute-start.18
  56.4 1.2 %collective-permute-done.18.refs_20_ = bf16[1,832,128]{2,1,0:T(8,128)(2,1)S(1)} collective-permute-done((bf16[1,832,128]{2,1,0:T(8,128)(2,1)S(1)}, bf16[1,832,128]{2,1,0:T(8,128)(2,1)S(1)}, u32[]{:S(2)}, u32[]{:S(2)}) %collective-permute-start.18) | collective-permute-done | bytes 213024 | tf_op jit(solution)/shard_map/ppermute | solution.py:38
  57.6 0.0 collective-permute-done.13.refs_15_
  57.7 0.0 collective-permute-done.14.refs_16_
  57.7 0.0 collective-permute-done.15.refs_17_
  57.7 0.0 collective-permute-done.16.refs_18_
  57.7 0.0 copy-done.1
  57.7 12.5 %shard_map.68 = bf16[128,1024]{1,0:T(8,128)(2,1)} custom-call(s32[4]{0:T(128)S(1)} %pad_add_fusion.refs_2_.refs_0_, s32[64]{0:T(128)S(1)} %copy-done.1, bf16[128,1536]{1,0:T(8,128)(2,1)S(1)} %convolution_convert_fusion.refs_2_, bf16[2,832,128]{2,1,0:T(8,128)(2,1)S(1)} %pad_maximum_fusion.refs_1_.refs_3_, ...), custom_call_target="tpu_custom_call" | custom-call | flops 5704253440 | bytes 7209232 | tf_op jit(solution)/shard_map/pallas_call | solution.py:173
  (10 shorter events, 0.1 us)
Async XLA Ops:
  0.0 3.3 %copy-start = (bf16[16,1024]{1,0:T(8,128)(2,1)S(1)}, bf16[16,1024]{1,0:T(8,128)(2,1)}, u32[]{:S(2)}) copy-start(bf16[16,1024]{1,0:T(8,128)(2,1)} %param.9) | copy-start | bytes 98308
  0.0 8.9 %collective-permute-start = (bf16[576,128]{1,0:T(8,128)(2,1)}, bf16[576,128]{1,0:T(8,128)(2,1)S(1)}, u32[]{:S(2)}, u32[]{:S(2)}) collective-permute-start(bf16[576,128]{1,0:T(8,128)(2,1)} %bitcast.34), channel_id=1, source_target_pairs={{0,17},{17,0},{1,16},{16,1},{2,19},{19,2},{3,18},{18,3},{4,21},{21... | collective-permute-start | bytes 442376 | tf_op jit(solution)/shard_map/ppermute | solution.py:203
  4.1 4.8 %collective-permute-start.1 = (bf16[256,128]{1,0:T(8,128)(2,1)S(1)}, bf16[256,128]{1,0:T(8,128)(2,1)S(1)}, u32[]{:S(2)}, u32[]{:S(2)}) collective-permute-start(bf16[256,128]{1,0:T(8,128)(2,1)S(1)} %pad_maximum_fusion.1), channel_id=1, source_target_pairs={{0,16},{16,0},{1,17},{17,1},{2,18},{18,2},{3,19},{19,3},{4,20},{20... | collective-permute-start | bytes 196616 | tf_op jit(solution)/shard_map/ppermute | solution.py:38
  9.0 12.5 %collective-permute-start.3 = (bf16[2,832,128]{2,1,0:T(8,128)(2,1)S(1)}, bf16[2,832,128]{2,1,0:T(8,128)(2,1)S(1)}, u32[]{:S(2)}, u32[]{:S(2)}) collective-permute-start(bf16[2,832,128]{2,1,0:T(8,128)(2,1)S(1)} %pad_maximum_fusion.refs_1_.refs_3_), channel_id=1, source_target_pairs={{0,224},{32,0},{64,32},{96,64},{128,96},{160,128},{192,160},{224,1... | collective-permute-start | bytes 1277960 | tf_op jit(solution)/shard_map/ppermute | solution.py:38
  14.5 10.4 %collective-permute-start.2 = (bf16[2,832,128]{2,1,0:T(8,128)(2,1)S(1)}, bf16[2,832,128]{2,1,0:T(8,128)(2,1)S(1)}, u32[]{:S(2)}, u32[]{:S(2)}) collective-permute-start(bf16[2,832,128]{2,1,0:T(8,128)(2,1)S(1)} %pad_maximum_fusion.refs_1_.refs_3_), channel_id=1, source_target_pairs={{0,32},{32,64},{64,96},{96,128},{128,160},{160,192},{192,224},{224... | collective-permute-start | bytes 1277960 | tf_op jit(solution)/shard_map/ppermute | solution.py:38
  16.2 11.0 %all-to-all-start = ((bf16[8,192,128]{2,1,0:T(8,128)(2,1)}), bf16[8,192,128]{2,1,0:T(8,128)(2,1)S(1)}, u32[]{:S(2)}, u32[]{:S(2)}) async-start(bf16[8,192,128]{2,1,0:T(8,128)(2,1)} %shard_map.64), calls=%async_computation | async-start | bytes 786432 | tf_op jit(solution)/shard_map/all_to_all | solution.py:212
  21.5 9.5 %collective-permute-start.8 = (bf16[2,832,128]{2,1,0:T(8,128)(2,1)S(1)}, bf16[2,832,128]{2,1,0:T(8,128)(2,1)S(1)}, u32[]{:S(2)}, u32[]{:S(2)}) collective-permute-start(bf16[2,832,128]{2,1,0:T(8,128)(2,1)S(1)} %collective-permute-done.3.refs_5_), channel_id=1, source_target_pairs={{0,224},{32,0},{64,32},{96,64},{128,96},{160,128},{192,160},{224,1... | collective-permute-start | bytes 1277960 | tf_op jit(solution)/shard_map/ppermute | solution.py:38
  25.0 9.2 %collective-permute-start.7 = (bf16[2,832,128]{2,1,0:T(8,128)(2,1)S(1)}, bf16[2,832,128]{2,1,0:T(8,128)(2,1)S(1)}, u32[]{:S(2)}, u32[]{:S(2)}) collective-permute-start(bf16[2,832,128]{2,1,0:T(8,128)(2,1)S(1)} %collective-permute-done.2.refs_4_), channel_id=1, source_target_pairs={{0,32},{32,64},{64,96},{96,128},{128,160},{160,192},{192,224},{224... | collective-permute-start | bytes 1277960 | tf_op jit(solution)/shard_map/ppermute | solution.py:38
  27.2 30.4 %copy-start.1 = (s32[64]{0:T(128)S(1)}, s32[64]{0:T(128)}, u32[]{:S(2)}) copy-start(s32[64]{0:T(128)} %refs_1_.1) | copy-start | bytes 772
  34.2 8.2 %collective-permute-start.9 = (bf16[2,832,128]{2,1,0:T(8,128)(2,1)S(1)}, bf16[2,832,128]{2,1,0:T(8,128)(2,1)S(1)}, u32[]{:S(2)}, u32[]{:S(2)}) collective-permute-start(bf16[2,832,128]{2,1,0:T(8,128)(2,1)S(1)} %get-tuple-element.13.refs_0_), channel_id=1, source_target_pairs={{0,32},{32,64},{64,96},{96,128},{128,160},{160,192},{192,224},{224... | collective-permute-start | bytes 1277960 | tf_op jit(solution)/shard_map/ppermute | solution.py:38
  34.2 8.2 %collective-permute-start.10 = (bf16[2,832,128]{2,1,0:T(8,128)(2,1)S(1)}, bf16[2,832,128]{2,1,0:T(8,128)(2,1)S(1)}, u32[]{:S(2)}, u32[]{:S(2)}) collective-permute-start(bf16[2,832,128]{2,1,0:T(8,128)(2,1)S(1)} %get-tuple-element.14.refs_1_), channel_id=1, source_target_pairs={{0,224},{32,0},{64,32},{96,64},{128,96},{160,128},{192,160},{224,1... | collective-permute-start | bytes 1277960 | tf_op jit(solution)/shard_map/ppermute | solution.py:38
  36.8 6.2 %collective-permute-start.4 = (bf16[2,832,128]{2,1,0:T(8,128)(2,1)S(1)}, bf16[2,832,128]{2,1,0:T(8,128)(2,1)S(1)}, u32[]{:S(2)}, u32[]{:S(2)}) collective-permute-start(bf16[2,832,128]{2,1,0:T(8,128)(2,1)S(1)} %pad_maximum_fusion.refs_1_.refs_3_), channel_id=1, source_target_pairs={{0,8},{8,0},{1,9},{9,1},{2,10},{10,2},{3,11},{11,3},{4,12},{12,4},... | collective-permute-start | bytes 1277960 | tf_op jit(solution)/shard_map/ppermute | solution.py:38
  41.6 2.0 %collective-permute-start.6 = (bf16[2,832,128]{2,1,0:T(8,128)(2,1)S(1)}, bf16[2,832,128]{2,1,0:T(8,128)(2,1)S(1)}, u32[]{:S(2)}, u32[]{:S(2)}) collective-permute-start(bf16[2,832,128]{2,1,0:T(8,128)(2,1)S(1)} %collective-permute-done.3.refs_5_), channel_id=1, source_target_pairs={{0,8},{8,0},{1,9},{9,1},{2,10},{10,2},{3,11},{11,3},{4,12},{12,4},... | collective-permute-start | bytes 1277960 | tf_op jit(solution)/shard_map/ppermute | solution.py:38
  41.6 2.6 %collective-permute-start.5 = (bf16[2,832,128]{2,1,0:T(8,128)(2,1)S(1)}, bf16[2,832,128]{2,1,0:T(8,128)(2,1)S(1)}, u32[]{:S(2)}, u32[]{:S(2)}) collective-permute-start(bf16[2,832,128]{2,1,0:T(8,128)(2,1)S(1)} %collective-permute-done.2.refs_4_), channel_id=1, source_target_pairs={{0,8},{8,0},{1,9},{9,1},{2,10},{10,2},{3,11},{11,3},{4,12},{12,4},... | collective-permute-start | bytes 1277960 | tf_op jit(solution)/shard_map/ppermute | solution.py:38
  44.2 7.0 %collective-permute-start.11 = (bf16[1,832,128]{2,1,0:T(8,128)(2,1)S(1)}, bf16[1,832,128]{2,1,0:T(8,128)(2,1)S(1)}, u32[]{:S(2)}, u32[]{:S(2)}) collective-permute-start(bf16[1,832,128]{2,1,0:T(8,128)(2,1)S(1)} %get-tuple-element.15.refs_4_), channel_id=1, source_target_pairs={{0,32},{32,64},{64,96},{96,128},{128,160},{160,192},{192,224},{224... | collective-permute-start | bytes 638984 | tf_op jit(solution)/shard_map/ppermute | solution.py:38
  44.3 10.7 %collective-permute-start.12 = (bf16[1,832,128]{2,1,0:T(8,128)(2,1)S(1)}, bf16[1,832,128]{2,1,0:T(8,128)(2,1)S(1)}, u32[]{:S(2)}, u32[]{:S(2)}) collective-permute-start(bf16[1,832,128]{2,1,0:T(8,128)(2,1)S(1)} %get-tuple-element.16.refs_5_), channel_id=1, source_target_pairs={{0,224},{32,0},{64,32},{96,64},{128,96},{160,128},{192,160},{224,1... | collective-permute-start | bytes 638984 | tf_op jit(solution)/shard_map/ppermute | solution.py:38
  46.9 10.7 %collective-permute-start.13 = (bf16[2,832,128]{2,1,0:T(8,128)(2,1)S(1)}, bf16[2,832,128]{2,1,0:T(8,128)(2,1)S(1)}, u32[]{:S(2)}, u32[]{:S(2)}) collective-permute-start(bf16[2,832,128]{2,1,0:T(8,128)(2,1)S(1)} %get-tuple-element.17.refs_9_), channel_id=1, source_target_pairs={{0,8},{8,0},{1,9},{9,1},{2,10},{10,2},{3,11},{11,3},{4,12},{12,4},... | collective-permute-start | bytes 1277960 | tf_op jit(solution)/shard_map/ppermute | solution.py:38
  51.2 6.5 %collective-permute-start.14 = (bf16[2,832,128]{2,1,0:T(8,128)(2,1)S(1)}, bf16[2,832,128]{2,1,0:T(8,128)(2,1)S(1)}, u32[]{:S(2)}, u32[]{:S(2)}) collective-permute-start(bf16[2,832,128]{2,1,0:T(8,128)(2,1)S(1)} %get-tuple-element.18.refs_10_), channel_id=1, source_target_pairs={{0,8},{8,0},{1,9},{9,1},{2,10},{10,2},{3,11},{11,3},{4,12},{12,4},... | collective-permute-start | bytes 1277960 | tf_op jit(solution)/shard_map/ppermute | solution.py:38
  51.2 4.8 %collective-permute-start.17 = (bf16[1,832,128]{2,1,0:T(8,128)(2,1)S(1)}, bf16[1,832,128]{2,1,0:T(8,128)(2,1)S(1)}, u32[]{:S(2)}, u32[]{:S(2)}) collective-permute-start(bf16[1,832,128]{2,1,0:T(8,128)(2,1)S(1)} %collective-permute-done.11.refs_13_), channel_id=1, source_target_pairs={{0,8},{8,0},{1,9},{9,1},{2,10},{10,2},{3,11},{11,3},{4,12},{12,4},... | collective-permute-start | bytes 638984 | tf_op jit(solution)/shard_map/ppermute | solution.py:38
  55.0 2.7 %collective-permute-start.15 = (bf16[2,832,128]{2,1,0:T(8,128)(2,1)S(1)}, bf16[2,832,128]{2,1,0:T(8,128)(2,1)S(1)}, u32[]{:S(2)}, u32[]{:S(2)}) collective-permute-start(bf16[2,832,128]{2,1,0:T(8,128)(2,1)S(1)} %get-tuple-element.19.refs_11_), channel_id=1, source_target_pairs={{0,8},{8,0},{1,9},{9,1},{2,10},{10,2},{3,11},{11,3},{4,12},{12,4},... | collective-permute-start | bytes 1277960 | tf_op jit(solution)/shard_map/ppermute | solution.py:38
  55.0 2.7 %collective-permute-start.16 = (bf16[2,832,128]{2,1,0:T(8,128)(2,1)S(1)}, bf16[2,832,128]{2,1,0:T(8,128)(2,1)S(1)}, u32[]{:S(2)}, u32[]{:S(2)}) collective-permute-start(bf16[2,832,128]{2,1,0:T(8,128)(2,1)S(1)} %get-tuple-element.20.refs_12_), channel_id=1, source_target_pairs={{0,8},{8,0},{1,9},{9,1},{2,10},{10,2},{3,11},{11,3},{4,12},{12,4},... | collective-permute-start | bytes 1277960 | tf_op jit(solution)/shard_map/ppermute | solution.py:38
  56.1 1.6 %collective-permute-start.18 = (bf16[1,832,128]{2,1,0:T(8,128)(2,1)S(1)}, bf16[1,832,128]{2,1,0:T(8,128)(2,1)S(1)}, u32[]{:S(2)}, u32[]{:S(2)}) collective-permute-start(bf16[1,832,128]{2,1,0:T(8,128)(2,1)S(1)} %collective-permute-done.12.refs_14_), channel_id=1, source_target_pairs={{0,8},{8,0},{1,9},{9,1},{2,10},{10,2},{3,11},{11,3},{4,12},{12,4},... | collective-permute-start | bytes 638984 | tf_op jit(solution)/shard_map/ppermute | solution.py:38
